TPU v7x, 128 devices: a whole 4x4x4 slice. The times are simulated.
128 devices in a mesh: grid: 32 (over y_lo, x, z), ch: 4 (over y_hi, core).
Axes of the slice: x: 4, y: 4 (y_hi: 2, y_lo: 2; y = y_hi * 2 + y_lo), z: 4, core: 2. Of those that a mesh axis runs over, the one named last changes fastest.
Arguments:
- inputs: bfloat16 [128, 1024, 512], P('grid', None, 'ch'), may hold values from -6 to 6
- w_gate: bfloat16 [512, 512], P(None, 'ch'), may hold values from -0.25 to 0.25
- w_value: bfloat16 [512, 512], P(None, 'ch'), may hold values from -0.25 to 0.25
- short_filter: bfloat16 [2, 3, 3, 512], P(None, None, None, 'ch'), may hold values from -2 to 2
- row_filter: bfloat16 [1024, 512], P(None, 'ch'), may hold values from -0.1875 to 0.1875
- column_filter: bfloat16 [128, 512], P(None, 'ch'), may hold values from -0.5 to 0.5
- cotangent: bfloat16 [128, 1024, 512], P('grid', None, 'ch'), may hold values from -6 to 6
Outputs:
- gated: bfloat16 [128, 1024, 512], P('grid', None, 'ch')
- input_grad: bfloat16 [128, 1024, 512], P('grid', None, 'ch')
- gate_grad: float32 [512, 512], P('grid', 'ch')
- value_grad: float32 [512, 512], P('grid', 'ch')
- short_grad: float32 [2, 3, 3, 512], P(None, None, None, 'ch')
- row_grad: float32 [1024, 512], P('grid', 'ch')
- column_grad: float32 [128, 512], P('grid', 'ch')
All inputs are finite; a program needn't handle non-finite values.
Results may differ from a plain program's by a relative error of at most 0.025.
Values may be sent and summed in bfloat16 or wider, within the bound.
No kernel may reach another device: no remote copies, remote signals or barrier semaphores. Data moves between devices by JAX's collectives and lax.ppermute only.
A program may use at most 128 MiB of HBM per device.

v0:
```python
import math

import jax
import jax.numpy as jnp
from jax import lax
from jax.sharding import PartitionSpec as P

highest = lax.Precision.HIGHEST


def extended(value, sides, width):
    for axis, dim in sides:
        size, length = (lax.axis_size(axis), value.shape[dim])
        up = [(i, (i + 1) % size) for i in range(size - 1)]
        down = [(j, i) for i, j in up]
        last = lax.slice_in_dim(value, length - width, length, axis=dim)
        initial = lax.slice_in_dim(value, 0, width, axis=dim)
        before = lax.ppermute(last, axis, up)
        after = lax.ppermute(initial, axis, down)
        value = jnp.concatenate([before, value, after], axis=dim)
    return value


def sent_to_all(value, axis):
    copies = jnp.broadcast_to(value, (lax.axis_size(axis), *value.shape))
    return lax.all_to_all(copies, axis, split_axis=0, concat_axis=0, tiled=True)


def taken_together(value, axis):
    return sent_to_all(value, axis).sum(axis=0)


def in_one_piece(arrays, axis, dim, along):
    both = jnp.concatenate(arrays, axis=along)
    out, at, finished = (lax.psum_scatter(both, axis, scatter_dimension=dim, tiled=True), 0, [])
    for a in arrays:
        finished.append(lax.slice_in_dim(out, at, at + a.shape[along], axis=along))
        at += a.shape[along]
    return tuple(finished)


def hartley(length):
    position = jnp.arange(length, dtype=jnp.int32)
    product = position[:, None] * position[None, :] % length
    phases = product.astype(jnp.float32) * (2.0 * math.pi / length)
    return jnp.cos(phases) + jnp.sin(phases)


def mirror(values, along):
    leading = lax.slice_in_dim(values, 0, 1, axis=along)
    remainder = lax.slice_in_dim(values, 1, values.shape[along], axis=along)
    return jnp.concatenate([leading, jnp.flip(remainder, along)], axis=along)


def even_odd(spectrum, along):
    reversed_spec = mirror(spectrum, along)
    return (0.5 * (spectrum + reversed_spec), 0.5 * (spectrum - reversed_spec))


def column_forward(row_cols, cas_height, col_even, col_odd):
    spec_rows = jnp.einsum("hwc,hk->kwc", row_cols, cas_height, precision=highest)
    second = spec_rows * col_even[:, None] + mirror(spec_rows, 0) * col_odd[:, None]
    mixed_cols = (
        jnp.einsum("kwc,kh->hwc", second, cas_height, precision=highest) / cas_height.shape[0]
    )
    return (spec_rows, mixed_cols)


def column_backward(grad_cols, spec_rows, cas_height, col_even, col_odd, scale):
    full_height = cas_height.shape[0]
    spec_grad = jnp.einsum("hwc,hk->kwc", grad_cols, cas_height, precision=highest)
    mirrored_grad = mirror(spec_grad, 0)
    back_cols = spec_grad * col_even[:, None] - mirrored_grad * col_odd[:, None]
    grad_row_cols = (
        jnp.einsum("kwc,kh->hwc", back_cols, cas_height, precision=highest) / full_height
    )
    rows_even, rows_odd = even_odd(spec_rows, 0)
    col_term = jnp.sum(spec_grad * rows_even - mirrored_grad * rows_odd, axis=1)
    col_grad = jnp.einsum("kc,km->mc", col_term, cas_height, precision=highest) * (
        scale / full_height
    )
    return (grad_row_cols, col_grad)


def local(inputs, w_gate, w_value, short_filter, row_filter, column_filter, cotangent):
    tile_rows, full_width, channels = inputs.shape
    gathered = lax.all_gather(inputs, "ch", axis=2, tiled=True)
    w_both = jnp.concatenate([w_gate, w_value], axis=1)
    stacked = jnp.einsum(
        "rwd,dc->rwc", gathered, w_both, preferred_element_type=jnp.float32
    ).astype(jnp.bfloat16)
    kernel = jnp.concatenate([short_filter[0], short_filter[1]], axis=-1).astype(jnp.float32)
    framed = extended(stacked, (("grid", 0),), 1)
    framed = jnp.pad(framed, ((0, 0), (1, 1), (0, 0))).astype(jnp.float32)
    featured = jnp.zeros((tile_rows, full_width, 2 * channels), jnp.float32)
    for row_shift in range(3):
        for col_shift in range(3):
            featured = (
                featured
                + kernel[row_shift, col_shift]
                * framed[row_shift : row_shift + tile_rows, col_shift : col_shift + full_width]
            )
    featured = featured.astype(jnp.bfloat16)
    gate_feat = featured[..., :channels].astype(jnp.float32)
    value_bf = featured[..., channels:]
    cas_width = hartley(full_width)
    width_high = cas_width.astype(jnp.bfloat16)
    width_low = (cas_width - width_high.astype(jnp.float32)).astype(jnp.bfloat16)
    spec_b = jnp.einsum("rwc,wk->rkc", value_bf, width_high, preferred_element_type=jnp.float32)
    spec_b = spec_b + jnp.einsum(
        "rwc,wk->rkc", value_bf, width_low, preferred_element_type=jnp.float32
    )
    row_spec = jnp.einsum("mc,mk->kc", row_filter.astype(jnp.float32), cas_width, precision=highest)
    row_even, row_odd = even_odd(row_spec, 0)
    row_mixed = spec_b * row_even + mirror(spec_b, 1) * row_odd
    mix_row = jnp.einsum("rkc,kw->rwc", row_mixed, cas_width, precision=highest) / full_width
    full_height = column_filter.shape[0]
    cas_height = hartley(full_height)
    col_spec = jnp.einsum(
        "mc,mk->kc", column_filter.astype(jnp.float32), cas_height, precision=highest
    )
    col_even, col_odd = even_odd(col_spec, 0)
    scale = 1.0 / math.sqrt(full_height * full_width)
    grad_out = cotangent.astype(jnp.float32)
    grad_mix = grad_out * gate_feat
    row_cols = lax.all_to_all(mix_row, "grid", split_axis=1, concat_axis=0, tiled=True)
    spec_rows, mixed_cols = column_forward(row_cols, cas_height, col_even, col_odd)
    mix_col = lax.all_to_all(mixed_cols, "grid", split_axis=0, concat_axis=1, tiled=True)
    grad_cols = lax.all_to_all(grad_mix, "grid", split_axis=1, concat_axis=0, tiled=True)
    grad_row_cols, col_grad = column_backward(
        grad_cols, spec_rows, cas_height, col_even, col_odd, scale
    )
    grad_row = lax.all_to_all(grad_row_cols, "grid", split_axis=0, concat_axis=1, tiled=True)
    gated = (gate_feat * mix_col).astype(jnp.bfloat16)
    grad_gate = grad_out * mix_col
    spec_gr = jnp.einsum("rwc,wk->rkc", grad_row, cas_width, precision=highest)
    mirrored_gr = mirror(spec_gr, 1)
    back_rows = spec_gr * row_even - mirrored_gr * row_odd
    grad_value = jnp.einsum("rkc,kw->rwc", back_rows, cas_width, precision=highest) / full_width
    value_even, value_odd = even_odd(spec_b, 1)
    row_term = jnp.sum(spec_gr * value_even - mirrored_gr * value_odd, axis=0)
    row_grad = jnp.einsum("kc,km->mc", row_term, cas_width, precision=highest) * (
        scale / full_width
    )
    grad_feat = jnp.concatenate([grad_gate, grad_value], axis=2)
    grad_framed = extended(grad_feat, (("grid", 0),), 1)
    grad_framed = jnp.pad(grad_framed, ((0, 0), (1, 1), (0, 0)))
    back_sum = jnp.zeros((tile_rows, full_width, 2 * channels), jnp.float32)
    short_rows = []
    for row_shift in range(3):
        short_cols = []
        for col_shift in range(3):
            back_sum = (
                back_sum
                + kernel[row_shift, col_shift]
                * grad_framed[
                    2 - row_shift : 2 - row_shift + tile_rows,
                    2 - col_shift : 2 - col_shift + full_width,
                ]
            )
            short_cols.append(
                jnp.sum(
                    grad_feat
                    * framed[row_shift : row_shift + tile_rows, col_shift : col_shift + full_width],
                    axis=(0, 1),
                )
            )
        short_rows.append(jnp.stack(short_cols))
    back_stack = back_sum.astype(jnp.bfloat16)
    short_term = jnp.stack(short_rows).reshape(3, 3, 2, channels).transpose(2, 0, 1, 3) * scale
    short_grad = taken_together(short_term, "grid")
    weight_term = (
        jnp.einsum("rwd,rwc->dc", gathered, back_stack, preferred_element_type=jnp.float32) * scale
    )
    gate_grad, value_grad, row_share, col_share = (
        *tuple(
            (
                part.astype(jnp.float32)
                for part in in_one_piece(
                    (
                        weight_term[:, :channels].astype(jnp.bfloat16),
                        weight_term[:, channels:].astype(jnp.bfloat16),
                    ),
                    "grid",
                    0,
                    1,
                )
            )
        ),
        lax.psum_scatter(
            row_grad.astype(jnp.bfloat16), "grid", scatter_dimension=0, tiled=True
        ).astype(jnp.float32),
        lax.psum_scatter(
            col_grad.astype(jnp.bfloat16), "grid", scatter_dimension=0, tiled=True
        ).astype(jnp.float32),
    )
    partial_term = jnp.einsum("rwc,dc->rwd", back_stack, w_both, preferred_element_type=jnp.float32)
    input_grad = lax.psum_scatter(
        partial_term.astype(jnp.bfloat16), "ch", scatter_dimension=2, tiled=True
    )
    return (gated, input_grad, gate_grad, value_grad, short_grad, row_share, col_share)


def solution(mesh):
    return jax.shard_map(
        local,
        mesh=mesh,
        in_specs=(
            P("grid", None, "ch"),
            P(None, "ch"),
            P(None, "ch"),
            P(None, None, None, "ch"),
            P(None, "ch"),
            P(None, "ch"),
            P("grid", None, "ch"),
        ),
        out_specs=(
            P("grid", None, "ch"),
            P("grid", None, "ch"),
            P("grid", "ch"),
            P("grid", "ch"),
            P(None, None, None, "ch"),
            P("grid", "ch"),
            P("grid", "ch"),
        ),
        check_vma=False,
    )
```

profile of v0, /device:TPU:1, one launch (start us, length us, event | category | flops | bytes accessed | tf_op | source)
XLA Modules:
  0.0 852.9 jit_solution(1161996941468640835)
XLA Ops:
  8.1 20.8 %fusion.43 = f32[1024,128]{1,0:T(8,128)S(1)} fusion(bf16[1024,128]{1,0:T(8,128)(2,1)S(1)} %copy-done), kind=kOutput, calls=%fused_computation.93 | convolution fusion | flops 1626341376 | bytes 786432 | tf_op jit(solution)/shard_map/mc,mk->kc/dot_general | solution.py:113
  30.1 22.3 %all-gather.2.cloned.1.call-done = bf16[4,1024,512]{2,1,0:T(8,128)(2,1)} async-done(((bf16[4,1024,128]{2,1,0:T(8,128)(2,1)}), bf16[4,1024,512]{2,1,0:T(8,128)(2,1)}) %all-gather.2.cloned.1.call-update) | async-done | bytes 4194320 | tf_op jit(solution)/shard_map/all_gather | solution.py:87
  52.4 3.5 convert_bitcast_fusion
  56.9 4.0 collective-permute-start
  62.2 2.7 rev.24
  66.2 5.2 collective-permute-done
  71.4 4.6 collective-permute-done.1
  76.0 3.2 fusion.22
  79.3 7.9 add_convert_fusion
  88.5 17.2 %fusion.26 = f32[1024,4,128]{2,0,1:T(8,128)S(1)} fusion(bf16[4,1024,256]{1,2,0:T(8,128)(2,1)S(1)} %add_convert_fusion), kind=kOutput, calls=%fused_computation.67 | convolution fusion | flops 1093664768 | bytes 3145728 | tf_op jit(solution)/shard_map/rwc,wk->rkc/dot_general | solution.py:110
  105.7 18.4 %add_bitcast_fusion = f32[4,1024,128]{2,1,0:T(8,128)S(1)} fusion(f32[1024,4,128]{2,0,1:T(8,128)S(1)} %fusion.26, bf16[4,1024,256]{1,2,0:T(8,128)(2,1)} %copy-done.11), kind=kOutput, calls=%fused_computation.90 | convolution fusion | flops 1091043328 | bytes 5242880 | tf_op jit(solution)/shard_map/rwc,wk->rkc/dot_general | solution.py:109
  124.1 1.6 slice.247
  125.7 17.4 %rev.25 = f32[4,1023,128]{2,1,0:T(8,128)} reverse(f32[4,1023,128]{2,1,0:T(8,128)} %slice.247), dimensions={1} | reverse | bytes 4190208 | tf_op jit(solution)/shard_map/jit(_flip)/rev | solution.py:52
  143.1 1.9 fusion.175
  145.1 30.1 %multiply_bitcast_fusion.1 = f32[4,1024,128]{1,2,0:T(8,128)S(1)} fusion(f32[4,1024,128]{2,1,0:T(8,128)S(1)} %fusion.175), kind=kOutput, calls=%fused_computation.86 | convolution fusion | flops 6458703872 | bytes 4194304 | tf_op jit(solution)/shard_map/rkc,kw->rwc/dot_general | solution.py:116
  175.2 1.9 copy.99
  177.1 8.8 %all-to-all-start = ((f32[4,1024,128]{2,0,1:T(4,128)}), f32[4,1024,128]{2,0,1:T(4,128)S(1)}, u32[]{:S(2)}, u32[]{:S(2)}) async-start(f32[4,1024,128]{2,0,1:T(4,128)} %copy.99), calls=%async_computation | async-start | bytes 4194304 | tf_op jit(solution)/shard_map/all_to_all | solution.py:126
  187.7 1.5 add_multiply_fusion.1
  189.2 22.6 %all-to-all-done = f32[4,1024,128]{2,0,1:T(4,128)S(1)} async-done(((f32[4,1024,128]{2,0,1:T(4,128)}), f32[4,1024,128]{2,0,1:T(4,128)S(1)}, u32[]{:S(2)}, u32[]{:S(2)}) %all-to-all-start) | async-done | bytes 2097184 | tf_op jit(solution)/shard_map/all_to_all | solution.py:126
  213.2 2.2 fusion.85
  215.4 1.6 slice.251
  217.0 16.6 %rev.27 = f32[127,32,128]{2,0,1:T(8,128)} reverse(f32[127,32,128]{2,0,1:T(8,128)} %slice.251), dimensions={0} | reverse | bytes 4161536 | tf_op jit(solution)/shard_map/jit(_flip)/rev | solution.py:52
  233.6 4.0 fusion.47
  237.7 2.5 copy.102
  240.2 8.4 all-to-all-start.1
  248.6 2.3 copy.105
  250.8 25.1 %all-to-all-done.1 = f32[128,32,128]{2,1,0:T(8,128)S(1)} async-done(((f32[128,32,128]{2,1,0:T(8,128)}), f32[128,32,128]{2,1,0:T(8,128)S(1)}, u32[]{:S(2)}, u32[]{:S(2)}) %all-to-all-start.1) | async-done | bytes 2097184 | tf_op jit(solution)/shard_map/all_to_all | solution.py:128
  275.9 1.5 copy.103
  277.4 1.9 copy.104
  279.4 4.5 convert_multiply_fusion
  283.9 2.0 copy.107
  285.9 33.2 %all_to_all.77 = f32[4,1024,128]{2,0,1:T(4,128)S(1)} all-to-all(f32[4,1024,128]{2,0,1:T(4,128)S(1)} %copy.107), channel_id=1, replica_groups=mesh['grid'=32,'ch'=4] {'grid'}, dimensions={1} | all-to-all | bytes 4194304 | tf_op jit(solution)/shard_map/all_to_all | solution.py:129
  320.7 2.2 fusion.82
  322.9 1.6 slice.253
  324.5 16.6 %rev.28 = f32[127,32,128]{2,0,1:T(8,128)} reverse(f32[127,32,128]{2,0,1:T(8,128)} %slice.253), dimensions={0} | reverse | bytes 4161536 | tf_op jit(solution)/shard_map/jit(_flip)/rev | solution.py:52
  341.1 4.0 fusion.50
  345.1 2.5 copy.110
  347.7 5.2 all-to-all-start.3
  353.0 17.9 %fusion.178 = f32[1024,1024,1]{1,0,2:T(8,128)} fusion(), kind=kLoop, calls=%fused_computation.39.clone.clone.clone.1 | loop fusion | flops 15728640 | bytes 4194304 | tf_op jit(solution)/shard_map/rwc,wk->rkc/dot_general | solution.py:136
  370.9 17.5 %sine_add_fusion.20 = f32[1024,1024]{1,0:T(8,128)} fusion(), kind=kLoop, calls=%fused_computation.52.clone.1.clone.1 | loop fusion | flops 15728640 | bytes 4194304
  388.6 2.0 copy-done.10
  390.6 6.8 fusion.53
  397.4 1.5 slice.255
  399.6 17.1 %rev.29 = f32[4,1023,128]{2,1,0:T(8,128)} reverse(f32[4,1023,128]{2,1,0:T(8,128)} %slice.255), dimensions={1} | reverse | bytes 4190208 | tf_op jit(solution)/shard_map/jit(_flip)/rev | solution.py:52
  416.7 6.0 subtract_reduce_fusion.1
  422.7 1.9 copy.113
  424.6 9.1 %fusion.41 = f32[1024,512]{0,1:S(1)} fusion(f32[1024,512]{0,1:T(8,128)S(1)} %bitcast.133, f32[1024,1024]{1,0:T(8,128)} %sine_add_fusion.20), kind=kOutput, calls=%fused_computation.91 | convolution fusion | flops 6442450944 | bytes 8388608
  435.3 1.5 fusion.68
  436.8 3.2 collective-permute-start.2
  441.3 25.0 %fusion.64 = bf16[1024,128]{1,0:T(8,128)(2,1)} fusion(f32[1024,128]{1,0:T(8,128)S(1)} %copy-done.14), kind=kOutput, calls=%fused_computation.102 | convolution fusion | flops 1626603520 | bytes 786432 | tf_op jit(solution)/shard_map/kc,km->mc/dot_general | solution.py:142
  466.4 8.7 %select_maximum_fusion = f32[6,1026,256]{1,2,0:T(8,128)} fusion(f32[1,1024,256]{1,2,0:T(8,128)} %collective-permute-done.3, f32[1,1024,256]{1,2,0:T(8,128)S(1)} %collective-permute-done.2, f32[4,1024,128]{1,2,0:T(8,128)S(1)} %multiply_bitcast_fusion, f32[4,1024,128]{1,2,0:T(8,128)} %get-tuple-element.56), kind=kLoop, calls=%fused_computation.2 | loop fusion | flops 15759360 | bytes 12595200 | tf_op jit(solution)/shard_map/concatenate | solution.py:20
  475.1 15.5 %fusion.5 = bf16[4,1024,256]{1,2,0:T(8,128)(2,1)} fusion(f32[6,1026,256]{1,2,0:T(8,128)} %select_maximum_fusion, f32[1,1024,256]{1,2,0:T(8,128)S(1)} %collective-permute-done.2, f32[4,1024,128]{1,2,0:T(8,128)S(1)} %multiply_bitcast_fusion, f32[4,1024,128]{1,2,0:T(8,128)} %get-tuple-element.56, f32[1,1024,256]{1,2,0:T(8,128)} %collective-permute-done.3, ...), kind=kLoop, calls=%fused_computation.19 | loop fusion | flops 24117248 | bytes 33563648 | tf_op jit(solution)/shard_map/convert_element_type | solution.py:169
  490.6 4.1 fusion.66
  495.6 5.0 convolution_convert_fusion
  500.6 8.3 copy.133
  508.9 6.5 copy.141
  518.6 4.5 subtract_reduce_fusion
  523.1 19.8 %multiply_reduce_fusion.7 = (f32[256]{0:T(256)S(1)}, f32[256]{0:T(256)S(1)}, f32[256]{0:T(256)S(1)}, f32[256]{0:T(256)S(1)}, f32[256]{0:T(256)S(1)}, /*index=5*/...) fusion(f32[6,1026,256]{1,2,0:T(8,128)} %copy-done.2, f32[4,1024,128]{1,2,0:T(8,128)S(1)} %multiply_bitcast_fusion, ...), kind=kLoop, calls=%fused_computation.49 | loop fusion | flops 19920640 | bytes 41952256 | tf_op jit(solution)/shard_map/reduce_sum | solution.py:162
  543.8 9.0 %all-to-all-start.4 = ((f32[32,2,3,3,128]{4,1,3,2,0:T(2,128)}), f32[32,2,3,3,128]{4,1,3,2,0:T(2,128)S(1)}, u32[]{:S(2)}, u32[]{:S(2)}) async-start(f32[32,2,3,3,128]{4,1,3,2,0:T(2,128)} %broadcast_in_dim.2), calls=%async_computation.4 | async-start | bytes 589824 | tf_op jit(solution)/shard_map/all_to_all | solution.py:26
  553.3 132.1 %all-reduce.2 = bf16[128,128]{1,0:T(8,128)(2,1)S(1)} all-reduce(bf16[128,128]{1,0:T(8,128)(2,1)S(1)} %fusion.67), channel_id=5, replica_groups=mesh['grid'=32,'ch'=4] {'grid'}, use_global_device_ids=true, to_apply=%region_15.16.clone | all-reduce | flops 16384 | bytes 65536
  687.9 79.1 %reduce-scatter.12.cloned.1.call-done = bf16[16,256]{1,0:T(8,128)(2,1)} async-done(((bf16[512,256]{1,0:T(8,128)(2,1)}), bf16[16,256]{1,0:T(8,128)(2,1)}) %reduce-scatter.12.cloned.1.call-update) | async-done | bytes 8208
  769.4 73.2 %reduce-scatter.10.cloned.1.call-done = bf16[128,4096]{1,0:T(8,128)(2,1)} async-done(((bf16[512,4096]{1,0:T(8,128)(2,1)}), bf16[128,4096]{1,0:T(8,128)(2,1)}) %reduce-scatter.10.cloned.1.call-update) | async-done | bytes 1048592
  842.5 1.8 reshape.54
  844.4 1.7 copy.134
  (95 shorter events, 25.1 us)
Async XLA Ops:
  7.2 1.0 copy-start
  7.2 45.2 %all-gather.2.cloned.1.call-start = ((), (), s32[]{:S(2)}) async-start(), calls=%async_computation.8 | async-start | bytes 5242880 | tf_op jit(solution)/shard_map/all_gather | solution.py:87
  8.1 21.7 %copy-start.16 = (bf16[512,128]{1,0:T(8,128)(2,1)S(1)}, bf16[512,128]{1,0:T(8,128)(2,1)}, u32[]{:S(2)}) copy-start(bf16[512,128]{1,0:T(8,128)(2,1)} %param.8) | copy-start | bytes 393220
  8.1 21.8 %copy-start.17 = (bf16[512,128]{1,0:T(8,128)(2,1)S(1)}, bf16[512,128]{1,0:T(8,128)(2,1)}, u32[]{:S(2)}) copy-start(bf16[512,128]{1,0:T(8,128)(2,1)} %param.9) | copy-start | bytes 393220
  29.0 0.8 copy-start.13
  30.1 32.1 %copy-start.18 = (bf16[2,3,3,128]{3,0,2,1:T(2,128)(2,1)S(1)}, bf16[2,3,3,128]{3,0,2,1:T(2,128)(2,1)}, u32[]{:S(2)}) copy-start(bf16[2,3,3,128]{3,0,2,1:T(2,128)(2,1)} %param.10) | copy-start | bytes 13828
  30.1 34.9 %slice-start = ((f32[1024,128]{1,0:T(8,128)}), f32[1,128]{1,0:T(1,128)S(1)}, s32[]{:S(2)}) async-start(f32[1024,128]{1,0:T(8,128)} %copy-done.13), calls=%async_computation.12 | async-start | bytes 1024 | tf_op jit(solution)/shard_map/slice | solution.py:50
  56.9 14.5 %collective-permute-start = (bf16[1,1024,256]{1,2,0:T(8,128)(2,1)}, bf16[1,1024,256]{1,2,0:T(8,128)(2,1)}, u32[]{:S(2)}, u32[]{:S(2)}) collective-permute-start(bf16[1,1024,256]{1,2,0:T(8,128)(2,1)} %get-tuple-element.57), channel_id=1, source_target_pairs={{0,4},{4,8},{8,12},{12,16},{16,20},{20,24},{24,28},{28,32},{32,36}... | collective-permute-start | bytes 1572872 | tf_op jit(solution)/shard_map/ppermute | solution.py:18
  60.9 15.1 %collective-permute-start.1 = (bf16[1,1024,256]{1,2,0:T(8,128)(2,1)}, bf16[1,1024,256]{1,2,0:T(8,128)(2,1)}, u32[]{:S(2)}, u32[]{:S(2)}) collective-permute-start(bf16[1,1024,256]{1,2,0:T(8,128)(2,1)} %get-tuple-element.58), channel_id=1, source_target_pairs={{4,0},{8,4},{12,8},{16,12},{20,16},{24,20},{28,24},{32,28},{36,32}... | collective-permute-start | bytes 1572872 | tf_op jit(solution)/shard_map/ppermute | solution.py:19
  79.2 7.9 copy-start.2
  87.2 1.3 copy-start.11
  124.1 19.1 %copy-start.7 = (f32[4,1024,128]{2,1,0:T(8,128)}, f32[4,1024,128]{2,1,0:T(8,128)S(1)}, u32[]{:S(2)}) copy-start(f32[4,1024,128]{2,1,0:T(8,128)S(1)} %add_bitcast_fusion) | copy-start | bytes 6291460
  175.2 10.7 %copy-start.19 = (bf16[128,128]{1,0:T(8,128)(2,1)S(1)}, bf16[128,128]{1,0:T(8,128)(2,1)}, u32[]{:S(2)}) copy-start(bf16[128,128]{1,0:T(8,128)(2,1)} %param.12) | copy-start | bytes 98308
  177.1 34.6 %all-to-all-start = ((f32[4,1024,128]{2,0,1:T(4,128)}), f32[4,1024,128]{2,0,1:T(4,128)S(1)}, u32[]{:S(2)}, u32[]{:S(2)}) async-start(f32[4,1024,128]{2,0,1:T(4,128)} %copy.99), calls=%async_computation | async-start | bytes 4194304 | tf_op jit(solution)/shard_map/all_to_all | solution.py:126
  186.4 0.6 copy-start.15
  215.4 18.2 %copy-start.5 = (f32[128,32,128]{2,0,1:T(8,128)}, f32[128,32,128]{2,0,1:T(8,128)S(1)}, u32[]{:S(2)}) copy-start(f32[128,32,128]{2,0,1:T(8,128)S(1)} %fusion.85) | copy-start | bytes 6291460
  240.2 35.7 %all-to-all-start.1 = ((f32[128,32,128]{2,1,0:T(8,128)}), f32[128,32,128]{2,1,0:T(8,128)S(1)}, u32[]{:S(2)}, u32[]{:S(2)}) async-start(f32[128,32,128]{2,1,0:T(8,128)} %copy.102), calls=%async_computation.1 | async-start | bytes 4194304 | tf_op jit(solution)/shard_map/all_to_all | solution.py:128
  322.8 18.2 %copy-start.6 = (f32[128,32,128]{2,0,1:T(8,128)}, f32[128,32,128]{2,0,1:T(8,128)S(1)}, u32[]{:S(2)}) copy-start(f32[128,32,128]{2,0,1:T(8,128)S(1)} %fusion.82) | copy-start | bytes 6291460
  347.7 40.8 %all-to-all-start.3 = ((f32[128,32,128]{2,1,0:T(8,128)}), f32[128,32,128]{2,1,0:T(8,128)S(1)}, u32[]{:S(2)}, u32[]{:S(2)}) async-start(f32[128,32,128]{2,1,0:T(8,128)} %copy.110), calls=%async_computation.3 | async-start | bytes 4194304 | tf_op jit(solution)/shard_map/all_to_all | solution.py:133
  352.9 333.7 %reduce-scatter.8.cloned.1.call-start = ((), (), s32[]{:S(2)}) async-start(), calls=%async_computation.9 | async-start | bytes 270336 | tf_op jit(solution)/shard_map/reduce_scatter | solution.py:190
  388.5 2.2 copy-start.10
  397.4 2.1 copy-start.9
  397.4 19.2 %copy-start.8 = (f32[4,1024,128]{2,1,0:T(8,128)S(1)}, f32[4,1024,128]{2,1,0:T(8,128)}, u32[]{:S(2)}) copy-start(f32[4,1024,128]{2,1,0:T(8,128)} %copy-done.7) | copy-start | bytes 6291460
  433.7 1.6 copy-start.3
  433.9 7.4 copy-start.14
  436.8 29.6 %collective-permute-start.2 = (f32[1,1024,256]{1,2,0:T(8,128)}, f32[1,1024,256]{1,2,0:T(8,128)S(1)}, u32[]{:S(2)}, u32[]{:S(2)}) collective-permute-start(f32[1,1024,256]{1,2,0:T(8,128)} %get-tuple-element.52), channel_id=1, source_target_pairs={{0,4},{4,8},{8,12},{12,16},{16,20},{20,24},{24,28},{28,32},{32,36}... | collective-permute-start | bytes 3145736 | tf_op jit(solution)/shard_map/ppermute | solution.py:18
  440.0 26.4 %collective-permute-start.3 = (f32[1,1024,256]{1,2,0:T(8,128)}, f32[1,1024,256]{1,2,0:T(8,128)}, u32[]{:S(2)}, u32[]{:S(2)}) collective-permute-start(f32[1,1024,256]{1,2,0:T(8,128)} %get-tuple-element.53), channel_id=1, source_target_pairs={{4,0},{8,4},{12,8},{16,12},{20,16},{24,20},{28,24},{32,28},{36,32}... | collective-permute-start | bytes 3145736 | tf_op jit(solution)/shard_map/ppermute | solution.py:19
  466.3 300.7 %reduce-scatter.12.cloned.1.call-start = ((), (), s32[]{:S(2)}) async-start(), calls=%async_computation.11 | async-start | bytes 270336
  495.6 347.0 %reduce-scatter.10.cloned.1.call-start = ((), (), s32[]{:S(2)}) async-start(), calls=%async_computation.10 | async-start | bytes 5242880
  515.4 0.7 copy-start.20
  515.4 1.9 copy-start.12
  518.6 4.5 copy-start.4
  523.1 323.0 %copy-start.1 = (bf16[1024,128]{1,0:T(8,128)(2,1)S(1)}, bf16[1024,128]{1,0:T(8,128)(2,1)}, u32[]{:S(2)}) copy-start(bf16[1024,128]{1,0:T(8,128)(2,1)} %param.11) | copy-start | bytes 786436
  543.8 142.2 %all-to-all-start.4 = ((f32[32,2,3,3,128]{4,1,3,2,0:T(2,128)}), f32[32,2,3,3,128]{4,1,3,2,0:T(2,128)S(1)}, u32[]{:S(2)}, u32[]{:S(2)}) async-start(f32[32,2,3,3,128]{4,1,3,2,0:T(2,128)} %broadcast_in_dim.2), calls=%async_computation.4 | async-start | bytes 589824 | tf_op jit(solution)/shard_map/all_to_all | solution.py:26
Sparse Core Ops, SparseCore 0:
  9.7 42.6 all-gather.1
  466.4 140.0 reduce-scatter.7
  608.9 158.1 reduce-scatter.11
  769.5 72.9 reduce-scatter.9
where the time goes:
time: 865 us; the launch traced here: 853 us
  waiting for transfers between devices  233 us (27%)
  blocking collectives  165 us (19%)
  matrix products  153 us (18%)
  local copies, waits for them, and re-layouts  130 us (15%)
  other arithmetic  115 us (13%)
  starting transfers between devices  41.3 us (5%)
  between operations  15.3 us (2%)
    unnamed x6, waiting for transfers between devices  153 us
    unnamed x1, blocking collectives  132 us
    rev x6, local copies, waits for them, and re-layouts, mirror(): return jnp.concatenate([leading, jnp.flip(remainder, along)], axis=along)  71.1 us
    all_to_all x1, blocking collectives, local(): lax.all_to_all(grad_mix, 'grid', split_axis=1, concat_axis=0, tiled=True)  33.2 us
    unnamed x58, local copies, waits for them, and re-layouts  32.9 us
    dot_general x1, matrix products, local(): jnp.einsum('rkc,kw->rwc', row_mixed, cas_width, precision=highest)  30.1 us
    all_to_all x1, waiting for transfers between devices, local(): lax.all_to_all(mixed_cols, 'grid', split_axis=0, concat_axis=1, tiled=True)  25.1 us
    dot_general x1, matrix products, local(): jnp.einsum('kc,km->mc', row_term, cas_width, precision=highest)  25 us
  transfers between devices with their start and end apart: 12, of which 7 were waited for; matrix products, arithmetic and copies ran while one was open for 20% of the time, Pallas kernels for 0%

commit v1 on v0

v1 whole, which is shorter than its diff:
```python
import functools
import math

import jax
import jax.numpy as jnp
from jax import lax
from jax.experimental import pallas as pl
from jax.experimental.pallas import tpu as pltpu
from jax.sharding import PartitionSpec as P


BF = jnp.bfloat16
F32 = jnp.float32
EDGE = 8
STEP = 32


def cosine(phase, period):
    folded = phase & (period - 1)
    folded = jnp.minimum(folded, period - folded)
    y = (folded - period // 4).astype(F32) * (2.0 * math.pi / period)
    z = y * y
    series = 1.0 + z * (-1 / 6 + z * (1 / 120 + z * (-1 / 5040 + z * (1 / 362880 - z / 39916800))))
    return -(y * series)


def frequencies(slots, width, owners):
    per_owner = width // owners
    half = per_owner // 2
    place = slots % per_owner
    top = slots == half
    freq = (slots // per_owner) * half + place % half
    freq = jnp.where(top, width // 2, freq)
    offset = jnp.where((place >= half) & ~top, width // 4, 0)
    return freq, offset


def row_matrix(width, owners, slot_dim):
    shape = (width, width)
    freq, offset = frequencies(lax.broadcasted_iota(jnp.int32, shape, slot_dim), width, owners)
    token = lax.broadcasted_iota(jnp.int32, shape, 1 - slot_dim)
    return cosine(freq * token + offset, width).astype(BF)


def column_matrix(height, sign):
    shape = (2 * height, 2 * height)
    i = lax.broadcasted_iota(jnp.int32, shape, 0)
    j = lax.broadcasted_iota(jnp.int32, shape, 1)
    turn = (j // height - i // height) * (-sign * (height // 4))
    return cosine((i % height) * (j % height) + turn + height, height)


def fill_framed(framed, rows_of, channels):
    width = rows_of[0][0].shape[1]
    zeros = jnp.zeros((EDGE, channels), F32)
    for branch in range(2):
        for r in range(len(rows_of)):
            framed[branch, r, pl.ds(0, EDGE), :] = zeros
            framed[branch, r, pl.ds(EDGE + width, EDGE), :] = zeros

    def body(t, _):
        at = pl.multiple_of(t * 32, 32)
        for r, (ref, row) in enumerate(rows_of):
            for branch in range(2):
                v = ref[row, pl.ds(at, 32), pl.ds(branch * channels, channels)]
                framed[branch, r, pl.ds(EDGE + at, 32), :] = v.astype(F32)
        return 0

    lax.fori_loop(0, width // 32, body, 0)


def taps_of(kern, branch, channels):
    return [jnp.broadcast_to(kern[pl.ds(branch * 9 + k, 1), :], (8, channels)) for k in range(9)]


def projected(xs, w):
    size = 2 * xs[0].shape[1]
    total = None
    for n in range(len(xs) // 2):
        pair = jnp.concatenate([xs[2 * n][...], xs[2 * n + 1][...]], axis=1)
        part = jnp.dot(pair, w[pl.ds(n * size, size), :], preferred_element_type=F32)
        total = part if total is None else total + part
    return total.astype(BF)


def project_edge_kernel(x0, x1, x2, x3, w, first, last):
    width = first.shape[1]
    both = projected((x0, x1, x2, x3), w)
    first[0] = both[:width]
    last[0] = both[width:]


def project_mid_kernel(x0, x1, x2, x3, w, middle):
    middle[...] = projected((x0, x1, x2, x3), w).reshape(middle.shape)


def forward_kernel(up, first, middle, last, down, cot, kern, mat, send, feat, framed, cols):
    rows, width, channels = cot.shape
    owners, _, per_owner, _ = send.shape
    inner = [(middle, r) for r in range(rows - 2)]
    fill_framed(framed, [(up, 0), (first, 0), *inner, (last, 0), (down, 0)], channels)
    for branch in range(2):
        taps = taps_of(kern, branch, channels)

        def body(t, _, branch=branch, taps=taps):
            base = pl.multiple_of(t * STEP, STEP)
            done = [[] for _ in range(rows)]
            for p in range(STEP // 8):
                acc = [None] * rows
                for r in range(rows + 2):
                    for j in range(3):
                        v = framed[branch, r, pl.ds(base + 8 * p + EDGE + j - 1, 8), :]
                        for i in range(3):
                            o = r - i
                            if 0 <= o < rows:
                                term = taps[i * 3 + j] * v
                                acc[o] = term if acc[o] is None else acc[o] + term
                for o in range(rows):
                    done[o].append(acc[o])
            for o in range(rows):
                f = jnp.concatenate(done[o], axis=0).astype(BF)
                if branch == 0:
                    feat[o, pl.ds(base, STEP), :] = f
                    g = cot[o, pl.ds(base, STEP), :].astype(F32) * f.astype(F32)
                    cols[pl.ds(base, STEP), pl.ds((rows + o) * channels, channels)] = g.astype(BF)
                else:
                    cols[pl.ds(base, STEP), pl.ds(o * channels, channels)] = f
            return 0

        lax.fori_loop(0, width // STEP, body, 0)
    for n in range(rows):
        spec = jnp.dot(
            mat[...], cols[:, pl.ds(2 * n * channels, 2 * channels)], preferred_element_type=F32
        ).astype(BF)
        for e in range(2):
            send[:, 2 * n + e] = spec[:, e * channels : (e + 1) * channels].reshape(
                owners, per_owner, channels
            )


def column_kernel(
    recv, coef, keep, colr, coli, fwd, inv, send, rowq, colp, stacked, spectra, er, ei
):
    owners, twice, per_owner, channels = recv.shape
    rows = twice // 2
    height = owners * rows
    half = per_owner // 2
    wide = half * channels
    group = 16 // rows

    def place(value, at, offset):
        turned = jnp.swapaxes(value, 0, 1)
        for k in range(half):
            lanes = pl.ds(k * channels + offset, channels)
            stacked[pl.ds(at, 16), lanes] = turned[k]
            stacked[pl.ds(at + height, 16), lanes] = turned[k + half]

    def unpack(n, _):
        at = pl.multiple_of(n * 16, 16)
        mixed = []
        for r in range(16):
            v = recv[n * group + r // rows, r % rows].astype(F32)
            br, bi = v[:half], v[half:]
            both = [br * coef[0] + bi * coef[1], br * coef[2] + bi * coef[3]]
            mixed.append(jnp.concatenate(both, axis=0).astype(BF))
        place(jnp.stack(mixed), at, 0)
        raw = [recv[n * group + r // rows, rows + r % rows] for r in range(16)]
        place(jnp.stack(raw), at, wide)
        return 0

    lax.fori_loop(0, height // 16, unpack, 0)
    for n in range(2 * wide // 512):
        lanes = pl.ds(n * 512, 512)
        spectra[:, lanes] = jnp.dot(fwd[...], stacked[:, lanes], preferred_element_type=F32)

    def products(n, _):
        at = pl.multiple_of(n * 16, 16)
        low, high = pl.ds(at, 16), pl.ds(at + height, 16)
        cr, ci = colr[low, :], coli[low, :]
        sr = jnp.zeros((16, channels), F32)
        si = jnp.zeros((16, channels), F32)
        for k in range(half):
            lanes = pl.ds(k * channels, channels)
            more = pl.ds(k * channels + wide, channels)
            tr, ti = spectra[low, lanes], spectra[high, lanes]
            fr, fi = spectra[low, more], spectra[high, more]
            sr = sr + (fr * tr + fi * ti)
            si = si + (fi * tr - fr * ti)
            stacked[low, lanes] = (tr * cr - ti * ci).astype(BF)
            stacked[high, lanes] = (tr * ci + ti * cr).astype(BF)
            stacked[low, more] = (fr * cr + fi * ci).astype(BF)
            stacked[high, more] = (fi * cr - fr * ci).astype(BF)
        er[low, :] = sr
        ei[low, :] = si
        return 0

    lax.fori_loop(0, height // 16, products, 0)
    for n in range(2 * wide // 512):
        lanes = pl.ds(n * 512, 512)
        spectra[:, lanes] = jnp.dot(inv[...], stacked[:, lanes], preferred_element_type=F32)

    e = jnp.concatenate([er[...], ei[...]], axis=0) * (1.0 / height)
    high = e.astype(BF)
    low = (e - high.astype(F32)).astype(BF)
    top = inv[pl.ds(0, height), :]
    colp[...] = jnp.dot(top, high, preferred_element_type=F32) + jnp.dot(
        top, low, preferred_element_type=F32
    )

    def pack(n, sums):
        p1, p2, p3 = sums
        at = pl.multiple_of(n * 16, 16)

        def taken(offset):
            slots = []
            for part in range(2):
                for k in range(half):
                    lanes = pl.ds(k * channels + offset, channels)
                    slots.append(spectra[pl.ds(at + part * height, 16), lanes])
            return jnp.stack(slots)

        mixed = jnp.swapaxes(taken(0).astype(BF), 0, 1)
        for r in range(16):
            send[n * group + r // rows, r % rows] = mixed[r]
        turned = jnp.swapaxes(taken(wide), 0, 1)
        for r in range(16):
            ar, ai = turned[r, :half], turned[r, half:]
            v = recv[n * group + r // rows, r % rows].astype(F32)
            br, bi = v[:half], v[half:]
            p1 = p1 + ar * br
            p2 = p2 + ai * bi
            p3 = p3 + (ai * br - ar * bi)
            both = [ar * coef[0] + ai * coef[2], ar * coef[1] + ai * coef[3]]
            send[n * group + r // rows, rows + r % rows] = jnp.concatenate(both, axis=0).astype(BF)
        return p1, p2, p3

    none = jnp.zeros((half, channels), F32)
    p1, p2, p3 = lax.fori_loop(0, height // 16, pack, (none, none, none))
    kept = keep[0]
    rowq[pl.ds(0, half), :] = p1 + kept * p2
    rowq[pl.ds(half, half), :] = kept * p3 + (1.0 - kept) * p2


def inverse_kernel(recv, mat, feat, cot, gated, first, middle, last):
    rows, width, channels = cot.shape
    for n in range(rows):
        spec = jnp.concatenate(
            [recv[:, 2 * n + e].reshape(width, channels) for e in range(2)], axis=1
        )
        back = jnp.dot(mat[...], spec, preferred_element_type=F32)
        for e in range(2):
            r = (2 * n + e) % rows
            value = back[:, e * channels : (e + 1) * channels]
            to, row = ((first, 0), *((middle, i) for i in range(rows - 2)), (last, 0))[r]
            if n < rows // 2:
                gated[r] = (feat[r].astype(F32) * value).astype(BF)
                to[row, :, pl.ds(0, channels)] = (cot[r].astype(F32) * value).astype(BF)
            else:
                to[row, :, pl.ds(channels, channels)] = value.astype(BF)


def spread_back(framed, kern, outs, width, channels):
    for branch in range(2):
        taps = taps_of(kern, branch, channels)

        def body(t, _, branch=branch, taps=taps):
            base = pl.multiple_of(t * STEP, STEP)
            done = [[] for _ in outs]
            for p in range(STEP // 8):
                acc = [None] * len(outs)
                needed = sorted({c + 1 - i for _, _, c in outs for i in range(3)})
                for r in needed:
                    for j in range(3):
                        v = framed[branch, r, pl.ds(base + 8 * p + EDGE + 1 - j, 8), :]
                        for n, (_, _, c) in enumerate(outs):
                            i = c + 1 - r
                            if 0 <= i < 3:
                                term = taps[i * 3 + j] * v
                                acc[n] = term if acc[n] is None else acc[n] + term
                for n in range(len(outs)):
                    done[n].append(acc[n])
            for n, (ref, row, _) in enumerate(outs):
                value = jnp.concatenate(done[n], axis=0).astype(BF)
                ref[row, pl.ds(base, STEP), pl.ds(branch * channels, channels)] = value
            return 0

        lax.fori_loop(0, width // STEP, body, 0)


def backward_mid_kernel(gfirst, gmiddle, glast, kern, back, gframed):
    width = gfirst.shape[1]
    channels = kern.shape[1]
    inner = gmiddle.shape[0]
    fill_framed(
        gframed, [(gfirst, 0), *((gmiddle, r) for r in range(inner)), (glast, 0)], channels
    )
    spread_back(gframed, kern, [(back, r, r + 1) for r in range(inner)], width, channels)


def short_kernel(up, first, middle, last, down, gfirst, gmiddle, glast, short, framed):
    width = first.shape[1]
    channels = short.shape[1]
    inner = middle.shape[0]
    rows = inner + 2
    fill_framed(
        framed,
        [(up, 0), (first, 0), *((middle, r) for r in range(inner)), (last, 0), (down, 0)],
        channels,
    )
    grads = [(gfirst, 0), *((gmiddle, r) for r in range(inner)), (glast, 0)]
    for branch in range(2):
        lanes = pl.ds(branch * channels, channels)

        def terms(t, sums, branch=branch, lanes=lanes):
            base = pl.multiple_of(t * 16, 16)
            sums = list(sums)
            both = [ref[row, pl.ds(base, 16), lanes].astype(F32) for ref, row in grads]
            for p in range(2):
                at = base + 8 * p + EDGE
                g = [v[8 * p : 8 * p + 8] for v in both]
                for r in range(rows + 2):
                    for j in range(3):
                        v = framed[branch, r, pl.ds(at + j - 1, 8), :]
                        for i in range(3):
                            o = r - i
                            if 0 <= o < rows:
                                sums[i * 3 + j] = sums[i * 3 + j] + g[o] * v
            return tuple(sums)

        sums = lax.fori_loop(
            0, width // 16, terms, tuple(jnp.zeros((8, channels), F32) for _ in range(9))
        )
        for k in range(9):
            short[pl.ds(branch * 9 + k, 1), :] = jnp.sum(sums[k], axis=0, keepdims=True)


def backward_edge_kernel(gup, gfirst, gmiddle, glast, gdown, kern, back, gframed):
    width = gfirst.shape[1]
    channels = kern.shape[1]
    inner = gmiddle.shape[0]
    fill_framed(
        gframed,
        [(gup, 0), (gfirst, 0), (gmiddle, 0), (gmiddle, inner - 1), (glast, 0), (gdown, 0)],
        channels,
    )
    spread_back(gframed, kern, [(back, 0, 1), (back, 1, 4)], width, channels)


def finish_kernel(kept_edge, edge, kept_mid, mid, grad):
    width = grad.shape[1]
    inner = grad.shape[0] - 2
    for r in range(inner):
        at = pl.ds(r * width, width)
        grad[r + 1] = (kept_mid[at, :] + mid[at, :].astype(F32)).astype(BF)
    for r in range(2):
        at = pl.ds(r * width, width)
        grad[r * (inner + 1)] = (kept_edge[at, :] + edge[at, :].astype(F32)).astype(BF)


def sum_kernel(parts, *outs, scale):
    total = parts[0].astype(F32)
    for n in range(1, parts.shape[0]):
        total = total + parts[n].astype(F32)
    total = total * scale
    at = 0
    for out in outs:
        out[...] = total[at : at + out.shape[0]]
        at += out.shape[0]


def pack_kernel(ch, grad_w, row_part, small, packed):
    owners, _, channels = packed.shape
    parts = 4
    size = grad_w.shape[0] // parts
    each = owners // parts
    deep = size // each
    for k in range(parts):
        at = pl.ds((ch[0] ^ k) * each, each)
        for branch in range(2):
            v = grad_w[pl.ds(k * size, size), pl.ds(branch * channels, channels)].astype(BF)
            packed[at, pl.ds(branch * deep, deep), :] = v.reshape(each, deep, channels)
    per_owner = row_part.shape[0] // owners
    packed[:, pl.ds(2 * deep, per_owner), :] = (
        row_part[...].astype(BF).reshape(owners, per_owner, channels)
    )
    packed[:, pl.ds(2 * deep + per_owner, small.shape[1]), :] = small[...]


def kernel_call(body, outs, scratch, limit, scalars=0, operands=0):
    specs = {}
    if scalars:
        whole = [pl.BlockSpec(memory_space=pltpu.SMEM)] * scalars
        specs["in_specs"] = whole + [pl.BlockSpec(memory_space=pltpu.VMEM)] * operands
    return pl.pallas_call(
        body,
        out_shape=[jax.ShapeDtypeStruct(s, d) for s, d in outs],
        scratch_shapes=[pltpu.VMEM(s, d) for s, d in scratch],
        compiler_params=pltpu.CompilerParams(vmem_limit_bytes=limit << 20),
        **specs,
    )


def local(inputs, w_gate, w_value, short_filter, row_filter, column_filter, cotangent):
    rows, width, channels = inputs.shape
    owners = lax.axis_size("grid")
    parts = lax.axis_size("ch")
    height = column_filter.shape[0]
    per_owner = width // owners
    half = per_owner // 2
    inner = rows - 2
    scale = 1.0 / math.sqrt(height * width)
    ch = lax.axis_index("ch")
    place = lax.axis_index("grid")

    def flipped(value, bit):
        return lax.ppermute(value, "ch", [(i, i ^ bit) for i in range(parts)])

    def halos(first, last):
        up = lax.ppermute(last, "grid", [(i, i + 1) for i in range(owners - 1)])
        down = lax.ppermute(first, "grid", [(i + 1, i) for i in range(owners - 1)])
        return up, down

    def blocks(value):
        size = value.shape[0] // parts
        return [lax.dynamic_slice_in_dim(value, (ch ^ k) * size, size, axis=0) for k in range(parts)]

    edge = jnp.concatenate([inputs[0], inputs[rows - 1]], axis=0)
    mid = inputs[1 : rows - 1].reshape(inner * width, channels)
    edge_across = flipped(edge, 2)
    mid_across = flipped(mid, 2)
    edge_beside = flipped(edge, 1)
    mid_beside = flipped(mid, 1)
    edge_corner = flipped(edge_across, 1)

    w_blocks = blocks(jnp.concatenate([w_gate, w_value], axis=1))
    w_all = jnp.concatenate(w_blocks, axis=0)

    mat = row_matrix(width, owners, 0)
    mat_t = row_matrix(width, owners, 1)
    fwd = column_matrix(height, 1).astype(BF)
    inv = column_matrix(height, -1).astype(BF)
    mine = lax.dynamic_slice_in_dim(mat, place * per_owner, per_owner, axis=0)
    rspec = jnp.dot(mine, row_filter, preferred_element_type=F32)
    is_top = (place == 0) & (jnp.arange(half)[:, None] == 0)
    weight = jnp.where(is_top, 1.0, 2.0) / width
    rre, rim = rspec[:half] * weight, rspec[half:] * weight
    coef = jnp.stack(
        [rre, jnp.where(is_top, 0.0, -rim), jnp.where(is_top, 0.0, rim), jnp.where(is_top, rim, rre)]
    )
    keep = jnp.broadcast_to(jnp.where(is_top, 0.0, 1.0), (1, half, channels))
    cspec = jnp.dot(fwd[:, :height], column_filter, preferred_element_type=F32) / height
    colr, coli = cspec[:height], cspec[height:]
    kern = short_filter.reshape(18, channels).astype(F32)

    line = ((1, width, 2 * channels), BF)
    lines = ((inner, width, 2 * channels), BF)
    edge_blocks = (edge, edge_beside, edge_across, edge_corner)
    first, last = kernel_call(project_edge_kernel, [line, line], [], 12)(*edge_blocks, w_all)
    up, down = halos(first, last)
    mid_across, mat, mat_t, fwd, inv, mine, coef, keep, colr, coli, kern = lax.optimization_barrier(
        (mid_across, mat, mat_t, fwd, inv, mine, coef, keep, colr, coli, kern)
    )
    mid_corner = flipped(mid_across, 1)
    mid_blocks = (mid, mid_beside, mid_across, mid_corner)
    middle = kernel_call(project_mid_kernel, [lines], [], 12)(*mid_blocks, w_all)[0]
    middle, edge_blocks, mid_blocks = lax.optimization_barrier((middle, edge_blocks, mid_blocks))
    gathered_edge = jnp.concatenate(edge_blocks, axis=1)
    gathered_mid = jnp.concatenate(mid_blocks, axis=1)

    def framed(count):
        return ((2, count, width + 2 * EDGE, channels), F32)

    spread = ((owners, 2 * rows, per_owner, channels), BF)
    tile = ((rows, width, channels), BF)
    send, feat = kernel_call(
        forward_kernel, [spread, tile], [framed(rows + 2), ((width, 2 * rows * channels), BF)], 24
    )(up, first, middle, last, down, cotangent, kern, mat)
    recv = lax.all_to_all(send, "grid", split_axis=0, concat_axis=0, tiled=True)
    tall = (2 * height, 2 * half * channels)
    turned, rowq, colp = kernel_call(
        column_kernel,
        [spread, ((per_owner, channels), F32), ((height, channels), F32)],
        [(tall, BF), (tall, F32), ((height, channels), F32), ((height, channels), F32)],
        20,
    )(recv, coef, keep, colr, coli, fwd, inv)
    returned = lax.all_to_all(turned, "grid", split_axis=0, concat_axis=0, tiled=True)
    gated, gfirst, gmiddle, glast = kernel_call(
        inverse_kernel, [tile, line, lines, line], [], 20
    )(returned, mat_t, feat, cotangent)
    gup, gdown = halos(gfirst, glast)
    back_mid = kernel_call(backward_mid_kernel, [lines], [framed(rows)], 16)(
        gfirst, gmiddle, glast, kern
    )[0]
    short = kernel_call(
        short_kernel, [((18, channels), F32)], [framed(rows + 2)], 20
    )(up, first, middle, last, down, gfirst, gmiddle, glast)[0]
    back_edge = kernel_call(backward_edge_kernel, [lines], [framed(6)], 16)(
        gup, gfirst, gmiddle, glast, gdown, kern
    )[0]

    contract = (((1,), (1,)), ((), ()))
    over_tokens = (((0,), (0,)), ((), ()))

    def collected(back):
        def share(k):
            return lax.dot_general(back, w_blocks[k], contract, preferred_element_type=F32)

        beside = flipped(share(3).astype(BF), 1)
        theirs = (share(2) + beside.astype(F32)).astype(BF)
        across = flipped(theirs, 2)
        kept = share(0) + flipped(share(1).astype(BF), 1).astype(F32)
        return kept, across

    back_mid = back_mid.reshape(inner * width, 2 * channels)
    back_edge = back_edge.reshape(2 * width, 2 * channels)
    kept_mid, across_mid = collected(back_mid)
    kept_edge, across_edge = collected(back_edge)
    input_grad = kernel_call(finish_kernel, [tile], [], 12)(
        kept_edge, across_edge, kept_mid, across_mid
    )[0]

    grad_w = lax.dot_general(gathered_mid, back_mid, over_tokens, preferred_element_type=F32)
    grad_w = lax.optimization_barrier(grad_w)
    grad_w = grad_w + lax.dot_general(
        gathered_edge, back_edge, over_tokens, preferred_element_type=F32
    )
    tops = jnp.where(
        (place == 0) & (jnp.arange(per_owner)[:, None] % half == 0), 1.0, 2.0
    ) / width
    row_part = lax.dot_general(mine, (rowq * tops).astype(BF), over_tokens, preferred_element_type=F32)
    small = jnp.concatenate(
        [
            colp.astype(BF).reshape(owners, -1, channels),
            jnp.broadcast_to(short.astype(BF), (owners, 18, channels)),
            jnp.zeros((owners, 2, channels), BF),
        ],
        axis=1,
    )
    small = lax.optimization_barrier(small)
    deep = parts * channels // owners
    packed = kernel_call(
        pack_kernel,
        [((owners, 2 * deep + per_owner + small.shape[1], channels), BF)],
        [],
        16,
        scalars=1,
        operands=3,
    )(ch.reshape(1), grad_w, row_part, small)[0]
    total = lax.all_to_all(packed, "grid", split_axis=0, concat_axis=0, tiled=True)
    sizes = (deep, deep, per_owner, height // owners, 18)
    gate_grad, value_grad, row_share, col_share, short_sum = kernel_call(
        functools.partial(sum_kernel, scale=scale),
        [((size, channels), F32) for size in sizes],
        [],
        12,
    )(total)
    short_grad = short_sum.reshape(2, 3, 3, channels)
    return (gated, input_grad, gate_grad, value_grad, short_grad, row_share, col_share)


def solution(mesh):
    return jax.shard_map(
        local,
        mesh=mesh,
        in_specs=(
            P("grid", None, "ch"),
            P(None, "ch"),
            P(None, "ch"),
            P(None, None, None, "ch"),
            P(None, "ch"),
            P(None, "ch"),
            P("grid", None, "ch"),
        ),
        out_specs=(
            P("grid", None, "ch"),
            P("grid", None, "ch"),
            P("grid", "ch"),
            P("grid", "ch"),
            P(None, None, None, "ch"),
            P("grid", "ch"),
            P("grid", "ch"),
        ),
        check_vma=False,
    )
```

time: 865 us -> 210 us (0.24); the launches traced: 853 us -> 209 us
  waiting for transfers between devices: 233 us -> 63.8 us
  matrix products: 153 us -> 14.1 us
  blocking collectives: 165 us -> 35.7 us
  local copies, waits for them, and re-layouts: 130 us -> 9.34 us
  other arithmetic: 115 us -> 11.2 us
  Pallas kernels: 0 us -> 31.9 us
  between operations: 15.3 us -> 1.46 us
    unnamed x6 -> x0, waiting for transfers between devices: 153 us -> none
    unnamed x1 -> x0, blocking collectives: 132 us -> none
    dot_general x15 -> x13, matrix products: 144 us -> 14.1 us  [the longest x8 7.93 us: share(): lax.dot_general(back, w_blocks[k], contract, preferred_element_type=F32)]
    rev x6 -> x0, local copies, waits for them, and re-layouts: 71.1 us -> none  [mirror(): return jnp.concatenate([leading, jnp.flip(remainder, along)], axis=along)]
    pallas_call x0 -> x11, Pallas kernels: none -> 31.9 us  [the longest x1 5.95 us: local(): kernel_call(forward_kernel, [spread, tile], [framed(rows + 2), ((width, 2...]
    reduce_sum x4 -> x0, other arithmetic: 31.1 us -> none  [the longest x1 19.8 us: local(): jnp.sum(grad_feat * framed[row_shift:row_shift + tile_rows, col_shift:col...]
    ppermute x4 -> x16, waiting for transfers between devices: 9.77 us -> 39.5 us  [the longest x12 27.9 us: flipped(): return lax.ppermute(value, 'ch', [(i, i ^ bit) for i in range(parts)])]
    unnamed x58 -> x78, local copies, waits for them, and re-layouts: 32.9 us -> 5.23 us
  transfers between devices with their start and end apart: 12 -> 18, of which waited for: 7 -> 7; matrix products, arithmetic and copies ran while one was open for 20% -> 14% of each run, Pallas kernels for 0% -> 7%
where the time goes in v1:
time: 210 us; the launch traced here: 209 us
  waiting for transfers between devices  63.8 us (30%)
  starting transfers between devices  41 us (20%)
  blocking collectives  35.7 us (17%)
  Pallas kernels  31.9 us (15%)
  matrix products  14.1 us (7%)
  other arithmetic  11.2 us (5%)
  local copies, waits for them, and re-layouts  9.34 us (4%)
    all_to_all x1, blocking collectives, local(): recv = lax.all_to_all(send, 'grid', split_axis=0, concat_axis=0, tiled=True)  35.7 us
    ppermute x12, waiting for transfers between devices, flipped(): return lax.ppermute(value, 'ch', [(i, i ^ bit) for i in range(parts)])  27.9 us
    all_to_all x1, waiting for transfers between devices, local(): lax.all_to_all(turned, 'grid', split_axis=0, concat_axis=0, tiled=True)  24.3 us
    ppermute x12, starting transfers between devices, flipped(): return lax.ppermute(value, 'ch', [(i, i ^ bit) for i in range(parts)])  15.9 us
    convert_element_type x1, other arithmetic, row_matrix(): return cosine(freq * token + offset, width).astype(BF)  10.2 us
    all_to_all x1, starting transfers between devices, local(): lax.all_to_all(packed, 'grid', split_axis=0, concat_axis=0, tiled=True)  9.42 us
    dot_general x8, matrix products, share(): lax.dot_general(back, w_blocks[k], contract, preferred_element_type=F32)  7.93 us
    ppermute x2, waiting for transfers between devices, halos(): up = lax.ppermute(last, 'grid', [(i, i + 1) for i in range(owners - 1)])  7.41 us
  transfers between devices with their start and end apart: 18, of which 7 were waited for; matrix products, arithmetic and copies ran while one was open for 14% of the time, Pallas kernels for 7%

profile of v1, /device:TPU:1, one launch (start us, length us, event | category | flops | bytes accessed | tf_op | source)
XLA Modules:
  0.0 208.6 jit_solution(5707663807892550729)
XLA Ops:
  0.7 1.1 slice.26
  1.8 3.8 %collective-permute-start.5 = (bf16[2048,128]{1,0:T(8,128)(2,1)S(1)}, bf16[2048,128]{1,0:T(8,128)(2,1)}, u32[]{:S(2)}, u32[]{:S(2)}) collective-permute-start(bf16[2048,128]{1,0:T(8,128)(2,1)S(1)} %bitcast.49), channel_id=1, source_target_pairs={{0,2},{1,3},{2,0},{3,1},{4,6},{5,7},{6,4},{7,5},{8,10},{9,11},{10,... | collective-permute-start | bytes 1572872 | tf_op jit(solution)/shard_map/ppermute | solution.py:416
  5.6 1.0 collective-permute-start.4
  6.6 1.1 slice_bitcast_fusion.1
  7.7 0.1 collective-permute-start.1
  7.8 0.2 collective-permute-start
  8.1 0.7 constant_dynamic-update-slice_fusion.1
  8.8 10.2 %negate_convert_fusion = (bf16[1024,1024]{1,0:T(8,128)(2,1)}, bf16[1024,1024]{1,0:T(8,128)(2,1)S(1)}) fusion(s32[1024]{0:T(1024)S(1)} %get-tuple-element.112, s32[1024]{0:T(1024)S(1)} %get-tuple-element.115, s32[1024]{0:T(1024)S(1)} %get-tuple-element.111, s32[1024]{0:T(1024)S(1)} %get-tuple-element.116, pred[1024]{0:T(1024)(128)(4,1)S(1)} %get-tuple-element.118, ...), kind=kLoop, calls=%fused_computation.32 | loop fusion | flops 85983232 | bytes 4214784 | tf_op jit(solution)/shard_map/convert_element_type | solution.py:42
  19.0 0.2 fusion.72
  19.2 0.7 constant_dynamic-update-slice_fusion
  19.8 0.1 select_bitcast_fusion.2
  20.0 1.0 constant_dynamic-slice_fusion.4
  21.1 0.7 negate_convert_fusion.2
  21.8 6.6 %collective-permute-done.1.x2 = bf16[2048,128]{1,0:T(8,128)(2,1)} collective-permute-done((bf16[2048,128]{1,0:T(8,128)(2,1)S(1)}, bf16[2048,128]{1,0:T(8,128)(2,1)}, u32[]{:S(2)}, u32[]{:S(2)}) %collective-permute-start.1) | collective-permute-done | bytes 524320 | tf_op jit(solution)/shard_map/ppermute | solution.py:416
  28.4 1.5 collective-permute-start.2
  29.9 0.1 convolution_multiply_fusion
  30.0 0.1 broadcast_in_dim.75.keep
  30.2 1.4 collective-permute-done.2.x3
  31.6 2.1 %shard_map.126 = (bf16[1,1024,256]{2,1,0:T(8,128)(2,1)S(1)}, bf16[1,1024,256]{2,1,0:T(8,128)(2,1)S(1)}) custom-call(bf16[2048,128]{1,0:T(8,128)(2,1)S(1)} %pad_maximum_fusion.x0, bf16[2048,128]{1,0:T(8,128)(2,1)} %collective-permute-done.x1, bf16[2048,128]{1,0:T(8,128)(2,1)} %collective-permute-done.1.x2, bf16[2048,128]{1,0:T(8,128)(2,1)S(1)} %collective-permute-done.2.x3, ...), custom_call_target="tpu_custom_call" | custom-call | tf_op jit(solution)/shard_map/pallas_call | solution.py:458
  33.7 3.8 %collective-permute-start.3 = (bf16[1,1024,256]{2,1,0:T(8,128)(2,1)S(1)}, bf16[1,1024,256]{2,1,0:T(8,128)(2,1)S(1)}, u32[]{:S(2)}, u32[]{:S(2)}) collective-permute-start(bf16[1,1024,256]{2,1,0:T(8,128)(2,1)S(1)} %get-tuple-element.43.last), channel_id=1, source_target_pairs={{0,4},{4,8},{8,12},{12,16},{16,20},{20,24},{24,28},{28,32},{32,36}... | collective-permute-start | bytes 1572872 | tf_op jit(solution)/shard_map/ppermute | solution.py:419
  37.5 1.3 collective-permute-start.7
  38.8 2.1 %shard_map.127.middle = bf16[2,1024,256]{2,1,0:T(8,128)(2,1)S(1)} custom-call(bf16[2048,128]{1,0:T(8,128)(2,1)S(1)} %bitcast.51, bf16[2048,128]{1,0:T(8,128)(2,1)} %collective-permute-done.4.x1, bf16[2048,128]{1,0:T(8,128)(2,1)} %collective-permute-done.5.x2, bf16[2048,128]{1,0:T(8,128)(2,1)S(1)} %collective-permute-done.6.x3, ...), custom_call_target="tpu_custom_call" | custom-call | tf_op jit(solution)/shard_map/pallas_call | solution.py:465
  41.0 7.4 %collective-permute-done.3.up = bf16[1,1024,256]{2,1,0:T(8,128)(2,1)S(1)} collective-permute-done((bf16[1,1024,256]{2,1,0:T(8,128)(2,1)S(1)}, bf16[1,1024,256]{2,1,0:T(8,128)(2,1)S(1)}, u32[]{:S(2)}, u32[]{:S(2)}) %collective-permute-start.3) | collective-permute-done | bytes 524320 | tf_op jit(solution)/shard_map/ppermute | solution.py:419
  48.4 4.2 %collective-permute-done.7.down = bf16[1,1024,256]{2,1,0:T(8,128)(2,1)S(1)} collective-permute-done((bf16[1,1024,256]{2,1,0:T(8,128)(2,1)S(1)}, bf16[1,1024,256]{2,1,0:T(8,128)(2,1)S(1)}, u32[]{:S(2)}, u32[]{:S(2)}) %collective-permute-start.7) | collective-permute-done | bytes 524320 | tf_op jit(solution)/shard_map/ppermute | solution.py:420
  52.5 6.0 %shard_map.128 = (bf16[32,8,32,128]{3,2,1,0:T(8,128)(2,1)S(1)}, bf16[4,1024,128]{2,1,0:T(8,128)(2,1)S(1)}) custom-call(bf16[1,1024,256]{2,1,0:T(8,128)(2,1)S(1)} %collective-permute-done.3.up, bf16[1,1024,256]{2,1,0:T(8,128)(2,1)S(1)} %get-tuple-element.44.first, bf16[2,1024,256]{2,1,0:T(8,128)(2,1)S(1)} %shard_map.127.middle, ...), custom_call_target="tpu_custom_call" | custom-call | tf_op jit(solution)/shard_map/pallas_call | solution.py:475
  58.6 35.7 %all_to_all.15.recv = bf16[32,8,32,128]{3,2,1,0:T(8,128)(2,1)S(1)} all-to-all(bf16[32,8,32,128]{3,2,1,0:T(8,128)(2,1)S(1)} %get-tuple-element.49), channel_id=1, replica_groups=mesh['grid'=32,'ch'=4] {'grid'}, dimensions={0} | all-to-all | bytes 4194304 | tf_op jit(solution)/shard_map/all_to_all | solution.py:478
  94.3 4.6 %shard_map.129 = (bf16[32,8,32,128]{3,2,1,0:T(8,128)(2,1)S(1)}, f32[32,128]{1,0:T(8,128)S(1)}, f32[128,128]{1,0:T(8,128)S(1)}) custom-call(bf16[32,8,32,128]{3,2,1,0:T(8,128)(2,1)S(1)} %all_to_all.15.recv, f32[4,16,128]{2,1,0:T(8,128)S(1)} %pad_maximum_fusion.2.coef, f32[1,16,128]{2,1,0:T(8,128)S(1)} %broadcast_in_dim.75.keep, ...), custom_call_target="tpu_custom_call" | custom-call | tf_op jit(solution)/shard_map/pallas_call | solution.py:480
  98.9 1.3 copy-done.5
  100.2 6.1 %all-to-all-start.1 = ((bf16[32,8,32,128]{3,2,1,0:T(8,128)(2,1)}), bf16[32,8,32,128]{3,2,1,0:T(8,128)(2,1)}, u32[]{:S(2)}, u32[]{:S(2)}) async-start(bf16[32,8,32,128]{3,2,1,0:T(8,128)(2,1)} %copy-done.5), calls=%async_computation.1 | async-start | bytes 4194304 | tf_op jit(solution)/shard_map/all_to_all | solution.py:486
  106.3 0.1 pad.2.clone
  106.4 1.9 fusion.56.row_part
  108.3 24.3 %all-to-all-done.1.recv = bf16[32,8,32,128]{3,2,1,0:T(8,128)(2,1)} async-done(((bf16[32,8,32,128]{3,2,1,0:T(8,128)(2,1)}), bf16[32,8,32,128]{3,2,1,0:T(8,128)(2,1)}, u32[]{:S(2)}, u32[]{:S(2)}) %all-to-all-start.1) | async-done | bytes 2097184 | tf_op jit(solution)/shard_map/all_to_all | solution.py:486
  132.6 1.2 copy-done.3
  133.8 1.2 copy-done.20
  135.1 4.0 %shard_map.130 = (bf16[4,1024,128]{2,1,0:T(8,128)(2,1)}, bf16[1,1024,256]{2,1,0:T(8,128)(2,1)S(1)}, bf16[2,1024,256]{2,1,0:T(8,128)(2,1)S(1)}, bf16[1,1024,256]{2,1,0:T(8,128)(2,1)S(1)}) custom-call(bf16[32,8,32,128]{3,2,1,0:T(8,128)(2,1)} %all-to-all-done.1.recv, bf16[1024,1024]{1,0:T(8,128)(2,1)S(1)} %copy-done.1, bf16[4,1024,128]{2,1,0:T(8,128)(2,1)S(1)} %copy-done.20, ...), custom_call_target="tpu_custom_call" | custom-call | tf_op jit(solution)/shard_map/pallas_call | solution.py:487
  139.1 3.2 %collective-permute-start.8 = (bf16[1,1024,256]{2,1,0:T(8,128)(2,1)S(1)}, bf16[1,1024,256]{2,1,0:T(8,128)(2,1)S(1)}, u32[]{:S(2)}, u32[]{:S(2)}) collective-permute-start(bf16[1,1024,256]{2,1,0:T(8,128)(2,1)S(1)} %get-tuple-element.60.glast), channel_id=1, source_target_pairs={{0,4},{4,8},{8,12},{12,16},{16,20},{20,24},{24,28},{28,32},{32,36}... | collective-permute-start | bytes 1572872 | tf_op jit(solution)/shard_map/ppermute | solution.py:419
  142.4 1.3 collective-permute-start.9
  143.7 2.0 shard_map.132
  145.8 3.8 %shard_map.134 = f32[18,128]{1,0:T(8,128)S(1)} custom-call(bf16[1,1024,256]{2,1,0:T(8,128)(2,1)S(1)} %copy-done.16, bf16[1,1024,256]{2,1,0:T(8,128)(2,1)S(1)} %copy-done.12, bf16[2,1024,256]{2,1,0:T(8,128)(2,1)S(1)} %shard_map.127.middle, bf16[1,1024,256]{2,1,0:T(8,128)(2,1)S(1)} %copy-done.14, bf16[1,1024,256]{2,1,0:T(8,128)(2,1)S(1)} %copy-done.18, ...), custom_call_target="tpu_custom_call" | custom-call | tf_op jit(solution)/shard_map/pallas_call | solution.py:494
  149.6 0.1 maximum_maximum_fusion.small
  149.7 2.0 fusion.27
  151.7 1.2 convolution_convert_fusion
  153.0 2.3 %collective-permute-start.14 = (bf16[2048,128]{1,0:T(8,128)(2,1)}, bf16[2048,128]{1,0:T(8,128)(2,1)}, u32[]{:S(2)}, u32[]{:S(2)}) collective-permute-start(bf16[2048,128]{1,0:T(8,128)(2,1)} %convolution_convert_fusion), channel_id=1, source_target_pairs={{0,1},{1,0},{2,3},{3,2},{4,5},{5,4},{6,7},{7,6},{8,9},{9,8},{10,11... | collective-permute-start | bytes 1572872 | tf_op jit(solution)/shard_map/ppermute | solution.py:416
  155.3 0.4 convolution_convert_fusion.1
  155.8 0.1 collective-permute-start.13
  155.9 2.2 %shard_map.131 = bf16[2,1024,256]{2,1,0:T(8,128)(2,1)S(1)} custom-call(bf16[1,1024,256]{2,1,0:T(8,128)(2,1)S(1)} %collective-permute-done.8.gup, bf16[1,1024,256]{2,1,0:T(8,128)(2,1)S(1)} %get-tuple-element.61.gfirst, bf16[2,1024,256]{2,1,0:T(8,128)(2,1)S(1)} %get-tuple-element.62.gmiddle, bf16[1,1024,256]{2,1,0:T(8,128)(2,1)S(1)} %get-tuple-element.60.glast, ...), custom_call_target="tpu_custom_call" | custom-call | tf_op jit(solution)/shard_map/pallas_call | solution.py:497
  158.1 2.0 fusion.35
  160.1 0.1 add.228.grad_w
  160.2 0.9 shard_map.135
  161.2 9.4 %all-to-all-start.2 = ((bf16[32,88,128]{2,1,0:T(8,128)(2,1)}), bf16[32,88,128]{2,1,0:T(8,128)(2,1)}, u32[]{:S(2)}, u32[]{:S(2)}) async-start(bf16[32,88,128]{2,1,0:T(8,128)(2,1)} %shard_map.135), calls=%async_computation.2 | async-start | bytes 1441792 | tf_op jit(solution)/shard_map/all_to_all | solution.py:549
  170.6 0.4 convolution_convert_fusion.2
  171.0 3.6 %collective-permute-start.11 = (bf16[2048,128]{1,0:T(8,128)(2,1)S(1)}, bf16[2048,128]{1,0:T(8,128)(2,1)S(1)}, u32[]{:S(2)}, u32[]{:S(2)}) collective-permute-start(bf16[2048,128]{1,0:T(8,128)(2,1)S(1)} %convolution_convert_fusion.2), channel_id=1, source_target_pairs={{0,1},{1,0},{2,3},{3,2},{4,5},{5,4},{6,7},{7,6},{8,9},{9,8},{10,11... | collective-permute-start | bytes 1572872 | tf_op jit(solution)/shard_map/ppermute | solution.py:416
  174.6 2.3 %add_convert_fusion = bf16[2048,128]{1,0:T(8,128)(2,1)} fusion(bf16[2048,128]{1,0:T(8,128)(2,1)} %collective-permute-done.14, bf16[2048,256]{1,0:T(8,128)(2,1)S(1)} %bitcast.47, bf16[128,256]{1,0:T(8,128)(2,1)S(1)} %copy-done.26), kind=kOutput, calls=%fused_computation.72 | convolution fusion | flops 135004160 | bytes 2162688 | tf_op jit(solution)/shard_map/dot_general | solution.py:506
  176.9 3.0 %collective-permute-start.15 = (bf16[2048,128]{1,0:T(8,128)(2,1)}, bf16[2048,128]{1,0:T(8,128)(2,1)}, u32[]{:S(2)}, u32[]{:S(2)}) collective-permute-start(bf16[2048,128]{1,0:T(8,128)(2,1)} %add_convert_fusion), channel_id=1, source_target_pairs={{0,2},{1,3},{2,0},{3,1},{4,6},{5,7},{6,4},{7,5},{8,10},{9,11},{10,... | collective-permute-start | bytes 1572872 | tf_op jit(solution)/shard_map/ppermute | solution.py:416
  179.9 0.4 convolution_convert_fusion.3
  180.3 0.4 collective-permute-start.10
  180.7 1.2 fusion.26
  181.9 1.5 convert_add_fusion.kept_mid
  183.4 0.4 convolution_add_fusion.1.kept_edge
  183.9 1.8 shard_map.136
  185.7 0.6 copy.17
  186.3 8.7 %collective-permute-done.15.mid = bf16[2048,128]{1,0:T(8,128)(2,1)} collective-permute-done((bf16[2048,128]{1,0:T(8,128)(2,1)}, bf16[2048,128]{1,0:T(8,128)(2,1)}, u32[]{:S(2)}, u32[]{:S(2)}) %collective-permute-start.15) | collective-permute-done | bytes 524320 | tf_op jit(solution)/shard_map/ppermute | solution.py:416
  195.0 11.2 %collective-permute-done.12.edge = bf16[2048,128]{1,0:T(8,128)(2,1)} collective-permute-done((bf16[2048,128]{1,0:T(8,128)(2,1)}, bf16[2048,128]{1,0:T(8,128)(2,1)}, u32[]{:S(2)}, u32[]{:S(2)}) %collective-permute-start.12) | collective-permute-done | bytes 524320 | tf_op jit(solution)/shard_map/ppermute | solution.py:416
  206.2 2.3 %shard_map.133 = bf16[4,1024,128]{2,1,0:T(8,128)(2,1)} custom-call(f32[2048,128]{1,0:T(8,128)S(1)} %convolution_add_fusion.1.kept_edge, bf16[2048,128]{1,0:T(8,128)(2,1)} %collective-permute-done.12.edge, f32[2048,128]{1,0:T(8,128)S(1)} %convert_add_fusion.kept_mid, bf16[2048,128]{1,0:T(8,128)(2,1)} %collective-permute-done.15.mid), custom_call_target="tpu_custom_call" | custom-call | tf_op jit(solution)/shard_map/pallas_call | solution.py:518
  (109 shorter events, 0.4 us)
Async XLA Ops:
  0.6 18.3 %copy-start = (bf16[1024,128]{1,0:T(8,128)(2,1)S(1)}, bf16[1024,128]{1,0:T(8,128)(2,1)}, u32[]{:S(2)}) copy-start(bf16[1024,128]{1,0:T(8,128)(2,1)} %param.11) | copy-start | bytes 786436
  0.6 7.4 %copy-start.34 = (bf16[512,128]{1,0:T(8,128)(2,1)S(1)}, bf16[512,128]{1,0:T(8,128)(2,1)}, u32[]{:S(2)}) copy-start(bf16[512,128]{1,0:T(8,128)(2,1)} %param.8) | copy-start | bytes 393220
  1.8 17.1 %copy-start.8 = (bf16[2,1024,128]{2,1,0:T(8,128)(2,1)}, bf16[2,1024,128]{2,1,0:T(8,128)(2,1)S(1)}, u32[]{:S(2)}) copy-start(bf16[2,1024,128]{2,1,0:T(8,128)(2,1)S(1)} %slice.26) | copy-start | bytes 1572868
  1.8 28.2 %collective-permute-start.5 = (bf16[2048,128]{1,0:T(8,128)(2,1)S(1)}, bf16[2048,128]{1,0:T(8,128)(2,1)}, u32[]{:S(2)}, u32[]{:S(2)}) collective-permute-start(bf16[2048,128]{1,0:T(8,128)(2,1)S(1)} %bitcast.49), channel_id=1, source_target_pairs={{0,2},{1,3},{2,0},{3,1},{4,6},{5,7},{6,4},{7,5},{8,10},{9,11},{10,... | collective-permute-start | bytes 1572872 | tf_op jit(solution)/shard_map/ppermute | solution.py:416
  5.6 33.2 %collective-permute-start.4 = (bf16[2048,128]{1,0:T(8,128)(2,1)S(1)}, bf16[2048,128]{1,0:T(8,128)(2,1)}, u32[]{:S(2)}, u32[]{:S(2)}) collective-permute-start(bf16[2048,128]{1,0:T(8,128)(2,1)S(1)} %bitcast.50), channel_id=1, source_target_pairs={{0,1},{1,0},{2,3},{3,2},{4,5},{5,4},{6,7},{7,6},{8,9},{9,8},{10,11... | collective-permute-start | bytes 1572872 | tf_op jit(solution)/shard_map/ppermute | solution.py:416
  7.7 23.9 %copy-start.6 = (bf16[2048,128]{1,0:T(8,128)(2,1)}, bf16[2048,128]{1,0:T(8,128)(2,1)S(1)}, u32[]{:S(2)}) copy-start(bf16[2048,128]{1,0:T(8,128)(2,1)S(1)} %pad_maximum_fusion.x0) | copy-start | bytes 1572868
  7.7 20.7 %collective-permute-start.1 = (bf16[2048,128]{1,0:T(8,128)(2,1)S(1)}, bf16[2048,128]{1,0:T(8,128)(2,1)}, u32[]{:S(2)}, u32[]{:S(2)}) collective-permute-start(bf16[2048,128]{1,0:T(8,128)(2,1)S(1)} %pad_maximum_fusion.x0), channel_id=1, source_target_pairs={{0,2},{1,3},{2,0},{3,1},{4,6},{5,7},{6,4},{7,5},{8,10},{9,11},{10,... | collective-permute-start | bytes 1572872 | tf_op jit(solution)/shard_map/ppermute | solution.py:416
  7.8 22.3 %collective-permute-start = (bf16[2048,128]{1,0:T(8,128)(2,1)S(1)}, bf16[2048,128]{1,0:T(8,128)(2,1)}, u32[]{:S(2)}, u32[]{:S(2)}) collective-permute-start(bf16[2048,128]{1,0:T(8,128)(2,1)S(1)} %pad_maximum_fusion.x0), channel_id=1, source_target_pairs={{0,1},{1,0},{2,3},{3,2},{4,5},{5,4},{6,7},{7,6},{8,9},{9,8},{10,11... | collective-permute-start | bytes 1572872 | tf_op jit(solution)/shard_map/ppermute | solution.py:416
  8.8 10.4 %copy-start.35 = (bf16[512,128]{1,0:T(8,128)(2,1)S(1)}, bf16[512,128]{1,0:T(8,128)(2,1)}, u32[]{:S(2)}) copy-start(bf16[512,128]{1,0:T(8,128)(2,1)} %param.9) | copy-start | bytes 393220
  8.8 11.2 %copy-start.37 = (bf16[2,3,3,128]{3,0,2,1:T(2,128)(2,1)S(1)}, bf16[2,3,3,128]{3,0,2,1:T(2,128)(2,1)}, u32[]{:S(2)}) copy-start(bf16[2,3,3,128]{3,0,2,1:T(2,128)(2,1)} %param.10) | copy-start | bytes 13828
  18.9 10.9 %copy-start.36 = (bf16[128,128]{1,0:T(8,128)(2,1)S(1)}, bf16[128,128]{1,0:T(8,128)(2,1)}, u32[]{:S(2)}) copy-start(bf16[128,128]{1,0:T(8,128)(2,1)} %param.12) | copy-start | bytes 98308
  19.0 0.9 copy-start.33
  20.0 18.8 %copy-start.9 = (bf16[2,1024,128]{2,1,0:T(8,128)(2,1)S(1)}, bf16[2,1024,128]{2,1,0:T(8,128)(2,1)}, u32[]{:S(2)}) copy-start(bf16[2,1024,128]{2,1,0:T(8,128)(2,1)} %copy-done.8) | copy-start | bytes 1572868
  21.0 9.1 %copy-start.25 = (bf16[128,256]{1,0:T(8,128)(2,1)}, bf16[128,256]{1,0:T(8,128)(2,1)S(1)}, u32[]{:S(2)}) copy-start(bf16[128,256]{1,0:T(8,128)(2,1)S(1)} %get-tuple-element.97) | copy-start | bytes 196612
  21.0 9.1 %copy-start.27 = (bf16[128,256]{1,0:T(8,128)(2,1)}, bf16[128,256]{1,0:T(8,128)(2,1)S(1)}, u32[]{:S(2)}) copy-start(bf16[128,256]{1,0:T(8,128)(2,1)S(1)} %get-tuple-element.98) | copy-start | bytes 196612
  21.0 9.1 %copy-start.29 = (bf16[128,256]{1,0:T(8,128)(2,1)}, bf16[128,256]{1,0:T(8,128)(2,1)S(1)}, u32[]{:S(2)}) copy-start(bf16[128,256]{1,0:T(8,128)(2,1)S(1)} %get-tuple-element.96) | copy-start | bytes 196612
  21.1 9.1 %copy-start.31 = (bf16[128,256]{1,0:T(8,128)(2,1)}, bf16[128,256]{1,0:T(8,128)(2,1)S(1)}, u32[]{:S(2)}) copy-start(bf16[128,256]{1,0:T(8,128)(2,1)S(1)} %get-tuple-element.95) | copy-start | bytes 196612
  28.4 3.2 %collective-permute-start.2 = (bf16[2048,128]{1,0:T(8,128)(2,1)}, bf16[2048,128]{1,0:T(8,128)(2,1)S(1)}, u32[]{:S(2)}, u32[]{:S(2)}) collective-permute-start(bf16[2048,128]{1,0:T(8,128)(2,1)} %collective-permute-done.1.x2), channel_id=1, source_target_pairs={{0,1},{1,0},{2,3},{3,2},{4,5},{5,4},{6,7},{7,6},{8,9},{9,8},{10,11... | collective-permute-start | bytes 1572872 | tf_op jit(solution)/shard_map/ppermute | solution.py:416
  30.1 8.7 %collective-permute-start.6 = (bf16[2048,128]{1,0:T(8,128)(2,1)}, bf16[2048,128]{1,0:T(8,128)(2,1)S(1)}, u32[]{:S(2)}, u32[]{:S(2)}) collective-permute-start(bf16[2048,128]{1,0:T(8,128)(2,1)} %collective-permute-done.5.x2), channel_id=1, source_target_pairs={{0,1},{1,0},{2,3},{3,2},{4,5},{5,4},{6,7},{7,6},{8,9},{9,8},{10,11... | collective-permute-start | bytes 1572872 | tf_op jit(solution)/shard_map/ppermute | solution.py:416
  31.6 2.1 %copy-start.21 = (bf16[2048,128]{1,0:T(8,128)(2,1)}, bf16[2048,128]{1,0:T(8,128)(2,1)S(1)}, u32[]{:S(2)}) copy-start(bf16[2048,128]{1,0:T(8,128)(2,1)S(1)} %collective-permute-done.2.x3) | copy-start | bytes 1572868
  33.7 24.8 %copy-start.11 = (bf16[1,1024,256]{2,1,0:T(8,128)(2,1)}, bf16[1,1024,256]{2,1,0:T(8,128)(2,1)S(1)}, u32[]{:S(2)}) copy-start(bf16[1,1024,256]{2,1,0:T(8,128)(2,1)S(1)} %get-tuple-element.44.first) | copy-start | bytes 1572868
  33.7 24.8 %copy-start.13 = (bf16[1,1024,256]{2,1,0:T(8,128)(2,1)}, bf16[1,1024,256]{2,1,0:T(8,128)(2,1)S(1)}, u32[]{:S(2)}) copy-start(bf16[1,1024,256]{2,1,0:T(8,128)(2,1)S(1)} %get-tuple-element.43.last) | copy-start | bytes 1572868
  33.7 18.8 %copy-start.2 = (bf16[4,1024,128]{2,1,0:T(8,128)(2,1)S(1)}, bf16[4,1024,128]{2,1,0:T(8,128)(2,1)}, u32[]{:S(2)}) copy-start(bf16[4,1024,128]{2,1,0:T(8,128)(2,1)} %cot.3) | copy-start | bytes 3145732
  33.7 14.6 %collective-permute-start.3 = (bf16[1,1024,256]{2,1,0:T(8,128)(2,1)S(1)}, bf16[1,1024,256]{2,1,0:T(8,128)(2,1)S(1)}, u32[]{:S(2)}, u32[]{:S(2)}) collective-permute-start(bf16[1,1024,256]{2,1,0:T(8,128)(2,1)S(1)} %get-tuple-element.43.last), channel_id=1, source_target_pairs={{0,4},{4,8},{8,12},{12,16},{16,20},{20,24},{24,28},{28,32},{32,36}... | collective-permute-start | bytes 1572872 | tf_op jit(solution)/shard_map/ppermute | solution.py:419
  37.5 15.0 %collective-permute-start.7 = (bf16[1,1024,256]{2,1,0:T(8,128)(2,1)S(1)}, bf16[1,1024,256]{2,1,0:T(8,128)(2,1)S(1)}, u32[]{:S(2)}, u32[]{:S(2)}) collective-permute-start(bf16[1,1024,256]{2,1,0:T(8,128)(2,1)S(1)} %get-tuple-element.44.first), channel_id=1, source_target_pairs={{4,0},{8,4},{12,8},{16,12},{20,16},{24,20},{28,24},{32,28},{36,32}... | collective-permute-start | bytes 1572872 | tf_op jit(solution)/shard_map/ppermute | solution.py:420
  38.8 9.5 %copy-start.23 = (bf16[2048,128]{1,0:T(8,128)(2,1)}, bf16[2048,128]{1,0:T(8,128)(2,1)S(1)}, u32[]{:S(2)}) copy-start(bf16[2048,128]{1,0:T(8,128)(2,1)S(1)} %collective-permute-done.6.x3) | copy-start | bytes 1572868
  48.4 10.2 %copy-start.15 = (bf16[1,1024,256]{2,1,0:T(8,128)(2,1)}, bf16[1,1024,256]{2,1,0:T(8,128)(2,1)S(1)}, u32[]{:S(2)}) copy-start(bf16[1,1024,256]{2,1,0:T(8,128)(2,1)S(1)} %collective-permute-done.3.up) | copy-start | bytes 1572868
  52.5 6.0 %copy-start.17 = (bf16[1,1024,256]{2,1,0:T(8,128)(2,1)}, bf16[1,1024,256]{2,1,0:T(8,128)(2,1)S(1)}, u32[]{:S(2)}) copy-start(bf16[1,1024,256]{2,1,0:T(8,128)(2,1)S(1)} %collective-permute-done.7.down) | copy-start | bytes 1572868
  58.5 35.7 %copy-start.19 = (bf16[4,1024,128]{2,1,0:T(8,128)(2,1)}, bf16[4,1024,128]{2,1,0:T(8,128)(2,1)S(1)}, u32[]{:S(2)}) copy-start(bf16[4,1024,128]{2,1,0:T(8,128)(2,1)S(1)} %get-tuple-element.58.feat) | copy-start | bytes 3145732
  98.9 1.3 copy-start.5
  100.2 32.4 %copy-start.1 = (bf16[1024,1024]{1,0:T(8,128)(2,1)S(1)}, bf16[1024,1024]{1,0:T(8,128)(2,1)}, u32[]{:S(2)}) copy-start(bf16[1024,1024]{1,0:T(8,128)(2,1)} %get-tuple-element.57.mat) | copy-start | bytes 6291460
  100.2 32.4 %all-to-all-start.1 = ((bf16[32,8,32,128]{3,2,1,0:T(8,128)(2,1)}), bf16[32,8,32,128]{3,2,1,0:T(8,128)(2,1)}, u32[]{:S(2)}, u32[]{:S(2)}) async-start(bf16[32,8,32,128]{3,2,1,0:T(8,128)(2,1)} %copy-done.5), calls=%async_computation.1 | async-start | bytes 4194304 | tf_op jit(solution)/shard_map/all_to_all | solution.py:486
  132.6 1.2 copy-start.3
  133.8 1.2 copy-start.20
  139.1 6.6 %copy-start.12 = (bf16[1,1024,256]{2,1,0:T(8,128)(2,1)S(1)}, bf16[1,1024,256]{2,1,0:T(8,128)(2,1)}, u32[]{:S(2)}) copy-start(bf16[1,1024,256]{2,1,0:T(8,128)(2,1)} %copy-done.11) | copy-start | bytes 1572868
  139.1 6.6 %copy-start.14 = (bf16[1,1024,256]{2,1,0:T(8,128)(2,1)S(1)}, bf16[1,1024,256]{2,1,0:T(8,128)(2,1)}, u32[]{:S(2)}) copy-start(bf16[1,1024,256]{2,1,0:T(8,128)(2,1)} %copy-done.13) | copy-start | bytes 1572868
  139.1 6.6 %copy-start.16 = (bf16[1,1024,256]{2,1,0:T(8,128)(2,1)S(1)}, bf16[1,1024,256]{2,1,0:T(8,128)(2,1)}, u32[]{:S(2)}) copy-start(bf16[1,1024,256]{2,1,0:T(8,128)(2,1)} %copy-done.15) | copy-start | bytes 1572868
  139.1 6.6 %copy-start.18 = (bf16[1,1024,256]{2,1,0:T(8,128)(2,1)S(1)}, bf16[1,1024,256]{2,1,0:T(8,128)(2,1)}, u32[]{:S(2)}) copy-start(bf16[1,1024,256]{2,1,0:T(8,128)(2,1)} %copy-done.17) | copy-start | bytes 1572868
  139.1 16.7 %collective-permute-start.8 = (bf16[1,1024,256]{2,1,0:T(8,128)(2,1)S(1)}, bf16[1,1024,256]{2,1,0:T(8,128)(2,1)S(1)}, u32[]{:S(2)}, u32[]{:S(2)}) collective-permute-start(bf16[1,1024,256]{2,1,0:T(8,128)(2,1)S(1)} %get-tuple-element.60.glast), channel_id=1, source_target_pairs={{0,4},{4,8},{8,12},{12,16},{16,20},{20,24},{24,28},{28,32},{32,36}... | collective-permute-start | bytes 1572872 | tf_op jit(solution)/shard_map/ppermute | solution.py:419
  142.4 13.5 %collective-permute-start.9 = (bf16[1,1024,256]{2,1,0:T(8,128)(2,1)S(1)}, bf16[1,1024,256]{2,1,0:T(8,128)(2,1)S(1)}, u32[]{:S(2)}, u32[]{:S(2)}) collective-permute-start(bf16[1,1024,256]{2,1,0:T(8,128)(2,1)S(1)} %get-tuple-element.61.gfirst), channel_id=1, source_target_pairs={{4,0},{8,4},{12,8},{16,12},{20,16},{24,20},{28,24},{32,28},{36,32}... | collective-permute-start | bytes 1572872 | tf_op jit(solution)/shard_map/ppermute | solution.py:420
  145.7 4.0 %copy-start.10 = (bf16[2,1024,128]{2,1,0:T(8,128)(2,1)S(1)}, bf16[2,1024,128]{2,1,0:T(8,128)(2,1)}, u32[]{:S(2)}) copy-start(bf16[2,1024,128]{2,1,0:T(8,128)(2,1)} %copy-done.8) | copy-start | bytes 1572868
  145.7 4.0 %copy-start.24 = (bf16[2048,128]{1,0:T(8,128)(2,1)S(1)}, bf16[2048,128]{1,0:T(8,128)(2,1)}, u32[]{:S(2)}) copy-start(bf16[2048,128]{1,0:T(8,128)(2,1)} %copy-done.23) | copy-start | bytes 1572868
  149.7 2.0 copy-start.30
  149.7 5.6 %copy-start.28 = (bf16[128,256]{1,0:T(8,128)(2,1)S(1)}, bf16[128,256]{1,0:T(8,128)(2,1)}, u32[]{:S(2)}) copy-start(bf16[128,256]{1,0:T(8,128)(2,1)} %copy-done.27) | copy-start | bytes 196612
  153.0 21.6 %collective-permute-start.14 = (bf16[2048,128]{1,0:T(8,128)(2,1)}, bf16[2048,128]{1,0:T(8,128)(2,1)}, u32[]{:S(2)}, u32[]{:S(2)}) collective-permute-start(bf16[2048,128]{1,0:T(8,128)(2,1)} %convolution_convert_fusion), channel_id=1, source_target_pairs={{0,1},{1,0},{2,3},{3,2},{4,5},{5,4},{6,7},{7,6},{8,9},{9,8},{10,11... | collective-permute-start | bytes 1572872 | tf_op jit(solution)/shard_map/ppermute | solution.py:416
  155.7 2.4 %copy-start.7 = (bf16[2048,128]{1,0:T(8,128)(2,1)S(1)}, bf16[2048,128]{1,0:T(8,128)(2,1)}, u32[]{:S(2)}) copy-start(bf16[2048,128]{1,0:T(8,128)(2,1)} %copy-done.6) | copy-start | bytes 1572868
  155.7 2.4 %copy-start.22 = (bf16[2048,128]{1,0:T(8,128)(2,1)S(1)}, bf16[2048,128]{1,0:T(8,128)(2,1)}, u32[]{:S(2)}) copy-start(bf16[2048,128]{1,0:T(8,128)(2,1)} %copy-done.21) | copy-start | bytes 1572868
  155.8 26.2 %collective-permute-start.13 = (bf16[2048,128]{1,0:T(8,128)(2,1)S(1)}, bf16[2048,128]{1,0:T(8,128)(2,1)}, u32[]{:S(2)}, u32[]{:S(2)}) collective-permute-start(bf16[2048,128]{1,0:T(8,128)(2,1)S(1)} %convolution_convert_fusion.1), channel_id=1, source_target_pairs={{0,1},{1,0},{2,3},{3,2},{4,5},{5,4},{6,7},{7,6},{8,9},{9,8},{10,11... | collective-permute-start | bytes 1572872 | tf_op jit(solution)/shard_map/ppermute | solution.py:416
  158.1 2.1 %copy-start.4 = (f32[1024,128]{1,0:T(8,128)S(1)}, f32[1024,128]{1,0:T(8,128)}, u32[]{:S(2)}) copy-start(f32[1024,128]{1,0:T(8,128)} %fusion.56.row_part) | copy-start | bytes 1572868
  160.2 14.4 %copy-start.26 = (bf16[128,256]{1,0:T(8,128)(2,1)S(1)}, bf16[128,256]{1,0:T(8,128)(2,1)}, u32[]{:S(2)}) copy-start(bf16[128,256]{1,0:T(8,128)(2,1)} %copy-done.25) | copy-start | bytes 196612
  161.2 22.7 %all-to-all-start.2 = ((bf16[32,88,128]{2,1,0:T(8,128)(2,1)}), bf16[32,88,128]{2,1,0:T(8,128)(2,1)}, u32[]{:S(2)}, u32[]{:S(2)}) async-start(bf16[32,88,128]{2,1,0:T(8,128)(2,1)} %shard_map.135), calls=%async_computation.2 | async-start | bytes 1441792 | tf_op jit(solution)/shard_map/all_to_all | solution.py:549
  171.0 9.7 %collective-permute-start.11 = (bf16[2048,128]{1,0:T(8,128)(2,1)S(1)}, bf16[2048,128]{1,0:T(8,128)(2,1)S(1)}, u32[]{:S(2)}, u32[]{:S(2)}) collective-permute-start(bf16[2048,128]{1,0:T(8,128)(2,1)S(1)} %convolution_convert_fusion.2), channel_id=1, source_target_pairs={{0,1},{1,0},{2,3},{3,2},{4,5},{5,4},{6,7},{7,6},{8,9},{9,8},{10,11... | collective-permute-start | bytes 1572872 | tf_op jit(solution)/shard_map/ppermute | solution.py:416
  176.9 5.1 %copy-start.32 = (bf16[128,256]{1,0:T(8,128)(2,1)S(1)}, bf16[128,256]{1,0:T(8,128)(2,1)}, u32[]{:S(2)}) copy-start(bf16[128,256]{1,0:T(8,128)(2,1)} %copy-done.31) | copy-start | bytes 196612
  176.9 18.1 %collective-permute-start.15 = (bf16[2048,128]{1,0:T(8,128)(2,1)}, bf16[2048,128]{1,0:T(8,128)(2,1)}, u32[]{:S(2)}, u32[]{:S(2)}) collective-permute-start(bf16[2048,128]{1,0:T(8,128)(2,1)} %add_convert_fusion), channel_id=1, source_target_pairs={{0,2},{1,3},{2,0},{3,1},{4,6},{5,7},{6,4},{7,5},{8,10},{9,11},{10,... | collective-permute-start | bytes 1572872 | tf_op jit(solution)/shard_map/ppermute | solution.py:416
  180.3 3.1 %collective-permute-start.10 = (bf16[2048,128]{1,0:T(8,128)(2,1)S(1)}, bf16[2048,128]{1,0:T(8,128)(2,1)S(1)}, u32[]{:S(2)}, u32[]{:S(2)}) collective-permute-start(bf16[2048,128]{1,0:T(8,128)(2,1)S(1)} %convolution_convert_fusion.3), channel_id=1, source_target_pairs={{0,1},{1,0},{2,3},{3,2},{4,5},{5,4},{6,7},{7,6},{8,9},{9,8},{10,11... | collective-permute-start | bytes 1572872 | tf_op jit(solution)/shard_map/ppermute | solution.py:416
  181.9 24.3 %collective-permute-start.12 = (bf16[2048,128]{1,0:T(8,128)(2,1)}, bf16[2048,128]{1,0:T(8,128)(2,1)}, u32[]{:S(2)}, u32[]{:S(2)}) collective-permute-start(bf16[2048,128]{1,0:T(8,128)(2,1)} %fusion.26), channel_id=1, source_target_pairs={{0,2},{1,3},{2,0},{3,1},{4,6},{5,7},{6,4},{7,5},{8,10},{9,11},{10,... | collective-permute-start | bytes 1572872 | tf_op jit(solution)/shard_map/ppermute | solution.py:416

commit v2 on v1

--- a/solution.py
+++ b/solution.py
@@ -27,27 +27,95 @@
 def frequencies(slots, width, owners):
     per_owner = width // owners
     half = per_owner // 2
-    place = slots % per_owner
+    place = slots & (per_owner - 1)
     top = slots == half
-    freq = (slots // per_owner) * half + place % half
+    freq = (slots // per_owner) * half + (place & (half - 1))
     freq = jnp.where(top, width // 2, freq)
     offset = jnp.where((place >= half) & ~top, width // 4, 0)
     return freq, offset
 
 
-def row_matrix(width, owners, slot_dim):
-    shape = (width, width)
-    freq, offset = frequencies(lax.broadcasted_iota(jnp.int32, shape, slot_dim), width, owners)
-    token = lax.broadcasted_iota(jnp.int32, shape, 1 - slot_dim)
-    return cosine(freq * token + offset, width).astype(BF)
+def turning(store, phase, step, period, count):
+    quarter = period - period // 4
+    c, s = cosine(phase, period), cosine(phase + quarter, period)
+    dc, ds = cosine(step, period), cosine(step + quarter, period)
+    for n in range(count):
+        store(n, c)
+        c, s = c * dc - s * ds, s * dc + c * ds
 
 
 def column_matrix(height, sign):
     shape = (2 * height, 2 * height)
     i = lax.broadcasted_iota(jnp.int32, shape, 0)
     j = lax.broadcasted_iota(jnp.int32, shape, 1)
-    turn = (j // height - i // height) * (-sign * (height // 4))
-    return cosine((i % height) * (j % height) + turn + height, height)
+    turn = (jnp.where(j >= height, 1, 0) - jnp.where(i >= height, 1, 0)) * (-sign * (height // 4))
+    return cosine((i & (height - 1)) * (j & (height - 1)) + turn + height, height)
+
+
+def tables_kernel(
+    where, w_gate, w_value, short_filter, row_filter, column_filter,
+    mat, mat_t, mine, fwd, inv, coef, keep, colr, coli, kern, w_all,
+):
+    ch, place = where[0], where[1]
+    width, channels = row_filter.shape
+    height = column_filter.shape[0]
+    _, half, _ = coef.shape
+    per_owner = 2 * half
+    owners = width // per_owner
+    shape = (16, 128)
+    lane = lax.broadcasted_iota(jnp.int32, shape, 1)
+    row = lax.broadcasted_iota(jnp.int32, shape, 0)
+
+    def build(n, _):
+        at = pl.multiple_of(n * 16, 16)
+        freq, offset = frequencies(row + at, width, owners)
+
+        def along(m, value):
+            mat[pl.ds(at, 16), pl.ds(m * 128, 128)] = value.astype(BF)
+
+        turning(along, freq * lane + offset, freq * 128, width, width // 128)
+        token = row + at
+        per_block = 128 // per_owner * half
+        freq, offset = frequencies(lane + 128, width, owners)
+        freq = freq - per_block
+        highest = 1.0 - 2.0 * (token & 1).astype(F32)
+
+        def across(m, value):
+            if m == 0:
+                value = jnp.where(lane == half, highest, value)
+            mat_t[pl.ds(at, 16), pl.ds(m * 128, 128)] = value.astype(BF)
+
+        turning(across, freq * token + offset, token * per_block, width, width // 128)
+        return 0
+
+    lax.fori_loop(0, width // 16, build, 0)
+    fwd[...] = column_matrix(height, 1).astype(BF)
+    inv[...] = column_matrix(height, -1).astype(BF)
+    mine[...] = mat[pl.ds(pl.multiple_of(place * per_owner, per_owner), per_owner), :]
+    rspec = jnp.dot(mine[...], row_filter[...], preferred_element_type=F32)
+    first = lax.broadcasted_iota(jnp.int32, (half, channels), 0) == 0
+    top = jnp.where(first, jnp.where(place == 0, 1.0, 0.0), 0.0)
+    weight = (2.0 - top) * (1.0 / width)
+    rre, rim = rspec[:half] * weight, rspec[half:] * weight
+    rest = 1.0 - top
+    coef[0] = rre
+    coef[1] = -rim * rest
+    coef[2] = rim * rest
+    coef[3] = rre * rest + rim * top
+    keep[0] = rest
+    cspec = jnp.dot(fwd[:, pl.ds(0, height)], column_filter[...], preferred_element_type=F32)
+    cspec = cspec * (1.0 / height)
+    colr[...] = cspec[:height]
+    coli[...] = cspec[height:]
+    for b in range(2):
+        for i in range(3):
+            kern[pl.ds(b * 9 + i * 3, 3), :] = short_filter[b, i].astype(F32)
+    parts = w_gate.shape[0] // channels
+    for k in range(parts):
+        at = pl.ds(pl.multiple_of((ch ^ k) * channels, channels), channels)
+        to = pl.ds(k * channels, channels)
+        w_all[to, pl.ds(0, channels)] = w_gate[at, :]
+        w_all[to, pl.ds(channels, channels)] = w_value[at, :]
 
 
 def fill_framed(framed, rows_of, channels):
@@ -139,7 +207,7 @@
 
 
 def column_kernel(
-    recv, coef, keep, colr, coli, fwd, inv, send, rowq, colp, stacked, spectra, er, ei
+    recv, coef, keep, colr, coli, fwd, inv, mine, send, rowp, colp, stacked, spectra, er, ei
 ):
     owners, twice, per_owner, channels = recv.shape
     rows = twice // 2
@@ -236,9 +304,17 @@
 
     none = jnp.zeros((half, channels), F32)
     p1, p2, p3 = lax.fori_loop(0, height // 16, pack, (none, none, none))
+    width = owners * per_owner
     kept = keep[0]
-    rowq[pl.ds(0, half), :] = p1 + kept * p2
-    rowq[pl.ds(half, half), :] = kept * p3 + (1.0 - kept) * p2
+    twofold = (1.0 + kept) * (1.0 / width)
+    qr = (p1 + kept * p2) * twofold
+    qi = (kept * p3 + (1.0 - kept) * p2) * twofold
+    rowp[...] = lax.dot_general(
+        mine[...],
+        jnp.concatenate([qr, qi], axis=0).astype(BF),
+        (((0,), (0,)), ((), ())),
+        preferred_element_type=F32,
+    ).astype(BF)
 
 
 def inverse_kernel(recv, mat, feat, cot, gated, first, middle, last):
@@ -297,41 +373,48 @@
     spread_back(gframed, kern, [(back, r, r + 1) for r in range(inner)], width, channels)
 
 
-def short_kernel(up, first, middle, last, down, gfirst, gmiddle, glast, short, framed):
+def short_kernel(up, first, middle, last, down, gfirst, gmiddle, glast, short, framed, *, branch):
     width = first.shape[1]
     channels = short.shape[1]
     inner = middle.shape[0]
     rows = inner + 2
-    fill_framed(
-        framed,
-        [(up, 0), (first, 0), *((middle, r) for r in range(inner)), (last, 0), (down, 0)],
-        channels,
-    )
+    lanes = pl.ds(branch * channels, channels)
+    tokens = [(up, 0), (first, 0), *((middle, r) for r in range(inner)), (last, 0), (down, 0)]
     grads = [(gfirst, 0), *((gmiddle, r) for r in range(inner)), (glast, 0)]
-    for branch in range(2):
-        lanes = pl.ds(branch * channels, channels)
-
-        def terms(t, sums, branch=branch, lanes=lanes):
-            base = pl.multiple_of(t * 16, 16)
-            sums = list(sums)
-            both = [ref[row, pl.ds(base, 16), lanes].astype(F32) for ref, row in grads]
-            for p in range(2):
-                at = base + 8 * p + EDGE
-                g = [v[8 * p : 8 * p + 8] for v in both]
-                for r in range(rows + 2):
-                    for j in range(3):
-                        v = framed[branch, r, pl.ds(at + j - 1, 8), :]
-                        for i in range(3):
-                            o = r - i
-                            if 0 <= o < rows:
-                                sums[i * 3 + j] = sums[i * 3 + j] + g[o] * v
-            return tuple(sums)
-
-        sums = lax.fori_loop(
-            0, width // 16, terms, tuple(jnp.zeros((8, channels), F32) for _ in range(9))
-        )
-        for k in range(9):
-            short[pl.ds(branch * 9 + k, 1), :] = jnp.sum(sums[k], axis=0, keepdims=True)
+    zeros = jnp.zeros((EDGE, channels), F32)
+    for r in range(rows + 2):
+        framed[r, pl.ds(0, EDGE), :] = zeros
+        framed[r, pl.ds(EDGE + width, EDGE), :] = zeros
+
+    def fill(t, _):
+        at = pl.multiple_of(t * 32, 32)
+        for r, (ref, row) in enumerate(tokens):
+            framed[r, pl.ds(EDGE + at, 32), :] = ref[row, pl.ds(at, 32), lanes].astype(F32)
+        return 0
+
+    lax.fori_loop(0, width // 32, fill, 0)
+
+    def terms(t, sums):
+        base = pl.multiple_of(t * 16, 16)
+        sums = list(sums)
+        both = [ref[row, pl.ds(base, 16), lanes].astype(F32) for ref, row in grads]
+        for p in range(2):
+            at = base + 8 * p + EDGE
+            g = [v[8 * p : 8 * p + 8] for v in both]
+            for r in range(rows + 2):
+                for j in range(3):
+                    v = framed[r, pl.ds(at + j - 1, 8), :]
+                    for i in range(3):
+                        o = r - i
+                        if 0 <= o < rows:
+                            sums[i * 3 + j] = sums[i * 3 + j] + g[o] * v
+        return tuple(sums)
+
+    sums = lax.fori_loop(
+        0, width // 16, terms, tuple(jnp.zeros((8, channels), F32) for _ in range(9))
+    )
+    for k in range(9):
+        short[pl.ds(k, 1), :] = jnp.sum(sums[k], axis=0, keepdims=True)
 
 
 def backward_edge_kernel(gup, gfirst, gmiddle, glast, gdown, kern, back, gframed):
@@ -381,7 +464,7 @@
             packed[at, pl.ds(branch * deep, deep), :] = v.reshape(each, deep, channels)
     per_owner = row_part.shape[0] // owners
     packed[:, pl.ds(2 * deep, per_owner), :] = (
-        row_part[...].astype(BF).reshape(owners, per_owner, channels)
+        row_part[...].reshape(owners, per_owner, channels)
     )
     packed[:, pl.ds(2 * deep + per_owner, small.shape[1]), :] = small[...]
 
@@ -420,10 +503,6 @@
         down = lax.ppermute(first, "grid", [(i + 1, i) for i in range(owners - 1)])
         return up, down
 
-    def blocks(value):
-        size = value.shape[0] // parts
-        return [lax.dynamic_slice_in_dim(value, (ch ^ k) * size, size, axis=0) for k in range(parts)]
-
     edge = jnp.concatenate([inputs[0], inputs[rows - 1]], axis=0)
     mid = inputs[1 : rows - 1].reshape(inner * width, channels)
     edge_across = flipped(edge, 2)
@@ -432,34 +511,33 @@
     mid_beside = flipped(mid, 1)
     edge_corner = flipped(edge_across, 1)
 
-    w_blocks = blocks(jnp.concatenate([w_gate, w_value], axis=1))
-    w_all = jnp.concatenate(w_blocks, axis=0)
-
-    mat = row_matrix(width, owners, 0)
-    mat_t = row_matrix(width, owners, 1)
-    fwd = column_matrix(height, 1).astype(BF)
-    inv = column_matrix(height, -1).astype(BF)
-    mine = lax.dynamic_slice_in_dim(mat, place * per_owner, per_owner, axis=0)
-    rspec = jnp.dot(mine, row_filter, preferred_element_type=F32)
-    is_top = (place == 0) & (jnp.arange(half)[:, None] == 0)
-    weight = jnp.where(is_top, 1.0, 2.0) / width
-    rre, rim = rspec[:half] * weight, rspec[half:] * weight
-    coef = jnp.stack(
-        [rre, jnp.where(is_top, 0.0, -rim), jnp.where(is_top, 0.0, rim), jnp.where(is_top, rim, rre)]
-    )
-    keep = jnp.broadcast_to(jnp.where(is_top, 0.0, 1.0), (1, half, channels))
-    cspec = jnp.dot(fwd[:, :height], column_filter, preferred_element_type=F32) / height
-    colr, coli = cspec[:height], cspec[height:]
-    kern = short_filter.reshape(18, channels).astype(F32)
+    (mat, mat_t, mine, fwd, inv, coef, keep, colr, coli, kern, w_all) = kernel_call(
+        tables_kernel,
+        [
+            ((width, width), BF),
+            ((width, width), BF),
+            ((per_owner, width), BF),
+            ((2 * height, 2 * height), BF),
+            ((2 * height, 2 * height), BF),
+            ((4, half, channels), F32),
+            ((1, half, channels), F32),
+            ((height, channels), F32),
+            ((height, channels), F32),
+            ((18, channels), F32),
+            ((parts * channels, 2 * channels), BF),
+        ],
+        [],
+        12,
+        scalars=1,
+        operands=5,
+    )(jnp.stack([ch, place]), w_gate, w_value, short_filter, row_filter, column_filter)
+    w_blocks = [w_all[k * channels : (k + 1) * channels] for k in range(parts)]
 
     line = ((1, width, 2 * channels), BF)
     lines = ((inner, width, 2 * channels), BF)
     edge_blocks = (edge, edge_beside, edge_across, edge_corner)
     first, last = kernel_call(project_edge_kernel, [line, line], [], 12)(*edge_blocks, w_all)
     up, down = halos(first, last)
-    mid_across, mat, mat_t, fwd, inv, mine, coef, keep, colr, coli, kern = lax.optimization_barrier(
-        (mid_across, mat, mat_t, fwd, inv, mine, coef, keep, colr, coli, kern)
-    )
     mid_corner = flipped(mid_across, 1)
     mid_blocks = (mid, mid_beside, mid_across, mid_corner)
     middle = kernel_call(project_mid_kernel, [lines], [], 12)(*mid_blocks, w_all)[0]
@@ -477,12 +555,12 @@
     )(up, first, middle, last, down, cotangent, kern, mat)
     recv = lax.all_to_all(send, "grid", split_axis=0, concat_axis=0, tiled=True)
     tall = (2 * height, 2 * half * channels)
-    turned, rowq, colp = kernel_call(
+    turned, row_part, colp = kernel_call(
         column_kernel,
-        [spread, ((per_owner, channels), F32), ((height, channels), F32)],
+        [spread, ((width, channels), BF), ((height, channels), F32)],
         [(tall, BF), (tall, F32), ((height, channels), F32), ((height, channels), F32)],
         20,
-    )(recv, coef, keep, colr, coli, fwd, inv)
+    )(recv, coef, keep, colr, coli, fwd, inv, mine)
     returned = lax.all_to_all(turned, "grid", split_axis=0, concat_axis=0, tiled=True)
     gated, gfirst, gmiddle, glast = kernel_call(
         inverse_kernel, [tile, line, lines, line], [], 20
@@ -491,9 +569,15 @@
     back_mid = kernel_call(backward_mid_kernel, [lines], [framed(rows)], 16)(
         gfirst, gmiddle, glast, kern
     )[0]
-    short = kernel_call(
-        short_kernel, [((18, channels), F32)], [framed(rows + 2)], 20
-    )(up, first, middle, last, down, gfirst, gmiddle, glast)[0]
+    shorts = [
+        kernel_call(
+            functools.partial(short_kernel, branch=n),
+            [((9, channels), F32)],
+            [((rows + 2, width + 2 * EDGE, channels), F32)],
+            12,
+        )(up, first, middle, last, down, gfirst, gmiddle, glast)[0]
+        for n in range(2)
+    ]
     back_edge = kernel_call(backward_edge_kernel, [lines], [framed(6)], 16)(
         gup, gfirst, gmiddle, glast, gdown, kern
     )[0]
@@ -508,6 +592,7 @@
         beside = flipped(share(3).astype(BF), 1)
         theirs = (share(2) + beside.astype(F32)).astype(BF)
         across = flipped(theirs, 2)
+        back, _ = lax.optimization_barrier((back, theirs))
         kept = share(0) + flipped(share(1).astype(BF), 1).astype(F32)
         return kept, across
 
@@ -524,14 +609,10 @@
     grad_w = grad_w + lax.dot_general(
         gathered_edge, back_edge, over_tokens, preferred_element_type=F32
     )
-    tops = jnp.where(
-        (place == 0) & (jnp.arange(per_owner)[:, None] % half == 0), 1.0, 2.0
-    ) / width
-    row_part = lax.dot_general(mine, (rowq * tops).astype(BF), over_tokens, preferred_element_type=F32)
     small = jnp.concatenate(
         [
             colp.astype(BF).reshape(owners, -1, channels),
-            jnp.broadcast_to(short.astype(BF), (owners, 18, channels)),
+            *(jnp.broadcast_to(v.astype(BF), (owners, 9, channels)) for v in shorts),
             jnp.zeros((owners, 2, channels), BF),
         ],
         axis=1,

time: 210 us -> 208 us (level)
  other arithmetic: 11.2 us -> 0.96 us
  Pallas kernels: 31.9 us -> 36.4 us
  waiting for transfers between devices: 63.8 us -> 67.2 us
  matrix products: 14.1 us -> 11.3 us
  starting transfers between devices: 41 us -> 43.1 us
    convert_element_type x3 -> x2, other arithmetic: 10.9 us -> 0.01 us  [local(): v.astype(BF)]
    pallas_call x2 -> x4, Pallas kernels: 8.38 us -> 16 us  [the longest x1 7.18 us: local(): kernel_call(tables_kernel, [((width, width), BF), ((width, width), BF), (...]
    unnamed x78, local copies, waits for them, and re-layouts: 5.23 us -> 9.55 us
    ppermute x12, starting transfers between devices: 15.9 us -> 18.2 us  [flipped(): return lax.ppermute(value, 'ch', [(i, i ^ bit) for i in range(parts)])]
    dot_general x3 -> x0, matrix products: 2.2 us -> none  [the longest x1 1.9 us: local(): lax.dot_general(mine, (rowq * tops).astype(BF), over_tokens, preferred_el...]
  transfers between devices with their start and end apart: 18 -> 18, of which waited for: 7 -> 6; matrix products, arithmetic and copies ran while one was open for 14% -> 6% of each run, Pallas kernels for 7% -> 10%
where the time goes in v2:
time: 208 us; the launch traced here: 207 us
  waiting for transfers between devices  67.2 us (32%)
  starting transfers between devices  43.1 us (21%)
  Pallas kernels  36.4 us (18%)
  blocking collectives  35.9 us (17%)
  matrix products  11.3 us (5%)
  local copies, waits for them, and re-layouts  10.9 us (5%)
    all_to_all x1, blocking collectives, local(): recv = lax.all_to_all(send, 'grid', split_axis=0, concat_axis=0, tiled=True)  35.9 us
    ppermute x12, waiting for transfers between devices, flipped(): return lax.ppermute(value, 'ch', [(i, i ^ bit) for i in range(parts)])  29.5 us
    all_to_all x1, waiting for transfers between devices, local(): lax.all_to_all(turned, 'grid', split_axis=0, concat_axis=0, tiled=True)  25.8 us
    ppermute x12, starting transfers between devices, flipped(): return lax.ppermute(value, 'ch', [(i, i ^ bit) for i in range(parts)])  18.2 us
    all_to_all x1, starting transfers between devices, local(): lax.all_to_all(packed, 'grid', split_axis=0, concat_axis=0, tiled=True)  9.56 us
    unnamed x78, local copies, waits for them, and re-layouts  9.55 us
    dot_general x8, matrix products, share(): lax.dot_general(back, w_blocks[k], contract, preferred_element_type=F32)  8.75 us
    ppermute x2, waiting for transfers between devices, halos(): up = lax.ppermute(last, 'grid', [(i, i + 1) for i in range(owners - 1)])  7.73 us
  transfers between devices with their start and end apart: 18, of which 6 were waited for; matrix products, arithmetic and copies ran while one was open for 6% of the time, Pallas kernels for 10%

profile of v2, /device:TPU:1, one launch (start us, length us, event | category | flops | bytes accessed | tf_op | source)
XLA Modules:
  0.0 206.9 jit_solution(15884943867510959714)
XLA Ops:
  0.7 1.2 slice_bitcast_fusion.1
  1.9 3.8 %collective-permute-start.1 = (bf16[2048,128]{1,0:T(8,128)(2,1)S(1)}, bf16[2048,128]{1,0:T(8,128)(2,1)S(1)}, u32[]{:S(2)}, u32[]{:S(2)}) collective-permute-start(bf16[2048,128]{1,0:T(8,128)(2,1)S(1)} %pad_maximum_fusion.x0), channel_id=1, source_target_pairs={{0,2},{1,3},{2,0},{3,1},{4,6},{5,7},{6,4},{7,5},{8,10},{9,11},{10,... | collective-permute-start | bytes 1572872 | tf_op jit(solution)/shard_map/ppermute | solution.py:499
  5.7 0.1 collective-permute-start.5
  5.9 1.1 collective-permute-start
  7.0 10.1 %collective-permute-done.1.x2 = bf16[2048,128]{1,0:T(8,128)(2,1)S(1)} collective-permute-done((bf16[2048,128]{1,0:T(8,128)(2,1)S(1)}, bf16[2048,128]{1,0:T(8,128)(2,1)S(1)}, u32[]{:S(2)}, u32[]{:S(2)}) %collective-permute-start.1) | collective-permute-done | bytes 524320 | tf_op jit(solution)/shard_map/ppermute | solution.py:499
  17.1 2.5 %collective-permute-start.2 = (bf16[2048,128]{1,0:T(8,128)(2,1)S(1)}, bf16[2048,128]{1,0:T(8,128)(2,1)S(1)}, u32[]{:S(2)}, u32[]{:S(2)}) collective-permute-start(bf16[2048,128]{1,0:T(8,128)(2,1)S(1)} %collective-permute-done.1.x2), channel_id=1, source_target_pairs={{0,1},{1,0},{2,3},{3,2},{4,5},{5,4},{6,7},{7,6},{8,9},{9,8},{10,11... | collective-permute-start | bytes 1572872 | tf_op jit(solution)/shard_map/ppermute | solution.py:499
  19.7 0.1 pad_add_fusion.where
  19.7 0.9 copy-done.31
  20.7 0.9 copy-done.33
  21.6 0.8 copy-done.34
  22.3 7.2 %shard_map.126 = (bf16[1024,1024]{1,0:T(8,128)(2,1)S(1)}, bf16[1024,1024]{1,0:T(8,128)(2,1)S(1)}, bf16[32,1024]{1,0:T(8,128)(2,1)S(1)}, bf16[256,256]{1,0:T(8,12...) custom-call(s32[2]{0:T(128)S(1)} %pad_add_fusion.where, ...), custom_call_target="tpu_custom_call" | custom-call | tf_op jit(solution)/shard_map/pallas_call | solution.py:514
  29.5 0.6 collective-permute-start.6
  30.1 0.7 shard_map.127
  30.9 0.0 copy-start.8
  30.9 3.8 %collective-permute-start.3 = (bf16[1,1024,256]{2,1,0:T(8,128)(2,1)S(1)}, bf16[1,1024,256]{2,1,0:T(8,128)(2,1)S(1)}, u32[]{:S(2)}, u32[]{:S(2)}) collective-permute-start(bf16[1,1024,256]{2,1,0:T(8,128)(2,1)S(1)} %get-tuple-element.46.last), channel_id=1, source_target_pairs={{0,4},{4,8},{8,12},{12,16},{16,20},{20,24},{24,28},{28,32},{32,36}... | collective-permute-start | bytes 1572872 | tf_op jit(solution)/shard_map/ppermute | solution.py:502
  34.7 1.3 collective-permute-start.7
  36.1 1.9 shard_map.128.middle
  38.1 7.7 %collective-permute-done.3.up = bf16[1,1024,256]{2,1,0:T(8,128)(2,1)S(1)} collective-permute-done((bf16[1,1024,256]{2,1,0:T(8,128)(2,1)S(1)}, bf16[1,1024,256]{2,1,0:T(8,128)(2,1)S(1)}, u32[]{:S(2)}, u32[]{:S(2)}) %collective-permute-start.3) | collective-permute-done | bytes 524320 | tf_op jit(solution)/shard_map/ppermute | solution.py:502
  45.8 4.2 %collective-permute-done.7.down = bf16[1,1024,256]{2,1,0:T(8,128)(2,1)S(1)} collective-permute-done((bf16[1,1024,256]{2,1,0:T(8,128)(2,1)S(1)}, bf16[1,1024,256]{2,1,0:T(8,128)(2,1)S(1)}, u32[]{:S(2)}, u32[]{:S(2)}) %collective-permute-start.7) | collective-permute-done | bytes 524320 | tf_op jit(solution)/shard_map/ppermute | solution.py:503
  50.0 6.0 %shard_map.129 = (bf16[32,8,32,128]{3,2,1,0:T(8,128)(2,1)S(1)}, bf16[4,1024,128]{2,1,0:T(8,128)(2,1)S(1)}) custom-call(bf16[1,1024,256]{2,1,0:T(8,128)(2,1)S(1)} %collective-permute-done.3.up, bf16[1,1024,256]{2,1,0:T(8,128)(2,1)S(1)} %get-tuple-element.47.first, bf16[2,1024,256]{2,1,0:T(8,128)(2,1)S(1)} %shard_map.128.middle, ...), custom_call_target="tpu_custom_call" | custom-call | tf_op jit(solution)/shard_map/pallas_call | solution.py:553
  56.0 35.9 %all_to_all.15.recv = bf16[32,8,32,128]{3,2,1,0:T(8,128)(2,1)S(1)} all-to-all(bf16[32,8,32,128]{3,2,1,0:T(8,128)(2,1)S(1)} %get-tuple-element.51), channel_id=1, replica_groups=mesh['grid'=32,'ch'=4] {'grid'}, dimensions={0} | all-to-all | bytes 4194304 | tf_op jit(solution)/shard_map/all_to_all | solution.py:556
  91.9 5.0 %shard_map.130 = (bf16[32,8,32,128]{3,2,1,0:T(8,128)(2,1)S(1)}, bf16[1024,128]{1,0:T(8,128)(2,1)S(1)}, f32[128,128]{1,0:T(8,128)S(1)}) custom-call(bf16[32,8,32,128]{3,2,1,0:T(8,128)(2,1)S(1)} %all_to_all.15.recv, f32[4,16,128]{2,1,0:T(8,128)S(1)} %get-tuple-element.52.coef, f32[1,16,128]{2,1,0:T(8,128)S(1)} %get-tuple-element.53.keep, ...), custom_call_target="tpu_custom_call" | custom-call | tf_op jit(solution)/shard_map/pallas_call | solution.py:558
  96.9 1.4 copy-done.12
  98.3 0.7 copy-done.29
  99.0 5.4 %all-to-all-start.1 = ((bf16[32,8,32,128]{3,2,1,0:T(8,128)(2,1)}), bf16[32,8,32,128]{3,2,1,0:T(8,128)(2,1)S(1)}, u32[]{:S(2)}, u32[]{:S(2)}) async-start(bf16[32,8,32,128]{3,2,1,0:T(8,128)(2,1)} %copy-done.12), calls=%async_computation.1 | async-start | bytes 4194304 | tf_op jit(solution)/shard_map/all_to_all | solution.py:564
  104.4 0.1 pad.3.clone
  104.5 0.6 convert_element_type.49
  105.1 25.8 %all-to-all-done.1.recv = bf16[32,8,32,128]{3,2,1,0:T(8,128)(2,1)S(1)} async-done(((bf16[32,8,32,128]{3,2,1,0:T(8,128)(2,1)}), bf16[32,8,32,128]{3,2,1,0:T(8,128)(2,1)S(1)}, u32[]{:S(2)}, u32[]{:S(2)}) %all-to-all-start.1) | async-done | bytes 2097184 | tf_op jit(solution)/shard_map/all_to_all | solution.py:564
  130.9 1.2 copy-done.9
  132.1 1.6 copy-done.11
  133.7 1.2 copy-done.18
  134.9 2.5 %shard_map.131 = (bf16[4,1024,128]{2,1,0:T(8,128)(2,1)}, bf16[1,1024,256]{2,1,0:T(8,128)(2,1)S(1)}, bf16[2,1024,256]{2,1,0:T(8,128)(2,1)S(1)}, bf16[1,1024,256]{2,1,0:T(8,128)(2,1)S(1)}) custom-call(bf16[32,8,32,128]{3,2,1,0:T(8,128)(2,1)S(1)} %all-to-all-done.1.recv, bf16[1024,1024]{1,0:T(8,128)(2,1)S(1)} %copy-done.11, ...), custom_call_target="tpu_custom_call" | custom-call | tf_op jit(solution)/shard_map/pallas_call | solution.py:565
  137.4 3.3 %collective-permute-start.8 = (bf16[1,1024,256]{2,1,0:T(8,128)(2,1)S(1)}, bf16[1,1024,256]{2,1,0:T(8,128)(2,1)S(1)}, u32[]{:S(2)}, u32[]{:S(2)}) collective-permute-start(bf16[1,1024,256]{2,1,0:T(8,128)(2,1)S(1)} %get-tuple-element.63.glast), channel_id=1, source_target_pairs={{0,4},{4,8},{8,12},{12,16},{16,20},{20,24},{24,28},{28,32},{32,36}... | collective-permute-start | bytes 1572872 | tf_op jit(solution)/shard_map/ppermute | solution.py:502
  140.7 1.5 collective-permute-start.9
  142.2 2.0 shard_map.133
  144.3 1.9 shard_map.135
  146.2 1.9 shard_map.136
  148.2 0.2 maximum_maximum_fusion.small
  148.4 1.8 fusion.1
  150.2 1.2 convolution_convert_fusion.1
  151.5 2.4 %collective-permute-start.13 = (bf16[2048,128]{1,0:T(8,128)(2,1)}, bf16[2048,128]{1,0:T(8,128)(2,1)}, u32[]{:S(2)}, u32[]{:S(2)}) collective-permute-start(bf16[2048,128]{1,0:T(8,128)(2,1)} %convolution_convert_fusion.1), channel_id=1, source_target_pairs={{0,1},{1,0},{2,3},{3,2},{4,5},{5,4},{6,7},{7,6},{8,9},{9,8},{10,11... | collective-permute-start | bytes 1572872 | tf_op jit(solution)/shard_map/ppermute | solution.py:499
  153.9 2.2 %shard_map.132 = bf16[2,1024,256]{2,1,0:T(8,128)(2,1)S(1)} custom-call(bf16[1,1024,256]{2,1,0:T(8,128)(2,1)S(1)} %collective-permute-done.8.gup, bf16[1,1024,256]{2,1,0:T(8,128)(2,1)S(1)} %get-tuple-element.64.gfirst, bf16[2,1024,256]{2,1,0:T(8,128)(2,1)S(1)} %get-tuple-element.65.gmiddle, bf16[1,1024,256]{2,1,0:T(8,128)(2,1)S(1)} %get-tuple-element.63.glast, ...), custom_call_target="tpu_custom_call" | custom-call | tf_op jit(solution)/shard_map/pallas_call | solution.py:581
  156.1 0.7 fusion.9
  156.9 0.1 add.19.grad_w
  157.0 0.1 copy-done.30
  157.1 0.9 shard_map.137
  158.0 9.6 %all-to-all-start.2 = ((bf16[32,88,128]{2,1,0:T(8,128)(2,1)}), bf16[32,88,128]{2,1,0:T(8,128)(2,1)}, u32[]{:S(2)}, u32[]{:S(2)}) async-start(bf16[32,88,128]{2,1,0:T(8,128)(2,1)} %shard_map.137), calls=%async_computation.2 | async-start | bytes 1441792 | tf_op jit(solution)/shard_map/all_to_all | solution.py:630
  167.6 0.4 convolution_convert_fusion.3
  168.0 3.9 %collective-permute-start.10 = (bf16[2048,128]{1,0:T(8,128)(2,1)S(1)}, bf16[2048,128]{1,0:T(8,128)(2,1)S(1)}, u32[]{:S(2)}, u32[]{:S(2)}) collective-permute-start(bf16[2048,128]{1,0:T(8,128)(2,1)S(1)} %convolution_convert_fusion.3), channel_id=1, source_target_pairs={{0,1},{1,0},{2,3},{3,2},{4,5},{5,4},{6,7},{7,6},{8,9},{9,8},{10,11... | collective-permute-start | bytes 1572872 | tf_op jit(solution)/shard_map/ppermute | solution.py:499
  171.9 2.3 %add_convert_fusion = bf16[2048,128]{1,0:T(8,128)(2,1)} fusion(bf16[2048,128]{1,0:T(8,128)(2,1)} %collective-permute-done.13, bf16[2048,256]{1,0:T(8,128)(2,1)S(1)} %bitcast.27, bf16[512,256]{1,0:T(8,128)(2,1)S(1)} %get-tuple-element.45.w), kind=kOutput, calls=%fused_computation.23 | convolution fusion | flops 135004160 | bytes 2162688 | tf_op jit(solution)/shard_map/dot_general | solution.py:590
  174.2 0.4 convolution_convert_fusion
  174.6 0.1 collective-permute-start.14
  174.7 1.2 fusion
  175.9 1.2 convolution_convert_fusion.2
  177.2 0.5 collective-permute-start.11
  177.6 3.2 %collective-permute-start.15 = (bf16[2048,128]{1,0:T(8,128)(2,1)}, bf16[2048,128]{1,0:T(8,128)(2,1)}, u32[]{:S(2)}, u32[]{:S(2)}) collective-permute-start(bf16[2048,128]{1,0:T(8,128)(2,1)} %add_convert_fusion), channel_id=1, source_target_pairs={{0,2},{1,3},{2,0},{3,1},{4,6},{5,7},{6,4},{7,5},{8,10},{9,11},{10,... | collective-permute-start | bytes 1572872 | tf_op jit(solution)/shard_map/ppermute | solution.py:499
  180.8 0.0 collective-permute-start.12
  180.8 0.4 convert_add_fusion.kept_mid
  181.3 1.8 shard_map.138
  183.1 0.6 copy.17
  183.7 1.5 convert_add_fusion.1.kept_edge
  185.2 8.2 %collective-permute-done.15.mid = bf16[2048,128]{1,0:T(8,128)(2,1)} collective-permute-done((bf16[2048,128]{1,0:T(8,128)(2,1)}, bf16[2048,128]{1,0:T(8,128)(2,1)}, u32[]{:S(2)}, u32[]{:S(2)}) %collective-permute-start.15) | collective-permute-done | bytes 524320 | tf_op jit(solution)/shard_map/ppermute | solution.py:499
  193.3 11.2 %collective-permute-done.12.edge = bf16[2048,128]{1,0:T(8,128)(2,1)} collective-permute-done((bf16[2048,128]{1,0:T(8,128)(2,1)}, bf16[2048,128]{1,0:T(8,128)(2,1)}, u32[]{:S(2)}, u32[]{:S(2)}) %collective-permute-start.12) | collective-permute-done | bytes 524320 | tf_op jit(solution)/shard_map/ppermute | solution.py:499
  204.6 2.3 %shard_map.134 = bf16[4,1024,128]{2,1,0:T(8,128)(2,1)} custom-call(f32[2048,128]{1,0:T(8,128)S(1)} %convert_add_fusion.1.kept_edge, bf16[2048,128]{1,0:T(8,128)(2,1)} %collective-permute-done.12.edge, f32[2048,128]{1,0:T(8,128)S(1)} %convert_add_fusion.kept_mid, bf16[2048,128]{1,0:T(8,128)(2,1)} %collective-permute-done.15.mid), custom_call_target="tpu_custom_call" | custom-call | tf_op jit(solution)/shard_map/pallas_call | solution.py:603
  (88 shorter events, 0.3 us)
Async XLA Ops:
  0.6 5.1 %copy-start.35 = (bf16[4,1024,128]{2,1,0:T(8,128)(2,1)S(1)}, bf16[4,1024,128]{2,1,0:T(8,128)(2,1)}, u32[]{:S(2)}) copy-start(bf16[4,1024,128]{2,1,0:T(8,128)(2,1)} %param.7) | copy-start | bytes 3145732
  0.6 19.0 %copy-start.37 = (bf16[2,3,3,128]{3,0,2,1:T(2,128)(2,1)S(1)}, bf16[2,3,3,128]{3,0,2,1:T(2,128)(2,1)}, u32[]{:S(2)}) copy-start(bf16[2,3,3,128]{3,0,2,1:T(2,128)(2,1)} %param.10) | copy-start | bytes 13828
  0.7 19.1 %copy-start.32 = (bf16[512,128]{1,0:T(8,128)(2,1)S(1)}, bf16[512,128]{1,0:T(8,128)(2,1)}, u32[]{:S(2)}) copy-start(bf16[512,128]{1,0:T(8,128)(2,1)} %w_gate.1) | copy-start | bytes 393220
  1.9 34.2 %copy-start.13 = (bf16[2048,128]{1,0:T(8,128)(2,1)}, bf16[2048,128]{1,0:T(8,128)(2,1)S(1)}, u32[]{:S(2)}) copy-start(bf16[2048,128]{1,0:T(8,128)(2,1)S(1)} %pad_maximum_fusion.x0) | copy-start | bytes 1572868
  1.9 15.2 %collective-permute-start.1 = (bf16[2048,128]{1,0:T(8,128)(2,1)S(1)}, bf16[2048,128]{1,0:T(8,128)(2,1)S(1)}, u32[]{:S(2)}, u32[]{:S(2)}) collective-permute-start(bf16[2048,128]{1,0:T(8,128)(2,1)S(1)} %pad_maximum_fusion.x0), channel_id=1, source_target_pairs={{0,2},{1,3},{2,0},{3,1},{4,6},{5,7},{6,4},{7,5},{8,10},{9,11},{10,... | collective-permute-start | bytes 1572872 | tf_op jit(solution)/shard_map/ppermute | solution.py:499
  5.7 32.3 %copy-start.15 = (bf16[2,1024,128]{2,1,0:T(8,128)(2,1)}, bf16[2,1024,128]{2,1,0:T(8,128)(2,1)S(1)}, u32[]{:S(2)}) copy-start(bf16[2,1024,128]{2,1,0:T(8,128)(2,1)S(1)} %slice.23) | copy-start | bytes 1572868
  5.7 23.8 %collective-permute-start.5 = (bf16[2048,128]{1,0:T(8,128)(2,1)S(1)}, bf16[2048,128]{1,0:T(8,128)(2,1)S(1)}, u32[]{:S(2)}, u32[]{:S(2)}) collective-permute-start(bf16[2048,128]{1,0:T(8,128)(2,1)S(1)} %bitcast.30), channel_id=1, source_target_pairs={{0,2},{1,3},{2,0},{3,1},{4,6},{5,7},{6,4},{7,5},{8,10},{9,11},{10,... | collective-permute-start | bytes 1572872 | tf_op jit(solution)/shard_map/ppermute | solution.py:499
  5.9 24.3 %collective-permute-start = (bf16[2048,128]{1,0:T(8,128)(2,1)S(1)}, bf16[2048,128]{1,0:T(8,128)(2,1)S(1)}, u32[]{:S(2)}, u32[]{:S(2)}) collective-permute-start(bf16[2048,128]{1,0:T(8,128)(2,1)S(1)} %pad_maximum_fusion.x0), channel_id=1, source_target_pairs={{0,1},{1,0},{2,3},{3,2},{4,5},{5,4},{6,7},{7,6},{8,9},{9,8},{10,11... | collective-permute-start | bytes 1572872 | tf_op jit(solution)/shard_map/ppermute | solution.py:499
  17.1 18.9 %copy-start.19 = (bf16[2048,128]{1,0:T(8,128)(2,1)}, bf16[2048,128]{1,0:T(8,128)(2,1)S(1)}, u32[]{:S(2)}) copy-start(bf16[2048,128]{1,0:T(8,128)(2,1)S(1)} %collective-permute-done.1.x2) | copy-start | bytes 1572868
  17.1 13.0 %collective-permute-start.2 = (bf16[2048,128]{1,0:T(8,128)(2,1)S(1)}, bf16[2048,128]{1,0:T(8,128)(2,1)S(1)}, u32[]{:S(2)}, u32[]{:S(2)}) collective-permute-start(bf16[2048,128]{1,0:T(8,128)(2,1)S(1)} %collective-permute-done.1.x2), channel_id=1, source_target_pairs={{0,1},{1,0},{2,3},{3,2},{4,5},{5,4},{6,7},{7,6},{8,9},{9,8},{10,11... | collective-permute-start | bytes 1572872 | tf_op jit(solution)/shard_map/ppermute | solution.py:499
  19.6 16.4 %collective-permute-start.4 = (bf16[2048,128]{1,0:T(8,128)(2,1)S(1)}, bf16[2048,128]{1,0:T(8,128)(2,1)}, u32[]{:S(2)}, u32[]{:S(2)}) collective-permute-start(bf16[2048,128]{1,0:T(8,128)(2,1)S(1)} %bitcast.31), channel_id=1, source_target_pairs={{0,1},{1,0},{2,3},{3,2},{4,5},{5,4},{6,7},{7,6},{8,9},{9,8},{10,11... | collective-permute-start | bytes 1572872 | tf_op jit(solution)/shard_map/ppermute | solution.py:499
  19.7 1.0 copy-start.31
  20.7 0.9 copy-start.33
  21.6 0.8 copy-start.34
  29.5 8.5 %copy-start.10 = (bf16[1024,1024]{1,0:T(8,128)(2,1)}, bf16[1024,1024]{1,0:T(8,128)(2,1)S(1)}, u32[]{:S(2)}) copy-start(bf16[1024,1024]{1,0:T(8,128)(2,1)S(1)} %get-tuple-element.60.mat) | copy-start | bytes 6291460
  29.5 8.5 %copy-start.25 = (bf16[2048,128]{1,0:T(8,128)(2,1)}, bf16[2048,128]{1,0:T(8,128)(2,1)S(1)}, u32[]{:S(2)}) copy-start(bf16[2048,128]{1,0:T(8,128)(2,1)S(1)} %collective-permute-done.5.x2) | copy-start | bytes 1572868
  29.5 6.5 %collective-permute-start.6 = (bf16[2048,128]{1,0:T(8,128)(2,1)S(1)}, bf16[2048,128]{1,0:T(8,128)(2,1)S(1)}, u32[]{:S(2)}, u32[]{:S(2)}) collective-permute-start(bf16[2048,128]{1,0:T(8,128)(2,1)S(1)} %collective-permute-done.5.x2), channel_id=1, source_target_pairs={{0,1},{1,0},{2,3},{3,2},{4,5},{5,4},{6,7},{7,6},{8,9},{9,8},{10,11... | collective-permute-start | bytes 1572872 | tf_op jit(solution)/shard_map/ppermute | solution.py:499
  30.1 7.9 %copy-start.21 = (bf16[2048,128]{1,0:T(8,128)(2,1)}, bf16[2048,128]{1,0:T(8,128)(2,1)S(1)}, u32[]{:S(2)}) copy-start(bf16[2048,128]{1,0:T(8,128)(2,1)S(1)} %collective-permute-done.x1) | copy-start | bytes 1572868
  30.1 7.9 %copy-start.23 = (bf16[2048,128]{1,0:T(8,128)(2,1)}, bf16[2048,128]{1,0:T(8,128)(2,1)S(1)}, u32[]{:S(2)}) copy-start(bf16[2048,128]{1,0:T(8,128)(2,1)S(1)} %collective-permute-done.2.x3) | copy-start | bytes 1572868
  30.9 25.1 %copy-start = (bf16[1,1024,256]{2,1,0:T(8,128)(2,1)}, bf16[1,1024,256]{2,1,0:T(8,128)(2,1)S(1)}, u32[]{:S(2)}) copy-start(bf16[1,1024,256]{2,1,0:T(8,128)(2,1)S(1)} %get-tuple-element.47.first) | copy-start | bytes 1572868
  30.9 25.1 %copy-start.2 = (bf16[1,1024,256]{2,1,0:T(8,128)(2,1)}, bf16[1,1024,256]{2,1,0:T(8,128)(2,1)S(1)}, u32[]{:S(2)}) copy-start(bf16[1,1024,256]{2,1,0:T(8,128)(2,1)S(1)} %get-tuple-element.46.last) | copy-start | bytes 1572868
  30.9 19.1 %copy-start.8 = (bf16[4,1024,128]{2,1,0:T(8,128)(2,1)S(1)}, bf16[4,1024,128]{2,1,0:T(8,128)(2,1)}, u32[]{:S(2)}) copy-start(bf16[4,1024,128]{2,1,0:T(8,128)(2,1)} %cot.3) | copy-start | bytes 3145732
  30.9 14.9 %collective-permute-start.3 = (bf16[1,1024,256]{2,1,0:T(8,128)(2,1)S(1)}, bf16[1,1024,256]{2,1,0:T(8,128)(2,1)S(1)}, u32[]{:S(2)}, u32[]{:S(2)}) collective-permute-start(bf16[1,1024,256]{2,1,0:T(8,128)(2,1)S(1)} %get-tuple-element.46.last), channel_id=1, source_target_pairs={{0,4},{4,8},{8,12},{12,16},{16,20},{20,24},{24,28},{28,32},{32,36}... | collective-permute-start | bytes 1572872 | tf_op jit(solution)/shard_map/ppermute | solution.py:502
  34.7 15.2 %collective-permute-start.7 = (bf16[1,1024,256]{2,1,0:T(8,128)(2,1)S(1)}, bf16[1,1024,256]{2,1,0:T(8,128)(2,1)S(1)}, u32[]{:S(2)}, u32[]{:S(2)}) collective-permute-start(bf16[1,1024,256]{2,1,0:T(8,128)(2,1)S(1)} %get-tuple-element.47.first), channel_id=1, source_target_pairs={{4,0},{8,4},{12,8},{16,12},{20,16},{24,20},{28,24},{32,28},{36,32}... | collective-permute-start | bytes 1572872 | tf_op jit(solution)/shard_map/ppermute | solution.py:503
  36.1 13.9 %copy-start.27 = (bf16[2048,128]{1,0:T(8,128)(2,1)}, bf16[2048,128]{1,0:T(8,128)(2,1)S(1)}, u32[]{:S(2)}) copy-start(bf16[2048,128]{1,0:T(8,128)(2,1)S(1)} %collective-permute-done.6.x3) | copy-start | bytes 1572868
  45.8 10.2 %copy-start.4 = (bf16[1,1024,256]{2,1,0:T(8,128)(2,1)}, bf16[1,1024,256]{2,1,0:T(8,128)(2,1)S(1)}, u32[]{:S(2)}) copy-start(bf16[1,1024,256]{2,1,0:T(8,128)(2,1)S(1)} %collective-permute-done.3.up) | copy-start | bytes 1572868
  50.0 6.0 %copy-start.6 = (bf16[1,1024,256]{2,1,0:T(8,128)(2,1)}, bf16[1,1024,256]{2,1,0:T(8,128)(2,1)S(1)}, u32[]{:S(2)}) copy-start(bf16[1,1024,256]{2,1,0:T(8,128)(2,1)S(1)} %collective-permute-done.7.down) | copy-start | bytes 1572868
  56.0 35.9 %copy-start.17 = (bf16[4,1024,128]{2,1,0:T(8,128)(2,1)}, bf16[4,1024,128]{2,1,0:T(8,128)(2,1)S(1)}, u32[]{:S(2)}) copy-start(bf16[4,1024,128]{2,1,0:T(8,128)(2,1)S(1)} %get-tuple-element.61.feat) | copy-start | bytes 3145732
  96.9 1.4 copy-start.12
  98.3 0.7 copy-start.29
  99.0 31.9 %all-to-all-start.1 = ((bf16[32,8,32,128]{3,2,1,0:T(8,128)(2,1)}), bf16[32,8,32,128]{3,2,1,0:T(8,128)(2,1)S(1)}, u32[]{:S(2)}, u32[]{:S(2)}) async-start(bf16[32,8,32,128]{3,2,1,0:T(8,128)(2,1)} %copy-done.12), calls=%async_computation.1 | async-start | bytes 4194304 | tf_op jit(solution)/shard_map/all_to_all | solution.py:564
  130.9 1.2 copy-start.9
  132.1 1.6 copy-start.11
  133.7 1.2 copy-start.18
  137.4 6.8 %copy-start.1 = (bf16[1,1024,256]{2,1,0:T(8,128)(2,1)S(1)}, bf16[1,1024,256]{2,1,0:T(8,128)(2,1)}, u32[]{:S(2)}) copy-start(bf16[1,1024,256]{2,1,0:T(8,128)(2,1)} %copy-done) | copy-start | bytes 1572868
  137.4 6.8 %copy-start.3 = (bf16[1,1024,256]{2,1,0:T(8,128)(2,1)S(1)}, bf16[1,1024,256]{2,1,0:T(8,128)(2,1)}, u32[]{:S(2)}) copy-start(bf16[1,1024,256]{2,1,0:T(8,128)(2,1)} %copy-done.2) | copy-start | bytes 1572868
  137.4 6.8 %copy-start.5 = (bf16[1,1024,256]{2,1,0:T(8,128)(2,1)S(1)}, bf16[1,1024,256]{2,1,0:T(8,128)(2,1)}, u32[]{:S(2)}) copy-start(bf16[1,1024,256]{2,1,0:T(8,128)(2,1)} %copy-done.4) | copy-start | bytes 1572868
  137.4 6.8 %copy-start.7 = (bf16[1,1024,256]{2,1,0:T(8,128)(2,1)S(1)}, bf16[1,1024,256]{2,1,0:T(8,128)(2,1)}, u32[]{:S(2)}) copy-start(bf16[1,1024,256]{2,1,0:T(8,128)(2,1)} %copy-done.6) | copy-start | bytes 1572868
  137.4 16.4 %collective-permute-start.8 = (bf16[1,1024,256]{2,1,0:T(8,128)(2,1)S(1)}, bf16[1,1024,256]{2,1,0:T(8,128)(2,1)S(1)}, u32[]{:S(2)}, u32[]{:S(2)}) collective-permute-start(bf16[1,1024,256]{2,1,0:T(8,128)(2,1)S(1)} %get-tuple-element.63.glast), channel_id=1, source_target_pairs={{0,4},{4,8},{8,12},{12,16},{16,20},{20,24},{24,28},{28,32},{32,36}... | collective-permute-start | bytes 1572872 | tf_op jit(solution)/shard_map/ppermute | solution.py:502
  140.7 13.1 %collective-permute-start.9 = (bf16[1,1024,256]{2,1,0:T(8,128)(2,1)S(1)}, bf16[1,1024,256]{2,1,0:T(8,128)(2,1)S(1)}, u32[]{:S(2)}, u32[]{:S(2)}) collective-permute-start(bf16[1,1024,256]{2,1,0:T(8,128)(2,1)S(1)} %get-tuple-element.64.gfirst), channel_id=1, source_target_pairs={{4,0},{8,4},{12,8},{16,12},{20,16},{24,20},{28,24},{32,28},{36,32}... | collective-permute-start | bytes 1572872 | tf_op jit(solution)/shard_map/ppermute | solution.py:503
  146.2 2.0 copy-start.36
  146.2 2.2 %copy-start.16 = (bf16[2,1024,128]{2,1,0:T(8,128)(2,1)S(1)}, bf16[2,1024,128]{2,1,0:T(8,128)(2,1)}, u32[]{:S(2)}) copy-start(bf16[2,1024,128]{2,1,0:T(8,128)(2,1)} %copy-done.15) | copy-start | bytes 1572868
  146.2 2.2 %copy-start.26 = (bf16[2048,128]{1,0:T(8,128)(2,1)S(1)}, bf16[2048,128]{1,0:T(8,128)(2,1)}, u32[]{:S(2)}) copy-start(bf16[2048,128]{1,0:T(8,128)(2,1)} %copy-done.25) | copy-start | bytes 1572868
  146.2 2.2 %copy-start.28 = (bf16[2048,128]{1,0:T(8,128)(2,1)S(1)}, bf16[2048,128]{1,0:T(8,128)(2,1)}, u32[]{:S(2)}) copy-start(bf16[2048,128]{1,0:T(8,128)(2,1)} %copy-done.27) | copy-start | bytes 1572868
  151.5 4.6 %copy-start.14 = (bf16[2048,128]{1,0:T(8,128)(2,1)S(1)}, bf16[2048,128]{1,0:T(8,128)(2,1)}, u32[]{:S(2)}) copy-start(bf16[2048,128]{1,0:T(8,128)(2,1)} %copy-done.13) | copy-start | bytes 1572868
  151.5 4.7 %copy-start.20 = (bf16[2048,128]{1,0:T(8,128)(2,1)S(1)}, bf16[2048,128]{1,0:T(8,128)(2,1)}, u32[]{:S(2)}) copy-start(bf16[2048,128]{1,0:T(8,128)(2,1)} %copy-done.19) | copy-start | bytes 1572868
  151.5 4.7 %copy-start.22 = (bf16[2048,128]{1,0:T(8,128)(2,1)S(1)}, bf16[2048,128]{1,0:T(8,128)(2,1)}, u32[]{:S(2)}) copy-start(bf16[2048,128]{1,0:T(8,128)(2,1)} %copy-done.21) | copy-start | bytes 1572868
  151.5 4.7 %copy-start.24 = (bf16[2048,128]{1,0:T(8,128)(2,1)S(1)}, bf16[2048,128]{1,0:T(8,128)(2,1)}, u32[]{:S(2)}) copy-start(bf16[2048,128]{1,0:T(8,128)(2,1)} %copy-done.23) | copy-start | bytes 1572868
  151.5 20.4 %collective-permute-start.13 = (bf16[2048,128]{1,0:T(8,128)(2,1)}, bf16[2048,128]{1,0:T(8,128)(2,1)}, u32[]{:S(2)}, u32[]{:S(2)}) collective-permute-start(bf16[2048,128]{1,0:T(8,128)(2,1)} %convolution_convert_fusion.1), channel_id=1, source_target_pairs={{0,1},{1,0},{2,3},{3,2},{4,5},{5,4},{6,7},{7,6},{8,9},{9,8},{10,11... | collective-permute-start | bytes 1572872 | tf_op jit(solution)/shard_map/ppermute | solution.py:499
  156.1 1.0 copy-start.30
  158.0 23.3 %all-to-all-start.2 = ((bf16[32,88,128]{2,1,0:T(8,128)(2,1)}), bf16[32,88,128]{2,1,0:T(8,128)(2,1)}, u32[]{:S(2)}, u32[]{:S(2)}) async-start(bf16[32,88,128]{2,1,0:T(8,128)(2,1)} %shard_map.137), calls=%async_computation.2 | async-start | bytes 1441792 | tf_op jit(solution)/shard_map/all_to_all | solution.py:630
  168.0 6.7 %collective-permute-start.10 = (bf16[2048,128]{1,0:T(8,128)(2,1)S(1)}, bf16[2048,128]{1,0:T(8,128)(2,1)S(1)}, u32[]{:S(2)}, u32[]{:S(2)}) collective-permute-start(bf16[2048,128]{1,0:T(8,128)(2,1)S(1)} %convolution_convert_fusion.3), channel_id=1, source_target_pairs={{0,1},{1,0},{2,3},{3,2},{4,5},{5,4},{6,7},{7,6},{8,9},{9,8},{10,11... | collective-permute-start | bytes 1572872 | tf_op jit(solution)/shard_map/ppermute | solution.py:499
  174.6 6.3 %collective-permute-start.14 = (bf16[2048,128]{1,0:T(8,128)(2,1)S(1)}, bf16[2048,128]{1,0:T(8,128)(2,1)S(1)}, u32[]{:S(2)}, u32[]{:S(2)}) collective-permute-start(bf16[2048,128]{1,0:T(8,128)(2,1)S(1)} %convolution_convert_fusion), channel_id=1, source_target_pairs={{0,1},{1,0},{2,3},{3,2},{4,5},{5,4},{6,7},{7,6},{8,9},{9,8},{10,11... | collective-permute-start | bytes 1572872 | tf_op jit(solution)/shard_map/ppermute | solution.py:499
  177.2 6.6 %collective-permute-start.11 = (bf16[2048,128]{1,0:T(8,128)(2,1)}, bf16[2048,128]{1,0:T(8,128)(2,1)}, u32[]{:S(2)}, u32[]{:S(2)}) collective-permute-start(bf16[2048,128]{1,0:T(8,128)(2,1)} %convolution_convert_fusion.2), channel_id=1, source_target_pairs={{0,1},{1,0},{2,3},{3,2},{4,5},{5,4},{6,7},{7,6},{8,9},{9,8},{10,11... | collective-permute-start | bytes 1572872 | tf_op jit(solution)/shard_map/ppermute | solution.py:499
  177.6 15.7 %collective-permute-start.15 = (bf16[2048,128]{1,0:T(8,128)(2,1)}, bf16[2048,128]{1,0:T(8,128)(2,1)}, u32[]{:S(2)}, u32[]{:S(2)}) collective-permute-start(bf16[2048,128]{1,0:T(8,128)(2,1)} %add_convert_fusion), channel_id=1, source_target_pairs={{0,2},{1,3},{2,0},{3,1},{4,6},{5,7},{6,4},{7,5},{8,10},{9,11},{10,... | collective-permute-start | bytes 1572872 | tf_op jit(solution)/shard_map/ppermute | solution.py:499
  180.8 23.8 %collective-permute-start.12 = (bf16[2048,128]{1,0:T(8,128)(2,1)}, bf16[2048,128]{1,0:T(8,128)(2,1)}, u32[]{:S(2)}, u32[]{:S(2)}) collective-permute-start(bf16[2048,128]{1,0:T(8,128)(2,1)} %fusion), channel_id=1, source_target_pairs={{0,2},{1,3},{2,0},{3,1},{4,6},{5,7},{6,4},{7,5},{8,10},{9,11},{10,... | collective-permute-start | bytes 1572872 | tf_op jit(solution)/shard_map/ppermute | solution.py:499

commit v3 on v2

--- a/solution.py
+++ b/solution.py
@@ -118,20 +118,23 @@
         w_all[to, pl.ds(channels, channels)] = w_value[at, :]
 
 
-def fill_framed(framed, rows_of, channels):
-    width = rows_of[0][0].shape[1]
+def fill_framed(framed, rows_of, channels, branches=(0, 1)):
+    width = sum(ref.shape[-2] for ref, _ in rows_of[-2])
     zeros = jnp.zeros((EDGE, channels), F32)
-    for branch in range(2):
+    for n in range(len(branches)):
         for r in range(len(rows_of)):
-            framed[branch, r, pl.ds(0, EDGE), :] = zeros
-            framed[branch, r, pl.ds(EDGE + width, EDGE), :] = zeros
+            framed[n, r, pl.ds(0, EDGE), :] = zeros
+            framed[n, r, pl.ds(EDGE + width, EDGE), :] = zeros
 
     def body(t, _):
-        at = pl.multiple_of(t * 32, 32)
-        for r, (ref, row) in enumerate(rows_of):
-            for branch in range(2):
-                v = ref[row, pl.ds(at, 32), pl.ds(branch * channels, channels)]
-                framed[branch, r, pl.ds(EDGE + at, 32), :] = v.astype(F32)
+        at = pl.multiple_of(t * 16, 16)
+        for r, pieces in enumerate(rows_of):
+            for side in range(2):
+                ref, row = pieces[side % len(pieces)]
+                start = at + (side * width // 2 if len(pieces) == 1 else 0)
+                for n, branch in enumerate(branches):
+                    v = ref[row, pl.ds(start, 16), pl.ds(branch * channels, channels)]
+                    framed[n, r, pl.ds(EDGE + at + side * width // 2, 16), :] = v.astype(F32)
         return 0
 
     lax.fori_loop(0, width // 32, body, 0)
@@ -162,48 +165,87 @@
     middle[...] = projected((x0, x1, x2, x3), w).reshape(middle.shape)
 
 
-def forward_kernel(up, first, middle, last, down, cot, kern, mat, send, feat, framed, cols):
-    rows, width, channels = cot.shape
-    owners, _, per_owner, _ = send.shape
-    inner = [(middle, r) for r in range(rows - 2)]
-    fill_framed(framed, [(up, 0), (first, 0), *inner, (last, 0), (down, 0)], channels)
+def forward_rows(framed, outs, cot, kern, mat, feat, cols, put):
+    _, width, channels = cot.shape
     for branch in range(2):
         taps = taps_of(kern, branch, channels)
 
         def body(t, _, branch=branch, taps=taps):
             base = pl.multiple_of(t * STEP, STEP)
-            done = [[] for _ in range(rows)]
+            done = [[] for _ in outs]
             for p in range(STEP // 8):
-                acc = [None] * rows
-                for r in range(rows + 2):
+                acc = [None] * len(outs)
+                for r in sorted({c + i - 1 for _, c in outs for i in range(3)}):
                     for j in range(3):
                         v = framed[branch, r, pl.ds(base + 8 * p + EDGE + j - 1, 8), :]
-                        for i in range(3):
-                            o = r - i
-                            if 0 <= o < rows:
+                        for n, (_, c) in enumerate(outs):
+                            i = r - c + 1
+                            if 0 <= i < 3:
                                 term = taps[i * 3 + j] * v
-                                acc[o] = term if acc[o] is None else acc[o] + term
-                for o in range(rows):
-                    done[o].append(acc[o])
-            for o in range(rows):
-                f = jnp.concatenate(done[o], axis=0).astype(BF)
+                                acc[n] = term if acc[n] is None else acc[n] + term
+                for n in range(len(outs)):
+                    done[n].append(acc[n])
+            for n, (row, _) in enumerate(outs):
+                f = jnp.concatenate(done[n], axis=0).astype(BF)
                 if branch == 0:
-                    feat[o, pl.ds(base, STEP), :] = f
-                    g = cot[o, pl.ds(base, STEP), :].astype(F32) * f.astype(F32)
-                    cols[pl.ds(base, STEP), pl.ds((rows + o) * channels, channels)] = g.astype(BF)
+                    feat[n, pl.ds(base, STEP), :] = f
+                    g = cot[row, pl.ds(base, STEP), :].astype(F32) * f.astype(F32)
+                    lanes = pl.ds((len(outs) + n) * channels, channels)
+                    cols[pl.ds(base, STEP), lanes] = g.astype(BF)
                 else:
-                    cols[pl.ds(base, STEP), pl.ds(o * channels, channels)] = f
+                    cols[pl.ds(base, STEP), pl.ds(n * channels, channels)] = f
             return 0
 
         lax.fori_loop(0, width // STEP, body, 0)
-    for n in range(rows):
+    for n in range(len(outs)):
         spec = jnp.dot(
             mat[...], cols[:, pl.ds(2 * n * channels, 2 * channels)], preferred_element_type=F32
         ).astype(BF)
         for e in range(2):
-            send[:, 2 * n + e] = spec[:, e * channels : (e + 1) * channels].reshape(
-                owners, per_owner, channels
-            )
+            put(2 * n + e, spec[:, e * channels : (e + 1) * channels])
+
+
+def forward_mid_kernel(f0, f1, middle, l0, l1, cot, kern, mat, part, feat, framed, cols):
+    channels = cot.shape[2]
+    inner = middle.shape[0]
+    owners, _, per_owner, _ = part.shape
+    whole = [((middle, r),) for r in range(inner)]
+    fill_framed(framed, [((f0, 0), (f1, 0)), *whole, ((l0, 0), (l1, 0))], channels)
+
+    def put(block, spec):
+        part[:, block] = spec.reshape(owners, per_owner, channels)
+
+    outs = [(r + 1, r + 1) for r in range(inner)]
+    forward_rows(framed, outs, cot, kern, mat, feat, cols, put)
+
+
+def forward_edge_kernel(
+    u0, u1, f0, f1, middle, l0, l1, d0, d1, cot, kern, mat, part, send, feat, framed, cols
+):
+    rows, _, channels = cot.shape
+    inner = rows - 2
+    owners, _, per_owner, _ = send.shape
+    for r in range(inner):
+        send[:, r + 1] = part[:, r]
+        send[:, rows + r + 1] = part[:, inner + r]
+    fill_framed(
+        framed,
+        [
+            ((u0, 0), (u1, 0)),
+            ((f0, 0), (f1, 0)),
+            ((middle, 0),),
+            ((middle, inner - 1),),
+            ((l0, 0), (l1, 0)),
+            ((d0, 0), (d1, 0)),
+        ],
+        channels,
+    )
+
+    def put(block, spec):
+        to = (block // 2) * rows + (block % 2) * (rows - 1)
+        send[:, to] = spec.reshape(owners, per_owner, channels)
+
+    forward_rows(framed, [(0, 1), (rows - 1, 4)], cot, kern, mat, feat, cols, put)
 
 
 def column_kernel(
@@ -317,7 +359,7 @@
     ).astype(BF)
 
 
-def inverse_kernel(recv, mat, feat, cot, gated, first, middle, last):
+def inverse_kernel(recv, mat, feat_edge, feat_mid, cot, gated, first, middle, last):
     rows, width, channels = cot.shape
     for n in range(rows):
         spec = jnp.concatenate(
@@ -329,13 +371,14 @@
             value = back[:, e * channels : (e + 1) * channels]
             to, row = ((first, 0), *((middle, i) for i in range(rows - 2)), (last, 0))[r]
             if n < rows // 2:
-                gated[r] = (feat[r].astype(F32) * value).astype(BF)
+                feat = feat_mid[r - 1] if 0 < r < rows - 1 else feat_edge[r // (rows - 1)]
+                gated[r] = (feat.astype(F32) * value).astype(BF)
                 to[row, :, pl.ds(0, channels)] = (cot[r].astype(F32) * value).astype(BF)
             else:
                 to[row, :, pl.ds(channels, channels)] = value.astype(BF)
 
 
-def spread_back(framed, kern, outs, width, channels):
+def spread_back(framed, kern, outs, width, channels, skip=0):
     for branch in range(2):
         taps = taps_of(kern, branch, channels)
 
@@ -347,7 +390,7 @@
                 needed = sorted({c + 1 - i for _, _, c in outs for i in range(3)})
                 for r in needed:
                     for j in range(3):
-                        v = framed[branch, r, pl.ds(base + 8 * p + EDGE + 1 - j, 8), :]
+                        v = framed[branch, r, pl.ds(base + skip + 8 * p + EDGE + 1 - j, 8), :]
                         for n, (_, _, c) in enumerate(outs):
                             i = c + 1 - r
                             if 0 <= i < 3:
@@ -367,32 +410,23 @@
     width = gfirst.shape[1]
     channels = kern.shape[1]
     inner = gmiddle.shape[0]
-    fill_framed(
-        gframed, [(gfirst, 0), *((gmiddle, r) for r in range(inner)), (glast, 0)], channels
-    )
+    whole = [((gmiddle, r),) for r in range(inner)]
+    fill_framed(gframed, [((gfirst, 0),), *whole, ((glast, 0),)], channels)
     spread_back(gframed, kern, [(back, r, r + 1) for r in range(inner)], width, channels)
 
 
-def short_kernel(up, first, middle, last, down, gfirst, gmiddle, glast, short, framed, *, branch):
-    width = first.shape[1]
+def short_kernel(
+    u0, u1, f0, f1, middle, l0, l1, d0, d1, gfirst, gmiddle, glast, short, framed, *, branch
+):
+    width = gfirst.shape[1]
     channels = short.shape[1]
     inner = middle.shape[0]
     rows = inner + 2
     lanes = pl.ds(branch * channels, channels)
-    tokens = [(up, 0), (first, 0), *((middle, r) for r in range(inner)), (last, 0), (down, 0)]
+    whole = [((middle, r),) for r in range(inner)]
+    halves = [((u0, 0), (u1, 0)), ((f0, 0), (f1, 0))], [((l0, 0), (l1, 0)), ((d0, 0), (d1, 0))]
+    fill_framed(framed, [*halves[0], *whole, *halves[1]], channels, (branch,))
     grads = [(gfirst, 0), *((gmiddle, r) for r in range(inner)), (glast, 0)]
-    zeros = jnp.zeros((EDGE, channels), F32)
-    for r in range(rows + 2):
-        framed[r, pl.ds(0, EDGE), :] = zeros
-        framed[r, pl.ds(EDGE + width, EDGE), :] = zeros
-
-    def fill(t, _):
-        at = pl.multiple_of(t * 32, 32)
-        for r, (ref, row) in enumerate(tokens):
-            framed[r, pl.ds(EDGE + at, 32), :] = ref[row, pl.ds(at, 32), lanes].astype(F32)
-        return 0
-
-    lax.fori_loop(0, width // 32, fill, 0)
 
     def terms(t, sums):
         base = pl.multiple_of(t * 16, 16)
@@ -403,7 +437,7 @@
             g = [v[8 * p : 8 * p + 8] for v in both]
             for r in range(rows + 2):
                 for j in range(3):
-                    v = framed[r, pl.ds(at + j - 1, 8), :]
+                    v = framed[0, r, pl.ds(at + j - 1, 8), :]
                     for i in range(3):
                         o = r - i
                         if 0 <= o < rows:
@@ -418,15 +452,24 @@
 
 
 def backward_edge_kernel(gup, gfirst, gmiddle, glast, gdown, kern, back, gframed):
-    width = gfirst.shape[1]
     channels = kern.shape[1]
     inner = gmiddle.shape[0]
     fill_framed(
         gframed,
-        [(gup, 0), (gfirst, 0), (gmiddle, 0), (gmiddle, inner - 1), (glast, 0), (gdown, 0)],
+        [
+            ((gup, 0),),
+            ((gfirst, 0),),
+            ((gmiddle, 0),),
+            ((gmiddle, inner - 1),),
+            ((glast, 0),),
+            ((gdown, 0),),
+        ],
         channels,
     )
-    spread_back(gframed, kern, [(back, 0, 1), (back, 1, 4)], width, channels)
+    size = back.shape[2]
+    for side in range(2):
+        to = back.at[side]
+        spread_back(gframed, kern, [(to, 0, 1), (to, 1, 4)], size, channels, side * size)
 
 
 def finish_kernel(kept_edge, edge, kept_mid, mid, grad):
@@ -435,9 +478,12 @@
     for r in range(inner):
         at = pl.ds(r * width, width)
         grad[r + 1] = (kept_mid[at, :] + mid[at, :].astype(F32)).astype(BF)
-    for r in range(2):
-        at = pl.ds(r * width, width)
-        grad[r * (inner + 1)] = (kept_edge[at, :] + edge[at, :].astype(F32)).astype(BF)
+    size = width // 2
+    for side in range(2):
+        for r in range(2):
+            at = pl.ds(side * width + r * size, size)
+            value = (kept_edge[at, :] + edge[at, :].astype(F32)).astype(BF)
+            grad[r * (inner + 1), pl.ds(side * size, size), :] = value
 
 
 def sum_kernel(parts, *outs, scale):
@@ -503,13 +549,16 @@
         down = lax.ppermute(first, "grid", [(i + 1, i) for i in range(owners - 1)])
         return up, down
 
-    edge = jnp.concatenate([inputs[0], inputs[rows - 1]], axis=0)
+    size = width // 2
+    edges, edges_across, edges_beside = [], [], []
+    for n in range(2):
+        lines_of = [inputs[r, n * size : (n + 1) * size] for r in (0, rows - 1)]
+        edges.append(jnp.concatenate(lines_of, axis=0))
+        edges_across.append(flipped(edges[n], 2))
     mid = inputs[1 : rows - 1].reshape(inner * width, channels)
-    edge_across = flipped(edge, 2)
     mid_across = flipped(mid, 2)
-    edge_beside = flipped(edge, 1)
+    edges_beside = [flipped(edge, 1) for edge in edges]
     mid_beside = flipped(mid, 1)
-    edge_corner = flipped(edge_across, 1)
 
     (mat, mat_t, mine, fwd, inv, coef, keep, colr, coli, kern, w_all) = kernel_call(
         tables_kernel,
@@ -535,14 +584,20 @@
 
     line = ((1, width, 2 * channels), BF)
     lines = ((inner, width, 2 * channels), BF)
-    edge_blocks = (edge, edge_beside, edge_across, edge_corner)
-    first, last = kernel_call(project_edge_kernel, [line, line], [], 12)(*edge_blocks, w_all)
-    up, down = halos(first, last)
+    side = ((1, size, 2 * channels), BF)
+    edge_blocks, ends, around = [], [], []
+    for n in range(2):
+        corner = flipped(edges_across[n], 1)
+        edge_blocks.append((edges[n], edges_beside[n], edges_across[n], corner))
+        ends.append(kernel_call(project_edge_kernel, [side, side], [], 12)(*edge_blocks[n], w_all))
+        around.append(halos(*ends[n]))
+    firsts, lasts = zip(*ends)
+    ups, downs = zip(*around)
     mid_corner = flipped(mid_across, 1)
     mid_blocks = (mid, mid_beside, mid_across, mid_corner)
     middle = kernel_call(project_mid_kernel, [lines], [], 12)(*mid_blocks, w_all)[0]
     middle, edge_blocks, mid_blocks = lax.optimization_barrier((middle, edge_blocks, mid_blocks))
-    gathered_edge = jnp.concatenate(edge_blocks, axis=1)
+    gathered_edge = jnp.concatenate([jnp.concatenate(b, axis=1) for b in edge_blocks], axis=0)
     gathered_mid = jnp.concatenate(mid_blocks, axis=1)
 
     def framed(count):
@@ -550,9 +605,17 @@
 
     spread = ((owners, 2 * rows, per_owner, channels), BF)
     tile = ((rows, width, channels), BF)
-    send, feat = kernel_call(
-        forward_kernel, [spread, tile], [framed(rows + 2), ((width, 2 * rows * channels), BF)], 24
-    )(up, first, middle, last, down, cotangent, kern, mat)
+    pair = ((2, width, channels), BF)
+    cols = ((width, 4 * channels), BF)
+    part, feat_mid = kernel_call(
+        forward_mid_kernel,
+        [((owners, rows, per_owner, channels), BF), pair],
+        [framed(rows), cols],
+        16,
+    )(*firsts, middle, *lasts, cotangent, kern, mat)
+    send, feat_edge = kernel_call(
+        forward_edge_kernel, [spread, pair], [framed(6), cols], 20
+    )(*ups, *firsts, middle, *lasts, *downs, cotangent, kern, mat, part)
     recv = lax.all_to_all(send, "grid", split_axis=0, concat_axis=0, tiled=True)
     tall = (2 * height, 2 * half * channels)
     turned, row_part, colp = kernel_call(
@@ -564,7 +627,7 @@
     returned = lax.all_to_all(turned, "grid", split_axis=0, concat_axis=0, tiled=True)
     gated, gfirst, gmiddle, glast = kernel_call(
         inverse_kernel, [tile, line, lines, line], [], 20
-    )(returned, mat_t, feat, cotangent)
+    )(returned, mat_t, feat_edge, feat_mid, cotangent)
     gup, gdown = halos(gfirst, glast)
     back_mid = kernel_call(backward_mid_kernel, [lines], [framed(rows)], 16)(
         gfirst, gmiddle, glast, kern
@@ -573,12 +636,13 @@
         kernel_call(
             functools.partial(short_kernel, branch=n),
             [((9, channels), F32)],
-            [((rows + 2, width + 2 * EDGE, channels), F32)],
+            [((1, rows + 2, width + 2 * EDGE, channels), F32)],
             12,
-        )(up, first, middle, last, down, gfirst, gmiddle, glast)[0]
+        )(*ups, *firsts, middle, *lasts, *downs, gfirst, gmiddle, glast)[0]
         for n in range(2)
     ]
-    back_edge = kernel_call(backward_edge_kernel, [lines], [framed(6)], 16)(
+    halved = ((2, 2, size, 2 * channels), BF)
+    back_edge = kernel_call(backward_edge_kernel, [halved], [framed(6)], 16)(
         gup, gfirst, gmiddle, glast, gdown, kern
     )[0]
 

time: 208 us -> 227 us (1.091)
  starting transfers between devices: 43.1 us -> 54 us
  waiting for transfers between devices: 67.2 us -> 59.1 us
  local copies, waits for them, and re-layouts: 10.9 us -> 16.7 us
  blocking collectives: 35.9 us -> 41.4 us
  Pallas kernels: 36.4 us -> 40.7 us
    ppermute x2 -> x3, waiting for transfers between devices: 7.73 us -> 0.01 us  [halos(): up = lax.ppermute(last, 'grid', [(i, i + 1) for i in range(owners - 1)])]
    all_to_all x1, blocking collectives: 35.9 us -> 41.4 us  [local(): recv = lax.all_to_all(send, 'grid', split_axis=0, concat_axis=0, tiled=True)]
    ppermute x2 -> x3, starting transfers between devices: 7.11 us -> 12.5 us  [halos(): up = lax.ppermute(last, 'grid', [(i, i + 1) for i in range(owners - 1)])]
    ppermute x2 -> x3, waiting for transfers between devices: 4.17 us -> 0.01 us  [halos(): down = lax.ppermute(first, 'grid', [(i + 1, i) for i in range(owners - 1)])]
    ppermute x12 -> x15, waiting for transfers between devices: 29.5 us -> 33.6 us  [flipped(): return lax.ppermute(value, 'ch', [(i, i ^ bit) for i in range(parts)])]
    unnamed x78 -> x82, local copies, waits for them, and re-layouts: 9.55 us -> 13.5 us
    ppermute x12 -> x15, starting transfers between devices: 18.2 us -> 22 us  [flipped(): return lax.ppermute(value, 'ch', [(i, i ^ bit) for i in range(parts)])]
    pallas_call x3 -> x5, Pallas kernels: 8.89 us -> 11.3 us  [the longest x1 3.79 us: local(): kernel_call(forward_edge_kernel, [spread, pair], [framed(6), cols], 20)]
  transfers between devices with their start and end apart: 18 -> 23, of which waited for: 6 -> 5; matrix products, arithmetic and copies ran while one was open for 6% -> 7% of each run, Pallas kernels for 10% -> 11%
where the time goes in v3:
time: 227 us; the launch traced here: 226 us
  waiting for transfers between devices  59.1 us (26%)
  starting transfers between devices  54 us (24%)
  blocking collectives  41.4 us (18%)
  Pallas kernels  40.7 us (18%)
  local copies, waits for them, and re-layouts  16.7 us (7%)
  matrix products  12.7 us (6%)
    all_to_all x1, blocking collectives, local(): recv = lax.all_to_all(send, 'grid', split_axis=0, concat_axis=0, tiled=True)  41.4 us
    ppermute x15, waiting for transfers between devices, flipped(): return lax.ppermute(value, 'ch', [(i, i ^ bit) for i in range(parts)])  33.6 us
    all_to_all x1, waiting for transfers between devices, local(): lax.all_to_all(turned, 'grid', split_axis=0, concat_axis=0, tiled=True)  25.5 us
    ppermute x15, starting transfers between devices, flipped(): return lax.ppermute(value, 'ch', [(i, i ^ bit) for i in range(parts)])  22 us
    unnamed x82, local copies, waits for them, and re-layouts  13.5 us
    ppermute x3, starting transfers between devices, halos(): up = lax.ppermute(last, 'grid', [(i, i + 1) for i in range(owners - 1)])  12.5 us
    all_to_all x1, starting transfers between devices, local(): lax.all_to_all(packed, 'grid', split_axis=0, concat_axis=0, tiled=True)  9.46 us
    dot_general x8, matrix products, share(): lax.dot_general(back, w_blocks[k], contract, preferred_element_type=F32)  8.72 us
  transfers between devices with their start and end apart: 23, of which 5 were waited for; matrix products, arithmetic and copies ran while one was open for 7% of the time, Pallas kernels for 11%

profile of v3, /device:TPU:1, one launch (start us, length us, event | category | flops | bytes accessed | tf_op | source)
XLA Modules:
  0.0 226.3 jit_solution(9513499717965805421)
XLA Ops:
  0.7 1.9 slice.31
  2.6 3.7 %collective-permute-start.9 = (bf16[2048,128]{1,0:T(8,128)(2,1)}, bf16[2048,128]{1,0:T(8,128)(2,1)}, u32[]{:S(2)}, u32[]{:S(2)}) collective-permute-start(bf16[2048,128]{1,0:T(8,128)(2,1)} %bitcast.6.x0), channel_id=1, source_target_pairs={{0,2},{1,3},{2,0},{3,1},{4,6},{5,7},{6,4},{7,5},{8,10},{9,11},{10,... | collective-permute-start | bytes 1572872 | tf_op jit(solution)/shard_map/ppermute | solution.py:545
  6.3 1.1 slice_bitcast_fusion.1
  7.6 3.0 %collective-permute-start.1 = (bf16[1024,128]{1,0:T(8,128)(2,1)S(1)}, bf16[1024,128]{1,0:T(8,128)(2,1)S(1)}, u32[]{:S(2)}, u32[]{:S(2)}) collective-permute-start(bf16[1024,128]{1,0:T(8,128)(2,1)S(1)} %pad_maximum_fusion.x0), channel_id=1, source_target_pairs={{0,2},{1,3},{2,0},{3,1},{4,6},{5,7},{6,4},{7,5},{8,10},{9,11},{10,... | collective-permute-start | bytes 786440 | tf_op jit(solution)/shard_map/ppermute | solution.py:545
  10.7 1.5 collective-permute-start.4
  12.2 11.4 %collective-permute-done.5.x2 = bf16[1024,128]{1,0:T(8,128)(2,1)S(1)} collective-permute-done((bf16[1024,128]{1,0:T(8,128)(2,1)S(1)}, bf16[1024,128]{1,0:T(8,128)(2,1)S(1)}, u32[]{:S(2)}, u32[]{:S(2)}) %collective-permute-start.5) | collective-permute-done | bytes 262176 | tf_op jit(solution)/shard_map/ppermute | solution.py:545
  23.6 2.6 %collective-permute-start.6 = (bf16[1024,128]{1,0:T(8,128)(2,1)S(1)}, bf16[1024,128]{1,0:T(8,128)(2,1)S(1)}, u32[]{:S(2)}, u32[]{:S(2)}) collective-permute-start(bf16[1024,128]{1,0:T(8,128)(2,1)S(1)} %collective-permute-done.5.x2), channel_id=1, source_target_pairs={{0,1},{1,0},{2,3},{3,2},{4,5},{5,4},{6,7},{7,6},{8,9},{9,8},{10,11... | collective-permute-start | bytes 786440 | tf_op jit(solution)/shard_map/ppermute | solution.py:545
  26.2 3.0 %collective-permute-done.1.x2 = bf16[1024,128]{1,0:T(8,128)(2,1)S(1)} collective-permute-done((bf16[1024,128]{1,0:T(8,128)(2,1)S(1)}, bf16[1024,128]{1,0:T(8,128)(2,1)S(1)}, u32[]{:S(2)}, u32[]{:S(2)}) %collective-permute-start.1) | collective-permute-done | bytes 262176 | tf_op jit(solution)/shard_map/ppermute | solution.py:545
  29.2 1.5 collective-permute-start
  30.7 0.7 copy-done.23
  31.5 7.2 %shard_map.126 = (bf16[1024,1024]{1,0:T(8,128)(2,1)S(1)}, bf16[1024,1024]{1,0:T(8,128)(2,1)S(1)}, bf16[32,1024]{1,0:T(8,128)(2,1)S(1)}, bf16[256,256]{1,0:T(8,12...) custom-call(s32[2]{0:T(128)S(1)} %pad_add_fusion.where, ...), custom_call_target="tpu_custom_call" | custom-call | tf_op jit(solution)/shard_map/pallas_call | solution.py:563
  38.7 1.3 copy-done.9
  40.0 0.4 shard_map.128
  40.4 0.7 copy-done.26
  41.1 1.3 collective-permute-start.12
  42.4 0.7 copy-done.30
  43.1 4.4 %collective-permute-start.7 = (bf16[1,512,256]{2,1,0:T(8,128)(2,1)S(1)}, bf16[1,512,256]{2,1,0:T(8,128)(2,1)S(1)}, u32[]{:S(2)}, u32[]{:S(2)}) collective-permute-start(bf16[1,512,256]{2,1,0:T(8,128)(2,1)S(1)} %get-tuple-element.55.l1), channel_id=1, source_target_pairs={{0,4},{4,8},{8,12},{12,16},{16,20},{20,24},{24,28},{28,32},{32,36}... | collective-permute-start | bytes 786440 | tf_op jit(solution)/shard_map/ppermute | solution.py:548
  47.6 0.9 copy-done.15
  48.5 0.9 copy-done.24
  49.5 0.9 copy-done.31
  50.4 1.4 shard_map.127
  51.8 1.3 collective-permute-start.11
  53.1 4.2 %collective-permute-start.3 = (bf16[1,512,256]{2,1,0:T(8,128)(2,1)S(1)}, bf16[1,512,256]{2,1,0:T(8,128)(2,1)S(1)}, u32[]{:S(2)}, u32[]{:S(2)}) collective-permute-start(bf16[1,512,256]{2,1,0:T(8,128)(2,1)S(1)} %get-tuple-element.54.l0), channel_id=1, source_target_pairs={{0,4},{4,8},{8,12},{12,16},{16,20},{20,24},{24,28},{28,32},{32,36}... | collective-permute-start | bytes 786440 | tf_op jit(solution)/shard_map/ppermute | solution.py:548
  57.3 2.2 shard_map.129.middle
  59.5 3.5 %shard_map.130 = (bf16[32,4,32,128]{3,2,1,0:T(8,128)(2,1)S(1)}, bf16[2,1024,128]{2,1,0:T(8,128)(2,1)S(1)}) custom-call(bf16[1,512,256]{2,1,0:T(8,128)(2,1)S(1)} %get-tuple-element.56.f0, bf16[1,512,256]{2,1,0:T(8,128)(2,1)S(1)} %get-tuple-element.57.f1, bf16[2,1024,256]{2,1,0:T(8,128)(2,1)S(1)} %shard_map.129.middle, ...), custom_call_target="tpu_custom_call" | custom-call | tf_op jit(solution)/shard_map/pallas_call | solution.py:610
  63.0 0.8 copy-done.17
  63.9 3.8 %shard_map.131 = (bf16[32,8,32,128]{3,2,1,0:T(8,128)(2,1)S(1)}, bf16[2,1024,128]{2,1,0:T(8,128)(2,1)S(1)}) custom-call(bf16[1,512,256]{2,1,0:T(8,128)(2,1)S(1)} %collective-permute-done.3.u0, bf16[1,512,256]{2,1,0:T(8,128)(2,1)S(1)} %collective-permute-done.7.u1, bf16[1,512,256]{2,1,0:T(8,128)(2,1)S(1)} %get-tuple-element.56.f0, ...), custom_call_target="tpu_custom_call" | custom-call | tf_op jit(solution)/shard_map/pallas_call | solution.py:616
  67.7 41.4 %all_to_all.15.recv = bf16[32,8,32,128]{3,2,1,0:T(8,128)(2,1)S(1)} all-to-all(bf16[32,8,32,128]{3,2,1,0:T(8,128)(2,1)S(1)} %get-tuple-element.62), channel_id=1, replica_groups=mesh['grid'=32,'ch'=4] {'grid'}, dimensions={0} | all-to-all | bytes 4194304 | tf_op jit(solution)/shard_map/all_to_all | solution.py:619
  109.1 5.0 %shard_map.132 = (bf16[32,8,32,128]{3,2,1,0:T(8,128)(2,1)S(1)}, bf16[1024,128]{1,0:T(8,128)(2,1)S(1)}, f32[128,128]{1,0:T(8,128)S(1)}) custom-call(bf16[32,8,32,128]{3,2,1,0:T(8,128)(2,1)S(1)} %all_to_all.15.recv, f32[4,16,128]{2,1,0:T(8,128)S(1)} %get-tuple-element.63.coef, f32[1,16,128]{2,1,0:T(8,128)S(1)} %get-tuple-element.64.keep, ...), custom_call_target="tpu_custom_call" | custom-call | tf_op jit(solution)/shard_map/pallas_call | solution.py:621
  114.1 1.3 copy-done.11
  115.4 0.7 copy-done.33
  116.1 6.0 %all-to-all-start.1 = ((bf16[32,8,32,128]{3,2,1,0:T(8,128)(2,1)}), bf16[32,8,32,128]{3,2,1,0:T(8,128)(2,1)}, u32[]{:S(2)}, u32[]{:S(2)}) async-start(bf16[32,8,32,128]{3,2,1,0:T(8,128)(2,1)} %copy-done.11), calls=%async_computation.1 | async-start | bytes 4194304 | tf_op jit(solution)/shard_map/all_to_all | solution.py:627
  122.2 25.5 %all-to-all-done.1.recv = bf16[32,8,32,128]{3,2,1,0:T(8,128)(2,1)} async-done(((bf16[32,8,32,128]{3,2,1,0:T(8,128)(2,1)}), bf16[32,8,32,128]{3,2,1,0:T(8,128)(2,1)}, u32[]{:S(2)}, u32[]{:S(2)}) %all-to-all-start.1) | async-done | bytes 2097184 | tf_op jit(solution)/shard_map/all_to_all | solution.py:627
  147.7 1.6 copy-done.10
  149.3 1.0 copy-done.18
  150.3 1.0 copy-done.20
  151.4 4.0 %shard_map.133 = (bf16[4,1024,128]{2,1,0:T(8,128)(2,1)}, bf16[1,1024,256]{2,1,0:T(8,128)(2,1)S(1)}, bf16[2,1024,256]{2,1,0:T(8,128)(2,1)S(1)}, bf16[1,1024,256]{2,1,0:T(8,128)(2,1)S(1)}) custom-call(bf16[32,8,32,128]{3,2,1,0:T(8,128)(2,1)} %all-to-all-done.1.recv, bf16[1024,1024]{1,0:T(8,128)(2,1)S(1)} %copy-done.10, bf16[2,1024,128]{2,1,0:T(8,128)(2,1)S(1)} %copy-done.20, ...), custom_call_target="tpu_custom_call" | custom-call | tf_op jit(solution)/shard_map/pallas_call | solution.py:628
  155.5 4.0 %collective-permute-start.13 = (bf16[1,1024,256]{2,1,0:T(8,128)(2,1)S(1)}, bf16[1,1024,256]{2,1,0:T(8,128)(2,1)S(1)}, u32[]{:S(2)}, u32[]{:S(2)}) collective-permute-start(bf16[1,1024,256]{2,1,0:T(8,128)(2,1)S(1)} %get-tuple-element.75.glast), channel_id=1, source_target_pairs={{0,4},{4,8},{8,12},{12,16},{16,20},{20,24},{24,28},{28,32},{32,36}... | collective-permute-start | bytes 1572872 | tf_op jit(solution)/shard_map/ppermute | solution.py:548
  159.4 1.5 collective-permute-start.14
  160.9 2.0 shard_map.135
  163.0 1.9 shard_map.137
  164.9 1.9 shard_map.138
  167.1 2.3 fusion.1
  169.3 1.2 convolution_convert_fusion.1
  170.6 2.6 %collective-permute-start.18 = (bf16[2048,128]{1,0:T(8,128)(2,1)}, bf16[2048,128]{1,0:T(8,128)(2,1)}, u32[]{:S(2)}, u32[]{:S(2)}) collective-permute-start(bf16[2048,128]{1,0:T(8,128)(2,1)} %convolution_convert_fusion.1), channel_id=1, source_target_pairs={{0,1},{1,0},{2,3},{3,2},{4,5},{5,4},{6,7},{7,6},{8,9},{9,8},{10,11... | collective-permute-start | bytes 1572872 | tf_op jit(solution)/shard_map/ppermute | solution.py:545
  173.2 2.2 shard_map.134
  175.5 1.7 fusion.9
  177.3 0.9 shard_map.139
  178.2 9.5 %all-to-all-start.2 = ((bf16[32,88,128]{2,1,0:T(8,128)(2,1)}), bf16[32,88,128]{2,1,0:T(8,128)(2,1)}, u32[]{:S(2)}, u32[]{:S(2)}) async-start(bf16[32,88,128]{2,1,0:T(8,128)(2,1)} %shard_map.139), calls=%async_computation.2 | async-start | bytes 1441792 | tf_op jit(solution)/shard_map/all_to_all | solution.py:694
  187.7 0.4 convolution_convert_fusion.3
  188.1 3.4 %collective-permute-start.15 = (bf16[2048,128]{1,0:T(8,128)(2,1)S(1)}, bf16[2048,128]{1,0:T(8,128)(2,1)S(1)}, u32[]{:S(2)}, u32[]{:S(2)}) collective-permute-start(bf16[2048,128]{1,0:T(8,128)(2,1)S(1)} %convolution_convert_fusion.3), channel_id=1, source_target_pairs={{0,1},{1,0},{2,3},{3,2},{4,5},{5,4},{6,7},{7,6},{8,9},{9,8},{10,11... | collective-permute-start | bytes 1572872 | tf_op jit(solution)/shard_map/ppermute | solution.py:545
  191.6 2.3 add_convert_fusion
  193.9 0.4 convolution_convert_fusion
  194.4 1.3 fusion
  195.7 1.2 convolution_convert_fusion.2
  196.9 0.5 collective-permute-start.16
  197.4 2.9 %collective-permute-start.20 = (bf16[2048,128]{1,0:T(8,128)(2,1)}, bf16[2048,128]{1,0:T(8,128)(2,1)}, u32[]{:S(2)}, u32[]{:S(2)}) collective-permute-start(bf16[2048,128]{1,0:T(8,128)(2,1)} %add_convert_fusion), channel_id=1, source_target_pairs={{0,2},{1,3},{2,0},{3,1},{4,6},{5,7},{6,4},{7,5},{8,10},{9,11},{10,... | collective-permute-start | bytes 1572872 | tf_op jit(solution)/shard_map/ppermute | solution.py:545
  200.3 0.4 convert_add_fusion.kept_mid
  200.8 1.8 shard_map.140
  202.6 0.6 copy.17
  203.2 1.5 convert_add_fusion.1.kept_edge
  204.7 8.0 %collective-permute-done.20.mid = bf16[2048,128]{1,0:T(8,128)(2,1)} collective-permute-done((bf16[2048,128]{1,0:T(8,128)(2,1)}, bf16[2048,128]{1,0:T(8,128)(2,1)}, u32[]{:S(2)}, u32[]{:S(2)}) %collective-permute-start.20) | collective-permute-done | bytes 524320 | tf_op jit(solution)/shard_map/ppermute | solution.py:545
  212.6 11.2 %collective-permute-done.17.edge = bf16[2048,128]{1,0:T(8,128)(2,1)} collective-permute-done((bf16[2048,128]{1,0:T(8,128)(2,1)}, bf16[2048,128]{1,0:T(8,128)(2,1)}, u32[]{:S(2)}, u32[]{:S(2)}) %collective-permute-start.17) | collective-permute-done | bytes 524320 | tf_op jit(solution)/shard_map/ppermute | solution.py:545
  223.9 2.4 %shard_map.136 = bf16[4,1024,128]{2,1,0:T(8,128)(2,1)} custom-call(f32[2048,128]{1,0:T(8,128)S(1)} %convert_add_fusion.1.kept_edge, bf16[2048,128]{1,0:T(8,128)(2,1)} %collective-permute-done.17.edge, f32[2048,128]{1,0:T(8,128)S(1)} %convert_add_fusion.kept_mid, bf16[2048,128]{1,0:T(8,128)(2,1)} %collective-permute-done.20.mid), custom_call_target="tpu_custom_call" | custom-call | tf_op jit(solution)/shard_map/pallas_call | solution.py:667
  (105 shorter events, 1.0 us)
Async XLA Ops:
  0.6 30.7 %copy-start.39 = (bf16[2,3,3,128]{3,0,2,1:T(2,128)(2,1)S(1)}, bf16[2,3,3,128]{3,0,2,1:T(2,128)(2,1)}, u32[]{:S(2)}) copy-start(bf16[2,3,3,128]{3,0,2,1:T(2,128)(2,1)} %param.10) | copy-start | bytes 13828
  0.6 30.8 %copy-start.35 = (bf16[1024,128]{1,0:T(8,128)(2,1)S(1)}, bf16[1024,128]{1,0:T(8,128)(2,1)}, u32[]{:S(2)}) copy-start(bf16[1024,128]{1,0:T(8,128)(2,1)} %row_filter.1) | copy-start | bytes 786436
  0.7 30.8 %copy-start.38 = (bf16[128,128]{1,0:T(8,128)(2,1)S(1)}, bf16[128,128]{1,0:T(8,128)(2,1)}, u32[]{:S(2)}) copy-start(bf16[128,128]{1,0:T(8,128)(2,1)} %column_filter.1) | copy-start | bytes 98308
  0.7 30.8 %copy-start.36 = (bf16[512,128]{1,0:T(8,128)(2,1)S(1)}, bf16[512,128]{1,0:T(8,128)(2,1)}, u32[]{:S(2)}) copy-start(bf16[512,128]{1,0:T(8,128)(2,1)} %w_gate.1) | copy-start | bytes 393220
  0.7 30.8 %copy-start.37 = (bf16[512,128]{1,0:T(8,128)(2,1)S(1)}, bf16[512,128]{1,0:T(8,128)(2,1)}, u32[]{:S(2)}) copy-start(bf16[512,128]{1,0:T(8,128)(2,1)} %w_value.1) | copy-start | bytes 393220
  2.6 23.5 %collective-permute-start.9 = (bf16[2048,128]{1,0:T(8,128)(2,1)}, bf16[2048,128]{1,0:T(8,128)(2,1)}, u32[]{:S(2)}, u32[]{:S(2)}) collective-permute-start(bf16[2048,128]{1,0:T(8,128)(2,1)} %bitcast.6.x0), channel_id=1, source_target_pairs={{0,2},{1,3},{2,0},{3,1},{4,6},{5,7},{6,4},{7,5},{8,10},{9,11},{10,... | collective-permute-start | bytes 1572872 | tf_op jit(solution)/shard_map/ppermute | solution.py:545
  7.5 40.0 %copy-start.12 = (bf16[1024,128]{1,0:T(8,128)(2,1)}, bf16[1024,128]{1,0:T(8,128)(2,1)S(1)}, u32[]{:S(2)}) copy-start(bf16[1024,128]{1,0:T(8,128)(2,1)S(1)} %pad_maximum_fusion.1.x0) | copy-start | bytes 786436
  7.5 16.1 %collective-permute-start.5 = (bf16[1024,128]{1,0:T(8,128)(2,1)S(1)}, bf16[1024,128]{1,0:T(8,128)(2,1)S(1)}, u32[]{:S(2)}, u32[]{:S(2)}) collective-permute-start(bf16[1024,128]{1,0:T(8,128)(2,1)S(1)} %pad_maximum_fusion.1.x0), channel_id=1, source_target_pairs={{0,2},{1,3},{2,0},{3,1},{4,6},{5,7},{6,4},{7,5},{8,10},{9,11},{10,... | collective-permute-start | bytes 786440 | tf_op jit(solution)/shard_map/ppermute | solution.py:545
  7.6 39.9 %copy-start.14 = (bf16[1024,128]{1,0:T(8,128)(2,1)}, bf16[1024,128]{1,0:T(8,128)(2,1)S(1)}, u32[]{:S(2)}) copy-start(bf16[1024,128]{1,0:T(8,128)(2,1)S(1)} %pad_maximum_fusion.x0) | copy-start | bytes 786436
  7.6 21.5 %collective-permute-start.1 = (bf16[1024,128]{1,0:T(8,128)(2,1)S(1)}, bf16[1024,128]{1,0:T(8,128)(2,1)S(1)}, u32[]{:S(2)}, u32[]{:S(2)}) collective-permute-start(bf16[1024,128]{1,0:T(8,128)(2,1)S(1)} %pad_maximum_fusion.x0), channel_id=1, source_target_pairs={{0,2},{1,3},{2,0},{3,1},{4,6},{5,7},{6,4},{7,5},{8,10},{9,11},{10,... | collective-permute-start | bytes 786440 | tf_op jit(solution)/shard_map/ppermute | solution.py:545
  10.7 20.0 %collective-permute-start.4 = (bf16[1024,128]{1,0:T(8,128)(2,1)S(1)}, bf16[1024,128]{1,0:T(8,128)(2,1)S(1)}, u32[]{:S(2)}, u32[]{:S(2)}) collective-permute-start(bf16[1024,128]{1,0:T(8,128)(2,1)S(1)} %pad_maximum_fusion.1.x0), channel_id=1, source_target_pairs={{0,1},{1,0},{2,3},{3,2},{4,5},{5,4},{6,7},{7,6},{8,9},{9,8},{10,11... | collective-permute-start | bytes 786440 | tf_op jit(solution)/shard_map/ppermute | solution.py:545
  12.2 40.9 %collective-permute-start.8 = (bf16[2048,128]{1,0:T(8,128)(2,1)}, bf16[2048,128]{1,0:T(8,128)(2,1)}, u32[]{:S(2)}, u32[]{:S(2)}) collective-permute-start(bf16[2048,128]{1,0:T(8,128)(2,1)} %bitcast.6.x0), channel_id=1, source_target_pairs={{0,1},{1,0},{2,3},{3,2},{4,5},{5,4},{6,7},{7,6},{8,9},{9,8},{10,11... | collective-permute-start | bytes 1572872 | tf_op jit(solution)/shard_map/ppermute | solution.py:545
  23.6 24.0 %copy-start.21 = (bf16[1024,128]{1,0:T(8,128)(2,1)}, bf16[1024,128]{1,0:T(8,128)(2,1)S(1)}, u32[]{:S(2)}) copy-start(bf16[1024,128]{1,0:T(8,128)(2,1)S(1)} %collective-permute-done.5.x2) | copy-start | bytes 786436
  23.6 16.4 %collective-permute-start.6 = (bf16[1024,128]{1,0:T(8,128)(2,1)S(1)}, bf16[1024,128]{1,0:T(8,128)(2,1)S(1)}, u32[]{:S(2)}, u32[]{:S(2)}) collective-permute-start(bf16[1024,128]{1,0:T(8,128)(2,1)S(1)} %collective-permute-done.5.x2), channel_id=1, source_target_pairs={{0,1},{1,0},{2,3},{3,2},{4,5},{5,4},{6,7},{7,6},{8,9},{9,8},{10,11... | collective-permute-start | bytes 786440 | tf_op jit(solution)/shard_map/ppermute | solution.py:545
  26.1 31.2 %collective-permute-start.10 = (bf16[2048,128]{1,0:T(8,128)(2,1)}, bf16[2048,128]{1,0:T(8,128)(2,1)}, u32[]{:S(2)}, u32[]{:S(2)}) collective-permute-start(bf16[2048,128]{1,0:T(8,128)(2,1)} %collective-permute-done.9.x2), channel_id=1, source_target_pairs={{0,1},{1,0},{2,3},{3,2},{4,5},{5,4},{6,7},{7,6},{8,9},{9,8},{10,11... | collective-permute-start | bytes 1572872 | tf_op jit(solution)/shard_map/ppermute | solution.py:545
  29.2 13.2 %collective-permute-start = (bf16[1024,128]{1,0:T(8,128)(2,1)S(1)}, bf16[1024,128]{1,0:T(8,128)(2,1)S(1)}, u32[]{:S(2)}, u32[]{:S(2)}) collective-permute-start(bf16[1024,128]{1,0:T(8,128)(2,1)S(1)} %pad_maximum_fusion.x0), channel_id=1, source_target_pairs={{0,1},{1,0},{2,3},{3,2},{4,5},{5,4},{6,7},{7,6},{8,9},{9,8},{10,11... | collective-permute-start | bytes 786440 | tf_op jit(solution)/shard_map/ppermute | solution.py:545
  30.7 16.9 %collective-permute-start.2 = (bf16[1024,128]{1,0:T(8,128)(2,1)S(1)}, bf16[1024,128]{1,0:T(8,128)(2,1)}, u32[]{:S(2)}, u32[]{:S(2)}) collective-permute-start(bf16[1024,128]{1,0:T(8,128)(2,1)S(1)} %collective-permute-done.1.x2), channel_id=1, source_target_pairs={{0,1},{1,0},{2,3},{3,2},{4,5},{5,4},{6,7},{7,6},{8,9},{9,8},{10,11... | collective-permute-start | bytes 786440 | tf_op jit(solution)/shard_map/ppermute | solution.py:545
  30.7 0.7 copy-start.23
  38.7 1.3 copy-start.9
  40.0 7.5 %copy-start.28 = (bf16[1024,128]{1,0:T(8,128)(2,1)}, bf16[1024,128]{1,0:T(8,128)(2,1)S(1)}, u32[]{:S(2)}) copy-start(bf16[1024,128]{1,0:T(8,128)(2,1)S(1)} %collective-permute-done.6.x3) | copy-start | bytes 786436
  40.4 0.7 copy-start.26
  41.1 22.7 %collective-permute-start.12 = (bf16[1,512,256]{2,1,0:T(8,128)(2,1)S(1)}, bf16[1,512,256]{2,1,0:T(8,128)(2,1)S(1)}, u32[]{:S(2)}, u32[]{:S(2)}) collective-permute-start(bf16[1,512,256]{2,1,0:T(8,128)(2,1)S(1)} %get-tuple-element.57.f1), channel_id=1, source_target_pairs={{4,0},{8,4},{12,8},{16,12},{20,16},{24,20},{28,24},{32,28},{36,32}... | collective-permute-start | bytes 786440 | tf_op jit(solution)/shard_map/ppermute | solution.py:549
  42.4 0.7 copy-start.30
  43.1 16.4 %copy-start = (bf16[4,1024,128]{2,1,0:T(8,128)(2,1)S(1)}, bf16[4,1024,128]{2,1,0:T(8,128)(2,1)}, u32[]{:S(2)}) copy-start(bf16[4,1024,128]{2,1,0:T(8,128)(2,1)} %cot.5) | copy-start | bytes 3145732
  43.1 20.7 %collective-permute-start.7 = (bf16[1,512,256]{2,1,0:T(8,128)(2,1)S(1)}, bf16[1,512,256]{2,1,0:T(8,128)(2,1)S(1)}, u32[]{:S(2)}, u32[]{:S(2)}) collective-permute-start(bf16[1,512,256]{2,1,0:T(8,128)(2,1)S(1)} %get-tuple-element.55.l1), channel_id=1, source_target_pairs={{0,4},{4,8},{8,12},{12,16},{16,20},{20,24},{24,28},{28,32},{32,36}... | collective-permute-start | bytes 786440 | tf_op jit(solution)/shard_map/ppermute | solution.py:548
  47.6 1.0 copy-start.15
  48.5 0.9 copy-start.24
  49.5 0.9 copy-start.31
  51.8 12.1 %collective-permute-start.11 = (bf16[1,512,256]{2,1,0:T(8,128)(2,1)S(1)}, bf16[1,512,256]{2,1,0:T(8,128)(2,1)S(1)}, u32[]{:S(2)}, u32[]{:S(2)}) collective-permute-start(bf16[1,512,256]{2,1,0:T(8,128)(2,1)S(1)} %get-tuple-element.56.f0), channel_id=1, source_target_pairs={{4,0},{8,4},{12,8},{16,12},{20,16},{24,20},{28,24},{32,28},{36,32}... | collective-permute-start | bytes 786440 | tf_op jit(solution)/shard_map/ppermute | solution.py:549
  53.1 10.8 %collective-permute-start.3 = (bf16[1,512,256]{2,1,0:T(8,128)(2,1)S(1)}, bf16[1,512,256]{2,1,0:T(8,128)(2,1)S(1)}, u32[]{:S(2)}, u32[]{:S(2)}) collective-permute-start(bf16[1,512,256]{2,1,0:T(8,128)(2,1)S(1)} %get-tuple-element.54.l0), channel_id=1, source_target_pairs={{0,4},{4,8},{8,12},{12,16},{16,20},{20,24},{24,28},{28,32},{32,36}... | collective-permute-start | bytes 786440 | tf_op jit(solution)/shard_map/ppermute | solution.py:548
  63.0 0.8 copy-start.17
  63.8 3.9 %copy-start.1 = (bf16[1,512,256]{2,1,0:T(8,128)(2,1)}, bf16[1,512,256]{2,1,0:T(8,128)(2,1)S(1)}, u32[]{:S(2)}) copy-start(bf16[1,512,256]{2,1,0:T(8,128)(2,1)S(1)} %collective-permute-done.12.d1) | copy-start | bytes 786436
  63.8 3.9 %copy-start.3 = (bf16[1,512,256]{2,1,0:T(8,128)(2,1)}, bf16[1,512,256]{2,1,0:T(8,128)(2,1)S(1)}, u32[]{:S(2)}) copy-start(bf16[1,512,256]{2,1,0:T(8,128)(2,1)S(1)} %collective-permute-done.7.u1) | copy-start | bytes 786436
  63.9 3.8 %copy-start.5 = (bf16[1,512,256]{2,1,0:T(8,128)(2,1)}, bf16[1,512,256]{2,1,0:T(8,128)(2,1)S(1)}, u32[]{:S(2)}) copy-start(bf16[1,512,256]{2,1,0:T(8,128)(2,1)S(1)} %collective-permute-done.11.d0) | copy-start | bytes 786436
  63.9 3.8 %copy-start.7 = (bf16[1,512,256]{2,1,0:T(8,128)(2,1)}, bf16[1,512,256]{2,1,0:T(8,128)(2,1)S(1)}, u32[]{:S(2)}) copy-start(bf16[1,512,256]{2,1,0:T(8,128)(2,1)S(1)} %collective-permute-done.3.u0) | copy-start | bytes 786436
  67.7 41.4 %copy-start.19 = (bf16[2,1024,128]{2,1,0:T(8,128)(2,1)}, bf16[2,1024,128]{2,1,0:T(8,128)(2,1)S(1)}, u32[]{:S(2)}) copy-start(bf16[2,1024,128]{2,1,0:T(8,128)(2,1)S(1)} %get-tuple-element.72.feat_edge) | copy-start | bytes 1572868
  114.1 1.3 copy-start.11
  115.4 0.7 copy-start.33
  116.1 31.6 %all-to-all-start.1 = ((bf16[32,8,32,128]{3,2,1,0:T(8,128)(2,1)}), bf16[32,8,32,128]{3,2,1,0:T(8,128)(2,1)}, u32[]{:S(2)}, u32[]{:S(2)}) async-start(bf16[32,8,32,128]{3,2,1,0:T(8,128)(2,1)} %copy-done.11), calls=%async_computation.1 | async-start | bytes 4194304 | tf_op jit(solution)/shard_map/all_to_all | solution.py:627
  147.7 1.6 copy-start.10
  149.3 1.0 copy-start.18
  150.3 1.0 copy-start.20
  155.4 7.5 %copy-start.2 = (bf16[1,512,256]{2,1,0:T(8,128)(2,1)S(1)}, bf16[1,512,256]{2,1,0:T(8,128)(2,1)}, u32[]{:S(2)}) copy-start(bf16[1,512,256]{2,1,0:T(8,128)(2,1)} %copy-done.1) | copy-start | bytes 786436
  155.4 7.5 %copy-start.4 = (bf16[1,512,256]{2,1,0:T(8,128)(2,1)S(1)}, bf16[1,512,256]{2,1,0:T(8,128)(2,1)}, u32[]{:S(2)}) copy-start(bf16[1,512,256]{2,1,0:T(8,128)(2,1)} %copy-done.3) | copy-start | bytes 786436
  155.4 7.5 %copy-start.6 = (bf16[1,512,256]{2,1,0:T(8,128)(2,1)S(1)}, bf16[1,512,256]{2,1,0:T(8,128)(2,1)}, u32[]{:S(2)}) copy-start(bf16[1,512,256]{2,1,0:T(8,128)(2,1)} %copy-done.5) | copy-start | bytes 786436
  155.5 7.5 %copy-start.8 = (bf16[1,512,256]{2,1,0:T(8,128)(2,1)S(1)}, bf16[1,512,256]{2,1,0:T(8,128)(2,1)}, u32[]{:S(2)}) copy-start(bf16[1,512,256]{2,1,0:T(8,128)(2,1)} %copy-done.7) | copy-start | bytes 786436
  155.5 17.7 %collective-permute-start.13 = (bf16[1,1024,256]{2,1,0:T(8,128)(2,1)S(1)}, bf16[1,1024,256]{2,1,0:T(8,128)(2,1)S(1)}, u32[]{:S(2)}, u32[]{:S(2)}) collective-permute-start(bf16[1,1024,256]{2,1,0:T(8,128)(2,1)S(1)} %get-tuple-element.75.glast), channel_id=1, source_target_pairs={{0,4},{4,8},{8,12},{12,16},{16,20},{20,24},{24,28},{28,32},{32,36}... | collective-permute-start | bytes 1572872 | tf_op jit(solution)/shard_map/ppermute | solution.py:548
  159.4 13.7 %collective-permute-start.14 = (bf16[1,1024,256]{2,1,0:T(8,128)(2,1)S(1)}, bf16[1,1024,256]{2,1,0:T(8,128)(2,1)S(1)}, u32[]{:S(2)}, u32[]{:S(2)}) collective-permute-start(bf16[1,1024,256]{2,1,0:T(8,128)(2,1)S(1)} %get-tuple-element.76.gfirst), channel_id=1, source_target_pairs={{4,0},{8,4},{12,8},{16,12},{20,16},{24,20},{28,24},{32,28},{36,32}... | collective-permute-start | bytes 1572872 | tf_op jit(solution)/shard_map/ppermute | solution.py:549
  170.6 4.9 %copy-start.13 = (bf16[1024,128]{1,0:T(8,128)(2,1)S(1)}, bf16[1024,128]{1,0:T(8,128)(2,1)}, u32[]{:S(2)}) copy-start(bf16[1024,128]{1,0:T(8,128)(2,1)} %copy-done.12) | copy-start | bytes 786436
  170.6 4.9 %copy-start.16 = (bf16[1024,128]{1,0:T(8,128)(2,1)S(1)}, bf16[1024,128]{1,0:T(8,128)(2,1)}, u32[]{:S(2)}) copy-start(bf16[1024,128]{1,0:T(8,128)(2,1)} %copy-done.14) | copy-start | bytes 786436
  170.6 4.9 %copy-start.22 = (bf16[1024,128]{1,0:T(8,128)(2,1)S(1)}, bf16[1024,128]{1,0:T(8,128)(2,1)}, u32[]{:S(2)}) copy-start(bf16[1024,128]{1,0:T(8,128)(2,1)} %copy-done.21) | copy-start | bytes 786436
  170.6 4.9 %copy-start.25 = (bf16[1024,128]{1,0:T(8,128)(2,1)S(1)}, bf16[1024,128]{1,0:T(8,128)(2,1)}, u32[]{:S(2)}) copy-start(bf16[1024,128]{1,0:T(8,128)(2,1)} %copy-done.23) | copy-start | bytes 786436
  170.6 4.9 %copy-start.27 = (bf16[1024,128]{1,0:T(8,128)(2,1)S(1)}, bf16[1024,128]{1,0:T(8,128)(2,1)}, u32[]{:S(2)}) copy-start(bf16[1024,128]{1,0:T(8,128)(2,1)} %copy-done.26) | copy-start | bytes 786436
  170.6 4.9 %copy-start.29 = (bf16[1024,128]{1,0:T(8,128)(2,1)S(1)}, bf16[1024,128]{1,0:T(8,128)(2,1)}, u32[]{:S(2)}) copy-start(bf16[1024,128]{1,0:T(8,128)(2,1)} %copy-done.28) | copy-start | bytes 786436
  170.6 4.9 %copy-start.32 = (bf16[1024,128]{1,0:T(8,128)(2,1)S(1)}, bf16[1024,128]{1,0:T(8,128)(2,1)}, u32[]{:S(2)}) copy-start(bf16[1024,128]{1,0:T(8,128)(2,1)} %copy-done.30) | copy-start | bytes 786436
  170.6 21.0 %collective-permute-start.18 = (bf16[2048,128]{1,0:T(8,128)(2,1)}, bf16[2048,128]{1,0:T(8,128)(2,1)}, u32[]{:S(2)}, u32[]{:S(2)}) collective-permute-start(bf16[2048,128]{1,0:T(8,128)(2,1)} %convolution_convert_fusion.1), channel_id=1, source_target_pairs={{0,1},{1,0},{2,3},{3,2},{4,5},{5,4},{6,7},{7,6},{8,9},{9,8},{10,11... | collective-permute-start | bytes 1572872 | tf_op jit(solution)/shard_map/ppermute | solution.py:545
  175.5 1.8 copy-start.34
  178.2 22.5 %all-to-all-start.2 = ((bf16[32,88,128]{2,1,0:T(8,128)(2,1)}), bf16[32,88,128]{2,1,0:T(8,128)(2,1)}, u32[]{:S(2)}, u32[]{:S(2)}) async-start(bf16[32,88,128]{2,1,0:T(8,128)(2,1)} %shard_map.139), calls=%async_computation.2 | async-start | bytes 1441792 | tf_op jit(solution)/shard_map/all_to_all | solution.py:694
  188.1 6.3 %collective-permute-start.15 = (bf16[2048,128]{1,0:T(8,128)(2,1)S(1)}, bf16[2048,128]{1,0:T(8,128)(2,1)S(1)}, u32[]{:S(2)}, u32[]{:S(2)}) collective-permute-start(bf16[2048,128]{1,0:T(8,128)(2,1)S(1)} %convolution_convert_fusion.3), channel_id=1, source_target_pairs={{0,1},{1,0},{2,3},{3,2},{4,5},{5,4},{6,7},{7,6},{8,9},{9,8},{10,11... | collective-permute-start | bytes 1572872 | tf_op jit(solution)/shard_map/ppermute | solution.py:545
  194.3 6.0 %collective-permute-start.19 = (bf16[2048,128]{1,0:T(8,128)(2,1)S(1)}, bf16[2048,128]{1,0:T(8,128)(2,1)S(1)}, u32[]{:S(2)}, u32[]{:S(2)}) collective-permute-start(bf16[2048,128]{1,0:T(8,128)(2,1)S(1)} %convolution_convert_fusion), channel_id=1, source_target_pairs={{0,1},{1,0},{2,3},{3,2},{4,5},{5,4},{6,7},{7,6},{8,9},{9,8},{10,11... | collective-permute-start | bytes 1572872 | tf_op jit(solution)/shard_map/ppermute | solution.py:545
  196.9 6.3 %collective-permute-start.16 = (bf16[2048,128]{1,0:T(8,128)(2,1)}, bf16[2048,128]{1,0:T(8,128)(2,1)}, u32[]{:S(2)}, u32[]{:S(2)}) collective-permute-start(bf16[2048,128]{1,0:T(8,128)(2,1)} %convolution_convert_fusion.2), channel_id=1, source_target_pairs={{0,1},{1,0},{2,3},{3,2},{4,5},{5,4},{6,7},{7,6},{8,9},{9,8},{10,11... | collective-permute-start | bytes 1572872 | tf_op jit(solution)/shard_map/ppermute | solution.py:545
  197.4 15.3 %collective-permute-start.20 = (bf16[2048,128]{1,0:T(8,128)(2,1)}, bf16[2048,128]{1,0:T(8,128)(2,1)}, u32[]{:S(2)}, u32[]{:S(2)}) collective-permute-start(bf16[2048,128]{1,0:T(8,128)(2,1)} %add_convert_fusion), channel_id=1, source_target_pairs={{0,2},{1,3},{2,0},{3,1},{4,6},{5,7},{6,4},{7,5},{8,10},{9,11},{10,... | collective-permute-start | bytes 1572872 | tf_op jit(solution)/shard_map/ppermute | solution.py:545
  200.2 23.6 %collective-permute-start.17 = (bf16[2048,128]{1,0:T(8,128)(2,1)}, bf16[2048,128]{1,0:T(8,128)(2,1)}, u32[]{:S(2)}, u32[]{:S(2)}) collective-permute-start(bf16[2048,128]{1,0:T(8,128)(2,1)} %fusion), channel_id=1, source_target_pairs={{0,2},{1,3},{2,0},{3,1},{4,6},{5,7},{6,4},{7,5},{8,10},{9,11},{10,... | collective-permute-start | bytes 1572872 | tf_op jit(solution)/shard_map/ppermute | solution.py:545

commit v4 on v2

--- a/solution.py
+++ b/solution.py
@@ -429,15 +429,32 @@
     spread_back(gframed, kern, [(back, 0, 1), (back, 1, 4)], width, channels)
 
 
-def finish_kernel(kept_edge, edge, kept_mid, mid, grad):
+def share_kernel(back, w, beside, out):
+    part = lax.dot_general(
+        back[...], w[...], (((1,), (1,)), ((), ())), preferred_element_type=F32
+    )
+    out[...] = (part + beside[...].astype(F32)).astype(BF)
+
+
+def finish_mid_kernel(kept, across, grad, rows, sem):
+    inner = grad.shape[0] - 2
+    rows[...] = (kept[...] + across[...].astype(F32)).astype(BF).reshape(rows.shape)
+    copy = pltpu.make_async_copy(rows, grad.at[pl.ds(1, inner)], sem)
+    copy.start()
+    copy.wait()
+
+
+def finish_edge_kernel(kept, across, middle, grad, rows, sems):
     width = grad.shape[1]
-    inner = grad.shape[0] - 2
-    for r in range(inner):
-        at = pl.ds(r * width, width)
-        grad[r + 1] = (kept_mid[at, :] + mid[at, :].astype(F32)).astype(BF)
+    copies = []
     for r in range(2):
         at = pl.ds(r * width, width)
-        grad[r * (inner + 1)] = (kept_edge[at, :] + edge[at, :].astype(F32)).astype(BF)
+        rows[r] = (kept[at, :] + across[at, :].astype(F32)).astype(BF)
+        to = r * (grad.shape[0] - 1)
+        copies.append(pltpu.make_async_copy(rows.at[r], grad.at[to], sems.at[r]))
+        copies[r].start()
+    for copy in copies:
+        copy.wait()
 
 
 def sum_kernel(parts, *outs, scale):
@@ -446,12 +463,17 @@
         total = total + parts[n].astype(F32)
     total = total * scale
     at = 0
-    for out in outs:
+    for out in outs[:-1]:
         out[...] = total[at : at + out.shape[0]]
         at += out.shape[0]
-
-
-def pack_kernel(ch, grad_w, row_part, small, packed):
+    short = outs[-1]
+    for b in range(2):
+        for k in range(9):
+            row = at + 9 * b + k
+            short[k // 3, k % 3, pl.ds(b, 1), :] = total[row : row + 1]
+
+
+def pack_kernel(ch, grad_w, row_part, small, out, packed, sem):
     owners, _, channels = packed.shape
     parts = 4
     size = grad_w.shape[0] // parts
@@ -463,21 +485,31 @@
             v = grad_w[pl.ds(k * size, size), pl.ds(branch * channels, channels)].astype(BF)
             packed[at, pl.ds(branch * deep, deep), :] = v.reshape(each, deep, channels)
     per_owner = row_part.shape[0] // owners
-    packed[:, pl.ds(2 * deep, per_owner), :] = (
-        row_part[...].reshape(owners, per_owner, channels)
-    )
+    packed[:, pl.ds(2 * deep, per_owner), :] = row_part[...].reshape(owners, per_owner, channels)
     packed[:, pl.ds(2 * deep + per_owner, small.shape[1]), :] = small[...]
-
-
-def kernel_call(body, outs, scratch, limit, scalars=0, operands=0):
+    copy = pltpu.make_async_copy(packed, out, sem)
+    copy.start()
+    copy.wait()
+
+
+def kernel_call(
+    body, outs, scratch, limit, scalars=0, operands=0, free=False, alias=None, sems=None
+):
     specs = {}
-    if scalars:
+    if scalars or alias is not None:
         whole = [pl.BlockSpec(memory_space=pltpu.SMEM)] * scalars
-        specs["in_specs"] = whole + [pl.BlockSpec(memory_space=pltpu.VMEM)] * operands
+        whole += [pl.BlockSpec(memory_space=pltpu.VMEM)] * operands
+        if alias is not None:
+            whole += [pl.BlockSpec(memory_space=pltpu.HBM)]
+            specs["input_output_aliases"] = {alias: 0}
+        specs["in_specs"] = whole
+    if free:
+        specs["out_specs"] = [pl.BlockSpec(memory_space=pltpu.HBM)] * len(outs)
+    semaphores = [] if sems is None else [pltpu.SemaphoreType.DMA(sems)]
     return pl.pallas_call(
         body,
         out_shape=[jax.ShapeDtypeStruct(s, d) for s, d in outs],
-        scratch_shapes=[pltpu.VMEM(s, d) for s, d in scratch],
+        scratch_shapes=[pltpu.VMEM(s, d) for s, d in scratch] + semaphores,
         compiler_params=pltpu.CompilerParams(vmem_limit_bytes=limit << 20),
         **specs,
     )
@@ -590,7 +622,9 @@
             return lax.dot_general(back, w_blocks[k], contract, preferred_element_type=F32)
 
         beside = flipped(share(3).astype(BF), 1)
-        theirs = (share(2) + beside.astype(F32)).astype(BF)
+        theirs = kernel_call(share_kernel, [(beside.shape, BF)], [], 10)(
+            back, w_blocks[2], beside
+        )[0]
         across = flipped(theirs, 2)
         back, _ = lax.optimization_barrier((back, theirs))
         kept = share(0) + flipped(share(1).astype(BF), 1).astype(F32)
@@ -600,9 +634,14 @@
     back_edge = back_edge.reshape(2 * width, 2 * channels)
     kept_mid, across_mid = collected(back_mid)
     kept_edge, across_edge = collected(back_edge)
-    input_grad = kernel_call(finish_kernel, [tile], [], 12)(
-        kept_edge, across_edge, kept_mid, across_mid
-    )[0]
+    begun = kernel_call(
+        finish_mid_kernel, [tile], [((inner, width, channels), BF)], 10,
+        free=True, sems=(),
+    )(kept_mid, across_mid)[0]
+    input_grad = kernel_call(
+        finish_edge_kernel, [tile], [((2, width, channels), BF)], 10,
+        operands=2, free=True, alias=2, sems=(2,),
+    )(kept_edge, across_edge, begun)[0]
 
     grad_w = lax.dot_general(gathered_mid, back_mid, over_tokens, preferred_element_type=F32)
     grad_w = lax.optimization_barrier(grad_w)
@@ -622,20 +661,22 @@
     packed = kernel_call(
         pack_kernel,
         [((owners, 2 * deep + per_owner + small.shape[1], channels), BF)],
-        [],
+        [((owners, 2 * deep + per_owner + small.shape[1], channels), BF)],
         16,
         scalars=1,
         operands=3,
+        free=True,
+        sems=(),
     )(ch.reshape(1), grad_w, row_part, small)[0]
     total = lax.all_to_all(packed, "grid", split_axis=0, concat_axis=0, tiled=True)
-    sizes = (deep, deep, per_owner, height // owners, 18)
+    sizes = (deep, deep, per_owner, height // owners)
     gate_grad, value_grad, row_share, col_share, short_sum = kernel_call(
         functools.partial(sum_kernel, scale=scale),
-        [((size, channels), F32) for size in sizes],
+        [((size, channels), F32) for size in sizes] + [((3, 3, 2, channels), F32)],
         [],
         12,
     )(total)
-    short_grad = short_sum.reshape(2, 3, 3, channels)
+    short_grad = short_sum.transpose(2, 0, 1, 3)
     return (gated, input_grad, gate_grad, value_grad, short_grad, row_share, col_share)
 
 

time: 208 us -> 201 us (0.966)
  waiting for transfers between devices: 67.2 us -> 58.9 us
  Pallas kernels: 36.4 us -> 39.8 us
    ppermute x12, waiting for transfers between devices: 29.5 us -> 19.6 us  [flipped(): return lax.ppermute(value, 'ch', [(i, i ^ bit) for i in range(parts)])]
    pallas_call x1 -> x4, Pallas kernels: 2.34 us -> 7.39 us  [the longest x2 3.51 us: collected(): kernel_call(share_kernel, [(beside.shape, BF)], [], 10)]
    dot_general x8 -> x6, matrix products: 8.75 us -> 7.06 us  [share(): lax.dot_general(back, w_blocks[k], contract, preferred_element_type=F32)]
    unnamed x78 -> x79, local copies, waits for them, and re-layouts: 9.55 us -> 9.81 us
  transfers between devices with their start and end apart: 18 -> 18, of which waited for: 6 -> 6; matrix products, arithmetic and copies ran while one was open for 6% -> 5% of each run, Pallas kernels for 10% -> 12%
where the time goes in v4:
time: 201 us; the launch traced here: 200 us
  waiting for transfers between devices  58.9 us (29%)
  starting transfers between devices  42.3 us (21%)
  Pallas kernels  39.8 us (20%)
  blocking collectives  35.9 us (18%)
  local copies, waits for them, and re-layouts  11.1 us (6%)
  matrix products  9.59 us (5%)
    all_to_all x1, blocking collectives, local(): recv = lax.all_to_all(send, 'grid', split_axis=0, concat_axis=0, tiled=True)  35.9 us
    all_to_all x1, waiting for transfers between devices, local(): lax.all_to_all(turned, 'grid', split_axis=0, concat_axis=0, tiled=True)  25.8 us
    ppermute x12, waiting for transfers between devices, flipped(): return lax.ppermute(value, 'ch', [(i, i ^ bit) for i in range(parts)])  19.6 us
    ppermute x12, starting transfers between devices, flipped(): return lax.ppermute(value, 'ch', [(i, i ^ bit) for i in range(parts)])  18.1 us
    unnamed x79, local copies, waits for them, and re-layouts  9.81 us
    all_to_all x1, starting transfers between devices, local(): lax.all_to_all(packed, 'grid', split_axis=0, concat_axis=0, tiled=True)  9.03 us
    ppermute x2, waiting for transfers between devices, halos(): up = lax.ppermute(last, 'grid', [(i, i + 1) for i in range(owners - 1)])  7.73 us
    pallas_call x1, Pallas kernels, local(): kernel_call(tables_kernel, [((width, width), BF), ((width, width), BF), (...  7.18 us
  transfers between devices with their start and end apart: 18, of which 6 were waited for; matrix products, arithmetic and copies ran while one was open for 5% of the time, Pallas kernels for 12%

profile of v4, /device:TPU:1, one launch (start us, length us, event | category | flops | bytes accessed | tf_op | source)
XLA Modules:
  0.0 200.0 jit_solution(16610692427883049122)
XLA Ops:
  0.7 1.2 slice_bitcast_fusion.1
  1.9 3.8 %collective-permute-start.1 = (bf16[2048,128]{1,0:T(8,128)(2,1)S(1)}, bf16[2048,128]{1,0:T(8,128)(2,1)S(1)}, u32[]{:S(2)}, u32[]{:S(2)}) collective-permute-start(bf16[2048,128]{1,0:T(8,128)(2,1)S(1)} %pad_maximum_fusion.x0), channel_id=1, source_target_pairs={{0,2},{1,3},{2,0},{3,1},{4,6},{5,7},{6,4},{7,5},{8,10},{9,11},{10,... | collective-permute-start | bytes 1572872 | tf_op jit(solution)/shard_map/ppermute | solution.py:531
  5.7 0.1 collective-permute-start.5
  5.9 1.1 collective-permute-start
  7.0 10.1 %collective-permute-done.1.x2 = bf16[2048,128]{1,0:T(8,128)(2,1)S(1)} collective-permute-done((bf16[2048,128]{1,0:T(8,128)(2,1)S(1)}, bf16[2048,128]{1,0:T(8,128)(2,1)S(1)}, u32[]{:S(2)}, u32[]{:S(2)}) %collective-permute-start.1) | collective-permute-done | bytes 524320 | tf_op jit(solution)/shard_map/ppermute | solution.py:531
  17.1 2.5 %collective-permute-start.2 = (bf16[2048,128]{1,0:T(8,128)(2,1)S(1)}, bf16[2048,128]{1,0:T(8,128)(2,1)S(1)}, u32[]{:S(2)}, u32[]{:S(2)}) collective-permute-start(bf16[2048,128]{1,0:T(8,128)(2,1)S(1)} %collective-permute-done.1.x2), channel_id=1, source_target_pairs={{0,1},{1,0},{2,3},{3,2},{4,5},{5,4},{6,7},{7,6},{8,9},{9,8},{10,11... | collective-permute-start | bytes 1572872 | tf_op jit(solution)/shard_map/ppermute | solution.py:531
  19.7 0.1 pad_add_fusion.where
  19.7 0.9 copy-done.32
  20.7 0.9 copy-done.34
  21.6 0.8 copy-done.35
  22.3 7.2 %shard_map.126 = (bf16[1024,1024]{1,0:T(8,128)(2,1)S(1)}, bf16[1024,1024]{1,0:T(8,128)(2,1)S(1)}, bf16[32,1024]{1,0:T(8,128)(2,1)S(1)}, bf16[256,256]{1,0:T(8,12...) custom-call(s32[2]{0:T(128)S(1)} %pad_add_fusion.where, ...), custom_call_target="tpu_custom_call" | custom-call | tf_op jit(solution)/shard_map/pallas_call | solution.py:546
  29.5 0.6 collective-permute-start.6
  30.1 0.7 shard_map.127
  30.9 3.8 %collective-permute-start.3 = (bf16[1,1024,256]{2,1,0:T(8,128)(2,1)S(1)}, bf16[1,1024,256]{2,1,0:T(8,128)(2,1)S(1)}, u32[]{:S(2)}, u32[]{:S(2)}) collective-permute-start(bf16[1,1024,256]{2,1,0:T(8,128)(2,1)S(1)} %get-tuple-element.46.last), channel_id=1, source_target_pairs={{0,4},{4,8},{8,12},{12,16},{16,20},{20,24},{24,28},{28,32},{32,36}... | collective-permute-start | bytes 1572872 | tf_op jit(solution)/shard_map/ppermute | solution.py:534
  34.7 1.3 collective-permute-start.7
  36.1 1.9 shard_map.128.middle
  38.1 7.7 %collective-permute-done.3.up = bf16[1,1024,256]{2,1,0:T(8,128)(2,1)S(1)} collective-permute-done((bf16[1,1024,256]{2,1,0:T(8,128)(2,1)S(1)}, bf16[1,1024,256]{2,1,0:T(8,128)(2,1)S(1)}, u32[]{:S(2)}, u32[]{:S(2)}) %collective-permute-start.3) | collective-permute-done | bytes 524320 | tf_op jit(solution)/shard_map/ppermute | solution.py:534
  45.8 4.2 %collective-permute-done.7.down = bf16[1,1024,256]{2,1,0:T(8,128)(2,1)S(1)} collective-permute-done((bf16[1,1024,256]{2,1,0:T(8,128)(2,1)S(1)}, bf16[1,1024,256]{2,1,0:T(8,128)(2,1)S(1)}, u32[]{:S(2)}, u32[]{:S(2)}) %collective-permute-start.7) | collective-permute-done | bytes 524320 | tf_op jit(solution)/shard_map/ppermute | solution.py:535
  50.0 6.0 %shard_map.129 = (bf16[32,8,32,128]{3,2,1,0:T(8,128)(2,1)S(1)}, bf16[4,1024,128]{2,1,0:T(8,128)(2,1)S(1)}) custom-call(bf16[1,1024,256]{2,1,0:T(8,128)(2,1)S(1)} %collective-permute-done.3.up, bf16[1,1024,256]{2,1,0:T(8,128)(2,1)S(1)} %get-tuple-element.47.first, bf16[2,1024,256]{2,1,0:T(8,128)(2,1)S(1)} %shard_map.128.middle, ...), custom_call_target="tpu_custom_call" | custom-call | tf_op jit(solution)/shard_map/pallas_call | solution.py:585
  56.0 35.9 %all_to_all.15.recv = bf16[32,8,32,128]{3,2,1,0:T(8,128)(2,1)S(1)} all-to-all(bf16[32,8,32,128]{3,2,1,0:T(8,128)(2,1)S(1)} %get-tuple-element.51), channel_id=1, replica_groups=mesh['grid'=32,'ch'=4] {'grid'}, dimensions={0} | all-to-all | bytes 4194304 | tf_op jit(solution)/shard_map/all_to_all | solution.py:588
  91.9 5.0 %shard_map.130 = (bf16[32,8,32,128]{3,2,1,0:T(8,128)(2,1)S(1)}, bf16[1024,128]{1,0:T(8,128)(2,1)S(1)}, f32[128,128]{1,0:T(8,128)S(1)}) custom-call(bf16[32,8,32,128]{3,2,1,0:T(8,128)(2,1)S(1)} %all_to_all.15.recv, f32[4,16,128]{2,1,0:T(8,128)S(1)} %get-tuple-element.52.coef, f32[1,16,128]{2,1,0:T(8,128)S(1)} %get-tuple-element.53.keep, ...), custom_call_target="tpu_custom_call" | custom-call | tf_op jit(solution)/shard_map/pallas_call | solution.py:590
  96.9 1.4 copy-done.13
  98.3 0.7 copy-done.30
  99.0 5.4 %all-to-all-start.1 = ((bf16[32,8,32,128]{3,2,1,0:T(8,128)(2,1)}), bf16[32,8,32,128]{3,2,1,0:T(8,128)(2,1)S(1)}, u32[]{:S(2)}, u32[]{:S(2)}) async-start(bf16[32,8,32,128]{3,2,1,0:T(8,128)(2,1)} %copy-done.13), calls=%async_computation.1 | async-start | bytes 4194304 | tf_op jit(solution)/shard_map/all_to_all | solution.py:596
  104.4 0.1 pad.3.clone
  104.5 0.6 convert_element_type.33
  105.1 25.8 %all-to-all-done.1.recv = bf16[32,8,32,128]{3,2,1,0:T(8,128)(2,1)S(1)} async-done(((bf16[32,8,32,128]{3,2,1,0:T(8,128)(2,1)}), bf16[32,8,32,128]{3,2,1,0:T(8,128)(2,1)S(1)}, u32[]{:S(2)}, u32[]{:S(2)}) %all-to-all-start.1) | async-done | bytes 2097184 | tf_op jit(solution)/shard_map/all_to_all | solution.py:596
  130.9 1.2 copy-done.9
  132.1 1.6 copy-done.12
  133.7 1.2 copy-done.19
  134.9 2.5 %shard_map.131 = (bf16[4,1024,128]{2,1,0:T(8,128)(2,1)}, bf16[1,1024,256]{2,1,0:T(8,128)(2,1)S(1)}, bf16[2,1024,256]{2,1,0:T(8,128)(2,1)S(1)}, bf16[1,1024,256]{2,1,0:T(8,128)(2,1)S(1)}) custom-call(bf16[32,8,32,128]{3,2,1,0:T(8,128)(2,1)S(1)} %all-to-all-done.1.recv, bf16[1024,1024]{1,0:T(8,128)(2,1)S(1)} %copy-done.12, ...), custom_call_target="tpu_custom_call" | custom-call | tf_op jit(solution)/shard_map/pallas_call | solution.py:597
  137.4 3.3 %collective-permute-start.8 = (bf16[1,1024,256]{2,1,0:T(8,128)(2,1)S(1)}, bf16[1,1024,256]{2,1,0:T(8,128)(2,1)S(1)}, u32[]{:S(2)}, u32[]{:S(2)}) collective-permute-start(bf16[1,1024,256]{2,1,0:T(8,128)(2,1)S(1)} %get-tuple-element.63.glast), channel_id=1, source_target_pairs={{0,4},{4,8},{8,12},{12,16},{16,20},{20,24},{24,28},{28,32},{32,36}... | collective-permute-start | bytes 1572872 | tf_op jit(solution)/shard_map/ppermute | solution.py:534
  140.7 1.3 collective-permute-start.9
  142.0 2.0 %shard_map.134 = bf16[2,1024,256]{2,1,0:T(8,128)(2,1)S(1)} custom-call(bf16[1,1024,256]{2,1,0:T(8,128)(2,1)S(1)} %get-tuple-element.64.gfirst, bf16[2,1024,256]{2,1,0:T(8,128)(2,1)S(1)} %get-tuple-element.65.gmiddle, bf16[1,1024,256]{2,1,0:T(8,128)(2,1)S(1)} %get-tuple-element.63.glast, f32[18,128]{1,0:T(8,128)S(1)} %get-tuple-element.49.kern), custom_call_target="tpu_custom_call" | custom-call | tf_op jit(solution)/shard_map/pallas_call | solution.py:601
  144.1 1.9 shard_map.138
  146.0 1.9 shard_map.139
  148.0 0.4 convolution_convert_fusion.1
  148.4 2.6 %collective-permute-start.13 = (bf16[2048,128]{1,0:T(8,128)(2,1)S(1)}, bf16[2048,128]{1,0:T(8,128)(2,1)S(1)}, u32[]{:S(2)}, u32[]{:S(2)}) collective-permute-start(bf16[2048,128]{1,0:T(8,128)(2,1)S(1)} %convolution_convert_fusion.1), channel_id=1, source_target_pairs={{0,1},{1,0},{2,3},{3,2},{4,5},{5,4},{6,7},{7,6},{8,9},{9,8},{10,11... | collective-permute-start | bytes 1572872 | tf_op jit(solution)/shard_map/ppermute | solution.py:531
  151.0 0.2 maximum_maximum_fusion.small
  151.2 1.8 fusion
  153.0 1.2 shard_map.135
  154.3 3.0 %collective-permute-start.15 = (bf16[2048,128]{1,0:T(8,128)(2,1)}, bf16[2048,128]{1,0:T(8,128)(2,1)}, u32[]{:S(2)}, u32[]{:S(2)}) collective-permute-start(bf16[2048,128]{1,0:T(8,128)(2,1)} %shard_map.135), channel_id=1, source_target_pairs={{0,2},{1,3},{2,0},{3,1},{4,6},{5,7},{6,4},{7,5},{8,10},{9,11},{10,... | collective-permute-start | bytes 1572872 | tf_op jit(solution)/shard_map/ppermute | solution.py:531
  157.3 2.2 %shard_map.132 = bf16[2,1024,256]{2,1,0:T(8,128)(2,1)S(1)} custom-call(bf16[1,1024,256]{2,1,0:T(8,128)(2,1)S(1)} %collective-permute-done.8.gup, bf16[1,1024,256]{2,1,0:T(8,128)(2,1)S(1)} %get-tuple-element.64.gfirst, bf16[2,1024,256]{2,1,0:T(8,128)(2,1)S(1)} %get-tuple-element.65.gmiddle, bf16[1,1024,256]{2,1,0:T(8,128)(2,1)S(1)} %get-tuple-element.63.glast, ...), custom_call_target="tpu_custom_call" | custom-call | tf_op jit(solution)/shard_map/pallas_call | solution.py:613
  159.6 1.2 convolution_convert_fusion.3
  160.8 0.7 collective-permute-start.10
  161.5 1.2 convolution_convert_fusion
  162.7 0.0 collective-permute-start.14
  162.7 0.7 fusion.8
  163.5 0.1 add.11.grad_w
  163.6 0.1 copy-done.31
  163.6 0.4 shard_map.140
  164.0 0.9 copy-done.10
  164.9 9.0 %all-to-all-start.2 = ((bf16[32,88,128]{2,1,0:T(8,128)(2,1)}), bf16[32,88,128]{2,1,0:T(8,128)(2,1)S(1)}, u32[]{:S(2)}, u32[]{:S(2)}) async-start(bf16[32,88,128]{2,1,0:T(8,128)(2,1)} %copy-done.10), calls=%async_computation.2 | async-start | bytes 1441792 | tf_op jit(solution)/shard_map/all_to_all | solution.py:671
  174.0 2.3 %shard_map.133 = bf16[2048,128]{1,0:T(8,128)(2,1)} custom-call(bf16[2048,256]{1,0:T(8,128)(2,1)S(1)} %bitcast.21, bf16[128,256]{1,0:T(8,128)(2,1)S(1)} %slice.24.w, bf16[2048,128]{1,0:T(8,128)(2,1)} %collective-permute-done.10.beside), custom_call_target="tpu_custom_call" | custom-call | tf_op jit(solution)/shard_map/pallas_call | solution.py:625
  176.2 1.2 convolution_convert_fusion.2
  177.5 0.7 collective-permute-start.11
  178.2 3.0 %collective-permute-start.12 = (bf16[2048,128]{1,0:T(8,128)(2,1)}, bf16[2048,128]{1,0:T(8,128)(2,1)}, u32[]{:S(2)}, u32[]{:S(2)}) collective-permute-start(bf16[2048,128]{1,0:T(8,128)(2,1)} %shard_map.133), channel_id=1, source_target_pairs={{0,2},{1,3},{2,0},{3,1},{4,6},{5,7},{6,4},{7,5},{8,10},{9,11},{10,... | collective-permute-start | bytes 1572872 | tf_op jit(solution)/shard_map/ppermute | solution.py:531
  181.1 1.5 convolution_add_fusion.kept
  182.6 2.0 shard_map.136.middle
  184.6 1.6 all-to-all-done.2.parts
  186.2 0.7 shard_map.141
  186.9 1.5 convolution_add_fusion.1.kept
  188.4 9.5 %collective-permute-done.12.across = bf16[2048,128]{1,0:T(8,128)(2,1)} collective-permute-done((bf16[2048,128]{1,0:T(8,128)(2,1)}, bf16[2048,128]{1,0:T(8,128)(2,1)}, u32[]{:S(2)}, u32[]{:S(2)}) %collective-permute-start.12) | collective-permute-done | bytes 524320 | tf_op jit(solution)/shard_map/ppermute | solution.py:531
  197.9 1.9 shard_map.137
  (90 shorter events, 0.3 us)
Async XLA Ops:
  0.6 5.1 %copy-start.36 = (bf16[4,1024,128]{2,1,0:T(8,128)(2,1)S(1)}, bf16[4,1024,128]{2,1,0:T(8,128)(2,1)}, u32[]{:S(2)}) copy-start(bf16[4,1024,128]{2,1,0:T(8,128)(2,1)} %param.7) | copy-start | bytes 3145732
  0.6 19.0 %copy-start.38 = (bf16[2,3,3,128]{3,0,2,1:T(2,128)(2,1)S(1)}, bf16[2,3,3,128]{3,0,2,1:T(2,128)(2,1)}, u32[]{:S(2)}) copy-start(bf16[2,3,3,128]{3,0,2,1:T(2,128)(2,1)} %param.10) | copy-start | bytes 13828
  0.7 19.1 %copy-start.33 = (bf16[512,128]{1,0:T(8,128)(2,1)S(1)}, bf16[512,128]{1,0:T(8,128)(2,1)}, u32[]{:S(2)}) copy-start(bf16[512,128]{1,0:T(8,128)(2,1)} %w_gate.1) | copy-start | bytes 393220
  1.9 34.2 %copy-start.14 = (bf16[2048,128]{1,0:T(8,128)(2,1)}, bf16[2048,128]{1,0:T(8,128)(2,1)S(1)}, u32[]{:S(2)}) copy-start(bf16[2048,128]{1,0:T(8,128)(2,1)S(1)} %pad_maximum_fusion.x0) | copy-start | bytes 1572868
  1.9 15.2 %collective-permute-start.1 = (bf16[2048,128]{1,0:T(8,128)(2,1)S(1)}, bf16[2048,128]{1,0:T(8,128)(2,1)S(1)}, u32[]{:S(2)}, u32[]{:S(2)}) collective-permute-start(bf16[2048,128]{1,0:T(8,128)(2,1)S(1)} %pad_maximum_fusion.x0), channel_id=1, source_target_pairs={{0,2},{1,3},{2,0},{3,1},{4,6},{5,7},{6,4},{7,5},{8,10},{9,11},{10,... | collective-permute-start | bytes 1572872 | tf_op jit(solution)/shard_map/ppermute | solution.py:531
  5.7 32.3 %copy-start.16 = (bf16[2,1024,128]{2,1,0:T(8,128)(2,1)}, bf16[2,1024,128]{2,1,0:T(8,128)(2,1)S(1)}, u32[]{:S(2)}) copy-start(bf16[2,1024,128]{2,1,0:T(8,128)(2,1)S(1)} %slice.23) | copy-start | bytes 1572868
  5.7 23.8 %collective-permute-start.5 = (bf16[2048,128]{1,0:T(8,128)(2,1)S(1)}, bf16[2048,128]{1,0:T(8,128)(2,1)S(1)}, u32[]{:S(2)}, u32[]{:S(2)}) collective-permute-start(bf16[2048,128]{1,0:T(8,128)(2,1)S(1)} %bitcast.29), channel_id=1, source_target_pairs={{0,2},{1,3},{2,0},{3,1},{4,6},{5,7},{6,4},{7,5},{8,10},{9,11},{10,... | collective-permute-start | bytes 1572872 | tf_op jit(solution)/shard_map/ppermute | solution.py:531
  5.9 24.3 %collective-permute-start = (bf16[2048,128]{1,0:T(8,128)(2,1)S(1)}, bf16[2048,128]{1,0:T(8,128)(2,1)S(1)}, u32[]{:S(2)}, u32[]{:S(2)}) collective-permute-start(bf16[2048,128]{1,0:T(8,128)(2,1)S(1)} %pad_maximum_fusion.x0), channel_id=1, source_target_pairs={{0,1},{1,0},{2,3},{3,2},{4,5},{5,4},{6,7},{7,6},{8,9},{9,8},{10,11... | collective-permute-start | bytes 1572872 | tf_op jit(solution)/shard_map/ppermute | solution.py:531
  17.1 18.9 %copy-start.20 = (bf16[2048,128]{1,0:T(8,128)(2,1)}, bf16[2048,128]{1,0:T(8,128)(2,1)S(1)}, u32[]{:S(2)}) copy-start(bf16[2048,128]{1,0:T(8,128)(2,1)S(1)} %collective-permute-done.1.x2) | copy-start | bytes 1572868
  17.1 13.0 %collective-permute-start.2 = (bf16[2048,128]{1,0:T(8,128)(2,1)S(1)}, bf16[2048,128]{1,0:T(8,128)(2,1)S(1)}, u32[]{:S(2)}, u32[]{:S(2)}) collective-permute-start(bf16[2048,128]{1,0:T(8,128)(2,1)S(1)} %collective-permute-done.1.x2), channel_id=1, source_target_pairs={{0,1},{1,0},{2,3},{3,2},{4,5},{5,4},{6,7},{7,6},{8,9},{9,8},{10,11... | collective-permute-start | bytes 1572872 | tf_op jit(solution)/shard_map/ppermute | solution.py:531
  19.6 16.4 %collective-permute-start.4 = (bf16[2048,128]{1,0:T(8,128)(2,1)S(1)}, bf16[2048,128]{1,0:T(8,128)(2,1)}, u32[]{:S(2)}, u32[]{:S(2)}) collective-permute-start(bf16[2048,128]{1,0:T(8,128)(2,1)S(1)} %bitcast.30), channel_id=1, source_target_pairs={{0,1},{1,0},{2,3},{3,2},{4,5},{5,4},{6,7},{7,6},{8,9},{9,8},{10,11... | collective-permute-start | bytes 1572872 | tf_op jit(solution)/shard_map/ppermute | solution.py:531
  19.7 1.0 copy-start.32
  20.7 0.9 copy-start.34
  21.6 0.8 copy-start.35
  29.5 8.5 %copy-start.11 = (bf16[1024,1024]{1,0:T(8,128)(2,1)}, bf16[1024,1024]{1,0:T(8,128)(2,1)S(1)}, u32[]{:S(2)}) copy-start(bf16[1024,1024]{1,0:T(8,128)(2,1)S(1)} %get-tuple-element.60.mat) | copy-start | bytes 6291460
  29.5 8.5 %copy-start.26 = (bf16[2048,128]{1,0:T(8,128)(2,1)}, bf16[2048,128]{1,0:T(8,128)(2,1)S(1)}, u32[]{:S(2)}) copy-start(bf16[2048,128]{1,0:T(8,128)(2,1)S(1)} %collective-permute-done.5.x2) | copy-start | bytes 1572868
  29.5 6.5 %collective-permute-start.6 = (bf16[2048,128]{1,0:T(8,128)(2,1)S(1)}, bf16[2048,128]{1,0:T(8,128)(2,1)S(1)}, u32[]{:S(2)}, u32[]{:S(2)}) collective-permute-start(bf16[2048,128]{1,0:T(8,128)(2,1)S(1)} %collective-permute-done.5.x2), channel_id=1, source_target_pairs={{0,1},{1,0},{2,3},{3,2},{4,5},{5,4},{6,7},{7,6},{8,9},{9,8},{10,11... | collective-permute-start | bytes 1572872 | tf_op jit(solution)/shard_map/ppermute | solution.py:531
  30.1 7.9 %copy-start.22 = (bf16[2048,128]{1,0:T(8,128)(2,1)}, bf16[2048,128]{1,0:T(8,128)(2,1)S(1)}, u32[]{:S(2)}) copy-start(bf16[2048,128]{1,0:T(8,128)(2,1)S(1)} %collective-permute-done.x1) | copy-start | bytes 1572868
  30.1 7.9 %copy-start.24 = (bf16[2048,128]{1,0:T(8,128)(2,1)}, bf16[2048,128]{1,0:T(8,128)(2,1)S(1)}, u32[]{:S(2)}) copy-start(bf16[2048,128]{1,0:T(8,128)(2,1)S(1)} %collective-permute-done.2.x3) | copy-start | bytes 1572868
  30.9 25.1 %copy-start = (bf16[1,1024,256]{2,1,0:T(8,128)(2,1)}, bf16[1,1024,256]{2,1,0:T(8,128)(2,1)S(1)}, u32[]{:S(2)}) copy-start(bf16[1,1024,256]{2,1,0:T(8,128)(2,1)S(1)} %get-tuple-element.47.first) | copy-start | bytes 1572868
  30.9 25.1 %copy-start.2 = (bf16[1,1024,256]{2,1,0:T(8,128)(2,1)}, bf16[1,1024,256]{2,1,0:T(8,128)(2,1)S(1)}, u32[]{:S(2)}) copy-start(bf16[1,1024,256]{2,1,0:T(8,128)(2,1)S(1)} %get-tuple-element.46.last) | copy-start | bytes 1572868
  30.9 19.1 %copy-start.8 = (bf16[4,1024,128]{2,1,0:T(8,128)(2,1)S(1)}, bf16[4,1024,128]{2,1,0:T(8,128)(2,1)}, u32[]{:S(2)}) copy-start(bf16[4,1024,128]{2,1,0:T(8,128)(2,1)} %cot.3) | copy-start | bytes 3145732
  30.9 14.9 %collective-permute-start.3 = (bf16[1,1024,256]{2,1,0:T(8,128)(2,1)S(1)}, bf16[1,1024,256]{2,1,0:T(8,128)(2,1)S(1)}, u32[]{:S(2)}, u32[]{:S(2)}) collective-permute-start(bf16[1,1024,256]{2,1,0:T(8,128)(2,1)S(1)} %get-tuple-element.46.last), channel_id=1, source_target_pairs={{0,4},{4,8},{8,12},{12,16},{16,20},{20,24},{24,28},{28,32},{32,36}... | collective-permute-start | bytes 1572872 | tf_op jit(solution)/shard_map/ppermute | solution.py:534
  34.7 15.2 %collective-permute-start.7 = (bf16[1,1024,256]{2,1,0:T(8,128)(2,1)S(1)}, bf16[1,1024,256]{2,1,0:T(8,128)(2,1)S(1)}, u32[]{:S(2)}, u32[]{:S(2)}) collective-permute-start(bf16[1,1024,256]{2,1,0:T(8,128)(2,1)S(1)} %get-tuple-element.47.first), channel_id=1, source_target_pairs={{4,0},{8,4},{12,8},{16,12},{20,16},{24,20},{28,24},{32,28},{36,32}... | collective-permute-start | bytes 1572872 | tf_op jit(solution)/shard_map/ppermute | solution.py:535
  36.1 13.9 %copy-start.28 = (bf16[2048,128]{1,0:T(8,128)(2,1)}, bf16[2048,128]{1,0:T(8,128)(2,1)S(1)}, u32[]{:S(2)}) copy-start(bf16[2048,128]{1,0:T(8,128)(2,1)S(1)} %collective-permute-done.6.x3) | copy-start | bytes 1572868
  45.8 10.2 %copy-start.4 = (bf16[1,1024,256]{2,1,0:T(8,128)(2,1)}, bf16[1,1024,256]{2,1,0:T(8,128)(2,1)S(1)}, u32[]{:S(2)}) copy-start(bf16[1,1024,256]{2,1,0:T(8,128)(2,1)S(1)} %collective-permute-done.3.up) | copy-start | bytes 1572868
  50.0 6.0 %copy-start.6 = (bf16[1,1024,256]{2,1,0:T(8,128)(2,1)}, bf16[1,1024,256]{2,1,0:T(8,128)(2,1)S(1)}, u32[]{:S(2)}) copy-start(bf16[1,1024,256]{2,1,0:T(8,128)(2,1)S(1)} %collective-permute-done.7.down) | copy-start | bytes 1572868
  56.0 35.9 %copy-start.18 = (bf16[4,1024,128]{2,1,0:T(8,128)(2,1)}, bf16[4,1024,128]{2,1,0:T(8,128)(2,1)S(1)}, u32[]{:S(2)}) copy-start(bf16[4,1024,128]{2,1,0:T(8,128)(2,1)S(1)} %get-tuple-element.61.feat) | copy-start | bytes 3145732
  96.9 1.4 copy-start.13
  98.3 0.7 copy-start.30
  99.0 31.9 %all-to-all-start.1 = ((bf16[32,8,32,128]{3,2,1,0:T(8,128)(2,1)}), bf16[32,8,32,128]{3,2,1,0:T(8,128)(2,1)S(1)}, u32[]{:S(2)}, u32[]{:S(2)}) async-start(bf16[32,8,32,128]{3,2,1,0:T(8,128)(2,1)} %copy-done.13), calls=%async_computation.1 | async-start | bytes 4194304 | tf_op jit(solution)/shard_map/all_to_all | solution.py:596
  130.9 1.2 copy-start.9
  132.1 1.6 copy-start.12
  133.7 1.2 copy-start.19
  137.4 6.7 %copy-start.1 = (bf16[1,1024,256]{2,1,0:T(8,128)(2,1)S(1)}, bf16[1,1024,256]{2,1,0:T(8,128)(2,1)}, u32[]{:S(2)}) copy-start(bf16[1,1024,256]{2,1,0:T(8,128)(2,1)} %copy-done) | copy-start | bytes 1572868
  137.4 6.7 %copy-start.3 = (bf16[1,1024,256]{2,1,0:T(8,128)(2,1)S(1)}, bf16[1,1024,256]{2,1,0:T(8,128)(2,1)}, u32[]{:S(2)}) copy-start(bf16[1,1024,256]{2,1,0:T(8,128)(2,1)} %copy-done.2) | copy-start | bytes 1572868
  137.4 6.7 %copy-start.5 = (bf16[1,1024,256]{2,1,0:T(8,128)(2,1)S(1)}, bf16[1,1024,256]{2,1,0:T(8,128)(2,1)}, u32[]{:S(2)}) copy-start(bf16[1,1024,256]{2,1,0:T(8,128)(2,1)} %copy-done.4) | copy-start | bytes 1572868
  137.4 6.7 %copy-start.7 = (bf16[1,1024,256]{2,1,0:T(8,128)(2,1)S(1)}, bf16[1,1024,256]{2,1,0:T(8,128)(2,1)}, u32[]{:S(2)}) copy-start(bf16[1,1024,256]{2,1,0:T(8,128)(2,1)} %copy-done.6) | copy-start | bytes 1572868
  137.4 19.9 %collective-permute-start.8 = (bf16[1,1024,256]{2,1,0:T(8,128)(2,1)S(1)}, bf16[1,1024,256]{2,1,0:T(8,128)(2,1)S(1)}, u32[]{:S(2)}, u32[]{:S(2)}) collective-permute-start(bf16[1,1024,256]{2,1,0:T(8,128)(2,1)S(1)} %get-tuple-element.63.glast), channel_id=1, source_target_pairs={{0,4},{4,8},{8,12},{12,16},{16,20},{20,24},{24,28},{28,32},{32,36}... | collective-permute-start | bytes 1572872 | tf_op jit(solution)/shard_map/ppermute | solution.py:534
  140.7 16.6 %collective-permute-start.9 = (bf16[1,1024,256]{2,1,0:T(8,128)(2,1)S(1)}, bf16[1,1024,256]{2,1,0:T(8,128)(2,1)S(1)}, u32[]{:S(2)}, u32[]{:S(2)}) collective-permute-start(bf16[1,1024,256]{2,1,0:T(8,128)(2,1)S(1)} %get-tuple-element.64.gfirst), channel_id=1, source_target_pairs={{4,0},{8,4},{12,8},{16,12},{20,16},{24,20},{28,24},{32,28},{36,32}... | collective-permute-start | bytes 1572872 | tf_op jit(solution)/shard_map/ppermute | solution.py:535
  146.0 5.0 %copy-start.37 = (bf16[128,128]{1,0:T(8,128)(2,1)S(1)}, bf16[128,128]{1,0:T(8,128)(2,1)}, u32[]{:S(2)}) copy-start(bf16[128,128]{1,0:T(8,128)(2,1)} %convert_element_type.33) | copy-start | bytes 98308
  147.9 3.2 %copy-start.17 = (bf16[2,1024,128]{2,1,0:T(8,128)(2,1)S(1)}, bf16[2,1024,128]{2,1,0:T(8,128)(2,1)}, u32[]{:S(2)}) copy-start(bf16[2,1024,128]{2,1,0:T(8,128)(2,1)} %copy-done.16) | copy-start | bytes 1572868
  147.9 3.2 %copy-start.27 = (bf16[2048,128]{1,0:T(8,128)(2,1)S(1)}, bf16[2048,128]{1,0:T(8,128)(2,1)}, u32[]{:S(2)}) copy-start(bf16[2048,128]{1,0:T(8,128)(2,1)} %copy-done.26) | copy-start | bytes 1572868
  148.0 3.2 %copy-start.29 = (bf16[2048,128]{1,0:T(8,128)(2,1)S(1)}, bf16[2048,128]{1,0:T(8,128)(2,1)}, u32[]{:S(2)}) copy-start(bf16[2048,128]{1,0:T(8,128)(2,1)} %copy-done.28) | copy-start | bytes 1572868
  148.4 4.6 %collective-permute-start.13 = (bf16[2048,128]{1,0:T(8,128)(2,1)S(1)}, bf16[2048,128]{1,0:T(8,128)(2,1)S(1)}, u32[]{:S(2)}, u32[]{:S(2)}) collective-permute-start(bf16[2048,128]{1,0:T(8,128)(2,1)S(1)} %convolution_convert_fusion.1), channel_id=1, source_target_pairs={{0,1},{1,0},{2,3},{3,2},{4,5},{5,4},{6,7},{7,6},{8,9},{9,8},{10,11... | collective-permute-start | bytes 1572872 | tf_op jit(solution)/shard_map/ppermute | solution.py:531
  154.3 28.4 %collective-permute-start.15 = (bf16[2048,128]{1,0:T(8,128)(2,1)}, bf16[2048,128]{1,0:T(8,128)(2,1)}, u32[]{:S(2)}, u32[]{:S(2)}) collective-permute-start(bf16[2048,128]{1,0:T(8,128)(2,1)} %shard_map.135), channel_id=1, source_target_pairs={{0,2},{1,3},{2,0},{3,1},{4,6},{5,7},{6,4},{7,5},{8,10},{9,11},{10,... | collective-permute-start | bytes 1572872 | tf_op jit(solution)/shard_map/ppermute | solution.py:531
  159.5 3.2 %copy-start.15 = (bf16[2048,128]{1,0:T(8,128)(2,1)S(1)}, bf16[2048,128]{1,0:T(8,128)(2,1)}, u32[]{:S(2)}) copy-start(bf16[2048,128]{1,0:T(8,128)(2,1)} %copy-done.14) | copy-start | bytes 1572868
  159.5 3.2 %copy-start.21 = (bf16[2048,128]{1,0:T(8,128)(2,1)S(1)}, bf16[2048,128]{1,0:T(8,128)(2,1)}, u32[]{:S(2)}) copy-start(bf16[2048,128]{1,0:T(8,128)(2,1)} %copy-done.20) | copy-start | bytes 1572868
  159.6 3.2 %copy-start.23 = (bf16[2048,128]{1,0:T(8,128)(2,1)S(1)}, bf16[2048,128]{1,0:T(8,128)(2,1)}, u32[]{:S(2)}) copy-start(bf16[2048,128]{1,0:T(8,128)(2,1)} %copy-done.22) | copy-start | bytes 1572868
  159.6 3.2 %copy-start.25 = (bf16[2048,128]{1,0:T(8,128)(2,1)S(1)}, bf16[2048,128]{1,0:T(8,128)(2,1)}, u32[]{:S(2)}) copy-start(bf16[2048,128]{1,0:T(8,128)(2,1)} %copy-done.24) | copy-start | bytes 1572868
  160.8 13.2 %collective-permute-start.10 = (bf16[2048,128]{1,0:T(8,128)(2,1)}, bf16[2048,128]{1,0:T(8,128)(2,1)}, u32[]{:S(2)}, u32[]{:S(2)}) collective-permute-start(bf16[2048,128]{1,0:T(8,128)(2,1)} %convolution_convert_fusion.3), channel_id=1, source_target_pairs={{0,1},{1,0},{2,3},{3,2},{4,5},{5,4},{6,7},{7,6},{8,9},{9,8},{10,11... | collective-permute-start | bytes 1572872 | tf_op jit(solution)/shard_map/ppermute | solution.py:531
  162.7 0.9 copy-start.31
  162.7 18.4 %collective-permute-start.14 = (bf16[2048,128]{1,0:T(8,128)(2,1)}, bf16[2048,128]{1,0:T(8,128)(2,1)}, u32[]{:S(2)}, u32[]{:S(2)}) collective-permute-start(bf16[2048,128]{1,0:T(8,128)(2,1)} %convolution_convert_fusion), channel_id=1, source_target_pairs={{0,1},{1,0},{2,3},{3,2},{4,5},{5,4},{6,7},{7,6},{8,9},{9,8},{10,11... | collective-permute-start | bytes 1572872 | tf_op jit(solution)/shard_map/ppermute | solution.py:531
  164.0 0.9 copy-start.10
  164.9 21.3 %all-to-all-start.2 = ((bf16[32,88,128]{2,1,0:T(8,128)(2,1)}), bf16[32,88,128]{2,1,0:T(8,128)(2,1)S(1)}, u32[]{:S(2)}, u32[]{:S(2)}) async-start(bf16[32,88,128]{2,1,0:T(8,128)(2,1)} %copy-done.10), calls=%async_computation.2 | async-start | bytes 1441792 | tf_op jit(solution)/shard_map/all_to_all | solution.py:671
  177.5 9.5 %collective-permute-start.11 = (bf16[2048,128]{1,0:T(8,128)(2,1)}, bf16[2048,128]{1,0:T(8,128)(2,1)}, u32[]{:S(2)}, u32[]{:S(2)}) collective-permute-start(bf16[2048,128]{1,0:T(8,128)(2,1)} %convolution_convert_fusion.2), channel_id=1, source_target_pairs={{0,1},{1,0},{2,3},{3,2},{4,5},{5,4},{6,7},{7,6},{8,9},{9,8},{10,11... | collective-permute-start | bytes 1572872 | tf_op jit(solution)/shard_map/ppermute | solution.py:531
  178.2 19.8 %collective-permute-start.12 = (bf16[2048,128]{1,0:T(8,128)(2,1)}, bf16[2048,128]{1,0:T(8,128)(2,1)}, u32[]{:S(2)}, u32[]{:S(2)}) collective-permute-start(bf16[2048,128]{1,0:T(8,128)(2,1)} %shard_map.133), channel_id=1, source_target_pairs={{0,2},{1,3},{2,0},{3,1},{4,6},{5,7},{6,4},{7,5},{8,10},{9,11},{10,... | collective-permute-start | bytes 1572872 | tf_op jit(solution)/shard_map/ppermute | solution.py:531

commit v5 on v4

--- a/solution.py
+++ b/solution.py
@@ -12,7 +12,7 @@
 BF = jnp.bfloat16
 F32 = jnp.float32
 EDGE = 8
-STEP = 32
+STEP = 128
 
 
 def cosine(phase, period):
@@ -54,7 +54,7 @@
 
 def tables_kernel(
     where, w_gate, w_value, short_filter, row_filter, column_filter,
-    mat, mat_t, mine, fwd, inv, coef, keep, colr, coli, kern, w_all,
+    mat, mat_t, mine, fwd, inv, coef, keep, colr, coli, kern, w_all, w_turned,
 ):
     ch, place = where[0], where[1]
     width, channels = row_filter.shape
@@ -116,6 +116,7 @@
         to = pl.ds(k * channels, channels)
         w_all[to, pl.ds(0, channels)] = w_gate[at, :]
         w_all[to, pl.ds(channels, channels)] = w_value[at, :]
+    w_turned[...] = w_all[...].astype(F32).T.astype(BF)
 
 
 def fill_framed(framed, rows_of, channels):
@@ -363,7 +364,17 @@
         lax.fori_loop(0, width // STEP, body, 0)
 
 
-def backward_mid_kernel(gfirst, gmiddle, glast, kern, back, gframed):
+def shares(back, w_turned, p0, p1, p2, p3):
+    tokens = back.shape[0] * back.shape[1]
+    channels = p0.shape[1]
+    total = jnp.dot(
+        back[...].reshape(tokens, back.shape[2]), w_turned[...], preferred_element_type=F32
+    )
+    for k, p in enumerate((p0, p1, p2, p3)):
+        p[...] = total[:, k * channels : (k + 1) * channels].astype(p.dtype)
+
+
+def backward_mid_kernel(gfirst, gmiddle, glast, kern, w_turned, back, p0, p1, p2, p3, gframed):
     width = gfirst.shape[1]
     channels = kern.shape[1]
     inner = gmiddle.shape[0]
@@ -371,6 +382,7 @@
         gframed, [(gfirst, 0), *((gmiddle, r) for r in range(inner)), (glast, 0)], channels
     )
     spread_back(gframed, kern, [(back, r, r + 1) for r in range(inner)], width, channels)
+    shares(back, w_turned, p0, p1, p2, p3)
 
 
 def short_kernel(up, first, middle, last, down, gfirst, gmiddle, glast, short, framed, *, branch):
@@ -417,7 +429,9 @@
         short[pl.ds(k, 1), :] = jnp.sum(sums[k], axis=0, keepdims=True)
 
 
-def backward_edge_kernel(gup, gfirst, gmiddle, glast, gdown, kern, back, gframed):
+def backward_edge_kernel(
+    gup, gfirst, gmiddle, glast, gdown, kern, w_turned, back, p0, p1, p2, p3, gframed
+):
     width = gfirst.shape[1]
     channels = kern.shape[1]
     inner = gmiddle.shape[0]
@@ -427,29 +441,25 @@
         channels,
     )
     spread_back(gframed, kern, [(back, 0, 1), (back, 1, 4)], width, channels)
-
-
-def share_kernel(back, w, beside, out):
-    part = lax.dot_general(
-        back[...], w[...], (((1,), (1,)), ((), ())), preferred_element_type=F32
-    )
-    out[...] = (part + beside[...].astype(F32)).astype(BF)
-
-
-def finish_mid_kernel(kept, across, grad, rows, sem):
+    shares(back, w_turned, p0, p1, p2, p3)
+
+
+def finish_mid_kernel(own, beside, across, grad, rows, sem):
     inner = grad.shape[0] - 2
-    rows[...] = (kept[...] + across[...].astype(F32)).astype(BF).reshape(rows.shape)
+    total = own[...] + beside[...].astype(F32) + across[...].astype(F32)
+    rows[...] = total.astype(BF).reshape(rows.shape)
     copy = pltpu.make_async_copy(rows, grad.at[pl.ds(1, inner)], sem)
     copy.start()
     copy.wait()
 
 
-def finish_edge_kernel(kept, across, middle, grad, rows, sems):
+def finish_edge_kernel(own, beside, across, middle, grad, rows, sems):
     width = grad.shape[1]
     copies = []
     for r in range(2):
         at = pl.ds(r * width, width)
-        rows[r] = (kept[at, :] + across[at, :].astype(F32)).astype(BF)
+        total = own[at, :] + beside[at, :].astype(F32) + across[at, :].astype(F32)
+        rows[r] = total.astype(BF)
         to = r * (grad.shape[0] - 1)
         copies.append(pltpu.make_async_copy(rows.at[r], grad.at[to], sems.at[r]))
         copies[r].start()
@@ -508,7 +518,7 @@
     semaphores = [] if sems is None else [pltpu.SemaphoreType.DMA(sems)]
     return pl.pallas_call(
         body,
-        out_shape=[jax.ShapeDtypeStruct(s, d) for s, d in outs],
+        out_shape=[(pltpu.HBM if free else jax.ShapeDtypeStruct)(s, d) for s, d in outs],
         scratch_shapes=[pltpu.VMEM(s, d) for s, d in scratch] + semaphores,
         compiler_params=pltpu.CompilerParams(vmem_limit_bytes=limit << 20),
         **specs,
@@ -543,7 +553,7 @@
     mid_beside = flipped(mid, 1)
     edge_corner = flipped(edge_across, 1)
 
-    (mat, mat_t, mine, fwd, inv, coef, keep, colr, coli, kern, w_all) = kernel_call(
+    (mat, mat_t, mine, fwd, inv, coef, keep, colr, coli, kern, w_all, w_turned) = kernel_call(
         tables_kernel,
         [
             ((width, width), BF),
@@ -557,13 +567,13 @@
             ((height, channels), F32),
             ((18, channels), F32),
             ((parts * channels, 2 * channels), BF),
+            ((2 * channels, parts * channels), BF),
         ],
         [],
         12,
         scalars=1,
         operands=5,
     )(jnp.stack([ch, place]), w_gate, w_value, short_filter, row_filter, column_filter)
-    w_blocks = [w_all[k * channels : (k + 1) * channels] for k in range(parts)]
 
     line = ((1, width, 2 * channels), BF)
     lines = ((inner, width, 2 * channels), BF)
@@ -598,9 +608,11 @@
         inverse_kernel, [tile, line, lines, line], [], 20
     )(returned, mat_t, feat, cotangent)
     gup, gdown = halos(gfirst, glast)
-    back_mid = kernel_call(backward_mid_kernel, [lines], [framed(rows)], 16)(
-        gfirst, gmiddle, glast, kern
-    )[0]
+    share = (2 * width, channels)
+    share_outs = [(share, F32), (share, BF), (share, F32), (share, BF)]
+    back_mid, *shares_mid = kernel_call(
+        backward_mid_kernel, [lines, *share_outs], [framed(rows)], 20
+    )(gfirst, gmiddle, glast, kern, w_turned)
     shorts = [
         kernel_call(
             functools.partial(short_kernel, branch=n),
@@ -610,38 +622,31 @@
         )(up, first, middle, last, down, gfirst, gmiddle, glast)[0]
         for n in range(2)
     ]
-    back_edge = kernel_call(backward_edge_kernel, [lines], [framed(6)], 16)(
-        gup, gfirst, gmiddle, glast, gdown, kern
-    )[0]
-
-    contract = (((1,), (1,)), ((), ()))
+    back_edge, *shares_edge = kernel_call(
+        backward_edge_kernel, [lines, *share_outs], [framed(6)], 22
+    )(gup, gfirst, gmiddle, glast, gdown, kern, w_turned)
+
     over_tokens = (((0,), (0,)), ((), ()))
 
-    def collected(back):
-        def share(k):
-            return lax.dot_general(back, w_blocks[k], contract, preferred_element_type=F32)
-
-        beside = flipped(share(3).astype(BF), 1)
-        theirs = kernel_call(share_kernel, [(beside.shape, BF)], [], 10)(
-            back, w_blocks[2], beside
-        )[0]
+    def collected(p0, p1, p2, p3):
+        beside = flipped(p3, 1)
+        theirs = (p2 + beside.astype(F32)).astype(BF)
         across = flipped(theirs, 2)
-        back, _ = lax.optimization_barrier((back, theirs))
-        kept = share(0) + flipped(share(1).astype(BF), 1).astype(F32)
-        return kept, across
+        kept = flipped(p1, 1)
+        return p0, kept, across
 
     back_mid = back_mid.reshape(inner * width, 2 * channels)
     back_edge = back_edge.reshape(2 * width, 2 * channels)
-    kept_mid, across_mid = collected(back_mid)
-    kept_edge, across_edge = collected(back_edge)
+    mid_parts = collected(*shares_mid)
+    edge_parts = collected(*shares_edge)
     begun = kernel_call(
         finish_mid_kernel, [tile], [((inner, width, channels), BF)], 10,
         free=True, sems=(),
-    )(kept_mid, across_mid)[0]
+    )(*mid_parts)[0]
     input_grad = kernel_call(
         finish_edge_kernel, [tile], [((2, width, channels), BF)], 10,
-        operands=2, free=True, alias=2, sems=(2,),
-    )(kept_edge, across_edge, begun)[0]
+        operands=3, free=True, alias=3, sems=(2,),
+    )(*edge_parts, begun)[0]
 
     grad_w = lax.dot_general(gathered_mid, back_mid, over_tokens, preferred_element_type=F32)
     grad_w = lax.optimization_barrier(grad_w)

time: 201 us -> 209 us (1.040)
  waiting for transfers between devices: 58.9 us -> 71.6 us
  matrix products: 9.59 us -> 2.56 us
  other arithmetic: 0.95 us -> 4.14 us
    ppermute x12, waiting for transfers between devices: 19.6 us -> 34 us  [flipped(): return lax.ppermute(value, 'ch', [(i, i ^ bit) for i in range(parts)])]
    dot_general x6 -> x0, matrix products: 7.06 us -> none  [share(): lax.dot_general(back, w_blocks[k], contract, preferred_element_type=F32)]
    convert_element_type x0 -> x2, other arithmetic: none -> 3.17 us  [collected(): theirs = (p2 + beside.astype(F32)).astype(BF)]
    unnamed x79 -> x85, local copies, waits for them, and re-layouts: 9.81 us -> 8.92 us
    pallas_call x4 -> x2, Pallas kernels: 7.75 us -> 6.92 us  [the longest x1 3.52 us: local(): kernel_call(backward_edge_kernel, [lines, *share_outs], [framed(6)], 22)]
  transfers between devices with their start and end apart: 18 -> 18, of which waited for: 6 -> 6; matrix products, arithmetic and copies ran while one was open for 5% -> 3% of each run, Pallas kernels for 12% -> 12%
where the time goes in v5:
time: 209 us; the launch traced here: 208 us
  waiting for transfers between devices  71.6 us (34%)
  starting transfers between devices  42.8 us (20%)
  Pallas kernels  39.3 us (19%)
  blocking collectives  35.9 us (17%)
  local copies, waits for them, and re-layouts  10.2 us (5%)
  other arithmetic  4.14 us (2%)
  matrix products  2.56 us (1%)
    all_to_all x1, blocking collectives, local(): recv = lax.all_to_all(send, 'grid', split_axis=0, concat_axis=0, tiled=True)  35.9 us
    ppermute x12, waiting for transfers between devices, flipped(): return lax.ppermute(value, 'ch', [(i, i ^ bit) for i in range(parts)])  34 us
    all_to_all x1, waiting for transfers between devices, local(): lax.all_to_all(turned, 'grid', split_axis=0, concat_axis=0, tiled=True)  25.8 us
    ppermute x12, starting transfers between devices, flipped(): return lax.ppermute(value, 'ch', [(i, i ^ bit) for i in range(parts)])  18 us
    all_to_all x1, starting transfers between devices, local(): lax.all_to_all(packed, 'grid', split_axis=0, concat_axis=0, tiled=True)  9.87 us
    unnamed x85, local copies, waits for them, and re-layouts  8.92 us
    ppermute x2, waiting for transfers between devices, halos(): up = lax.ppermute(last, 'grid', [(i, i + 1) for i in range(owners - 1)])  7.73 us
    pallas_call x1, Pallas kernels, local(): kernel_call(tables_kernel, [((width, width), BF), ((width, width), BF), (...  7.19 us
  transfers between devices with their start and end apart: 18, of which 6 were waited for; matrix products, arithmetic and copies ran while one was open for 3% of the time, Pallas kernels for 12%

profile of v5, /device:TPU:1, one launch (start us, length us, event | category | flops | bytes accessed | tf_op | source)
XLA Modules:
  0.0 208.0 jit_solution(8496601658023890250)
XLA Ops:
  0.7 1.2 slice_bitcast_fusion.1
  1.9 3.8 %collective-permute-start.1 = (bf16[2048,128]{1,0:T(8,128)(2,1)S(1)}, bf16[2048,128]{1,0:T(8,128)(2,1)S(1)}, u32[]{:S(2)}, u32[]{:S(2)}) collective-permute-start(bf16[2048,128]{1,0:T(8,128)(2,1)S(1)} %pad_maximum_fusion.x0), channel_id=1, source_target_pairs={{0,2},{1,3},{2,0},{3,1},{4,6},{5,7},{6,4},{7,5},{8,10},{9,11},{10,... | collective-permute-start | bytes 1572872 | tf_op jit(solution)/shard_map/ppermute | solution.py:541
  5.7 0.1 collective-permute-start.5
  5.9 1.1 collective-permute-start
  7.0 10.1 %collective-permute-done.1.x2 = bf16[2048,128]{1,0:T(8,128)(2,1)S(1)} collective-permute-done((bf16[2048,128]{1,0:T(8,128)(2,1)S(1)}, bf16[2048,128]{1,0:T(8,128)(2,1)S(1)}, u32[]{:S(2)}, u32[]{:S(2)}) %collective-permute-start.1) | collective-permute-done | bytes 524320 | tf_op jit(solution)/shard_map/ppermute | solution.py:541
  17.1 2.5 %collective-permute-start.2 = (bf16[2048,128]{1,0:T(8,128)(2,1)S(1)}, bf16[2048,128]{1,0:T(8,128)(2,1)S(1)}, u32[]{:S(2)}, u32[]{:S(2)}) collective-permute-start(bf16[2048,128]{1,0:T(8,128)(2,1)S(1)} %collective-permute-done.1.x2), channel_id=1, source_target_pairs={{0,1},{1,0},{2,3},{3,2},{4,5},{5,4},{6,7},{7,6},{8,9},{9,8},{10,11... | collective-permute-start | bytes 1572872 | tf_op jit(solution)/shard_map/ppermute | solution.py:541
  19.6 0.0 collective-permute-start.4
  19.7 0.1 pad_add_fusion.where
  19.7 0.9 copy-done.35
  20.7 0.9 copy-done.37
  21.6 0.8 copy-done.38
  22.3 7.2 %shard_map.126 = (bf16[1024,1024]{1,0:T(8,128)(2,1)S(1)}, bf16[1024,1024]{1,0:T(8,128)(2,1)S(1)}, bf16[32,1024]{1,0:T(8,128)(2,1)S(1)}, bf16[256,256]{1,0:T(8,12...) custom-call(s32[2]{0:T(128)S(1)} %pad_add_fusion.where, ...), custom_call_target="tpu_custom_call" | custom-call | tf_op jit(solution)/shard_map/pallas_call | solution.py:556
  29.5 0.0 collective-permute-done.5.x2
  29.6 0.6 collective-permute-start.6
  30.1 0.0 collective-permute-done.x1
  30.1 0.0 collective-permute-done.2.x3
  30.2 0.7 shard_map.127
  30.9 0.0 copy-start.8
  30.9 3.8 %collective-permute-start.3 = (bf16[1,1024,256]{2,1,0:T(8,128)(2,1)S(1)}, bf16[1,1024,256]{2,1,0:T(8,128)(2,1)S(1)}, u32[]{:S(2)}, u32[]{:S(2)}) collective-permute-start(bf16[1,1024,256]{2,1,0:T(8,128)(2,1)S(1)} %get-tuple-element.55.last), channel_id=1, source_target_pairs={{0,4},{4,8},{8,12},{12,16},{16,20},{20,24},{24,28},{28,32},{32,36}... | collective-permute-start | bytes 1572872 | tf_op jit(solution)/shard_map/ppermute | solution.py:544
  34.7 1.3 collective-permute-start.7
  36.0 0.0 collective-permute-done.4.x1
  36.1 1.9 shard_map.128.middle
  38.1 7.7 %collective-permute-done.3.up = bf16[1,1024,256]{2,1,0:T(8,128)(2,1)S(1)} collective-permute-done((bf16[1,1024,256]{2,1,0:T(8,128)(2,1)S(1)}, bf16[1,1024,256]{2,1,0:T(8,128)(2,1)S(1)}, u32[]{:S(2)}, u32[]{:S(2)}) %collective-permute-start.3) | collective-permute-done | bytes 524320 | tf_op jit(solution)/shard_map/ppermute | solution.py:544
  45.8 4.2 %collective-permute-done.7.down = bf16[1,1024,256]{2,1,0:T(8,128)(2,1)S(1)} collective-permute-done((bf16[1,1024,256]{2,1,0:T(8,128)(2,1)S(1)}, bf16[1,1024,256]{2,1,0:T(8,128)(2,1)S(1)}, u32[]{:S(2)}, u32[]{:S(2)}) %collective-permute-start.7) | collective-permute-done | bytes 524320 | tf_op jit(solution)/shard_map/ppermute | solution.py:545
  50.0 5.7 %shard_map.129 = (bf16[32,8,32,128]{3,2,1,0:T(8,128)(2,1)S(1)}, bf16[4,1024,128]{2,1,0:T(8,128)(2,1)S(1)}) custom-call(bf16[1,1024,256]{2,1,0:T(8,128)(2,1)S(1)} %collective-permute-done.3.up, bf16[1,1024,256]{2,1,0:T(8,128)(2,1)S(1)} %get-tuple-element.56.first, bf16[2,1024,256]{2,1,0:T(8,128)(2,1)S(1)} %shard_map.128.middle, ...), custom_call_target="tpu_custom_call" | custom-call | tf_op jit(solution)/shard_map/pallas_call | solution.py:595
  55.7 0.0 copy-start.21
  55.7 35.9 %all_to_all.15.recv = bf16[32,8,32,128]{3,2,1,0:T(8,128)(2,1)S(1)} all-to-all(bf16[32,8,32,128]{3,2,1,0:T(8,128)(2,1)S(1)} %get-tuple-element.60), channel_id=1, replica_groups=mesh['grid'=32,'ch'=4] {'grid'}, dimensions={0} | all-to-all | bytes 4194304 | tf_op jit(solution)/shard_map/all_to_all | solution.py:598
  91.6 5.0 %shard_map.130 = (bf16[32,8,32,128]{3,2,1,0:T(8,128)(2,1)S(1)}, bf16[1024,128]{1,0:T(8,128)(2,1)S(1)}, f32[128,128]{1,0:T(8,128)S(1)}) custom-call(bf16[32,8,32,128]{3,2,1,0:T(8,128)(2,1)S(1)} %all_to_all.15.recv, f32[4,16,128]{2,1,0:T(8,128)S(1)} %get-tuple-element.61.coef, f32[1,16,128]{2,1,0:T(8,128)S(1)} %get-tuple-element.62.keep, ...), custom_call_target="tpu_custom_call" | custom-call | tf_op jit(solution)/shard_map/pallas_call | solution.py:600
  96.7 1.3 copy-done.12
  98.0 0.7 copy-done.33
  98.7 5.4 %all-to-all-start.1 = ((bf16[32,8,32,128]{3,2,1,0:T(8,128)(2,1)}), bf16[32,8,32,128]{3,2,1,0:T(8,128)(2,1)S(1)}, u32[]{:S(2)}, u32[]{:S(2)}) async-start(bf16[32,8,32,128]{3,2,1,0:T(8,128)(2,1)} %copy-done.12), calls=%async_computation.1 | async-start | bytes 4194304 | tf_op jit(solution)/shard_map/all_to_all | solution.py:606
  104.1 0.1 pad.3.clone
  104.2 0.6 convert_element_type.25
  104.8 25.8 %all-to-all-done.1.recv = bf16[32,8,32,128]{3,2,1,0:T(8,128)(2,1)S(1)} async-done(((bf16[32,8,32,128]{3,2,1,0:T(8,128)(2,1)}), bf16[32,8,32,128]{3,2,1,0:T(8,128)(2,1)S(1)}, u32[]{:S(2)}, u32[]{:S(2)}) %all-to-all-start.1) | async-done | bytes 2097184 | tf_op jit(solution)/shard_map/all_to_all | solution.py:606
  130.6 1.2 copy-done.9
  131.8 1.6 copy-done.11
  133.4 1.2 copy-done.22
  134.7 2.5 %shard_map.131 = (bf16[4,1024,128]{2,1,0:T(8,128)(2,1)}, bf16[1,1024,256]{2,1,0:T(8,128)(2,1)S(1)}, bf16[2,1024,256]{2,1,0:T(8,128)(2,1)S(1)}, bf16[1,1024,256]{2,1,0:T(8,128)(2,1)S(1)}) custom-call(bf16[32,8,32,128]{3,2,1,0:T(8,128)(2,1)S(1)} %all-to-all-done.1.recv, bf16[1024,1024]{1,0:T(8,128)(2,1)S(1)} %copy-done.11, ...), custom_call_target="tpu_custom_call" | custom-call | tf_op jit(solution)/shard_map/pallas_call | solution.py:607
  137.1 3.2 %collective-permute-start.8 = (bf16[1,1024,256]{2,1,0:T(8,128)(2,1)S(1)}, bf16[1,1024,256]{2,1,0:T(8,128)(2,1)S(1)}, u32[]{:S(2)}, u32[]{:S(2)}) collective-permute-start(bf16[1,1024,256]{2,1,0:T(8,128)(2,1)S(1)} %get-tuple-element.72.glast), channel_id=1, source_target_pairs={{0,4},{4,8},{8,12},{12,16},{16,20},{20,24},{24,28},{28,32},{32,36}... | collective-permute-start | bytes 1572872 | tf_op jit(solution)/shard_map/ppermute | solution.py:544
  140.3 1.3 collective-permute-start.9
  141.6 1.9 shard_map.136
  143.6 1.9 shard_map.137
  145.5 3.4 %shard_map.133 = (bf16[2,1024,256]{2,1,0:T(8,128)(2,1)S(1)}, f32[2048,128]{1,0:T(8,128)S(1)}, bf16[2048,128]{1,0:T(8,128)(2,1)}, f32[2048,128]{1,0:T(8,128)S(1)}, bf16[2048,128]{1,0:T(8,128)(2,1)}) custom-call(bf16[1,1024,256]{2,1,0:T(8,128)(2,1)S(1)} %get-tuple-element.73.gfirst, bf16[2,1024,256]{2,1,0:T(8,128)(2,1)S(1)} %get-tuple-element.74.gmiddle, ...), custom_call_target="tpu_custom_call" | custom-call | tf_op jit(solution)/shard_map/pallas_call | solution.py:613
  148.9 2.3 %collective-permute-start.14 = (bf16[2048,128]{1,0:T(8,128)(2,1)}, bf16[2048,128]{1,0:T(8,128)(2,1)}, u32[]{:S(2)}, u32[]{:S(2)}) collective-permute-start(bf16[2048,128]{1,0:T(8,128)(2,1)} %get-tuple-element.83), channel_id=1, source_target_pairs={{0,1},{1,0},{2,3},{3,2},{4,5},{5,4},{6,7},{7,6},{8,9},{9,8},{10,11... | collective-permute-start | bytes 1572872 | tf_op jit(solution)/shard_map/ppermute | solution.py:541
  151.2 1.8 fusion
  153.1 0.2 maximum_maximum_fusion.small
  153.3 0.1 collective-permute-start.13
  153.4 3.5 %shard_map.132 = (bf16[2,1024,256]{2,1,0:T(8,128)(2,1)S(1)}, f32[2048,128]{1,0:T(8,128)S(1)}, bf16[2048,128]{1,0:T(8,128)(2,1)}, f32[2048,128]{1,0:T(8,128)S(1)}, bf16[2048,128]{1,0:T(8,128)(2,1)}) custom-call(bf16[1,1024,256]{2,1,0:T(8,128)(2,1)S(1)} %collective-permute-done.8.gup, bf16[1,1024,256]{2,1,0:T(8,128)(2,1)S(1)} %get-tuple-element.73.gfirst, ...), custom_call_target="tpu_custom_call" | custom-call | tf_op jit(solution)/shard_map/pallas_call | solution.py:625
  156.9 3.1 %collective-permute-start.11 = (bf16[2048,128]{1,0:T(8,128)(2,1)}, bf16[2048,128]{1,0:T(8,128)(2,1)}, u32[]{:S(2)}, u32[]{:S(2)}) collective-permute-start(bf16[2048,128]{1,0:T(8,128)(2,1)} %get-tuple-element.79), channel_id=1, source_target_pairs={{0,1},{1,0},{2,3},{3,2},{4,5},{5,4},{6,7},{7,6},{8,9},{9,8},{10,11... | collective-permute-start | bytes 1572872 | tf_op jit(solution)/shard_map/ppermute | solution.py:541
  160.1 0.8 fusion.8
  160.8 0.1 add.11.grad_w
  160.9 0.1 copy-done.34
  161.0 1.0 shard_map.138
  162.0 9.9 %all-to-all-start.2 = ((bf16[32,88,128]{2,1,0:T(8,128)(2,1)}), bf16[32,88,128]{2,1,0:T(8,128)(2,1)S(1)}, u32[]{:S(2)}, u32[]{:S(2)}) async-start(bf16[32,88,128]{2,1,0:T(8,128)(2,1)} %shard_map.138), calls=%async_computation.2 | async-start | bytes 1441792 | tf_op jit(solution)/shard_map/all_to_all | solution.py:676
  171.8 0.0 copy-start.18
  171.9 1.2 add_convert_fusion
  173.1 3.2 %collective-permute-start.15 = (bf16[2048,128]{1,0:T(8,128)(2,1)S(1)}, bf16[2048,128]{1,0:T(8,128)(2,1)S(1)}, u32[]{:S(2)}, u32[]{:S(2)}) collective-permute-start(bf16[2048,128]{1,0:T(8,128)(2,1)S(1)} %add_convert_fusion), channel_id=1, source_target_pairs={{0,2},{1,3},{2,0},{3,1},{4,6},{5,7},{6,4},{7,5},{8,10},{9,11},{10,... | collective-permute-start | bytes 1572872 | tf_op jit(solution)/shard_map/ppermute | solution.py:541
  176.3 1.1 collective-permute-start.10
  177.4 1.9 add_convert_fusion.1
  179.3 15.3 %collective-permute-done.15.across = bf16[2048,128]{1,0:T(8,128)(2,1)S(1)} collective-permute-done((bf16[2048,128]{1,0:T(8,128)(2,1)S(1)}, bf16[2048,128]{1,0:T(8,128)(2,1)S(1)}, u32[]{:S(2)}, u32[]{:S(2)}) %collective-permute-start.15) | collective-permute-done | bytes 524320 | tf_op jit(solution)/shard_map/ppermute | solution.py:541
  194.6 2.0 shard_map.134.middle
  196.6 0.7 shard_map.139
  197.3 8.6 %collective-permute-done.12.across = bf16[2048,128]{1,0:T(8,128)(2,1)} collective-permute-done((bf16[2048,128]{1,0:T(8,128)(2,1)}, bf16[2048,128]{1,0:T(8,128)(2,1)}, u32[]{:S(2)}, u32[]{:S(2)}) %collective-permute-start.12) | collective-permute-done | bytes 524320 | tf_op jit(solution)/shard_map/ppermute | solution.py:541
  206.0 1.9 shard_map.135
  (89 shorter events, 0.3 us)
Async XLA Ops:
  0.6 5.1 %copy-start.39 = (bf16[4,1024,128]{2,1,0:T(8,128)(2,1)S(1)}, bf16[4,1024,128]{2,1,0:T(8,128)(2,1)}, u32[]{:S(2)}) copy-start(bf16[4,1024,128]{2,1,0:T(8,128)(2,1)} %param.7) | copy-start | bytes 3145732
  0.6 19.0 %copy-start.41 = (bf16[2,3,3,128]{3,0,2,1:T(2,128)(2,1)S(1)}, bf16[2,3,3,128]{3,0,2,1:T(2,128)(2,1)}, u32[]{:S(2)}) copy-start(bf16[2,3,3,128]{3,0,2,1:T(2,128)(2,1)} %param.10) | copy-start | bytes 13828
  0.7 19.1 %copy-start.36 = (bf16[512,128]{1,0:T(8,128)(2,1)S(1)}, bf16[512,128]{1,0:T(8,128)(2,1)}, u32[]{:S(2)}) copy-start(bf16[512,128]{1,0:T(8,128)(2,1)} %w_gate.1) | copy-start | bytes 393220
  1.9 34.2 %copy-start.13 = (bf16[2048,128]{1,0:T(8,128)(2,1)}, bf16[2048,128]{1,0:T(8,128)(2,1)S(1)}, u32[]{:S(2)}) copy-start(bf16[2048,128]{1,0:T(8,128)(2,1)S(1)} %pad_maximum_fusion.x0) | copy-start | bytes 1572868
  1.9 15.2 %collective-permute-start.1 = (bf16[2048,128]{1,0:T(8,128)(2,1)S(1)}, bf16[2048,128]{1,0:T(8,128)(2,1)S(1)}, u32[]{:S(2)}, u32[]{:S(2)}) collective-permute-start(bf16[2048,128]{1,0:T(8,128)(2,1)S(1)} %pad_maximum_fusion.x0), channel_id=1, source_target_pairs={{0,2},{1,3},{2,0},{3,1},{4,6},{5,7},{6,4},{7,5},{8,10},{9,11},{10,... | collective-permute-start | bytes 1572872 | tf_op jit(solution)/shard_map/ppermute | solution.py:541
  5.7 32.3 %copy-start.15 = (bf16[2,1024,128]{2,1,0:T(8,128)(2,1)}, bf16[2,1024,128]{2,1,0:T(8,128)(2,1)S(1)}, u32[]{:S(2)}) copy-start(bf16[2,1024,128]{2,1,0:T(8,128)(2,1)S(1)} %slice.11) | copy-start | bytes 1572868
  5.7 23.8 %collective-permute-start.5 = (bf16[2048,128]{1,0:T(8,128)(2,1)S(1)}, bf16[2048,128]{1,0:T(8,128)(2,1)S(1)}, u32[]{:S(2)}, u32[]{:S(2)}) collective-permute-start(bf16[2048,128]{1,0:T(8,128)(2,1)S(1)} %bitcast.13), channel_id=1, source_target_pairs={{0,2},{1,3},{2,0},{3,1},{4,6},{5,7},{6,4},{7,5},{8,10},{9,11},{10,... | collective-permute-start | bytes 1572872 | tf_op jit(solution)/shard_map/ppermute | solution.py:541
  5.9 24.3 %collective-permute-start = (bf16[2048,128]{1,0:T(8,128)(2,1)S(1)}, bf16[2048,128]{1,0:T(8,128)(2,1)S(1)}, u32[]{:S(2)}, u32[]{:S(2)}) collective-permute-start(bf16[2048,128]{1,0:T(8,128)(2,1)S(1)} %pad_maximum_fusion.x0), channel_id=1, source_target_pairs={{0,1},{1,0},{2,3},{3,2},{4,5},{5,4},{6,7},{7,6},{8,9},{9,8},{10,11... | collective-permute-start | bytes 1572872 | tf_op jit(solution)/shard_map/ppermute | solution.py:541
  17.1 19.0 %copy-start.23 = (bf16[2048,128]{1,0:T(8,128)(2,1)}, bf16[2048,128]{1,0:T(8,128)(2,1)S(1)}, u32[]{:S(2)}) copy-start(bf16[2048,128]{1,0:T(8,128)(2,1)S(1)} %collective-permute-done.1.x2) | copy-start | bytes 1572868
  17.1 13.1 %collective-permute-start.2 = (bf16[2048,128]{1,0:T(8,128)(2,1)S(1)}, bf16[2048,128]{1,0:T(8,128)(2,1)S(1)}, u32[]{:S(2)}, u32[]{:S(2)}) collective-permute-start(bf16[2048,128]{1,0:T(8,128)(2,1)S(1)} %collective-permute-done.1.x2), channel_id=1, source_target_pairs={{0,1},{1,0},{2,3},{3,2},{4,5},{5,4},{6,7},{7,6},{8,9},{9,8},{10,11... | collective-permute-start | bytes 1572872 | tf_op jit(solution)/shard_map/ppermute | solution.py:541
  19.6 16.4 %collective-permute-start.4 = (bf16[2048,128]{1,0:T(8,128)(2,1)S(1)}, bf16[2048,128]{1,0:T(8,128)(2,1)}, u32[]{:S(2)}, u32[]{:S(2)}) collective-permute-start(bf16[2048,128]{1,0:T(8,128)(2,1)S(1)} %bitcast.14), channel_id=1, source_target_pairs={{0,1},{1,0},{2,3},{3,2},{4,5},{5,4},{6,7},{7,6},{8,9},{9,8},{10,11... | collective-permute-start | bytes 1572872 | tf_op jit(solution)/shard_map/ppermute | solution.py:541
  19.7 1.0 copy-start.35
  20.7 0.9 copy-start.37
  21.6 0.8 copy-start.38
  29.5 8.5 %copy-start.10 = (bf16[1024,1024]{1,0:T(8,128)(2,1)}, bf16[1024,1024]{1,0:T(8,128)(2,1)S(1)}, u32[]{:S(2)}) copy-start(bf16[1024,1024]{1,0:T(8,128)(2,1)S(1)} %get-tuple-element.69.mat) | copy-start | bytes 6291460
  29.6 8.5 %copy-start.29 = (bf16[2048,128]{1,0:T(8,128)(2,1)}, bf16[2048,128]{1,0:T(8,128)(2,1)S(1)}, u32[]{:S(2)}) copy-start(bf16[2048,128]{1,0:T(8,128)(2,1)S(1)} %collective-permute-done.5.x2) | copy-start | bytes 1572868
  29.6 6.5 %collective-permute-start.6 = (bf16[2048,128]{1,0:T(8,128)(2,1)S(1)}, bf16[2048,128]{1,0:T(8,128)(2,1)S(1)}, u32[]{:S(2)}, u32[]{:S(2)}) collective-permute-start(bf16[2048,128]{1,0:T(8,128)(2,1)S(1)} %collective-permute-done.5.x2), channel_id=1, source_target_pairs={{0,1},{1,0},{2,3},{3,2},{4,5},{5,4},{6,7},{7,6},{8,9},{9,8},{10,11... | collective-permute-start | bytes 1572872 | tf_op jit(solution)/shard_map/ppermute | solution.py:541
  30.1 7.9 %copy-start.25 = (bf16[2048,128]{1,0:T(8,128)(2,1)}, bf16[2048,128]{1,0:T(8,128)(2,1)S(1)}, u32[]{:S(2)}) copy-start(bf16[2048,128]{1,0:T(8,128)(2,1)S(1)} %collective-permute-done.x1) | copy-start | bytes 1572868
  30.2 7.9 %copy-start.27 = (bf16[2048,128]{1,0:T(8,128)(2,1)}, bf16[2048,128]{1,0:T(8,128)(2,1)S(1)}, u32[]{:S(2)}) copy-start(bf16[2048,128]{1,0:T(8,128)(2,1)S(1)} %collective-permute-done.2.x3) | copy-start | bytes 1572868
  30.9 24.8 %copy-start = (bf16[1,1024,256]{2,1,0:T(8,128)(2,1)}, bf16[1,1024,256]{2,1,0:T(8,128)(2,1)S(1)}, u32[]{:S(2)}) copy-start(bf16[1,1024,256]{2,1,0:T(8,128)(2,1)S(1)} %get-tuple-element.56.first) | copy-start | bytes 1572868
  30.9 24.8 %copy-start.2 = (bf16[1,1024,256]{2,1,0:T(8,128)(2,1)}, bf16[1,1024,256]{2,1,0:T(8,128)(2,1)S(1)}, u32[]{:S(2)}) copy-start(bf16[1,1024,256]{2,1,0:T(8,128)(2,1)S(1)} %get-tuple-element.55.last) | copy-start | bytes 1572868
  30.9 19.1 %copy-start.8 = (bf16[4,1024,128]{2,1,0:T(8,128)(2,1)S(1)}, bf16[4,1024,128]{2,1,0:T(8,128)(2,1)}, u32[]{:S(2)}) copy-start(bf16[4,1024,128]{2,1,0:T(8,128)(2,1)} %cot.3) | copy-start | bytes 3145732
  30.9 14.9 %collective-permute-start.3 = (bf16[1,1024,256]{2,1,0:T(8,128)(2,1)S(1)}, bf16[1,1024,256]{2,1,0:T(8,128)(2,1)S(1)}, u32[]{:S(2)}, u32[]{:S(2)}) collective-permute-start(bf16[1,1024,256]{2,1,0:T(8,128)(2,1)S(1)} %get-tuple-element.55.last), channel_id=1, source_target_pairs={{0,4},{4,8},{8,12},{12,16},{16,20},{20,24},{24,28},{28,32},{32,36}... | collective-permute-start | bytes 1572872 | tf_op jit(solution)/shard_map/ppermute | solution.py:544
  34.7 15.2 %collective-permute-start.7 = (bf16[1,1024,256]{2,1,0:T(8,128)(2,1)S(1)}, bf16[1,1024,256]{2,1,0:T(8,128)(2,1)S(1)}, u32[]{:S(2)}, u32[]{:S(2)}) collective-permute-start(bf16[1,1024,256]{2,1,0:T(8,128)(2,1)S(1)} %get-tuple-element.56.first), channel_id=1, source_target_pairs={{4,0},{8,4},{12,8},{16,12},{20,16},{24,20},{28,24},{32,28},{36,32}... | collective-permute-start | bytes 1572872 | tf_op jit(solution)/shard_map/ppermute | solution.py:545
  36.1 13.9 %copy-start.31 = (bf16[2048,128]{1,0:T(8,128)(2,1)}, bf16[2048,128]{1,0:T(8,128)(2,1)S(1)}, u32[]{:S(2)}) copy-start(bf16[2048,128]{1,0:T(8,128)(2,1)S(1)} %collective-permute-done.6.x3) | copy-start | bytes 1572868
  45.8 9.9 %copy-start.4 = (bf16[1,1024,256]{2,1,0:T(8,128)(2,1)}, bf16[1,1024,256]{2,1,0:T(8,128)(2,1)S(1)}, u32[]{:S(2)}) copy-start(bf16[1,1024,256]{2,1,0:T(8,128)(2,1)S(1)} %collective-permute-done.3.up) | copy-start | bytes 1572868
  50.0 5.7 %copy-start.6 = (bf16[1,1024,256]{2,1,0:T(8,128)(2,1)}, bf16[1,1024,256]{2,1,0:T(8,128)(2,1)S(1)}, u32[]{:S(2)}) copy-start(bf16[1,1024,256]{2,1,0:T(8,128)(2,1)S(1)} %collective-permute-done.7.down) | copy-start | bytes 1572868
  55.7 35.9 %copy-start.21 = (bf16[4,1024,128]{2,1,0:T(8,128)(2,1)}, bf16[4,1024,128]{2,1,0:T(8,128)(2,1)S(1)}, u32[]{:S(2)}) copy-start(bf16[4,1024,128]{2,1,0:T(8,128)(2,1)S(1)} %get-tuple-element.70.feat) | copy-start | bytes 3145732
  96.6 1.3 copy-start.12
  98.0 0.7 copy-start.33
  98.7 31.9 %all-to-all-start.1 = ((bf16[32,8,32,128]{3,2,1,0:T(8,128)(2,1)}), bf16[32,8,32,128]{3,2,1,0:T(8,128)(2,1)S(1)}, u32[]{:S(2)}, u32[]{:S(2)}) async-start(bf16[32,8,32,128]{3,2,1,0:T(8,128)(2,1)} %copy-done.12), calls=%async_computation.1 | async-start | bytes 4194304 | tf_op jit(solution)/shard_map/all_to_all | solution.py:606
  130.6 1.2 copy-start.9
  131.8 1.6 copy-start.11
  133.4 1.2 copy-start.22
  134.6 6.9 %copy-start.1 = (bf16[1,1024,256]{2,1,0:T(8,128)(2,1)S(1)}, bf16[1,1024,256]{2,1,0:T(8,128)(2,1)}, u32[]{:S(2)}) copy-start(bf16[1,1024,256]{2,1,0:T(8,128)(2,1)} %copy-done) | copy-start | bytes 1572868
  134.6 6.9 %copy-start.3 = (bf16[1,1024,256]{2,1,0:T(8,128)(2,1)S(1)}, bf16[1,1024,256]{2,1,0:T(8,128)(2,1)}, u32[]{:S(2)}) copy-start(bf16[1,1024,256]{2,1,0:T(8,128)(2,1)} %copy-done.2) | copy-start | bytes 1572868
  134.6 7.0 %copy-start.5 = (bf16[1,1024,256]{2,1,0:T(8,128)(2,1)S(1)}, bf16[1,1024,256]{2,1,0:T(8,128)(2,1)}, u32[]{:S(2)}) copy-start(bf16[1,1024,256]{2,1,0:T(8,128)(2,1)} %copy-done.4) | copy-start | bytes 1572868
  134.6 7.0 %copy-start.7 = (bf16[1,1024,256]{2,1,0:T(8,128)(2,1)S(1)}, bf16[1,1024,256]{2,1,0:T(8,128)(2,1)}, u32[]{:S(2)}) copy-start(bf16[1,1024,256]{2,1,0:T(8,128)(2,1)} %copy-done.6) | copy-start | bytes 1572868
  137.1 16.3 %collective-permute-start.8 = (bf16[1,1024,256]{2,1,0:T(8,128)(2,1)S(1)}, bf16[1,1024,256]{2,1,0:T(8,128)(2,1)S(1)}, u32[]{:S(2)}, u32[]{:S(2)}) collective-permute-start(bf16[1,1024,256]{2,1,0:T(8,128)(2,1)S(1)} %get-tuple-element.72.glast), channel_id=1, source_target_pairs={{0,4},{4,8},{8,12},{12,16},{16,20},{20,24},{24,28},{28,32},{32,36}... | collective-permute-start | bytes 1572872 | tf_op jit(solution)/shard_map/ppermute | solution.py:544
  140.3 13.1 %collective-permute-start.9 = (bf16[1,1024,256]{2,1,0:T(8,128)(2,1)S(1)}, bf16[1,1024,256]{2,1,0:T(8,128)(2,1)S(1)}, u32[]{:S(2)}, u32[]{:S(2)}) collective-permute-start(bf16[1,1024,256]{2,1,0:T(8,128)(2,1)S(1)} %get-tuple-element.73.gfirst), channel_id=1, source_target_pairs={{4,0},{8,4},{12,8},{16,12},{20,16},{24,20},{28,24},{32,28},{36,32}... | collective-permute-start | bytes 1572872 | tf_op jit(solution)/shard_map/ppermute | solution.py:545
  145.5 5.7 %copy-start.16 = (bf16[2,1024,128]{2,1,0:T(8,128)(2,1)S(1)}, bf16[2,1024,128]{2,1,0:T(8,128)(2,1)}, u32[]{:S(2)}) copy-start(bf16[2,1024,128]{2,1,0:T(8,128)(2,1)} %copy-done.15) | copy-start | bytes 1572868
  145.5 5.7 %copy-start.30 = (bf16[2048,128]{1,0:T(8,128)(2,1)S(1)}, bf16[2048,128]{1,0:T(8,128)(2,1)}, u32[]{:S(2)}) copy-start(bf16[2048,128]{1,0:T(8,128)(2,1)} %copy-done.29) | copy-start | bytes 1572868
  145.5 5.7 %copy-start.32 = (bf16[2048,128]{1,0:T(8,128)(2,1)S(1)}, bf16[2048,128]{1,0:T(8,128)(2,1)}, u32[]{:S(2)}) copy-start(bf16[2048,128]{1,0:T(8,128)(2,1)} %copy-done.31) | copy-start | bytes 1572868
  148.9 22.9 %collective-permute-start.14 = (bf16[2048,128]{1,0:T(8,128)(2,1)}, bf16[2048,128]{1,0:T(8,128)(2,1)}, u32[]{:S(2)}, u32[]{:S(2)}) collective-permute-start(bf16[2048,128]{1,0:T(8,128)(2,1)} %get-tuple-element.83), channel_id=1, source_target_pairs={{0,1},{1,0},{2,3},{3,2},{4,5},{5,4},{6,7},{7,6},{8,9},{9,8},{10,11... | collective-permute-start | bytes 1572872 | tf_op jit(solution)/shard_map/ppermute | solution.py:541
  151.2 1.9 copy-start.40
  153.0 7.0 %copy-start.14 = (bf16[2048,128]{1,0:T(8,128)(2,1)S(1)}, bf16[2048,128]{1,0:T(8,128)(2,1)}, u32[]{:S(2)}) copy-start(bf16[2048,128]{1,0:T(8,128)(2,1)} %copy-done.13) | copy-start | bytes 1572868
  153.1 7.0 %copy-start.24 = (bf16[2048,128]{1,0:T(8,128)(2,1)S(1)}, bf16[2048,128]{1,0:T(8,128)(2,1)}, u32[]{:S(2)}) copy-start(bf16[2048,128]{1,0:T(8,128)(2,1)} %copy-done.23) | copy-start | bytes 1572868
  153.1 7.0 %copy-start.26 = (bf16[2048,128]{1,0:T(8,128)(2,1)S(1)}, bf16[2048,128]{1,0:T(8,128)(2,1)}, u32[]{:S(2)}) copy-start(bf16[2048,128]{1,0:T(8,128)(2,1)} %copy-done.25) | copy-start | bytes 1572868
  153.1 7.0 %copy-start.28 = (bf16[2048,128]{1,0:T(8,128)(2,1)S(1)}, bf16[2048,128]{1,0:T(8,128)(2,1)}, u32[]{:S(2)}) copy-start(bf16[2048,128]{1,0:T(8,128)(2,1)} %copy-done.27) | copy-start | bytes 1572868
  153.3 26.0 %collective-permute-start.13 = (bf16[2048,128]{1,0:T(8,128)(2,1)}, bf16[2048,128]{1,0:T(8,128)(2,1)}, u32[]{:S(2)}, u32[]{:S(2)}) collective-permute-start(bf16[2048,128]{1,0:T(8,128)(2,1)} %get-tuple-element.81), channel_id=1, source_target_pairs={{0,1},{1,0},{2,3},{3,2},{4,5},{5,4},{6,7},{7,6},{8,9},{9,8},{10,11... | collective-permute-start | bytes 1572872 | tf_op jit(solution)/shard_map/ppermute | solution.py:541
  156.9 3.9 %copy-start.17 = (f32[2048,128]{1,0:T(8,128)}, f32[2048,128]{1,0:T(8,128)S(1)}, u32[]{:S(2)}) copy-start(f32[2048,128]{1,0:T(8,128)S(1)} %get-tuple-element.78) | copy-start | bytes 3145732
  156.9 3.9 %copy-start.19 = (f32[2048,128]{1,0:T(8,128)}, f32[2048,128]{1,0:T(8,128)S(1)}, u32[]{:S(2)}) copy-start(f32[2048,128]{1,0:T(8,128)S(1)} %get-tuple-element.76.own) | copy-start | bytes 3145732
  156.9 20.4 %collective-permute-start.11 = (bf16[2048,128]{1,0:T(8,128)(2,1)}, bf16[2048,128]{1,0:T(8,128)(2,1)}, u32[]{:S(2)}, u32[]{:S(2)}) collective-permute-start(bf16[2048,128]{1,0:T(8,128)(2,1)} %get-tuple-element.79), channel_id=1, source_target_pairs={{0,1},{1,0},{2,3},{3,2},{4,5},{5,4},{6,7},{7,6},{8,9},{9,8},{10,11... | collective-permute-start | bytes 1572872 | tf_op jit(solution)/shard_map/ppermute | solution.py:541
  160.0 1.0 copy-start.34
  162.0 34.7 %all-to-all-start.2 = ((bf16[32,88,128]{2,1,0:T(8,128)(2,1)}), bf16[32,88,128]{2,1,0:T(8,128)(2,1)S(1)}, u32[]{:S(2)}, u32[]{:S(2)}) async-start(bf16[32,88,128]{2,1,0:T(8,128)(2,1)} %shard_map.138), calls=%async_computation.2 | async-start | bytes 1441792 | tf_op jit(solution)/shard_map/all_to_all | solution.py:676
  171.8 5.6 %copy-start.18 = (f32[2048,128]{1,0:T(8,128)S(1)}, f32[2048,128]{1,0:T(8,128)}, u32[]{:S(2)}) copy-start(f32[2048,128]{1,0:T(8,128)} %copy-done.17) | copy-start | bytes 3145732
  173.1 21.5 %collective-permute-start.15 = (bf16[2048,128]{1,0:T(8,128)(2,1)S(1)}, bf16[2048,128]{1,0:T(8,128)(2,1)S(1)}, u32[]{:S(2)}, u32[]{:S(2)}) collective-permute-start(bf16[2048,128]{1,0:T(8,128)(2,1)S(1)} %add_convert_fusion), channel_id=1, source_target_pairs={{0,2},{1,3},{2,0},{3,1},{4,6},{5,7},{6,4},{7,5},{8,10},{9,11},{10,... | collective-permute-start | bytes 1572872 | tf_op jit(solution)/shard_map/ppermute | solution.py:541
  176.3 21.0 %collective-permute-start.10 = (bf16[2048,128]{1,0:T(8,128)(2,1)}, bf16[2048,128]{1,0:T(8,128)(2,1)S(1)}, u32[]{:S(2)}, u32[]{:S(2)}) collective-permute-start(bf16[2048,128]{1,0:T(8,128)(2,1)} %get-tuple-element.77), channel_id=1, source_target_pairs={{0,1},{1,0},{2,3},{3,2},{4,5},{5,4},{6,7},{7,6},{8,9},{9,8},{10,11... | collective-permute-start | bytes 1572872 | tf_op jit(solution)/shard_map/ppermute | solution.py:541
  179.3 26.6 %copy-start.20 = (f32[2048,128]{1,0:T(8,128)S(1)}, f32[2048,128]{1,0:T(8,128)}, u32[]{:S(2)}) copy-start(f32[2048,128]{1,0:T(8,128)} %copy-done.19) | copy-start | bytes 3145732
  179.3 26.6 %collective-permute-start.12 = (bf16[2048,128]{1,0:T(8,128)(2,1)}, bf16[2048,128]{1,0:T(8,128)(2,1)}, u32[]{:S(2)}, u32[]{:S(2)}) collective-permute-start(bf16[2048,128]{1,0:T(8,128)(2,1)} %add_convert_fusion.1), channel_id=1, source_target_pairs={{0,2},{1,3},{2,0},{3,1},{4,6},{5,7},{6,4},{7,5},{8,10},{9,11},{10,... | collective-permute-start | bytes 1572872 | tf_op jit(solution)/shard_map/ppermute | solution.py:541

commit v6 on v5

--- a/solution.py
+++ b/solution.py
@@ -238,35 +238,40 @@
         return 0
 
     lax.fori_loop(0, height // 16, unpack, 0)
-    for n in range(2 * wide // 512):
-        lanes = pl.ds(n * 512, 512)
-        spectra[:, lanes] = jnp.dot(fwd[...], stacked[:, lanes], preferred_element_type=F32)
-
-    def products(n, _):
-        at = pl.multiple_of(n * 16, 16)
-        low, high = pl.ds(at, 16), pl.ds(at + height, 16)
-        cr, ci = colr[low, :], coli[low, :]
-        sr = jnp.zeros((16, channels), F32)
-        si = jnp.zeros((16, channels), F32)
-        for k in range(half):
-            lanes = pl.ds(k * channels, channels)
-            more = pl.ds(k * channels + wide, channels)
-            tr, ti = spectra[low, lanes], spectra[high, lanes]
-            fr, fi = spectra[low, more], spectra[high, more]
-            sr = sr + (fr * tr + fi * ti)
-            si = si + (fi * tr - fr * ti)
-            stacked[low, lanes] = (tr * cr - ti * ci).astype(BF)
-            stacked[high, lanes] = (tr * ci + ti * cr).astype(BF)
-            stacked[low, more] = (fr * cr + fi * ci).astype(BF)
-            stacked[high, more] = (fi * cr - fr * ci).astype(BF)
-        er[low, :] = sr
-        ei[low, :] = si
-        return 0
-
-    lax.fori_loop(0, height // 16, products, 0)
-    for n in range(2 * wide // 512):
-        lanes = pl.ds(n * 512, 512)
-        spectra[:, lanes] = jnp.dot(inv[...], stacked[:, lanes], preferred_element_type=F32)
+    several = 4
+
+    def transform(matrix, n):
+        for offset in (0, wide):
+            lanes = pl.ds(n * several * channels + offset, several * channels)
+            spectra[:, lanes] = jnp.dot(matrix[...], stacked[:, lanes], preferred_element_type=F32)
+
+    def products(n):
+        for at in range(0, height, 16):
+            low, high = pl.ds(at, 16), pl.ds(at + height, 16)
+            cr, ci = colr[low, :], coli[low, :]
+            sr = si = None
+            for k in range(n * several, (n + 1) * several):
+                lanes = pl.ds(k * channels, channels)
+                more = pl.ds(k * channels + wide, channels)
+                tr, ti = spectra[low, lanes], spectra[high, lanes]
+                fr, fi = spectra[low, more], spectra[high, more]
+                pr, pi = fr * tr + fi * ti, fi * tr - fr * ti
+                sr = pr if sr is None else sr + pr
+                si = pi if si is None else si + pi
+                stacked[low, lanes] = (tr * cr - ti * ci).astype(BF)
+                stacked[high, lanes] = (tr * ci + ti * cr).astype(BF)
+                stacked[low, more] = (fr * cr + fi * ci).astype(BF)
+                stacked[high, more] = (fi * cr - fr * ci).astype(BF)
+            er[low, :] = sr if n == 0 else er[low, :] + sr
+            ei[low, :] = si if n == 0 else ei[low, :] + si
+
+    steps = half // several
+    transform(fwd, 0)
+    for n in range(steps):
+        if n + 1 < steps:
+            transform(fwd, n + 1)
+        products(n)
+        transform(inv, n)
 
     e = jnp.concatenate([er[...], ei[...]], axis=0) * (1.0 / height)
     high = e.astype(BF)

time: 209 us -> 209 us (level)
  no operation moved by 1% of the time
where the time goes in v6:
time: 209 us; the launch traced here: 208 us
  waiting for transfers between devices  71.6 us (34%)
  starting transfers between devices  42.8 us (20%)
  Pallas kernels  39 us (19%)
  blocking collectives  35.9 us (17%)
  local copies, waits for them, and re-layouts  10.2 us (5%)
  other arithmetic  4.14 us (2%)
  matrix products  2.56 us (1%)
    all_to_all x1, blocking collectives, local(): recv = lax.all_to_all(send, 'grid', split_axis=0, concat_axis=0, tiled=True)  35.9 us
    ppermute x12, waiting for transfers between devices, flipped(): return lax.ppermute(value, 'ch', [(i, i ^ bit) for i in range(parts)])  34 us
    all_to_all x1, waiting for transfers between devices, local(): lax.all_to_all(turned, 'grid', split_axis=0, concat_axis=0, tiled=True)  25.8 us
    ppermute x12, starting transfers between devices, flipped(): return lax.ppermute(value, 'ch', [(i, i ^ bit) for i in range(parts)])  17.8 us
    all_to_all x1, starting transfers between devices, local(): lax.all_to_all(packed, 'grid', split_axis=0, concat_axis=0, tiled=True)  9.85 us
    unnamed x85, local copies, waits for them, and re-layouts  8.92 us
    ppermute x2, waiting for transfers between devices, halos(): up = lax.ppermute(last, 'grid', [(i, i + 1) for i in range(owners - 1)])  7.73 us
    pallas_call x1, Pallas kernels, local(): kernel_call(tables_kernel, [((width, width), BF), ((width, width), BF), (...  7.19 us
  transfers between devices with their start and end apart: 18, of which 6 were waited for; matrix products, arithmetic and copies ran while one was open for 3% of the time, Pallas kernels for 12%

profile of v6, /device:TPU:1, one launch (start us, length us, event | category | flops | bytes accessed | tf_op | source)
XLA Modules:
  0.0 207.7 jit_solution(1930183833452691963)
XLA Ops:
  0.7 1.2 slice_bitcast_fusion.1
  1.9 3.8 %collective-permute-start.1 = (bf16[2048,128]{1,0:T(8,128)(2,1)S(1)}, bf16[2048,128]{1,0:T(8,128)(2,1)S(1)}, u32[]{:S(2)}, u32[]{:S(2)}) collective-permute-start(bf16[2048,128]{1,0:T(8,128)(2,1)S(1)} %pad_maximum_fusion.x0), channel_id=1, source_target_pairs={{0,2},{1,3},{2,0},{3,1},{4,6},{5,7},{6,4},{7,5},{8,10},{9,11},{10,... | collective-permute-start | bytes 1572872 | tf_op jit(solution)/shard_map/ppermute | solution.py:546
  5.7 0.1 collective-permute-start.5
  5.9 1.1 collective-permute-start
  7.0 10.1 %collective-permute-done.1.x2 = bf16[2048,128]{1,0:T(8,128)(2,1)S(1)} collective-permute-done((bf16[2048,128]{1,0:T(8,128)(2,1)S(1)}, bf16[2048,128]{1,0:T(8,128)(2,1)S(1)}, u32[]{:S(2)}, u32[]{:S(2)}) %collective-permute-start.1) | collective-permute-done | bytes 524320 | tf_op jit(solution)/shard_map/ppermute | solution.py:546
  17.1 2.5 %collective-permute-start.2 = (bf16[2048,128]{1,0:T(8,128)(2,1)S(1)}, bf16[2048,128]{1,0:T(8,128)(2,1)S(1)}, u32[]{:S(2)}, u32[]{:S(2)}) collective-permute-start(bf16[2048,128]{1,0:T(8,128)(2,1)S(1)} %collective-permute-done.1.x2), channel_id=1, source_target_pairs={{0,1},{1,0},{2,3},{3,2},{4,5},{5,4},{6,7},{7,6},{8,9},{9,8},{10,11... | collective-permute-start | bytes 1572872 | tf_op jit(solution)/shard_map/ppermute | solution.py:546
  19.6 0.0 collective-permute-start.4
  19.7 0.1 pad_add_fusion.where
  19.7 0.9 copy-done.35
  20.7 0.9 copy-done.37
  21.6 0.8 copy-done.38
  22.3 7.2 %shard_map.126 = (bf16[1024,1024]{1,0:T(8,128)(2,1)S(1)}, bf16[1024,1024]{1,0:T(8,128)(2,1)S(1)}, bf16[32,1024]{1,0:T(8,128)(2,1)S(1)}, bf16[256,256]{1,0:T(8,12...) custom-call(s32[2]{0:T(128)S(1)} %pad_add_fusion.where, ...), custom_call_target="tpu_custom_call" | custom-call | tf_op jit(solution)/shard_map/pallas_call | solution.py:561
  29.5 0.0 collective-permute-done.5.x2
  29.6 0.6 collective-permute-start.6
  30.1 0.0 collective-permute-done.x1
  30.1 0.0 collective-permute-done.2.x3
  30.2 0.7 shard_map.127
  30.9 0.0 copy-start.8
  30.9 3.8 %collective-permute-start.3 = (bf16[1,1024,256]{2,1,0:T(8,128)(2,1)S(1)}, bf16[1,1024,256]{2,1,0:T(8,128)(2,1)S(1)}, u32[]{:S(2)}, u32[]{:S(2)}) collective-permute-start(bf16[1,1024,256]{2,1,0:T(8,128)(2,1)S(1)} %get-tuple-element.55.last), channel_id=1, source_target_pairs={{0,4},{4,8},{8,12},{12,16},{16,20},{20,24},{24,28},{28,32},{32,36}... | collective-permute-start | bytes 1572872 | tf_op jit(solution)/shard_map/ppermute | solution.py:549
  34.7 1.3 collective-permute-start.7
  36.0 0.0 collective-permute-done.4.x1
  36.1 1.9 shard_map.128.middle
  38.1 7.7 %collective-permute-done.3.up = bf16[1,1024,256]{2,1,0:T(8,128)(2,1)S(1)} collective-permute-done((bf16[1,1024,256]{2,1,0:T(8,128)(2,1)S(1)}, bf16[1,1024,256]{2,1,0:T(8,128)(2,1)S(1)}, u32[]{:S(2)}, u32[]{:S(2)}) %collective-permute-start.3) | collective-permute-done | bytes 524320 | tf_op jit(solution)/shard_map/ppermute | solution.py:549
  45.8 4.2 %collective-permute-done.7.down = bf16[1,1024,256]{2,1,0:T(8,128)(2,1)S(1)} collective-permute-done((bf16[1,1024,256]{2,1,0:T(8,128)(2,1)S(1)}, bf16[1,1024,256]{2,1,0:T(8,128)(2,1)S(1)}, u32[]{:S(2)}, u32[]{:S(2)}) %collective-permute-start.7) | collective-permute-done | bytes 524320 | tf_op jit(solution)/shard_map/ppermute | solution.py:550
  50.0 5.7 %shard_map.129 = (bf16[32,8,32,128]{3,2,1,0:T(8,128)(2,1)S(1)}, bf16[4,1024,128]{2,1,0:T(8,128)(2,1)S(1)}) custom-call(bf16[1,1024,256]{2,1,0:T(8,128)(2,1)S(1)} %collective-permute-done.3.up, bf16[1,1024,256]{2,1,0:T(8,128)(2,1)S(1)} %get-tuple-element.56.first, bf16[2,1024,256]{2,1,0:T(8,128)(2,1)S(1)} %shard_map.128.middle, ...), custom_call_target="tpu_custom_call" | custom-call | tf_op jit(solution)/shard_map/pallas_call | solution.py:600
  55.7 0.0 copy-start.21
  55.7 35.9 %all_to_all.15.recv = bf16[32,8,32,128]{3,2,1,0:T(8,128)(2,1)S(1)} all-to-all(bf16[32,8,32,128]{3,2,1,0:T(8,128)(2,1)S(1)} %get-tuple-element.60), channel_id=1, replica_groups=mesh['grid'=32,'ch'=4] {'grid'}, dimensions={0} | all-to-all | bytes 4194304 | tf_op jit(solution)/shard_map/all_to_all | solution.py:603
  91.6 4.6 %shard_map.130 = (bf16[32,8,32,128]{3,2,1,0:T(8,128)(2,1)S(1)}, bf16[1024,128]{1,0:T(8,128)(2,1)S(1)}, f32[128,128]{1,0:T(8,128)S(1)}) custom-call(bf16[32,8,32,128]{3,2,1,0:T(8,128)(2,1)S(1)} %all_to_all.15.recv, f32[4,16,128]{2,1,0:T(8,128)S(1)} %get-tuple-element.61.coef, f32[1,16,128]{2,1,0:T(8,128)S(1)} %get-tuple-element.62.keep, ...), custom_call_target="tpu_custom_call" | custom-call | tf_op jit(solution)/shard_map/pallas_call | solution.py:605
  96.3 1.3 copy-done.12
  97.6 0.7 copy-done.33
  98.3 5.4 %all-to-all-start.1 = ((bf16[32,8,32,128]{3,2,1,0:T(8,128)(2,1)}), bf16[32,8,32,128]{3,2,1,0:T(8,128)(2,1)S(1)}, u32[]{:S(2)}, u32[]{:S(2)}) async-start(bf16[32,8,32,128]{3,2,1,0:T(8,128)(2,1)} %copy-done.12), calls=%async_computation.1 | async-start | bytes 4194304 | tf_op jit(solution)/shard_map/all_to_all | solution.py:611
  103.8 0.1 pad.3.clone
  103.9 0.6 convert_element_type.25
  104.5 25.8 %all-to-all-done.1.recv = bf16[32,8,32,128]{3,2,1,0:T(8,128)(2,1)S(1)} async-done(((bf16[32,8,32,128]{3,2,1,0:T(8,128)(2,1)}), bf16[32,8,32,128]{3,2,1,0:T(8,128)(2,1)S(1)}, u32[]{:S(2)}, u32[]{:S(2)}) %all-to-all-start.1) | async-done | bytes 2097184 | tf_op jit(solution)/shard_map/all_to_all | solution.py:611
  130.2 1.2 copy-done.9
  131.5 1.6 copy-done.11
  133.1 1.2 copy-done.22
  134.3 2.5 %shard_map.131 = (bf16[4,1024,128]{2,1,0:T(8,128)(2,1)}, bf16[1,1024,256]{2,1,0:T(8,128)(2,1)S(1)}, bf16[2,1024,256]{2,1,0:T(8,128)(2,1)S(1)}, bf16[1,1024,256]{2,1,0:T(8,128)(2,1)S(1)}) custom-call(bf16[32,8,32,128]{3,2,1,0:T(8,128)(2,1)S(1)} %all-to-all-done.1.recv, bf16[1024,1024]{1,0:T(8,128)(2,1)S(1)} %copy-done.11, ...), custom_call_target="tpu_custom_call" | custom-call | tf_op jit(solution)/shard_map/pallas_call | solution.py:612
  136.7 3.1 %collective-permute-start.8 = (bf16[1,1024,256]{2,1,0:T(8,128)(2,1)S(1)}, bf16[1,1024,256]{2,1,0:T(8,128)(2,1)S(1)}, u32[]{:S(2)}, u32[]{:S(2)}) collective-permute-start(bf16[1,1024,256]{2,1,0:T(8,128)(2,1)S(1)} %get-tuple-element.72.glast), channel_id=1, source_target_pairs={{0,4},{4,8},{8,12},{12,16},{16,20},{20,24},{24,28},{28,32},{32,36}... | collective-permute-start | bytes 1572872 | tf_op jit(solution)/shard_map/ppermute | solution.py:549
  139.9 1.5 collective-permute-start.9
  141.4 1.9 shard_map.136
  143.4 1.9 shard_map.137
  145.3 3.4 %shard_map.133 = (bf16[2,1024,256]{2,1,0:T(8,128)(2,1)S(1)}, f32[2048,128]{1,0:T(8,128)S(1)}, bf16[2048,128]{1,0:T(8,128)(2,1)}, f32[2048,128]{1,0:T(8,128)S(1)}, bf16[2048,128]{1,0:T(8,128)(2,1)}) custom-call(bf16[1,1024,256]{2,1,0:T(8,128)(2,1)S(1)} %get-tuple-element.73.gfirst, bf16[2,1024,256]{2,1,0:T(8,128)(2,1)S(1)} %get-tuple-element.74.gmiddle, ...), custom_call_target="tpu_custom_call" | custom-call | tf_op jit(solution)/shard_map/pallas_call | solution.py:618
  148.7 2.3 %collective-permute-start.14 = (bf16[2048,128]{1,0:T(8,128)(2,1)}, bf16[2048,128]{1,0:T(8,128)(2,1)}, u32[]{:S(2)}, u32[]{:S(2)}) collective-permute-start(bf16[2048,128]{1,0:T(8,128)(2,1)} %get-tuple-element.83), channel_id=1, source_target_pairs={{0,1},{1,0},{2,3},{3,2},{4,5},{5,4},{6,7},{7,6},{8,9},{9,8},{10,11... | collective-permute-start | bytes 1572872 | tf_op jit(solution)/shard_map/ppermute | solution.py:546
  151.1 1.8 fusion
  153.0 0.2 maximum_maximum_fusion.small
  153.1 0.1 collective-permute-start.13
  153.2 3.5 %shard_map.132 = (bf16[2,1024,256]{2,1,0:T(8,128)(2,1)S(1)}, f32[2048,128]{1,0:T(8,128)S(1)}, bf16[2048,128]{1,0:T(8,128)(2,1)}, f32[2048,128]{1,0:T(8,128)S(1)}, bf16[2048,128]{1,0:T(8,128)(2,1)}) custom-call(bf16[1,1024,256]{2,1,0:T(8,128)(2,1)S(1)} %collective-permute-done.8.gup, bf16[1,1024,256]{2,1,0:T(8,128)(2,1)S(1)} %get-tuple-element.73.gfirst, ...), custom_call_target="tpu_custom_call" | custom-call | tf_op jit(solution)/shard_map/pallas_call | solution.py:630
  156.8 2.9 %collective-permute-start.11 = (bf16[2048,128]{1,0:T(8,128)(2,1)}, bf16[2048,128]{1,0:T(8,128)(2,1)}, u32[]{:S(2)}, u32[]{:S(2)}) collective-permute-start(bf16[2048,128]{1,0:T(8,128)(2,1)} %get-tuple-element.79), channel_id=1, source_target_pairs={{0,1},{1,0},{2,3},{3,2},{4,5},{5,4},{6,7},{7,6},{8,9},{9,8},{10,11... | collective-permute-start | bytes 1572872 | tf_op jit(solution)/shard_map/ppermute | solution.py:546
  159.7 0.8 fusion.8
  160.5 0.1 add.11.grad_w
  160.5 0.1 copy-done.34
  160.6 1.0 shard_map.138
  161.6 9.8 %all-to-all-start.2 = ((bf16[32,88,128]{2,1,0:T(8,128)(2,1)}), bf16[32,88,128]{2,1,0:T(8,128)(2,1)S(1)}, u32[]{:S(2)}, u32[]{:S(2)}) async-start(bf16[32,88,128]{2,1,0:T(8,128)(2,1)} %shard_map.138), calls=%async_computation.2 | async-start | bytes 1441792 | tf_op jit(solution)/shard_map/all_to_all | solution.py:681
  171.4 0.0 copy-start.18
  171.5 1.2 add_convert_fusion
  172.7 3.3 %collective-permute-start.15 = (bf16[2048,128]{1,0:T(8,128)(2,1)S(1)}, bf16[2048,128]{1,0:T(8,128)(2,1)S(1)}, u32[]{:S(2)}, u32[]{:S(2)}) collective-permute-start(bf16[2048,128]{1,0:T(8,128)(2,1)S(1)} %add_convert_fusion), channel_id=1, source_target_pairs={{0,2},{1,3},{2,0},{3,1},{4,6},{5,7},{6,4},{7,5},{8,10},{9,11},{10,... | collective-permute-start | bytes 1572872 | tf_op jit(solution)/shard_map/ppermute | solution.py:546
  176.0 1.1 collective-permute-start.10
  177.0 1.9 add_convert_fusion.1
  179.0 15.3 %collective-permute-done.15.across = bf16[2048,128]{1,0:T(8,128)(2,1)S(1)} collective-permute-done((bf16[2048,128]{1,0:T(8,128)(2,1)S(1)}, bf16[2048,128]{1,0:T(8,128)(2,1)S(1)}, u32[]{:S(2)}, u32[]{:S(2)}) %collective-permute-start.15) | collective-permute-done | bytes 524320 | tf_op jit(solution)/shard_map/ppermute | solution.py:546
  194.2 2.0 shard_map.134.middle
  196.3 0.7 shard_map.139
  197.0 8.6 %collective-permute-done.12.across = bf16[2048,128]{1,0:T(8,128)(2,1)} collective-permute-done((bf16[2048,128]{1,0:T(8,128)(2,1)}, bf16[2048,128]{1,0:T(8,128)(2,1)}, u32[]{:S(2)}, u32[]{:S(2)}) %collective-permute-start.12) | collective-permute-done | bytes 524320 | tf_op jit(solution)/shard_map/ppermute | solution.py:546
  205.6 1.9 shard_map.135
  (89 shorter events, 0.3 us)
Async XLA Ops:
  0.6 5.1 %copy-start.39 = (bf16[4,1024,128]{2,1,0:T(8,128)(2,1)S(1)}, bf16[4,1024,128]{2,1,0:T(8,128)(2,1)}, u32[]{:S(2)}) copy-start(bf16[4,1024,128]{2,1,0:T(8,128)(2,1)} %param.7) | copy-start | bytes 3145732
  0.6 19.0 %copy-start.41 = (bf16[2,3,3,128]{3,0,2,1:T(2,128)(2,1)S(1)}, bf16[2,3,3,128]{3,0,2,1:T(2,128)(2,1)}, u32[]{:S(2)}) copy-start(bf16[2,3,3,128]{3,0,2,1:T(2,128)(2,1)} %param.10) | copy-start | bytes 13828
  0.7 19.1 %copy-start.36 = (bf16[512,128]{1,0:T(8,128)(2,1)S(1)}, bf16[512,128]{1,0:T(8,128)(2,1)}, u32[]{:S(2)}) copy-start(bf16[512,128]{1,0:T(8,128)(2,1)} %w_gate.1) | copy-start | bytes 393220
  1.9 34.2 %copy-start.13 = (bf16[2048,128]{1,0:T(8,128)(2,1)}, bf16[2048,128]{1,0:T(8,128)(2,1)S(1)}, u32[]{:S(2)}) copy-start(bf16[2048,128]{1,0:T(8,128)(2,1)S(1)} %pad_maximum_fusion.x0) | copy-start | bytes 1572868
  1.9 15.2 %collective-permute-start.1 = (bf16[2048,128]{1,0:T(8,128)(2,1)S(1)}, bf16[2048,128]{1,0:T(8,128)(2,1)S(1)}, u32[]{:S(2)}, u32[]{:S(2)}) collective-permute-start(bf16[2048,128]{1,0:T(8,128)(2,1)S(1)} %pad_maximum_fusion.x0), channel_id=1, source_target_pairs={{0,2},{1,3},{2,0},{3,1},{4,6},{5,7},{6,4},{7,5},{8,10},{9,11},{10,... | collective-permute-start | bytes 1572872 | tf_op jit(solution)/shard_map/ppermute | solution.py:546
  5.7 32.3 %copy-start.15 = (bf16[2,1024,128]{2,1,0:T(8,128)(2,1)}, bf16[2,1024,128]{2,1,0:T(8,128)(2,1)S(1)}, u32[]{:S(2)}) copy-start(bf16[2,1024,128]{2,1,0:T(8,128)(2,1)S(1)} %slice.11) | copy-start | bytes 1572868
  5.7 23.8 %collective-permute-start.5 = (bf16[2048,128]{1,0:T(8,128)(2,1)S(1)}, bf16[2048,128]{1,0:T(8,128)(2,1)S(1)}, u32[]{:S(2)}, u32[]{:S(2)}) collective-permute-start(bf16[2048,128]{1,0:T(8,128)(2,1)S(1)} %bitcast.13), channel_id=1, source_target_pairs={{0,2},{1,3},{2,0},{3,1},{4,6},{5,7},{6,4},{7,5},{8,10},{9,11},{10,... | collective-permute-start | bytes 1572872 | tf_op jit(solution)/shard_map/ppermute | solution.py:546
  5.9 24.3 %collective-permute-start = (bf16[2048,128]{1,0:T(8,128)(2,1)S(1)}, bf16[2048,128]{1,0:T(8,128)(2,1)S(1)}, u32[]{:S(2)}, u32[]{:S(2)}) collective-permute-start(bf16[2048,128]{1,0:T(8,128)(2,1)S(1)} %pad_maximum_fusion.x0), channel_id=1, source_target_pairs={{0,1},{1,0},{2,3},{3,2},{4,5},{5,4},{6,7},{7,6},{8,9},{9,8},{10,11... | collective-permute-start | bytes 1572872 | tf_op jit(solution)/shard_map/ppermute | solution.py:546
  17.1 19.0 %copy-start.23 = (bf16[2048,128]{1,0:T(8,128)(2,1)}, bf16[2048,128]{1,0:T(8,128)(2,1)S(1)}, u32[]{:S(2)}) copy-start(bf16[2048,128]{1,0:T(8,128)(2,1)S(1)} %collective-permute-done.1.x2) | copy-start | bytes 1572868
  17.1 13.1 %collective-permute-start.2 = (bf16[2048,128]{1,0:T(8,128)(2,1)S(1)}, bf16[2048,128]{1,0:T(8,128)(2,1)S(1)}, u32[]{:S(2)}, u32[]{:S(2)}) collective-permute-start(bf16[2048,128]{1,0:T(8,128)(2,1)S(1)} %collective-permute-done.1.x2), channel_id=1, source_target_pairs={{0,1},{1,0},{2,3},{3,2},{4,5},{5,4},{6,7},{7,6},{8,9},{9,8},{10,11... | collective-permute-start | bytes 1572872 | tf_op jit(solution)/shard_map/ppermute | solution.py:546
  19.6 16.4 %collective-permute-start.4 = (bf16[2048,128]{1,0:T(8,128)(2,1)S(1)}, bf16[2048,128]{1,0:T(8,128)(2,1)}, u32[]{:S(2)}, u32[]{:S(2)}) collective-permute-start(bf16[2048,128]{1,0:T(8,128)(2,1)S(1)} %bitcast.14), channel_id=1, source_target_pairs={{0,1},{1,0},{2,3},{3,2},{4,5},{5,4},{6,7},{7,6},{8,9},{9,8},{10,11... | collective-permute-start | bytes 1572872 | tf_op jit(solution)/shard_map/ppermute | solution.py:546
  19.7 1.0 copy-start.35
  20.7 0.9 copy-start.37
  21.6 0.8 copy-start.38
  29.5 8.5 %copy-start.10 = (bf16[1024,1024]{1,0:T(8,128)(2,1)}, bf16[1024,1024]{1,0:T(8,128)(2,1)S(1)}, u32[]{:S(2)}) copy-start(bf16[1024,1024]{1,0:T(8,128)(2,1)S(1)} %get-tuple-element.69.mat) | copy-start | bytes 6291460
  29.6 8.5 %copy-start.29 = (bf16[2048,128]{1,0:T(8,128)(2,1)}, bf16[2048,128]{1,0:T(8,128)(2,1)S(1)}, u32[]{:S(2)}) copy-start(bf16[2048,128]{1,0:T(8,128)(2,1)S(1)} %collective-permute-done.5.x2) | copy-start | bytes 1572868
  29.6 6.5 %collective-permute-start.6 = (bf16[2048,128]{1,0:T(8,128)(2,1)S(1)}, bf16[2048,128]{1,0:T(8,128)(2,1)S(1)}, u32[]{:S(2)}, u32[]{:S(2)}) collective-permute-start(bf16[2048,128]{1,0:T(8,128)(2,1)S(1)} %collective-permute-done.5.x2), channel_id=1, source_target_pairs={{0,1},{1,0},{2,3},{3,2},{4,5},{5,4},{6,7},{7,6},{8,9},{9,8},{10,11... | collective-permute-start | bytes 1572872 | tf_op jit(solution)/shard_map/ppermute | solution.py:546
  30.1 7.9 %copy-start.25 = (bf16[2048,128]{1,0:T(8,128)(2,1)}, bf16[2048,128]{1,0:T(8,128)(2,1)S(1)}, u32[]{:S(2)}) copy-start(bf16[2048,128]{1,0:T(8,128)(2,1)S(1)} %collective-permute-done.x1) | copy-start | bytes 1572868
  30.2 7.9 %copy-start.27 = (bf16[2048,128]{1,0:T(8,128)(2,1)}, bf16[2048,128]{1,0:T(8,128)(2,1)S(1)}, u32[]{:S(2)}) copy-start(bf16[2048,128]{1,0:T(8,128)(2,1)S(1)} %collective-permute-done.2.x3) | copy-start | bytes 1572868
  30.9 24.8 %copy-start = (bf16[1,1024,256]{2,1,0:T(8,128)(2,1)}, bf16[1,1024,256]{2,1,0:T(8,128)(2,1)S(1)}, u32[]{:S(2)}) copy-start(bf16[1,1024,256]{2,1,0:T(8,128)(2,1)S(1)} %get-tuple-element.56.first) | copy-start | bytes 1572868
  30.9 24.8 %copy-start.2 = (bf16[1,1024,256]{2,1,0:T(8,128)(2,1)}, bf16[1,1024,256]{2,1,0:T(8,128)(2,1)S(1)}, u32[]{:S(2)}) copy-start(bf16[1,1024,256]{2,1,0:T(8,128)(2,1)S(1)} %get-tuple-element.55.last) | copy-start | bytes 1572868
  30.9 19.1 %copy-start.8 = (bf16[4,1024,128]{2,1,0:T(8,128)(2,1)S(1)}, bf16[4,1024,128]{2,1,0:T(8,128)(2,1)}, u32[]{:S(2)}) copy-start(bf16[4,1024,128]{2,1,0:T(8,128)(2,1)} %cot.3) | copy-start | bytes 3145732
  30.9 14.9 %collective-permute-start.3 = (bf16[1,1024,256]{2,1,0:T(8,128)(2,1)S(1)}, bf16[1,1024,256]{2,1,0:T(8,128)(2,1)S(1)}, u32[]{:S(2)}, u32[]{:S(2)}) collective-permute-start(bf16[1,1024,256]{2,1,0:T(8,128)(2,1)S(1)} %get-tuple-element.55.last), channel_id=1, source_target_pairs={{0,4},{4,8},{8,12},{12,16},{16,20},{20,24},{24,28},{28,32},{32,36}... | collective-permute-start | bytes 1572872 | tf_op jit(solution)/shard_map/ppermute | solution.py:549
  34.7 15.2 %collective-permute-start.7 = (bf16[1,1024,256]{2,1,0:T(8,128)(2,1)S(1)}, bf16[1,1024,256]{2,1,0:T(8,128)(2,1)S(1)}, u32[]{:S(2)}, u32[]{:S(2)}) collective-permute-start(bf16[1,1024,256]{2,1,0:T(8,128)(2,1)S(1)} %get-tuple-element.56.first), channel_id=1, source_target_pairs={{4,0},{8,4},{12,8},{16,12},{20,16},{24,20},{28,24},{32,28},{36,32}... | collective-permute-start | bytes 1572872 | tf_op jit(solution)/shard_map/ppermute | solution.py:550
  36.1 13.9 %copy-start.31 = (bf16[2048,128]{1,0:T(8,128)(2,1)}, bf16[2048,128]{1,0:T(8,128)(2,1)S(1)}, u32[]{:S(2)}) copy-start(bf16[2048,128]{1,0:T(8,128)(2,1)S(1)} %collective-permute-done.6.x3) | copy-start | bytes 1572868
  45.8 9.9 %copy-start.4 = (bf16[1,1024,256]{2,1,0:T(8,128)(2,1)}, bf16[1,1024,256]{2,1,0:T(8,128)(2,1)S(1)}, u32[]{:S(2)}) copy-start(bf16[1,1024,256]{2,1,0:T(8,128)(2,1)S(1)} %collective-permute-done.3.up) | copy-start | bytes 1572868
  50.0 5.7 %copy-start.6 = (bf16[1,1024,256]{2,1,0:T(8,128)(2,1)}, bf16[1,1024,256]{2,1,0:T(8,128)(2,1)S(1)}, u32[]{:S(2)}) copy-start(bf16[1,1024,256]{2,1,0:T(8,128)(2,1)S(1)} %collective-permute-done.7.down) | copy-start | bytes 1572868
  55.7 35.9 %copy-start.21 = (bf16[4,1024,128]{2,1,0:T(8,128)(2,1)}, bf16[4,1024,128]{2,1,0:T(8,128)(2,1)S(1)}, u32[]{:S(2)}) copy-start(bf16[4,1024,128]{2,1,0:T(8,128)(2,1)S(1)} %get-tuple-element.70.feat) | copy-start | bytes 3145732
  96.3 1.3 copy-start.12
  97.6 0.7 copy-start.33
  98.3 31.9 %all-to-all-start.1 = ((bf16[32,8,32,128]{3,2,1,0:T(8,128)(2,1)}), bf16[32,8,32,128]{3,2,1,0:T(8,128)(2,1)S(1)}, u32[]{:S(2)}, u32[]{:S(2)}) async-start(bf16[32,8,32,128]{3,2,1,0:T(8,128)(2,1)} %copy-done.12), calls=%async_computation.1 | async-start | bytes 4194304 | tf_op jit(solution)/shard_map/all_to_all | solution.py:611
  130.2 1.2 copy-start.9
  131.5 1.6 copy-start.11
  133.1 1.2 copy-start.22
  134.3 7.1 %copy-start.1 = (bf16[1,1024,256]{2,1,0:T(8,128)(2,1)S(1)}, bf16[1,1024,256]{2,1,0:T(8,128)(2,1)}, u32[]{:S(2)}) copy-start(bf16[1,1024,256]{2,1,0:T(8,128)(2,1)} %copy-done) | copy-start | bytes 1572868
  134.3 7.1 %copy-start.3 = (bf16[1,1024,256]{2,1,0:T(8,128)(2,1)S(1)}, bf16[1,1024,256]{2,1,0:T(8,128)(2,1)}, u32[]{:S(2)}) copy-start(bf16[1,1024,256]{2,1,0:T(8,128)(2,1)} %copy-done.2) | copy-start | bytes 1572868
  134.3 7.1 %copy-start.5 = (bf16[1,1024,256]{2,1,0:T(8,128)(2,1)S(1)}, bf16[1,1024,256]{2,1,0:T(8,128)(2,1)}, u32[]{:S(2)}) copy-start(bf16[1,1024,256]{2,1,0:T(8,128)(2,1)} %copy-done.4) | copy-start | bytes 1572868
  134.3 7.1 %copy-start.7 = (bf16[1,1024,256]{2,1,0:T(8,128)(2,1)S(1)}, bf16[1,1024,256]{2,1,0:T(8,128)(2,1)}, u32[]{:S(2)}) copy-start(bf16[1,1024,256]{2,1,0:T(8,128)(2,1)} %copy-done.6) | copy-start | bytes 1572868
  136.7 16.5 %collective-permute-start.8 = (bf16[1,1024,256]{2,1,0:T(8,128)(2,1)S(1)}, bf16[1,1024,256]{2,1,0:T(8,128)(2,1)S(1)}, u32[]{:S(2)}, u32[]{:S(2)}) collective-permute-start(bf16[1,1024,256]{2,1,0:T(8,128)(2,1)S(1)} %get-tuple-element.72.glast), channel_id=1, source_target_pairs={{0,4},{4,8},{8,12},{12,16},{16,20},{20,24},{24,28},{28,32},{32,36}... | collective-permute-start | bytes 1572872 | tf_op jit(solution)/shard_map/ppermute | solution.py:549
  139.9 13.3 %collective-permute-start.9 = (bf16[1,1024,256]{2,1,0:T(8,128)(2,1)S(1)}, bf16[1,1024,256]{2,1,0:T(8,128)(2,1)S(1)}, u32[]{:S(2)}, u32[]{:S(2)}) collective-permute-start(bf16[1,1024,256]{2,1,0:T(8,128)(2,1)S(1)} %get-tuple-element.73.gfirst), channel_id=1, source_target_pairs={{4,0},{8,4},{12,8},{16,12},{20,16},{24,20},{28,24},{32,28},{36,32}... | collective-permute-start | bytes 1572872 | tf_op jit(solution)/shard_map/ppermute | solution.py:550
  145.3 5.8 %copy-start.16 = (bf16[2,1024,128]{2,1,0:T(8,128)(2,1)S(1)}, bf16[2,1024,128]{2,1,0:T(8,128)(2,1)}, u32[]{:S(2)}) copy-start(bf16[2,1024,128]{2,1,0:T(8,128)(2,1)} %copy-done.15) | copy-start | bytes 1572868
  145.3 5.8 %copy-start.30 = (bf16[2048,128]{1,0:T(8,128)(2,1)S(1)}, bf16[2048,128]{1,0:T(8,128)(2,1)}, u32[]{:S(2)}) copy-start(bf16[2048,128]{1,0:T(8,128)(2,1)} %copy-done.29) | copy-start | bytes 1572868
  145.3 5.8 %copy-start.32 = (bf16[2048,128]{1,0:T(8,128)(2,1)S(1)}, bf16[2048,128]{1,0:T(8,128)(2,1)}, u32[]{:S(2)}) copy-start(bf16[2048,128]{1,0:T(8,128)(2,1)} %copy-done.31) | copy-start | bytes 1572868
  148.7 22.7 %collective-permute-start.14 = (bf16[2048,128]{1,0:T(8,128)(2,1)}, bf16[2048,128]{1,0:T(8,128)(2,1)}, u32[]{:S(2)}, u32[]{:S(2)}) collective-permute-start(bf16[2048,128]{1,0:T(8,128)(2,1)} %get-tuple-element.83), channel_id=1, source_target_pairs={{0,1},{1,0},{2,3},{3,2},{4,5},{5,4},{6,7},{7,6},{8,9},{9,8},{10,11... | collective-permute-start | bytes 1572872 | tf_op jit(solution)/shard_map/ppermute | solution.py:546
  151.1 1.9 copy-start.40
  152.9 6.8 %copy-start.14 = (bf16[2048,128]{1,0:T(8,128)(2,1)S(1)}, bf16[2048,128]{1,0:T(8,128)(2,1)}, u32[]{:S(2)}) copy-start(bf16[2048,128]{1,0:T(8,128)(2,1)} %copy-done.13) | copy-start | bytes 1572868
  152.9 6.8 %copy-start.24 = (bf16[2048,128]{1,0:T(8,128)(2,1)S(1)}, bf16[2048,128]{1,0:T(8,128)(2,1)}, u32[]{:S(2)}) copy-start(bf16[2048,128]{1,0:T(8,128)(2,1)} %copy-done.23) | copy-start | bytes 1572868
  152.9 6.8 %copy-start.26 = (bf16[2048,128]{1,0:T(8,128)(2,1)S(1)}, bf16[2048,128]{1,0:T(8,128)(2,1)}, u32[]{:S(2)}) copy-start(bf16[2048,128]{1,0:T(8,128)(2,1)} %copy-done.25) | copy-start | bytes 1572868
  152.9 6.8 %copy-start.28 = (bf16[2048,128]{1,0:T(8,128)(2,1)S(1)}, bf16[2048,128]{1,0:T(8,128)(2,1)}, u32[]{:S(2)}) copy-start(bf16[2048,128]{1,0:T(8,128)(2,1)} %copy-done.27) | copy-start | bytes 1572868
  153.1 25.8 %collective-permute-start.13 = (bf16[2048,128]{1,0:T(8,128)(2,1)}, bf16[2048,128]{1,0:T(8,128)(2,1)}, u32[]{:S(2)}, u32[]{:S(2)}) collective-permute-start(bf16[2048,128]{1,0:T(8,128)(2,1)} %get-tuple-element.81), channel_id=1, source_target_pairs={{0,1},{1,0},{2,3},{3,2},{4,5},{5,4},{6,7},{7,6},{8,9},{9,8},{10,11... | collective-permute-start | bytes 1572872 | tf_op jit(solution)/shard_map/ppermute | solution.py:546
  156.8 3.7 %copy-start.17 = (f32[2048,128]{1,0:T(8,128)}, f32[2048,128]{1,0:T(8,128)S(1)}, u32[]{:S(2)}) copy-start(f32[2048,128]{1,0:T(8,128)S(1)} %get-tuple-element.78) | copy-start | bytes 3145732
  156.8 3.7 %copy-start.19 = (f32[2048,128]{1,0:T(8,128)}, f32[2048,128]{1,0:T(8,128)S(1)}, u32[]{:S(2)}) copy-start(f32[2048,128]{1,0:T(8,128)S(1)} %get-tuple-element.76.own) | copy-start | bytes 3145732
  156.8 20.3 %collective-permute-start.11 = (bf16[2048,128]{1,0:T(8,128)(2,1)}, bf16[2048,128]{1,0:T(8,128)(2,1)}, u32[]{:S(2)}, u32[]{:S(2)}) collective-permute-start(bf16[2048,128]{1,0:T(8,128)(2,1)} %get-tuple-element.79), channel_id=1, source_target_pairs={{0,1},{1,0},{2,3},{3,2},{4,5},{5,4},{6,7},{7,6},{8,9},{9,8},{10,11... | collective-permute-start | bytes 1572872 | tf_op jit(solution)/shard_map/ppermute | solution.py:546
  159.7 1.0 copy-start.34
  161.6 34.7 %all-to-all-start.2 = ((bf16[32,88,128]{2,1,0:T(8,128)(2,1)}), bf16[32,88,128]{2,1,0:T(8,128)(2,1)S(1)}, u32[]{:S(2)}, u32[]{:S(2)}) async-start(bf16[32,88,128]{2,1,0:T(8,128)(2,1)} %shard_map.138), calls=%async_computation.2 | async-start | bytes 1441792 | tf_op jit(solution)/shard_map/all_to_all | solution.py:681
  171.4 5.6 %copy-start.18 = (f32[2048,128]{1,0:T(8,128)S(1)}, f32[2048,128]{1,0:T(8,128)}, u32[]{:S(2)}) copy-start(f32[2048,128]{1,0:T(8,128)} %copy-done.17) | copy-start | bytes 3145732
  172.7 21.5 %collective-permute-start.15 = (bf16[2048,128]{1,0:T(8,128)(2,1)S(1)}, bf16[2048,128]{1,0:T(8,128)(2,1)S(1)}, u32[]{:S(2)}, u32[]{:S(2)}) collective-permute-start(bf16[2048,128]{1,0:T(8,128)(2,1)S(1)} %add_convert_fusion), channel_id=1, source_target_pairs={{0,2},{1,3},{2,0},{3,1},{4,6},{5,7},{6,4},{7,5},{8,10},{9,11},{10,... | collective-permute-start | bytes 1572872 | tf_op jit(solution)/shard_map/ppermute | solution.py:546
  176.0 21.0 %collective-permute-start.10 = (bf16[2048,128]{1,0:T(8,128)(2,1)}, bf16[2048,128]{1,0:T(8,128)(2,1)S(1)}, u32[]{:S(2)}, u32[]{:S(2)}) collective-permute-start(bf16[2048,128]{1,0:T(8,128)(2,1)} %get-tuple-element.77), channel_id=1, source_target_pairs={{0,1},{1,0},{2,3},{3,2},{4,5},{5,4},{6,7},{7,6},{8,9},{9,8},{10,11... | collective-permute-start | bytes 1572872 | tf_op jit(solution)/shard_map/ppermute | solution.py:546
  179.0 26.6 %copy-start.20 = (f32[2048,128]{1,0:T(8,128)S(1)}, f32[2048,128]{1,0:T(8,128)}, u32[]{:S(2)}) copy-start(f32[2048,128]{1,0:T(8,128)} %copy-done.19) | copy-start | bytes 3145732
  179.0 26.6 %collective-permute-start.12 = (bf16[2048,128]{1,0:T(8,128)(2,1)}, bf16[2048,128]{1,0:T(8,128)(2,1)}, u32[]{:S(2)}, u32[]{:S(2)}) collective-permute-start(bf16[2048,128]{1,0:T(8,128)(2,1)} %add_convert_fusion.1), channel_id=1, source_target_pairs={{0,2},{1,3},{2,0},{3,1},{4,6},{5,7},{6,4},{7,5},{8,10},{9,11},{10,... | collective-permute-start | bytes 1572872 | tf_op jit(solution)/shard_map/ppermute | solution.py:546

commit v7 on v6

--- a/solution.py
+++ b/solution.py
@@ -341,7 +341,7 @@
                 to[row, :, pl.ds(channels, channels)] = value.astype(BF)
 
 
-def spread_back(framed, kern, outs, width, channels):
+def spread_back(rows_at, kern, outs, width, channels):
     for branch in range(2):
         taps = taps_of(kern, branch, channels)
 
@@ -353,7 +353,8 @@
                 needed = sorted({c + 1 - i for _, _, c in outs for i in range(3)})
                 for r in needed:
                     for j in range(3):
-                        v = framed[branch, r, pl.ds(base + 8 * p + EDGE + 1 - j, 8), :]
+                        ref, row = rows_at[r]
+                        v = ref[branch, row, pl.ds(base + 8 * p + EDGE + 1 - j, 8), :]
                         for n, (_, _, c) in enumerate(outs):
                             i = c + 1 - r
                             if 0 <= i < 3:
@@ -386,7 +387,8 @@
     fill_framed(
         gframed, [(gfirst, 0), *((gmiddle, r) for r in range(inner)), (glast, 0)], channels
     )
-    spread_back(gframed, kern, [(back, r, r + 1) for r in range(inner)], width, channels)
+    rows_at = [(gframed, r) for r in range(inner + 2)]
+    spread_back(rows_at, kern, [(back, r, r + 1) for r in range(inner)], width, channels)
     shares(back, w_turned, p0, p1, p2, p3)
 
 
@@ -435,17 +437,15 @@
 
 
 def backward_edge_kernel(
-    gup, gfirst, gmiddle, glast, gdown, kern, w_turned, back, p0, p1, p2, p3, gframed
+    gup, gdown, gframed, kern, w_turned, back, p0, p1, p2, p3, around
 ):
-    width = gfirst.shape[1]
+    width = gup.shape[1]
     channels = kern.shape[1]
-    inner = gmiddle.shape[0]
-    fill_framed(
-        gframed,
-        [(gup, 0), (gfirst, 0), (gmiddle, 0), (gmiddle, inner - 1), (glast, 0), (gdown, 0)],
-        channels,
-    )
-    spread_back(gframed, kern, [(back, 0, 1), (back, 1, 4)], width, channels)
+    last = gframed.shape[1] - 1
+    fill_framed(around, [(gup, 0), (gdown, 0)], channels)
+    own = [(gframed, r) for r in (0, 1, last - 1, last)]
+    rows_at = [(around, 0), *own, (around, 1)]
+    spread_back(rows_at, kern, [(back, 0, 1), (back, 1, 4)], width, channels)
     shares(back, w_turned, p0, p1, p2, p3)
 
 
@@ -614,9 +614,9 @@
     )(returned, mat_t, feat, cotangent)
     gup, gdown = halos(gfirst, glast)
     share = (2 * width, channels)
-    share_outs = [(share, F32), (share, BF), (share, F32), (share, BF)]
-    back_mid, *shares_mid = kernel_call(
-        backward_mid_kernel, [lines, *share_outs], [framed(rows)], 20
+    share_outs = [(share, F32), (share, BF), (share, BF), (share, BF)]
+    back_mid, *shares_mid, gframed = kernel_call(
+        backward_mid_kernel, [lines, *share_outs, framed(rows)], [], 20
     )(gfirst, gmiddle, glast, kern, w_turned)
     shorts = [
         kernel_call(
@@ -628,14 +628,14 @@
         for n in range(2)
     ]
     back_edge, *shares_edge = kernel_call(
-        backward_edge_kernel, [lines, *share_outs], [framed(6)], 22
-    )(gup, gfirst, gmiddle, glast, gdown, kern, w_turned)
+        backward_edge_kernel, [lines, *share_outs], [framed(2)], 20
+    )(gup, gdown, gframed, kern, w_turned)
 
     over_tokens = (((0,), (0,)), ((), ()))
 
     def collected(p0, p1, p2, p3):
         beside = flipped(p3, 1)
-        theirs = (p2 + beside.astype(F32)).astype(BF)
+        theirs = (p2.astype(F32) + beside.astype(F32)).astype(BF)
         across = flipped(theirs, 2)
         kept = flipped(p1, 1)
         return p0, kept, across

time: 209 us -> 209 us (level)
  transfers between devices with their start and end apart: 18 -> 18, of which waited for: 6 -> 6; matrix products, arithmetic and copies ran while one was open for 3% -> 3% of each run, Pallas kernels for 12% -> 11%
where the time goes in v7:
time: 209 us; the launch traced here: 208 us
  waiting for transfers between devices  72.4 us (35%)
  starting transfers between devices  42.4 us (20%)
  Pallas kernels  38.5 us (18%)
  blocking collectives  35.9 us (17%)
  local copies, waits for them, and re-layouts  10.2 us (5%)
  other arithmetic  4.3 us (2%)
  matrix products  2.55 us (1%)
    all_to_all x1, blocking collectives, local(): recv = lax.all_to_all(send, 'grid', split_axis=0, concat_axis=0, tiled=True)  35.9 us
    ppermute x12, waiting for transfers between devices, flipped(): return lax.ppermute(value, 'ch', [(i, i ^ bit) for i in range(parts)])  34.7 us
    all_to_all x1, waiting for transfers between devices, local(): lax.all_to_all(turned, 'grid', split_axis=0, concat_axis=0, tiled=True)  25.8 us
    ppermute x12, starting transfers between devices, flipped(): return lax.ppermute(value, 'ch', [(i, i ^ bit) for i in range(parts)])  17.4 us
    all_to_all x1, starting transfers between devices, local(): lax.all_to_all(packed, 'grid', split_axis=0, concat_axis=0, tiled=True)  9.83 us
    unnamed x85, local copies, waits for them, and re-layouts  8.91 us
    ppermute x2, waiting for transfers between devices, halos(): up = lax.ppermute(last, 'grid', [(i, i + 1) for i in range(owners - 1)])  7.73 us
    pallas_call x1, Pallas kernels, local(): kernel_call(tables_kernel, [((width, width), BF), ((width, width), BF), (...  7.19 us
  transfers between devices with their start and end apart: 18, of which 6 were waited for; matrix products, arithmetic and copies ran while one was open for 3% of the time, Pallas kernels for 11%

profile of v7, /device:TPU:1, one launch (start us, length us, event | category | flops | bytes accessed | tf_op | source)
XLA Modules:
  0.0 207.7 jit_solution(11662716130447135341)
XLA Ops:
  0.7 1.2 slice_bitcast_fusion.1
  1.9 3.8 %collective-permute-start.1 = (bf16[2048,128]{1,0:T(8,128)(2,1)S(1)}, bf16[2048,128]{1,0:T(8,128)(2,1)S(1)}, u32[]{:S(2)}, u32[]{:S(2)}) collective-permute-start(bf16[2048,128]{1,0:T(8,128)(2,1)S(1)} %pad_maximum_fusion.x0), channel_id=1, source_target_pairs={{0,2},{1,3},{2,0},{3,1},{4,6},{5,7},{6,4},{7,5},{8,10},{9,11},{10,... | collective-permute-start | bytes 1572872 | tf_op jit(solution)/shard_map/ppermute | solution.py:546
  5.7 0.1 collective-permute-start.5
  5.9 1.1 collective-permute-start
  7.0 10.1 %collective-permute-done.1.x2 = bf16[2048,128]{1,0:T(8,128)(2,1)S(1)} collective-permute-done((bf16[2048,128]{1,0:T(8,128)(2,1)S(1)}, bf16[2048,128]{1,0:T(8,128)(2,1)S(1)}, u32[]{:S(2)}, u32[]{:S(2)}) %collective-permute-start.1) | collective-permute-done | bytes 524320 | tf_op jit(solution)/shard_map/ppermute | solution.py:546
  17.1 2.5 %collective-permute-start.2 = (bf16[2048,128]{1,0:T(8,128)(2,1)S(1)}, bf16[2048,128]{1,0:T(8,128)(2,1)S(1)}, u32[]{:S(2)}, u32[]{:S(2)}) collective-permute-start(bf16[2048,128]{1,0:T(8,128)(2,1)S(1)} %collective-permute-done.1.x2), channel_id=1, source_target_pairs={{0,1},{1,0},{2,3},{3,2},{4,5},{5,4},{6,7},{7,6},{8,9},{9,8},{10,11... | collective-permute-start | bytes 1572872 | tf_op jit(solution)/shard_map/ppermute | solution.py:546
  19.6 0.0 collective-permute-start.4
  19.7 0.1 pad_add_fusion.where
  19.7 0.9 copy-done.34
  20.7 0.9 copy-done.36
  21.6 0.8 copy-done.37
  22.3 7.2 %shard_map.126 = (bf16[1024,1024]{1,0:T(8,128)(2,1)S(1)}, bf16[1024,1024]{1,0:T(8,128)(2,1)S(1)}, bf16[32,1024]{1,0:T(8,128)(2,1)S(1)}, bf16[256,256]{1,0:T(8,12...) custom-call(s32[2]{0:T(128)S(1)} %pad_add_fusion.where, ...), custom_call_target="tpu_custom_call" | custom-call | tf_op jit(solution)/shard_map/pallas_call | solution.py:561
  29.5 0.0 collective-permute-done.5.x2
  29.6 0.6 collective-permute-start.6
  30.1 0.0 collective-permute-done.x1
  30.1 0.0 collective-permute-done.2.x3
  30.2 0.7 shard_map.127
  30.9 0.0 copy-start.8
  30.9 3.8 %collective-permute-start.3 = (bf16[1,1024,256]{2,1,0:T(8,128)(2,1)S(1)}, bf16[1,1024,256]{2,1,0:T(8,128)(2,1)S(1)}, u32[]{:S(2)}, u32[]{:S(2)}) collective-permute-start(bf16[1,1024,256]{2,1,0:T(8,128)(2,1)S(1)} %get-tuple-element.56.last), channel_id=1, source_target_pairs={{0,4},{4,8},{8,12},{12,16},{16,20},{20,24},{24,28},{28,32},{32,36}... | collective-permute-start | bytes 1572872 | tf_op jit(solution)/shard_map/ppermute | solution.py:549
  34.7 1.3 collective-permute-start.7
  36.0 0.0 collective-permute-done.4.x1
  36.1 1.9 shard_map.128.middle
  38.1 7.7 %collective-permute-done.3.up = bf16[1,1024,256]{2,1,0:T(8,128)(2,1)S(1)} collective-permute-done((bf16[1,1024,256]{2,1,0:T(8,128)(2,1)S(1)}, bf16[1,1024,256]{2,1,0:T(8,128)(2,1)S(1)}, u32[]{:S(2)}, u32[]{:S(2)}) %collective-permute-start.3) | collective-permute-done | bytes 524320 | tf_op jit(solution)/shard_map/ppermute | solution.py:549
  45.8 4.2 %collective-permute-done.7.down = bf16[1,1024,256]{2,1,0:T(8,128)(2,1)S(1)} collective-permute-done((bf16[1,1024,256]{2,1,0:T(8,128)(2,1)S(1)}, bf16[1,1024,256]{2,1,0:T(8,128)(2,1)S(1)}, u32[]{:S(2)}, u32[]{:S(2)}) %collective-permute-start.7) | collective-permute-done | bytes 524320 | tf_op jit(solution)/shard_map/ppermute | solution.py:550
  50.0 5.7 %shard_map.129 = (bf16[32,8,32,128]{3,2,1,0:T(8,128)(2,1)S(1)}, bf16[4,1024,128]{2,1,0:T(8,128)(2,1)S(1)}) custom-call(bf16[1,1024,256]{2,1,0:T(8,128)(2,1)S(1)} %collective-permute-done.3.up, bf16[1,1024,256]{2,1,0:T(8,128)(2,1)S(1)} %get-tuple-element.57.first, bf16[2,1024,256]{2,1,0:T(8,128)(2,1)S(1)} %shard_map.128.middle, ...), custom_call_target="tpu_custom_call" | custom-call | tf_op jit(solution)/shard_map/pallas_call | solution.py:600
  55.7 0.0 copy-start.17
  55.7 35.9 %all_to_all.15.recv = bf16[32,8,32,128]{3,2,1,0:T(8,128)(2,1)S(1)} all-to-all(bf16[32,8,32,128]{3,2,1,0:T(8,128)(2,1)S(1)} %get-tuple-element.61), channel_id=1, replica_groups=mesh['grid'=32,'ch'=4] {'grid'}, dimensions={0} | all-to-all | bytes 4194304 | tf_op jit(solution)/shard_map/all_to_all | solution.py:603
  91.6 4.6 %shard_map.130 = (bf16[32,8,32,128]{3,2,1,0:T(8,128)(2,1)S(1)}, bf16[1024,128]{1,0:T(8,128)(2,1)S(1)}, f32[128,128]{1,0:T(8,128)S(1)}) custom-call(bf16[32,8,32,128]{3,2,1,0:T(8,128)(2,1)S(1)} %all_to_all.15.recv, f32[4,16,128]{2,1,0:T(8,128)S(1)} %get-tuple-element.62.coef, f32[1,16,128]{2,1,0:T(8,128)S(1)} %get-tuple-element.63.keep, ...), custom_call_target="tpu_custom_call" | custom-call | tf_op jit(solution)/shard_map/pallas_call | solution.py:605
  96.3 1.3 copy-done.12
  97.6 0.7 copy-done.32
  98.3 5.4 %all-to-all-start.1 = ((bf16[32,8,32,128]{3,2,1,0:T(8,128)(2,1)}), bf16[32,8,32,128]{3,2,1,0:T(8,128)(2,1)S(1)}, u32[]{:S(2)}, u32[]{:S(2)}) async-start(bf16[32,8,32,128]{3,2,1,0:T(8,128)(2,1)} %copy-done.12), calls=%async_computation.1 | async-start | bytes 4194304 | tf_op jit(solution)/shard_map/all_to_all | solution.py:611
  103.8 0.1 pad.3.clone
  103.9 0.6 convert_element_type.33
  104.5 25.8 %all-to-all-done.1.recv = bf16[32,8,32,128]{3,2,1,0:T(8,128)(2,1)S(1)} async-done(((bf16[32,8,32,128]{3,2,1,0:T(8,128)(2,1)}), bf16[32,8,32,128]{3,2,1,0:T(8,128)(2,1)S(1)}, u32[]{:S(2)}, u32[]{:S(2)}) %all-to-all-start.1) | async-done | bytes 2097184 | tf_op jit(solution)/shard_map/all_to_all | solution.py:611
  130.2 1.2 copy-done.9
  131.5 1.6 copy-done.11
  133.1 1.2 copy-done.18
  134.3 2.5 %shard_map.131 = (bf16[4,1024,128]{2,1,0:T(8,128)(2,1)}, bf16[1,1024,256]{2,1,0:T(8,128)(2,1)S(1)}, bf16[2,1024,256]{2,1,0:T(8,128)(2,1)S(1)}, bf16[1,1024,256]{2,1,0:T(8,128)(2,1)S(1)}) custom-call(bf16[32,8,32,128]{3,2,1,0:T(8,128)(2,1)S(1)} %all-to-all-done.1.recv, bf16[1024,1024]{1,0:T(8,128)(2,1)S(1)} %copy-done.11, ...), custom_call_target="tpu_custom_call" | custom-call | tf_op jit(solution)/shard_map/pallas_call | solution.py:612
  136.8 3.1 %collective-permute-start.8 = (bf16[1,1024,256]{2,1,0:T(8,128)(2,1)S(1)}, bf16[1,1024,256]{2,1,0:T(8,128)(2,1)S(1)}, u32[]{:S(2)}, u32[]{:S(2)}) collective-permute-start(bf16[1,1024,256]{2,1,0:T(8,128)(2,1)S(1)} %get-tuple-element.73.glast), channel_id=1, source_target_pairs={{0,4},{4,8},{8,12},{12,16},{16,20},{20,24},{24,28},{28,32},{32,36}... | collective-permute-start | bytes 1572872 | tf_op jit(solution)/shard_map/ppermute | solution.py:549
  139.9 1.5 collective-permute-start.9
  141.4 1.9 shard_map.136
  143.4 1.9 shard_map.137
  145.3 3.4 %shard_map.132 = (bf16[2,1024,256]{2,1,0:T(8,128)(2,1)S(1)}, f32[2048,128]{1,0:T(8,128)S(1)}, bf16[2048,128]{1,0:T(8,128)(2,1)}, bf16[2048,128]{1,0:T(8,128)(2,1...) custom-call(bf16[1,1024,256]{2,1,0:T(8,128)(2,1)S(1)} %get-tuple-element.74.gfirst, ...), custom_call_target="tpu_custom_call" | custom-call | tf_op jit(solution)/shard_map/pallas_call | solution.py:618
  148.8 2.3 %collective-permute-start.14 = (bf16[2048,128]{1,0:T(8,128)(2,1)}, bf16[2048,128]{1,0:T(8,128)(2,1)}, u32[]{:S(2)}, u32[]{:S(2)}) collective-permute-start(bf16[2048,128]{1,0:T(8,128)(2,1)} %get-tuple-element.85), channel_id=1, source_target_pairs={{0,1},{1,0},{2,3},{3,2},{4,5},{5,4},{6,7},{7,6},{8,9},{9,8},{10,11... | collective-permute-start | bytes 1572872 | tf_op jit(solution)/shard_map/ppermute | solution.py:546
  151.1 1.8 fusion
  153.0 0.2 maximum_maximum_fusion.small
  153.1 0.3 collective-permute-start.13
  153.5 3.1 %shard_map.133 = (bf16[2,1024,256]{2,1,0:T(8,128)(2,1)S(1)}, f32[2048,128]{1,0:T(8,128)S(1)}, bf16[2048,128]{1,0:T(8,128)(2,1)S(1)}, bf16[2048,128]{1,0:T(8,128)(2,1)S(1)}, bf16[2048,128]{1,0:T(8,128)(2,1)}) custom-call(bf16[1,1024,256]{2,1,0:T(8,128)(2,1)S(1)} %collective-permute-done.8.gup, bf16[1,1024,256]{2,1,0:T(8,128)(2,1)S(1)} %collective-permute-done.9.gdown, ...), custom_call_target="tpu_custom_call" | custom-call | tf_op jit(solution)/shard_map/pallas_call | solution.py:630
  156.5 2.7 %collective-permute-start.11 = (bf16[2048,128]{1,0:T(8,128)(2,1)}, bf16[2048,128]{1,0:T(8,128)(2,1)}, u32[]{:S(2)}, u32[]{:S(2)}) collective-permute-start(bf16[2048,128]{1,0:T(8,128)(2,1)} %get-tuple-element.81), channel_id=1, source_target_pairs={{0,1},{1,0},{2,3},{3,2},{4,5},{5,4},{6,7},{7,6},{8,9},{9,8},{10,11... | collective-permute-start | bytes 1572872 | tf_op jit(solution)/shard_map/ppermute | solution.py:546
  159.3 0.8 fusion.8
  160.0 0.1 add.11.grad_w
  160.1 0.1 copy-done.33
  160.2 1.0 shard_map.138
  161.2 9.8 %all-to-all-start.2 = ((bf16[32,88,128]{2,1,0:T(8,128)(2,1)}), bf16[32,88,128]{2,1,0:T(8,128)(2,1)S(1)}, u32[]{:S(2)}, u32[]{:S(2)}) async-start(bf16[32,88,128]{2,1,0:T(8,128)(2,1)} %shard_map.138), calls=%async_computation.2 | async-start | bytes 1441792 | tf_op jit(solution)/shard_map/all_to_all | solution.py:681
  171.0 0.6 collective-permute-start.10
  171.6 1.2 add_convert_fusion
  172.8 3.3 %collective-permute-start.15 = (bf16[2048,128]{1,0:T(8,128)(2,1)S(1)}, bf16[2048,128]{1,0:T(8,128)(2,1)S(1)}, u32[]{:S(2)}, u32[]{:S(2)}) collective-permute-start(bf16[2048,128]{1,0:T(8,128)(2,1)S(1)} %add_convert_fusion), channel_id=1, source_target_pairs={{0,2},{1,3},{2,0},{3,1},{4,6},{5,7},{6,4},{7,5},{8,10},{9,11},{10,... | collective-permute-start | bytes 1572872 | tf_op jit(solution)/shard_map/ppermute | solution.py:546
  176.1 2.2 %add_convert_fusion.1 = bf16[2048,128]{1,0:T(8,128)(2,1)} fusion(bf16[2048,128]{1,0:T(8,128)(2,1)} %collective-permute-done.11, bf16[2048,128]{1,0:T(8,128)(2,1)} %copy-done.21), kind=kLoop, calls=%fused_computation.17 | loop fusion | flops 1048576 | bytes 1572864 | tf_op jit(solution)/shard_map/convert_element_type | solution.py:638
  178.2 0.0 collective-permute-start.12
  178.3 16.1 %collective-permute-done.15.across = bf16[2048,128]{1,0:T(8,128)(2,1)S(1)} collective-permute-done((bf16[2048,128]{1,0:T(8,128)(2,1)S(1)}, bf16[2048,128]{1,0:T(8,128)(2,1)S(1)}, u32[]{:S(2)}, u32[]{:S(2)}) %collective-permute-start.15) | collective-permute-done | bytes 524320 | tf_op jit(solution)/shard_map/ppermute | solution.py:546
  194.3 2.0 shard_map.134.middle
  196.4 0.7 shard_map.139
  197.1 8.5 %collective-permute-done.12.across = bf16[2048,128]{1,0:T(8,128)(2,1)S(1)} collective-permute-done((bf16[2048,128]{1,0:T(8,128)(2,1)}, bf16[2048,128]{1,0:T(8,128)(2,1)S(1)}, u32[]{:S(2)}, u32[]{:S(2)}) %collective-permute-start.12) | collective-permute-done | bytes 524320 | tf_op jit(solution)/shard_map/ppermute | solution.py:546
  205.6 1.9 shard_map.135
  (89 shorter events, 0.3 us)
Async XLA Ops:
  0.6 5.1 %copy-start.39 = (bf16[4,1024,128]{2,1,0:T(8,128)(2,1)S(1)}, bf16[4,1024,128]{2,1,0:T(8,128)(2,1)}, u32[]{:S(2)}) copy-start(bf16[4,1024,128]{2,1,0:T(8,128)(2,1)} %param.7) | copy-start | bytes 3145732
  0.6 19.0 %copy-start.41 = (bf16[2,3,3,128]{3,0,2,1:T(2,128)(2,1)S(1)}, bf16[2,3,3,128]{3,0,2,1:T(2,128)(2,1)}, u32[]{:S(2)}) copy-start(bf16[2,3,3,128]{3,0,2,1:T(2,128)(2,1)} %param.10) | copy-start | bytes 13828
  0.7 19.1 %copy-start.35 = (bf16[512,128]{1,0:T(8,128)(2,1)S(1)}, bf16[512,128]{1,0:T(8,128)(2,1)}, u32[]{:S(2)}) copy-start(bf16[512,128]{1,0:T(8,128)(2,1)} %w_gate.1) | copy-start | bytes 393220
  1.9 34.2 %copy-start.13 = (bf16[2048,128]{1,0:T(8,128)(2,1)}, bf16[2048,128]{1,0:T(8,128)(2,1)S(1)}, u32[]{:S(2)}) copy-start(bf16[2048,128]{1,0:T(8,128)(2,1)S(1)} %pad_maximum_fusion.x0) | copy-start | bytes 1572868
  1.9 15.2 %collective-permute-start.1 = (bf16[2048,128]{1,0:T(8,128)(2,1)S(1)}, bf16[2048,128]{1,0:T(8,128)(2,1)S(1)}, u32[]{:S(2)}, u32[]{:S(2)}) collective-permute-start(bf16[2048,128]{1,0:T(8,128)(2,1)S(1)} %pad_maximum_fusion.x0), channel_id=1, source_target_pairs={{0,2},{1,3},{2,0},{3,1},{4,6},{5,7},{6,4},{7,5},{8,10},{9,11},{10,... | collective-permute-start | bytes 1572872 | tf_op jit(solution)/shard_map/ppermute | solution.py:546
  5.7 32.3 %copy-start.15 = (bf16[2,1024,128]{2,1,0:T(8,128)(2,1)}, bf16[2,1024,128]{2,1,0:T(8,128)(2,1)S(1)}, u32[]{:S(2)}) copy-start(bf16[2,1024,128]{2,1,0:T(8,128)(2,1)S(1)} %slice.11) | copy-start | bytes 1572868
  5.7 23.8 %collective-permute-start.5 = (bf16[2048,128]{1,0:T(8,128)(2,1)S(1)}, bf16[2048,128]{1,0:T(8,128)(2,1)S(1)}, u32[]{:S(2)}, u32[]{:S(2)}) collective-permute-start(bf16[2048,128]{1,0:T(8,128)(2,1)S(1)} %bitcast.13), channel_id=1, source_target_pairs={{0,2},{1,3},{2,0},{3,1},{4,6},{5,7},{6,4},{7,5},{8,10},{9,11},{10,... | collective-permute-start | bytes 1572872 | tf_op jit(solution)/shard_map/ppermute | solution.py:546
  5.9 24.3 %collective-permute-start = (bf16[2048,128]{1,0:T(8,128)(2,1)S(1)}, bf16[2048,128]{1,0:T(8,128)(2,1)S(1)}, u32[]{:S(2)}, u32[]{:S(2)}) collective-permute-start(bf16[2048,128]{1,0:T(8,128)(2,1)S(1)} %pad_maximum_fusion.x0), channel_id=1, source_target_pairs={{0,1},{1,0},{2,3},{3,2},{4,5},{5,4},{6,7},{7,6},{8,9},{9,8},{10,11... | collective-permute-start | bytes 1572872 | tf_op jit(solution)/shard_map/ppermute | solution.py:546
  17.1 19.0 %copy-start.22 = (bf16[2048,128]{1,0:T(8,128)(2,1)}, bf16[2048,128]{1,0:T(8,128)(2,1)S(1)}, u32[]{:S(2)}) copy-start(bf16[2048,128]{1,0:T(8,128)(2,1)S(1)} %collective-permute-done.1.x2) | copy-start | bytes 1572868
  17.1 13.1 %collective-permute-start.2 = (bf16[2048,128]{1,0:T(8,128)(2,1)S(1)}, bf16[2048,128]{1,0:T(8,128)(2,1)S(1)}, u32[]{:S(2)}, u32[]{:S(2)}) collective-permute-start(bf16[2048,128]{1,0:T(8,128)(2,1)S(1)} %collective-permute-done.1.x2), channel_id=1, source_target_pairs={{0,1},{1,0},{2,3},{3,2},{4,5},{5,4},{6,7},{7,6},{8,9},{9,8},{10,11... | collective-permute-start | bytes 1572872 | tf_op jit(solution)/shard_map/ppermute | solution.py:546
  19.6 16.4 %collective-permute-start.4 = (bf16[2048,128]{1,0:T(8,128)(2,1)S(1)}, bf16[2048,128]{1,0:T(8,128)(2,1)}, u32[]{:S(2)}, u32[]{:S(2)}) collective-permute-start(bf16[2048,128]{1,0:T(8,128)(2,1)S(1)} %bitcast.14), channel_id=1, source_target_pairs={{0,1},{1,0},{2,3},{3,2},{4,5},{5,4},{6,7},{7,6},{8,9},{9,8},{10,11... | collective-permute-start | bytes 1572872 | tf_op jit(solution)/shard_map/ppermute | solution.py:546
  19.7 1.0 copy-start.34
  20.7 0.9 copy-start.36
  21.6 0.8 copy-start.37
  29.5 8.5 %copy-start.10 = (bf16[1024,1024]{1,0:T(8,128)(2,1)}, bf16[1024,1024]{1,0:T(8,128)(2,1)S(1)}, u32[]{:S(2)}) copy-start(bf16[1024,1024]{1,0:T(8,128)(2,1)S(1)} %get-tuple-element.70.mat) | copy-start | bytes 6291460
  29.6 8.5 %copy-start.28 = (bf16[2048,128]{1,0:T(8,128)(2,1)}, bf16[2048,128]{1,0:T(8,128)(2,1)S(1)}, u32[]{:S(2)}) copy-start(bf16[2048,128]{1,0:T(8,128)(2,1)S(1)} %collective-permute-done.5.x2) | copy-start | bytes 1572868
  29.6 6.5 %collective-permute-start.6 = (bf16[2048,128]{1,0:T(8,128)(2,1)S(1)}, bf16[2048,128]{1,0:T(8,128)(2,1)S(1)}, u32[]{:S(2)}, u32[]{:S(2)}) collective-permute-start(bf16[2048,128]{1,0:T(8,128)(2,1)S(1)} %collective-permute-done.5.x2), channel_id=1, source_target_pairs={{0,1},{1,0},{2,3},{3,2},{4,5},{5,4},{6,7},{7,6},{8,9},{9,8},{10,11... | collective-permute-start | bytes 1572872 | tf_op jit(solution)/shard_map/ppermute | solution.py:546
  30.1 7.9 %copy-start.24 = (bf16[2048,128]{1,0:T(8,128)(2,1)}, bf16[2048,128]{1,0:T(8,128)(2,1)S(1)}, u32[]{:S(2)}) copy-start(bf16[2048,128]{1,0:T(8,128)(2,1)S(1)} %collective-permute-done.x1) | copy-start | bytes 1572868
  30.2 7.9 %copy-start.26 = (bf16[2048,128]{1,0:T(8,128)(2,1)}, bf16[2048,128]{1,0:T(8,128)(2,1)S(1)}, u32[]{:S(2)}) copy-start(bf16[2048,128]{1,0:T(8,128)(2,1)S(1)} %collective-permute-done.2.x3) | copy-start | bytes 1572868
  30.9 24.8 %copy-start = (bf16[1,1024,256]{2,1,0:T(8,128)(2,1)}, bf16[1,1024,256]{2,1,0:T(8,128)(2,1)S(1)}, u32[]{:S(2)}) copy-start(bf16[1,1024,256]{2,1,0:T(8,128)(2,1)S(1)} %get-tuple-element.57.first) | copy-start | bytes 1572868
  30.9 24.8 %copy-start.2 = (bf16[1,1024,256]{2,1,0:T(8,128)(2,1)}, bf16[1,1024,256]{2,1,0:T(8,128)(2,1)S(1)}, u32[]{:S(2)}) copy-start(bf16[1,1024,256]{2,1,0:T(8,128)(2,1)S(1)} %get-tuple-element.56.last) | copy-start | bytes 1572868
  30.9 19.1 %copy-start.8 = (bf16[4,1024,128]{2,1,0:T(8,128)(2,1)S(1)}, bf16[4,1024,128]{2,1,0:T(8,128)(2,1)}, u32[]{:S(2)}) copy-start(bf16[4,1024,128]{2,1,0:T(8,128)(2,1)} %cot.3) | copy-start | bytes 3145732
  30.9 14.9 %collective-permute-start.3 = (bf16[1,1024,256]{2,1,0:T(8,128)(2,1)S(1)}, bf16[1,1024,256]{2,1,0:T(8,128)(2,1)S(1)}, u32[]{:S(2)}, u32[]{:S(2)}) collective-permute-start(bf16[1,1024,256]{2,1,0:T(8,128)(2,1)S(1)} %get-tuple-element.56.last), channel_id=1, source_target_pairs={{0,4},{4,8},{8,12},{12,16},{16,20},{20,24},{24,28},{28,32},{32,36}... | collective-permute-start | bytes 1572872 | tf_op jit(solution)/shard_map/ppermute | solution.py:549
  34.7 15.2 %collective-permute-start.7 = (bf16[1,1024,256]{2,1,0:T(8,128)(2,1)S(1)}, bf16[1,1024,256]{2,1,0:T(8,128)(2,1)S(1)}, u32[]{:S(2)}, u32[]{:S(2)}) collective-permute-start(bf16[1,1024,256]{2,1,0:T(8,128)(2,1)S(1)} %get-tuple-element.57.first), channel_id=1, source_target_pairs={{4,0},{8,4},{12,8},{16,12},{20,16},{24,20},{28,24},{32,28},{36,32}... | collective-permute-start | bytes 1572872 | tf_op jit(solution)/shard_map/ppermute | solution.py:550
  36.1 13.9 %copy-start.30 = (bf16[2048,128]{1,0:T(8,128)(2,1)}, bf16[2048,128]{1,0:T(8,128)(2,1)S(1)}, u32[]{:S(2)}) copy-start(bf16[2048,128]{1,0:T(8,128)(2,1)S(1)} %collective-permute-done.6.x3) | copy-start | bytes 1572868
  45.8 9.9 %copy-start.4 = (bf16[1,1024,256]{2,1,0:T(8,128)(2,1)}, bf16[1,1024,256]{2,1,0:T(8,128)(2,1)S(1)}, u32[]{:S(2)}) copy-start(bf16[1,1024,256]{2,1,0:T(8,128)(2,1)S(1)} %collective-permute-done.3.up) | copy-start | bytes 1572868
  50.0 5.7 %copy-start.6 = (bf16[1,1024,256]{2,1,0:T(8,128)(2,1)}, bf16[1,1024,256]{2,1,0:T(8,128)(2,1)S(1)}, u32[]{:S(2)}) copy-start(bf16[1,1024,256]{2,1,0:T(8,128)(2,1)S(1)} %collective-permute-done.7.down) | copy-start | bytes 1572868
  55.7 35.9 %copy-start.17 = (bf16[4,1024,128]{2,1,0:T(8,128)(2,1)}, bf16[4,1024,128]{2,1,0:T(8,128)(2,1)S(1)}, u32[]{:S(2)}) copy-start(bf16[4,1024,128]{2,1,0:T(8,128)(2,1)S(1)} %get-tuple-element.71.feat) | copy-start | bytes 3145732
  96.3 1.3 copy-start.12
  97.6 0.7 copy-start.32
  98.3 31.9 %all-to-all-start.1 = ((bf16[32,8,32,128]{3,2,1,0:T(8,128)(2,1)}), bf16[32,8,32,128]{3,2,1,0:T(8,128)(2,1)S(1)}, u32[]{:S(2)}, u32[]{:S(2)}) async-start(bf16[32,8,32,128]{3,2,1,0:T(8,128)(2,1)} %copy-done.12), calls=%async_computation.1 | async-start | bytes 4194304 | tf_op jit(solution)/shard_map/all_to_all | solution.py:611
  130.2 1.2 copy-start.9
  131.5 1.6 copy-start.11
  133.1 1.2 copy-start.18
  134.3 7.1 %copy-start.1 = (bf16[1,1024,256]{2,1,0:T(8,128)(2,1)S(1)}, bf16[1,1024,256]{2,1,0:T(8,128)(2,1)}, u32[]{:S(2)}) copy-start(bf16[1,1024,256]{2,1,0:T(8,128)(2,1)} %copy-done) | copy-start | bytes 1572868
  134.3 7.1 %copy-start.3 = (bf16[1,1024,256]{2,1,0:T(8,128)(2,1)S(1)}, bf16[1,1024,256]{2,1,0:T(8,128)(2,1)}, u32[]{:S(2)}) copy-start(bf16[1,1024,256]{2,1,0:T(8,128)(2,1)} %copy-done.2) | copy-start | bytes 1572868
  134.3 7.1 %copy-start.5 = (bf16[1,1024,256]{2,1,0:T(8,128)(2,1)S(1)}, bf16[1,1024,256]{2,1,0:T(8,128)(2,1)}, u32[]{:S(2)}) copy-start(bf16[1,1024,256]{2,1,0:T(8,128)(2,1)} %copy-done.4) | copy-start | bytes 1572868
  134.3 7.1 %copy-start.7 = (bf16[1,1024,256]{2,1,0:T(8,128)(2,1)S(1)}, bf16[1,1024,256]{2,1,0:T(8,128)(2,1)}, u32[]{:S(2)}) copy-start(bf16[1,1024,256]{2,1,0:T(8,128)(2,1)} %copy-done.6) | copy-start | bytes 1572868
  136.8 16.7 %collective-permute-start.8 = (bf16[1,1024,256]{2,1,0:T(8,128)(2,1)S(1)}, bf16[1,1024,256]{2,1,0:T(8,128)(2,1)S(1)}, u32[]{:S(2)}, u32[]{:S(2)}) collective-permute-start(bf16[1,1024,256]{2,1,0:T(8,128)(2,1)S(1)} %get-tuple-element.73.glast), channel_id=1, source_target_pairs={{0,4},{4,8},{8,12},{12,16},{16,20},{20,24},{24,28},{28,32},{32,36}... | collective-permute-start | bytes 1572872 | tf_op jit(solution)/shard_map/ppermute | solution.py:549
  139.9 13.5 %collective-permute-start.9 = (bf16[1,1024,256]{2,1,0:T(8,128)(2,1)S(1)}, bf16[1,1024,256]{2,1,0:T(8,128)(2,1)S(1)}, u32[]{:S(2)}, u32[]{:S(2)}) collective-permute-start(bf16[1,1024,256]{2,1,0:T(8,128)(2,1)S(1)} %get-tuple-element.74.gfirst), channel_id=1, source_target_pairs={{4,0},{8,4},{12,8},{16,12},{20,16},{24,20},{28,24},{32,28},{36,32}... | collective-permute-start | bytes 1572872 | tf_op jit(solution)/shard_map/ppermute | solution.py:550
  145.3 5.8 %copy-start.16 = (bf16[2,1024,128]{2,1,0:T(8,128)(2,1)S(1)}, bf16[2,1024,128]{2,1,0:T(8,128)(2,1)}, u32[]{:S(2)}) copy-start(bf16[2,1024,128]{2,1,0:T(8,128)(2,1)} %copy-done.15) | copy-start | bytes 1572868
  145.3 5.8 %copy-start.29 = (bf16[2048,128]{1,0:T(8,128)(2,1)S(1)}, bf16[2048,128]{1,0:T(8,128)(2,1)}, u32[]{:S(2)}) copy-start(bf16[2048,128]{1,0:T(8,128)(2,1)} %copy-done.28) | copy-start | bytes 1572868
  145.3 5.8 %copy-start.31 = (bf16[2048,128]{1,0:T(8,128)(2,1)S(1)}, bf16[2048,128]{1,0:T(8,128)(2,1)}, u32[]{:S(2)}) copy-start(bf16[2048,128]{1,0:T(8,128)(2,1)} %copy-done.30) | copy-start | bytes 1572868
  148.8 4.1 %copy-start.19 = (bf16[2048,128]{1,0:T(8,128)(2,1)}, bf16[2048,128]{1,0:T(8,128)(2,1)S(1)}, u32[]{:S(2)}) copy-start(bf16[2048,128]{1,0:T(8,128)(2,1)S(1)} %get-tuple-element.84) | copy-start | bytes 1572868
  148.8 22.8 %collective-permute-start.14 = (bf16[2048,128]{1,0:T(8,128)(2,1)}, bf16[2048,128]{1,0:T(8,128)(2,1)}, u32[]{:S(2)}, u32[]{:S(2)}) collective-permute-start(bf16[2048,128]{1,0:T(8,128)(2,1)} %get-tuple-element.85), channel_id=1, source_target_pairs={{0,1},{1,0},{2,3},{3,2},{4,5},{5,4},{6,7},{7,6},{8,9},{9,8},{10,11... | collective-permute-start | bytes 1572872 | tf_op jit(solution)/shard_map/ppermute | solution.py:546
  151.1 1.9 copy-start.40
  153.1 25.1 %collective-permute-start.13 = (bf16[2048,128]{1,0:T(8,128)(2,1)}, bf16[2048,128]{1,0:T(8,128)(2,1)}, u32[]{:S(2)}, u32[]{:S(2)}) collective-permute-start(bf16[2048,128]{1,0:T(8,128)(2,1)} %get-tuple-element.83), channel_id=1, source_target_pairs={{0,1},{1,0},{2,3},{3,2},{4,5},{5,4},{6,7},{7,6},{8,9},{9,8},{10,11... | collective-permute-start | bytes 1572872 | tf_op jit(solution)/shard_map/ppermute | solution.py:546
  153.4 5.8 %copy-start.14 = (bf16[2048,128]{1,0:T(8,128)(2,1)S(1)}, bf16[2048,128]{1,0:T(8,128)(2,1)}, u32[]{:S(2)}) copy-start(bf16[2048,128]{1,0:T(8,128)(2,1)} %copy-done.13) | copy-start | bytes 1572868
  153.4 5.8 %copy-start.23 = (bf16[2048,128]{1,0:T(8,128)(2,1)S(1)}, bf16[2048,128]{1,0:T(8,128)(2,1)}, u32[]{:S(2)}) copy-start(bf16[2048,128]{1,0:T(8,128)(2,1)} %copy-done.22) | copy-start | bytes 1572868
  153.4 5.8 %copy-start.25 = (bf16[2048,128]{1,0:T(8,128)(2,1)S(1)}, bf16[2048,128]{1,0:T(8,128)(2,1)}, u32[]{:S(2)}) copy-start(bf16[2048,128]{1,0:T(8,128)(2,1)} %copy-done.24) | copy-start | bytes 1572868
  153.4 5.8 %copy-start.27 = (bf16[2048,128]{1,0:T(8,128)(2,1)S(1)}, bf16[2048,128]{1,0:T(8,128)(2,1)}, u32[]{:S(2)}) copy-start(bf16[2048,128]{1,0:T(8,128)(2,1)} %copy-done.26) | copy-start | bytes 1572868
  156.5 3.5 %copy-start.21 = (bf16[2048,128]{1,0:T(8,128)(2,1)}, bf16[2048,128]{1,0:T(8,128)(2,1)S(1)}, u32[]{:S(2)}) copy-start(bf16[2048,128]{1,0:T(8,128)(2,1)S(1)} %get-tuple-element.80) | copy-start | bytes 1572868
  156.5 3.6 %copy-start.38 = (bf16[2048,128]{1,0:T(8,128)(2,1)}, bf16[2048,128]{1,0:T(8,128)(2,1)S(1)}, u32[]{:S(2)}) copy-start(bf16[2048,128]{1,0:T(8,128)(2,1)S(1)} %get-tuple-element.79) | copy-start | bytes 1572868
  156.5 19.5 %collective-permute-start.11 = (bf16[2048,128]{1,0:T(8,128)(2,1)}, bf16[2048,128]{1,0:T(8,128)(2,1)}, u32[]{:S(2)}, u32[]{:S(2)}) collective-permute-start(bf16[2048,128]{1,0:T(8,128)(2,1)} %get-tuple-element.81), channel_id=1, source_target_pairs={{0,1},{1,0},{2,3},{3,2},{4,5},{5,4},{6,7},{7,6},{8,9},{9,8},{10,11... | collective-permute-start | bytes 1572872 | tf_op jit(solution)/shard_map/ppermute | solution.py:546
  159.2 1.0 copy-start.33
  160.0 11.6 %copy-start.20 = (bf16[2048,128]{1,0:T(8,128)(2,1)S(1)}, bf16[2048,128]{1,0:T(8,128)(2,1)}, u32[]{:S(2)}) copy-start(bf16[2048,128]{1,0:T(8,128)(2,1)} %copy-done.19) | copy-start | bytes 1572868
  161.2 35.2 %all-to-all-start.2 = ((bf16[32,88,128]{2,1,0:T(8,128)(2,1)}), bf16[32,88,128]{2,1,0:T(8,128)(2,1)S(1)}, u32[]{:S(2)}, u32[]{:S(2)}) async-start(bf16[32,88,128]{2,1,0:T(8,128)(2,1)} %shard_map.138), calls=%async_computation.2 | async-start | bytes 1441792 | tf_op jit(solution)/shard_map/all_to_all | solution.py:681
  171.0 26.1 %collective-permute-start.10 = (bf16[2048,128]{1,0:T(8,128)(2,1)}, bf16[2048,128]{1,0:T(8,128)(2,1)}, u32[]{:S(2)}, u32[]{:S(2)}) collective-permute-start(bf16[2048,128]{1,0:T(8,128)(2,1)} %copy-done.38), channel_id=1, source_target_pairs={{0,1},{1,0},{2,3},{3,2},{4,5},{5,4},{6,7},{7,6},{8,9},{9,8},{10,11... | collective-permute-start | bytes 1572872 | tf_op jit(solution)/shard_map/ppermute | solution.py:546
  172.8 21.5 %collective-permute-start.15 = (bf16[2048,128]{1,0:T(8,128)(2,1)S(1)}, bf16[2048,128]{1,0:T(8,128)(2,1)S(1)}, u32[]{:S(2)}, u32[]{:S(2)}) collective-permute-start(bf16[2048,128]{1,0:T(8,128)(2,1)S(1)} %add_convert_fusion), channel_id=1, source_target_pairs={{0,2},{1,3},{2,0},{3,1},{4,6},{5,7},{6,4},{7,5},{8,10},{9,11},{10,... | collective-permute-start | bytes 1572872 | tf_op jit(solution)/shard_map/ppermute | solution.py:546
  178.2 27.3 %collective-permute-start.12 = (bf16[2048,128]{1,0:T(8,128)(2,1)}, bf16[2048,128]{1,0:T(8,128)(2,1)S(1)}, u32[]{:S(2)}, u32[]{:S(2)}) collective-permute-start(bf16[2048,128]{1,0:T(8,128)(2,1)} %add_convert_fusion.1), channel_id=1, source_target_pairs={{0,2},{1,3},{2,0},{3,1},{4,6},{5,7},{6,4},{7,5},{8,10},{9,11},{10,... | collective-permute-start | bytes 1572872 | tf_op jit(solution)/shard_map/ppermute | solution.py:546
